TPU v7x, 32 devices: a whole 2x2x4 slice. The times are simulated.
32 devices in a mesh: tile: 16 (over z, x, core), mem: 2 (over y).
Axes of the slice: x: 2, y: 2, z: 4, core: 2. Of those that a mesh axis runs over, the one named last changes fastest.
Arguments:
- atm_latent: bfloat16 [2, 8192, 256], P('mem', 'tile'), may hold values from -6 to 6
- ocean_state: bfloat16 [2, 8, 8192, 256], P('mem', None, 'tile'), may hold values from -6 to 6
- depth: int32 [8192], P('tile'), may hold values from 0 to 8
- src_blocks: int32 [64, 4], P('tile'), may hold values from 0 to 63, as said below
- live: int32 [64], P('tile'), may hold values from 2 to 4
- remap_weight: bfloat16 [64, 4, 128, 128], P('tile'), may hold values from -0.25 to 0.25
- conv_weight: bfloat16 [3, 3, 256, 256], replicated, may hold values from -0.125 to 0.125
- qkv_weight: bfloat16 [256, 768], replicated, may hold values from -5 to 5
- out_weight: bfloat16 [256, 256], replicated, may hold values from -0.375 to 0.375
Outputs:
- ocean_out: bfloat16 [2, 8, 8192, 256], P('mem', None, 'tile')
Inputs may be any that keep to these rules, and one draw needn't show every extreme that they name: `src_blocks`: the owner tile of a listed atmosphere block (block // 4) lies within 1 tile indices of the tile owning the ocean block (ocean block // 4); some entry of every tile lies exactly 1 away.
All inputs are finite; a program needn't handle non-finite values.
Results may differ from a plain program's by a relative error of at most 0.0055.
Values may be sent and summed in bfloat16 or wider, within the bound.
No kernel may reach another device: no remote copies, remote signals or barrier semaphores. Data moves between devices by JAX's collectives and lax.ppermute only.
A program may use at most 128 MiB of HBM per device.

v0:
```python
import math

import jax
import jax.numpy as jnp
from jax import lax
from jax.sharding import PartitionSpec as P

HEADS = 4
R = 1


EPS = 1e-06


def with_halo(cells, sides, width):
    for axis, dim in sides:
        count = lax.axis_size(axis)
        ends = count - 1
        head = lax.slice_in_dim(cells, 0, width, axis=dim)
        tail = lax.slice_in_dim(cells, cells.shape[dim] - width, cells.shape[dim], axis=dim)
        cells = jnp.concatenate(
            [
                lax.ppermute(tail, axis, [(i, (i + 1) % count) for i in range(ends)]),
                cells,
                lax.ppermute(head, axis, [((i + 1) % count, i) for i in range(ends)]),
            ],
            axis=dim,
        )
    return cells


def attend_columns(block, wet_block, qkv_weight, out_weight):
    mem_n, lev, count, width = block.shape
    head_size = width // HEADS
    xf = block.astype(jnp.float32)
    normed = (xf * lax.rsqrt(jnp.mean(xf * xf, axis=-1, keepdims=True) + EPS)).astype(jnp.bfloat16)
    qkv = jnp.dot(normed.reshape(-1, width), qkv_weight, preferred_element_type=jnp.float32).astype(
        jnp.bfloat16
    )
    qkv = qkv.reshape(mem_n * lev, count, 3, HEADS, head_size)
    query = qkv[:, :, 0]
    keys = qkv[:, :, 1]
    values = qkv[:, :, 2]
    scores = jnp.einsum("tnhd,snhd->nhts", query, keys, preferred_element_type=jnp.float32) * (
        1.0 / math.sqrt(head_size)
    )
    allowed = jnp.maximum(wet_block, 1.0 - wet_block[0:1])
    key_ok = jnp.tile(allowed.T, (1, mem_n))
    scores = jnp.where(key_ok[:, None, None, :] > 0, scores, -jnp.inf)
    top = jnp.max(scores, axis=-1, keepdims=True)
    probs = jnp.exp(scores - top)
    probs = probs / jnp.sum(probs, axis=-1, keepdims=True)
    attended = jnp.einsum(
        "nhts,snhd->tnhd", probs, values, preferred_element_type=jnp.float32
    ).astype(jnp.bfloat16)
    proj = jnp.dot(attended.reshape(-1, width), out_weight, preferred_element_type=jnp.float32)
    proj = proj.reshape(mem_n, lev, count, width)
    return (xf + wet_block[None, :, :, None] * proj).astype(jnp.bfloat16)


def body(
    atm_latent,
    ocean_state,
    depth,
    src_blocks,
    live,
    remap_weight,
    conv_weight,
    qkv_weight,
    out_weight,
):
    lev = ocean_state.shape[1]
    cells = ocean_state.shape[2]
    width = ocean_state.shape[3]
    npair = remap_weight.shape[1]
    cols = remap_weight.shape[2]
    rows = cells // cols
    atm_blk = atm_latent.shape[1] // cols
    levels = jnp.arange(lev, dtype=jnp.int32)
    wet = (levels[:, None] < depth[None, :]).astype(jnp.float32)
    surface = (levels == 0).astype(jnp.float32)
    pair_on = (jnp.arange(npair, dtype=jnp.int32)[None, :] < live[:, None]).astype(jnp.bfloat16)
    weights = remap_weight * pair_on[:, :, None, None]
    window = with_halo(atm_latent[0], (("tile", 0),), R * atm_latent.shape[1])
    first = (lax.axis_index("tile") - R) * atm_blk
    local_ids = src_blocks - first
    picked = window.reshape(-1, cols, width)[local_ids]
    forcing = jnp.einsum("bpij,bpjc->bic", weights, picked, preferred_element_type=jnp.float32)
    forcing = forcing.reshape(cells, width)
    masked = (ocean_state[0] * wet[:, :, None]).astype(jnp.bfloat16)
    padded = with_halo(masked.reshape(lev, rows, cols, width), (("tile", 1),), 1)
    padded = jnp.pad(padded, ((0, 0), (0, 0), (1, 1), (0, 0)))
    conv = jnp.zeros((lev * rows * cols, width), jnp.float32)
    for shift_row in range(3):
        for shift_col in range(3):
            stencil = padded[:, shift_row : shift_row + rows, shift_col : shift_col + cols].reshape(
                -1, width
            )
            conv = conv + jnp.dot(
                stencil, conv_weight[shift_row, shift_col], preferred_element_type=jnp.float32
            )
    total = conv.reshape(lev, cells, width) + surface[:, None, None] * forcing[None]
    mixed = (masked.astype(jnp.float32) + wet[:, :, None] * total).astype(jnp.bfloat16)
    member_count = lax.axis_size("mem")
    share = cells // member_count
    tokens = mixed.reshape(1, lev, member_count, share, width)
    wet_tokens = wet.reshape(1, lev, member_count, share, 1).astype(jnp.bfloat16)
    block = lax.all_to_all(tokens, "mem", split_axis=2, concat_axis=0, tiled=True)[:, :, 0]
    wet_block = lax.all_to_all(wet_tokens, "mem", split_axis=2, concat_axis=0, tiled=True)[
        0, :, 0, :, 0
    ].astype(jnp.float32)
    relaid = attend_columns(block, wet_block, qkv_weight, out_weight)[:, :, None]
    returned = lax.all_to_all(relaid, "mem", split_axis=0, concat_axis=2, tiled=True)
    return returned.reshape(1, lev, cells, width)


def solution(mesh):
    return jax.shard_map(
        body,
        mesh=mesh,
        in_specs=(
            P("mem", "tile", None),
            P("mem", None, "tile", None),
            P("tile"),
            P("tile", None),
            P("tile"),
            P("tile", None, None, None),
            P(),
            P(),
            P(),
        ),
        out_specs=P("mem", None, "tile", None),
        check_vma=False,
    )
```

profile of v0, /device:TPU:18, one launch (start us, length us, event | category | flops | bytes accessed | tf_op | source)
XLA Modules:
  0.0 173.6 jit_solution(4706970381357688822)
XLA Ops:
  0.0 2.0 %collective-permute-start.2 = (bf16[512,256]{1,0:T(8,128)(2,1)}, bf16[512,256]{1,0:T(8,128)(2,1)S(1)}, u32[]{:S(2)}, u32[]{:S(2)}) collective-permute-start(bf16[512,256]{1,0:T(8,128)(2,1)} %bitcast.148), channel_id=1, source_target_pairs={{0,2},{2,4},{4,6},{6,8},{8,10},{10,12},{12,14},{14,16},{16,18},{18... | collective-permute-start | bytes 786440 | tf_op jit(solution)/shard_map/ppermute | solution.py:23
  2.1 3.6 %collective-permute-start.3 = (bf16[512,256]{1,0:T(8,128)(2,1)}, bf16[512,256]{1,0:T(8,128)(2,1)}, u32[]{:S(2)}, u32[]{:S(2)}) collective-permute-start(bf16[512,256]{1,0:T(8,128)(2,1)} %bitcast.149), channel_id=1, source_target_pairs={{2,0},{4,2},{6,4},{8,6},{10,8},{12,10},{14,12},{16,14},{18,16},{20... | collective-permute-start | bytes 786440 | tf_op jit(solution)/shard_map/ppermute | solution.py:25
  5.7 2.0 %convert_element_type.189 = f32[1,8,512,256]{3,2,1,0:T(8,128)S(1)} convert(bf16[1,8,512,256]{3,2,1,0:T(8,128)(2,1)} %param.10) | non-fusion elementwise | flops 1048576 | bytes 6291456 | tf_op jit(solution)/shard_map/convert_element_type | solution.py:90
  8.5 1.0 fusion.56
  10.0 1.9 %collective-permute-start = (bf16[8,1,128,256]{3,2,1,0:T(8,128)(2,1)}, bf16[8,1,128,256]{3,2,1,0:T(8,128)(2,1)}, u32[]{:S(2)}, u32[]{:S(2)}) collective-permute-start(bf16[8,1,128,256]{3,2,1,0:T(8,128)(2,1)} %get-tuple-element.16), channel_id=1, source_target_pairs={{0,2},{2,4},{4,6},{6,8},{8,10},{10,12},{12,14},{14,16},{16,18},{18... | collective-permute-start | bytes 1572872 | tf_op jit(solution)/shard_map/ppermute | solution.py:23
  11.9 3.6 %collective-permute-start.1 = (bf16[8,1,128,256]{3,2,1,0:T(8,128)(2,1)}, bf16[8,1,128,256]{3,2,1,0:T(8,128)(2,1)}, u32[]{:S(2)}, u32[]{:S(2)}) collective-permute-start(bf16[8,1,128,256]{3,2,1,0:T(8,128)(2,1)} %get-tuple-element.17), channel_id=1, source_target_pairs={{2,0},{4,2},{6,4},{8,6},{10,8},{12,10},{14,12},{16,14},{18,16},{20... | collective-permute-start | bytes 1572872 | tf_op jit(solution)/shard_map/ppermute | solution.py:25
  16.1 3.8 %all-to-all-start.1 = ((bf16[1,8,2,256,1]{3,1,4,0,2:T(8,128)(2,1)}), bf16[1,8,2,256,1]{3,1,4,0,2:T(8,128)(2,1)}, u32[]{:S(2)}, u32[]{:S(2)}) async-start(bf16[1,8,2,256,1]{3,1,4,0,2:T(8,128)(2,1)} %convert_convert_fusion), calls=%async_computation.1 | async-start | bytes 16384 | tf_op jit(solution)/shard_map/all_to_all | solution.py:109
  20.0 2.9 %multiply_convert_fusion = bf16[1,8,512,256]{3,2,1,0:T(8,128)(2,1)} fusion(f32[8,512]{1,0:T(8,128)S(1)} %fusion.48, bf16[1,8,512,256]{3,2,1,0:T(8,128)(2,1)} %param.10), kind=kLoop, calls=%fused_computation.35 | loop fusion | flops 3145728 | bytes 4210688 | tf_op jit(solution)/shard_map/convert_element_type | solution.py:90
  25.5 1.1 pad_maximum_fusion.2
  26.6 1.7 gather_fusion
  28.3 1.7 %fusion.23 = f32[4,128,256,1]{2,1,3,0:T(8,128)S(1)} fusion(bf16[4,4,128,256]{3,2,1,0:T(8,128)(2,1)} %bitcast.145, bf16[4,4,128,128]{3,2,1,0:T(8,128)(2,1)} %param.14, bf16[4,4]{1,0:T(4,128)(2,1)} %fusion.50), kind=kOutput, calls=%fused_computation.48 | convolution fusion | flops 134479872 | bytes 2097184 | tf_op jit(solution)/shard_map/bpij,bpjc->bic/dot_general | solution.py:88
  30.1 2.8 %fusion.19 = bf16[8,6,130,256]{3,2,1,0:T(8,128)(2,1)S(1)} fusion(bf16[8,1,128,256]{3,2,1,0:T(8,128)(2,1)} %collective-permute-done.1, bf16[8,4,128,256]{3,2,1,0:T(8,128)(2,1)S(1)} %multiply_convert_fusion.1, bf16[8,1,128,256]{3,2,1,0:T(8,128)(2,1)} %collective-permute-done), kind=kLoop, calls=%fused_computation.43 | loop fusion | flops 19169280 | bytes 6340608 | tf_op jit(solution)/shard_map/concatenate | solution.py:21
  32.9 5.2 %fusion.55 = (bf16[8,4,128,256]{3,2,1,0:T(8,128)(2,1)S(1)}, bf16[8,4,128,256]{3,2,1,0:T(8,128)(2,1)S(1)}, bf16[8,4,128,256]{3,2,1,0:T(8,128)(2,1)S(1)}, bf16[8,4...) fusion(bf16[8,6,130,256]{3,2,1,0:T(8,128)(2,1)S(1)} %fusion.19), kind=kLoop, calls=%fused_computation.94 | loop fusion | bytes 25165824 | tf_op jit(solution)/shard_map/slice | solution.py:96
  39.5 1.5 pad_maximum_fusion
  43.3 0.8 copy-done.4
  44.9 0.8 convolution_add_fusion.2
  45.6 0.8 convolution_add_fusion.1
  47.1 1.5 copy-done.3
  48.6 1.0 add_convert_fusion
  49.6 1.5 copy.27
  51.1 3.9 %all-to-all-start = ((bf16[1,8,2,256,256]{4,3,1,0,2:T(8,128)(2,1)}), bf16[1,8,2,256,256]{4,3,1,0,2:T(8,128)(2,1)S(1)}, u32[]{:S(2)}, u32[]{:S(2)}) async-start(bf16[1,8,2,256,256]{4,3,1,0,2:T(8,128)(2,1)} %copy.27), calls=%async_computation | async-start | bytes 4194304 | tf_op jit(solution)/shard_map/all_to_all | solution.py:108
  56.5 24.6 %all-to-all-done = bf16[1,8,2,256,256]{4,3,1,0,2:T(8,128)(2,1)S(1)} async-done(((bf16[1,8,2,256,256]{4,3,1,0,2:T(8,128)(2,1)}), bf16[1,8,2,256,256]{4,3,1,0,2:T(8,128)(2,1)S(1)}, u32[]{:S(2)}, u32[]{:S(2)}) %all-to-all-start) | async-done | bytes 2097184 | tf_op jit(solution)/shard_map/all_to_all | solution.py:108
  82.5 4.4 %convolution_convert_fusion = bf16[4096,768]{1,0:T(8,128)(2,1)} fusion(bf16[4096,256]{1,0:T(8,128)(2,1)S(1)} %fusion.7, bf16[256,768]{1,0:T(8,128)(2,1)S(1)} %copy-done), kind=kOutput, calls=%fused_computation.8 | convolution fusion | flops 1613758464 | bytes 8781824 | tf_op jit(solution)/shard_map/dot_general | solution.py:37
  86.9 18.6 %reshape.271 = bf16[16,256,3,4,64]{4,3,2,1,0:T(4,128)(2,1)} reshape(bf16[4096,768]{1,0:T(8,128)(2,1)} %convolution_convert_fusion) | data formatting | bytes 12582912 | tf_op jit(solution)/shard_map/reshape | solution.py:40
  105.5 9.9 %fusion.54 = (bf16[16,256,1,4,64]{4,3,2,1,0:T(4,128)(2,1)S(1)}, bf16[16,256,1,4,64]{4,3,2,1,0:T(4,128)(2,1)}, bf16[16,256,1,4,64]{4,3,2,1,0:T(4,128)(2,1)}) fusion(bf16[16,256,3,4,64]{4,3,2,1,0:T(4,128)(2,1)} %reshape.271), kind=kLoop, calls=%fused_computation.93 | loop fusion | bytes 12582912 | tf_op jit(solution)/shard_map/slice | solution.py:43
  115.4 10.3 %fusion.2 = (f32[256,4,16]{2,1,0:T(4,128)S(1)}, f32[256,4,16,16]{2,3,1,0:T(8,128)S(1)}) fusion(pred[256,16]{1,0:T(8,128)(4,1)S(1)} %copy.31, bf16[16,256,1,4,64]{4,3,2,1,0:T(4,128)(2,1)} %get-tuple-element.7, bf16[16,256,1,4,64]{4,3,2,1,0:T(4,128)(2,1)} %get-tuple-element.6), kind=kOutput, calls=%fused_computation.7 | convolution fusion | flops 34324480 | bytes 5312512 | tf_op jit(solution)/shard_map/tnhd,snhd->nhts/dot_general | solution.py:44
  125.6 3.4 %fusion.4 = f32[256,4,16]{2,1,0:T(4,128)S(1)} fusion(f32[256,4,16,16]{2,3,1,0:T(8,128)S(1)} %get-tuple-element.21, f32[256,4,16]{2,1,0:T(4,128)S(1)} %get-tuple-element.20, pred[256,16]{1,0:T(8,128)(4,1)S(1)} %copy.31), kind=kLoop, calls=%fused_computation.10 | loop fusion | flops 1032192 | bytes 1183744 | tf_op jit(solution)/shard_map/reduce_sum | solution.py:52
  129.0 6.6 %convert_bitcast_fusion = bf16[16,256,4,64]{3,0,2,1:T(8,128)(2,1)} fusion(f32[256,4,16,16]{2,3,1,0:T(8,128)S(1)} %get-tuple-element.21, f32[256,4,16]{2,1,0:T(4,128)S(1)} %fusion.4, f32[256,4,16]{2,1,0:T(4,128)S(1)} %get-tuple-element.20, pred[256,16]{1,0:T(8,128)(4,1)S(1)} %copy.31, bf16[16,256,1,4,64]{4,3,2,1,0:T(4,128)(2,1)S(1)} %get-tuple-element.5), kind=kOutput, calls=%fused_computation.29 | convolution fusion | flops 35651584 | bytes 5378048 | tf_op jit(solution)/shard_map/nhts,snhd->tnhd/dot_general | solution.py:53
  135.6 6.0 %copy.35 = bf16[16,256,4,64]{1,3,2,0:T(8,128)(2,1)} copy(bf16[16,256,4,64]{3,0,2,1:T(8,128)(2,1)} %convert_bitcast_fusion) | data formatting | bytes 4194304 | tf_op jit(solution)/shard_map/convert_element_type | solution.py:55
  141.6 2.8 %fusion.22 = bf16[2,8,1,256,256]{4,3,1,2,0:T(8,128)(2,1)S(1)} fusion(bf16[2,8,256,256]{2,3,1,0:T(8,128)(2,1)} %bitcast.146, f32[8,256]{1,0:T(8,128)S(1)} %get-tuple-element.18, bf16[1,8,2,256,256]{4,3,1,0,2:T(8,128)(2,1)S(1)} %all-to-all-done, bf16[256,256]{1,0:T(8,128)(2,1)S(1)} %copy-done.11), kind=kOutput, calls=%fused_computation.46 | convolution fusion | flops 541065216 | bytes 6430720 | tf_op jit(solution)/shard_map/dot_general | solution.py:56
  144.3 27.8 %all_to_all.39 = bf16[2,8,1,256,256]{4,3,1,2,0:T(8,128)(2,1)S(1)} all-to-all(bf16[2,8,1,256,256]{4,3,1,2,0:T(8,128)(2,1)S(1)} %fusion.22), channel_id=1, replica_groups=mesh['tile'=16,'mem'=2] {'mem'}, dimensions={0} | all-to-all | bytes 4194304 | tf_op jit(solution)/shard_map/all_to_all | solution.py:113
  172.1 1.5 copy.38
  (56 shorter events, 12.4 us)
Async XLA Ops:
  0.0 82.5 %copy-start = (bf16[256,768]{1,0:T(8,128)(2,1)S(1)}, bf16[256,768]{1,0:T(8,128)(2,1)}, u32[]{:S(2)}) copy-start(bf16[256,768]{1,0:T(8,128)(2,1)} %param.16) | copy-start | bytes 1179652
  0.0 7.7 %copy-start.8 = (s32[512]{0:T(512)S(1)}, s32[512]{0:T(512)}, u32[]{:S(2)}) copy-start(s32[512]{0:T(512)} %param.11) | copy-start | bytes 6148
  0.0 24.8 %collective-permute-start.2 = (bf16[512,256]{1,0:T(8,128)(2,1)}, bf16[512,256]{1,0:T(8,128)(2,1)S(1)}, u32[]{:S(2)}, u32[]{:S(2)}) collective-permute-start(bf16[512,256]{1,0:T(8,128)(2,1)} %bitcast.148), channel_id=1, source_target_pairs={{0,2},{2,4},{4,6},{6,8},{8,10},{10,12},{12,14},{14,16},{16,18},{18... | collective-permute-start | bytes 786440 | tf_op jit(solution)/shard_map/ppermute | solution.py:23
  2.1 23.5 %collective-permute-start.3 = (bf16[512,256]{1,0:T(8,128)(2,1)}, bf16[512,256]{1,0:T(8,128)(2,1)}, u32[]{:S(2)}, u32[]{:S(2)}) collective-permute-start(bf16[512,256]{1,0:T(8,128)(2,1)} %bitcast.149), channel_id=1, source_target_pairs={{2,0},{4,2},{6,4},{8,6},{10,8},{12,10},{14,12},{16,14},{18,16},{20... | collective-permute-start | bytes 786440 | tf_op jit(solution)/shard_map/ppermute | solution.py:25
  7.7 2.3 %copy-start.2 = (f32[1,8,512,256]{3,2,1,0:T(8,128)}, f32[1,8,512,256]{3,2,1,0:T(8,128)S(1)}, u32[]{:S(2)}) copy-start(f32[1,8,512,256]{3,2,1,0:T(8,128)S(1)} %convert_element_type.189) | copy-start | bytes 12582916
  8.4 14.4 %copy-start.9 = (s32[4,4]{1,0:T(4,128)S(1)}, s32[4,4]{1,0:T(4,128)}, u32[]{:S(2)}) copy-start(s32[4,4]{1,0:T(4,128)} %param.12) | copy-start | bytes 196
  8.5 15.1 %copy-start.12 = (s32[4]{0:T(128)S(1)}, s32[4]{0:T(128)}, u32[]{:S(2)}) copy-start(s32[4]{0:T(128)} %param.13) | copy-start | bytes 52
  8.5 17.0 %copy-start.6 = (bf16[1,512,256]{2,1,0:T(8,128)(2,1)S(1)}, bf16[1,512,256]{2,1,0:T(8,128)(2,1)}, u32[]{:S(2)}) copy-start(bf16[1,512,256]{2,1,0:T(8,128)(2,1)} %param.9) | copy-start | bytes 786436
  10.0 20.1 %collective-permute-start = (bf16[8,1,128,256]{3,2,1,0:T(8,128)(2,1)}, bf16[8,1,128,256]{3,2,1,0:T(8,128)(2,1)}, u32[]{:S(2)}, u32[]{:S(2)}) collective-permute-start(bf16[8,1,128,256]{3,2,1,0:T(8,128)(2,1)} %get-tuple-element.16), channel_id=1, source_target_pairs={{0,2},{2,4},{4,6},{6,8},{8,10},{10,12},{12,14},{14,16},{16,18},{18... | collective-permute-start | bytes 1572872 | tf_op jit(solution)/shard_map/ppermute | solution.py:23
  11.9 18.2 %collective-permute-start.1 = (bf16[8,1,128,256]{3,2,1,0:T(8,128)(2,1)}, bf16[8,1,128,256]{3,2,1,0:T(8,128)(2,1)}, u32[]{:S(2)}, u32[]{:S(2)}) collective-permute-start(bf16[8,1,128,256]{3,2,1,0:T(8,128)(2,1)} %get-tuple-element.17), channel_id=1, source_target_pairs={{2,0},{4,2},{6,4},{8,6},{10,8},{12,10},{14,12},{16,14},{18,16},{20... | collective-permute-start | bytes 1572872 | tf_op jit(solution)/shard_map/ppermute | solution.py:25
  16.1 34.9 %all-to-all-start.1 = ((bf16[1,8,2,256,1]{3,1,4,0,2:T(8,128)(2,1)}), bf16[1,8,2,256,1]{3,1,4,0,2:T(8,128)(2,1)}, u32[]{:S(2)}, u32[]{:S(2)}) async-start(bf16[1,8,2,256,1]{3,1,4,0,2:T(8,128)(2,1)} %convert_convert_fusion), calls=%async_computation.1 | async-start | bytes 16384 | tf_op jit(solution)/shard_map/all_to_all | solution.py:109
  24.8 0.7 copy-start.7
  32.9 5.2 %copy-start.5 = (bf16[3,3,256,256]{3,2,1,0:T(8,128)(2,1)S(1)}, bf16[3,3,256,256]{3,2,1,0:T(8,128)(2,1)}, u32[]{:S(2)}) copy-start(bf16[3,3,256,256]{3,2,1,0:T(8,128)(2,1)} %param.15) | copy-start | bytes 3538948
  42.5 1.6 copy-start.4
  46.4 2.2 %copy-start.3 = (f32[1,8,512,256]{3,2,1,0:T(8,128)S(1)}, f32[1,8,512,256]{3,2,1,0:T(8,128)}, u32[]{:S(2)}) copy-start(f32[1,8,512,256]{3,2,1,0:T(8,128)} %copy-done.2) | copy-start | bytes 12582916
  46.4 2.2 %copy-start.10 = (f32[8]{0:T(128)S(1)}, f32[8]{0:T(128)}, u32[]{:S(2)}) copy-start(f32[8]{0:T(128)} %compare_convert_fusion.1) | copy-start | bytes 100
  51.1 30.0 %all-to-all-start = ((bf16[1,8,2,256,256]{4,3,1,0,2:T(8,128)(2,1)}), bf16[1,8,2,256,256]{4,3,1,0,2:T(8,128)(2,1)S(1)}, u32[]{:S(2)}, u32[]{:S(2)}) async-start(bf16[1,8,2,256,256]{4,3,1,0,2:T(8,128)(2,1)} %copy.27), calls=%async_computation | async-start | bytes 4194304 | tf_op jit(solution)/shard_map/all_to_all | solution.py:108
  135.6 6.0 %copy-start.11 = (bf16[256,256]{1,0:T(8,128)(2,1)S(1)}, bf16[256,256]{1,0:T(8,128)(2,1)}, u32[]{:S(2)}) copy-start(bf16[256,256]{1,0:T(8,128)(2,1)} %param.17) | copy-start | bytes 393220
  141.6 32.0 %copy-start.1 = (bf16[256,768]{1,0:T(8,128)(2,1)S(1)}, bf16[256,768]{1,0:T(8,128)(2,1)}, u32[]{:S(2)}) copy-start(bf16[256,768]{1,0:T(8,128)(2,1)} %param.16) | copy-start | bytes 1179652
where the time goes:
time: 175 us; the launch traced here: 174 us
  local copies, waits for them, and re-layouts  49 us (28%)
  matrix products  32.4 us (19%)
  blocking collectives  27.8 us (16%)
  waiting for transfers between devices  24.6 us (14%)
  other arithmetic  20.5 us (12%)
  starting transfers between devices  19 us (11%)
    all_to_all x1, blocking collectives, body(): lax.all_to_all(relaid, 'mem', split_axis=0, concat_axis=2, tiled=True)  27.8 us
    all_to_all x1, waiting for transfers between devices, body(): lax.all_to_all(tokens, 'mem', split_axis=2, concat_axis=0, tiled=True)  24.6 us
    reshape x1, local copies, waits for them, and re-layouts, attend_columns(): qkv = qkv.reshape(mem_n * lev, count, 3, HEADS, head_size)  18.6 us
    dot_general x1, matrix products, attend_columns(): jnp.einsum('tnhd,snhd->nhts', query, keys, preferred_element_type=jnp.flo...  10.3 us
    slice x1, local copies, waits for them, and re-layouts, attend_columns(): values = qkv[:, :, 2]  9.85 us
    ppermute x2, starting transfers between devices, with_halo(): lax.ppermute(head, axis, [((i + 1) % count, i) for i in range(ends)])  7.29 us
    dot_general x9, matrix products, body(): jnp.dot(stencil, conv_weight[shift_row, shift_col], preferred_element_typ...  6.64 us
    dot_general x1, matrix products, attend_columns(): jnp.einsum('nhts,snhd->tnhd', probs, values, preferred_element_type=jnp.f...  6.57 us
  transfers between devices with their start and end apart: 6, of which 1 were waited for; matrix products, arithmetic and copies ran while one was open for 19% of the time, Pallas kernels for 0%

commit v1 on v0

v1 whole, which is shorter than its diff:
```python
import functools
import math

import jax
import jax.numpy as jnp
from jax import lax
from jax.experimental import pallas as pl
from jax.experimental.pallas import tpu as pltpu
from jax.sharding import PartitionSpec as P

HEADS = 4
R = 1
GROUP = 16
EPS = 1e-06
NEG = -1e30
F32 = jnp.float32
BF16 = jnp.bfloat16
VMEM_LIMIT = 56 * 1024 * 1024


def params(steps=1):
    return pltpu.CompilerParams(
        dimension_semantics=("arbitrary",) * steps, vmem_limit_bytes=VMEM_LIMIT
    )


def cost(flops, nbytes):
    return pl.CostEstimate(flops=int(flops), bytes_accessed=int(nbytes), transcendentals=0)


def stencil(taps, weight_ref, cols):
    count = taps[0].shape[0]
    sums = []
    for dc in range(3):
        acc = jnp.dot(taps[0], weight_ref[0, dc], preferred_element_type=F32)
        for dr in (1, 2):
            acc = acc + jnp.dot(taps[dr], weight_ref[dr, dc], preferred_element_type=F32)
        sums.append(acc)
    col = lax.broadcasted_iota(jnp.int32, (count, 1), 0) % cols
    left = jnp.where(col == 0, 0.0, pltpu.roll(sums[0], 1, axis=0))
    right = jnp.where(col == cols - 1, 0.0, pltpu.roll(sums[2], count - 1, axis=0))
    return sums[1] + left + right


def finish(masked, wet, total, mixed_ref, normed_ref):
    mixed = (masked.astype(F32) + wet * total).astype(BF16)
    mixed_ref[0] = mixed
    mf = mixed.astype(F32)
    mean = jnp.mean(mf * mf, axis=-1, keepdims=True)
    normed_ref[0] = (mf * lax.rsqrt(mean + EPS)).astype(BF16)


def wet_of(depth_ref, level, width):
    wet = (depth_ref[...] > level.astype(F32)).astype(F32)
    return jnp.concatenate([wet] * (width // wet.shape[1]), axis=1)


def inner_kernel(cols, first, state_ref, depth_ref, weight_ref, mixed_ref, normed_ref):
    width = state_ref.shape[-1]
    wet = wet_of(depth_ref, pl.program_id(0) + first, width)
    x = state_ref[0, 0] * wet.astype(BF16)
    count = x.shape[0] - 2 * cols
    taps = [x[dr * cols : dr * cols + count] for dr in range(3)]
    total = stencil(taps, weight_ref, cols)
    finish(taps[1], wet[cols : cols + count], total, mixed_ref, normed_ref)


def surface_kernel(
    cols,
    ids_ref,
    live_ref,
    state_ref,
    depth_ref,
    weight_ref,
    before_ref,
    atm_ref,
    after_ref,
    remap_ref,
    mixed_ref,
    normed_ref,
    edge_ref,
    window_ref,
    forcing_ref,
):
    width = state_ref.shape[-1]
    own = atm_ref.shape[1]
    blocks, pairs = remap_ref.shape[0], remap_ref.shape[1]
    window_ref[0:own] = before_ref[...]
    window_ref[own : 2 * own] = atm_ref[0]
    window_ref[2 * own : 3 * own] = after_ref[...]
    for b in range(blocks):
        acc = jnp.zeros((cols, width), F32)
        for p in range(pairs):
            on = (p < live_ref[b]).astype(F32)
            start = pl.multiple_of(ids_ref[b, p] * cols, cols)
            acc = acc + on * jnp.dot(
                remap_ref[b, p], window_ref[pl.ds(start, cols), :], preferred_element_type=F32
            )
        forcing_ref[b * cols : (b + 1) * cols] = acc
    wet = wet_of(depth_ref, jnp.int32(0), width)
    x = state_ref[0, 0] * wet.astype(BF16)
    count = x.shape[0] - 2 * cols
    taps = [x[dr * cols : dr * cols + count] for dr in range(3)]
    total = stencil(taps, weight_ref, cols) + forcing_ref[cols : cols + count]
    finish(taps[1], wet[cols : cols + count], total, mixed_ref, normed_ref)
    edge_ref[0:cols] = forcing_ref[0:cols]
    edge_ref[cols : 2 * cols] = forcing_ref[cols + count :]


def edge_kernel(
    cols,
    state_ref,
    depth_ref,
    weight_ref,
    before_ref,
    after_ref,
    forcing_ref,
    mixed_ref,
    normed_ref,
):
    width = state_ref.shape[-1]
    level = pl.program_id(0)
    wet = wet_of(depth_ref, level, width)
    x = state_ref[0, 0] * wet.astype(BF16)
    cells = x.shape[0]
    top = [before_ref[...], x[0:cols], x[cols : 2 * cols]]
    low = [x[cells - 2 * cols : cells - cols], x[cells - cols :], after_ref[...]]
    taps = [jnp.concatenate([a, b], axis=0) for a, b in zip(top, low)]
    total = stencil(taps, weight_ref, cols)
    total = total + jnp.where(level == 0, 1.0, 0.0) * forcing_ref[...]
    edge_wet = jnp.concatenate([wet[0:cols], wet[cells - cols :]], axis=0)
    finish(taps[1], edge_wet, total, mixed_ref, normed_ref)


def attend_kernel(members, nparts, *refs):
    refs = list(refs)
    take = lambda k: [refs.pop(0) for _ in range(k)]
    normed = [take(nparts) for _ in range(members)]
    mixed = take(nparts)
    depth_ref, bias_ref, qkv_ref, wo_ref = take(4)
    if len(refs) == 6:
        take(1)
    out_ref, q_ref, k_ref, v_ref, att_ref = refs
    lev, count, width = q_ref.shape
    head = width // HEADS
    pair = 2 * head
    for m in range(members):
        x = jnp.concatenate([p[...].reshape(-1, width) for p in normed[m]], axis=0)
        rows = slice(m * lev, (m + 1) * lev)
        if m == 0:
            q = jnp.dot(x, qkv_ref[:, 0:width], preferred_element_type=F32).astype(BF16)
            q_ref[...] = (q * (1.0 / math.sqrt(head))).astype(BF16).reshape(lev, count, width)
        k = jnp.dot(x, qkv_ref[:, width : 2 * width], preferred_element_type=F32)
        k_ref[rows] = k.astype(BF16).reshape(lev, count, width)
        v = jnp.dot(x, qkv_ref[:, 2 * width :], preferred_element_type=F32)
        v_ref[rows] = v.astype(BF16).reshape(lev, count, width)
    nq, nk = lev * GROUP, members * lev * GROUP
    qc = lax.broadcasted_iota(jnp.int32, (nq, nk), 0) % GROUP
    kc = lax.broadcasted_iota(jnp.int32, (nq, nk), 1) % GROUP
    same = jnp.where(qc == kc, 0.0, NEG)
    lane = lax.broadcasted_iota(jnp.int32, (1, pair), 1)
    low = (lane < head).astype(F32).astype(BF16)
    high = (lane >= head).astype(F32).astype(BF16)
    for g in range(count // GROUP):
        cells = slice(g * GROUP, (g + 1) * GROUP)
        bias = same + jnp.concatenate([bias_ref[g]] * members, axis=1)
        bias = jnp.concatenate([bias, bias], axis=0)
        for h in range(HEADS // 2):
            lanes = slice(h * pair, (h + 1) * pair)
            q = q_ref[:, cells, lanes].reshape(nq, pair)
            q = jnp.concatenate([q * low, q * high], axis=0)
            k = k_ref[:, cells, lanes].reshape(nk, pair)
            v = v_ref[:, cells, lanes].reshape(nk, pair)
            s = lax.dot_general(q, k, (((1,), (1,)), ((), ())), preferred_element_type=F32) + bias
            p = jnp.exp(s - jnp.max(s, axis=-1, keepdims=True))
            norm = 1.0 / jnp.sum(p, axis=-1, keepdims=True)
            o = jnp.dot(p.astype(BF16), v, preferred_element_type=F32) * norm
            o = jnp.where(lane < head, o[:nq], o[nq:])
            att_ref[:, cells, lanes] = o.astype(BF16).reshape(lev, GROUP, pair)
    proj = jnp.dot(att_ref[...].reshape(-1, width), wo_ref[...], preferred_element_type=F32)
    base = jnp.concatenate([p[...].reshape(-1, width) for p in mixed], axis=0).astype(F32)
    for l in range(lev):
        rows = slice(l * count, (l + 1) * count)
        wet = wet_of(depth_ref, jnp.int32(l), width)
        out_ref[0, l] = (base[rows] + wet * proj[rows]).astype(BF16)


def attend(normed, mixed, depth_b, bias, qkv_weight, out_weight, cols, place, out, shape):
    members, nparts = len(normed), len(mixed)
    lev = sum(p.shape[0] for p in mixed)
    width = shape[-1]
    nblocks = mixed[0].shape[1] // cols
    groups = cols // GROUP
    part = [pl.BlockSpec((p.shape[0], cols, width), lambda i: (0, i, 0)) for p in mixed]
    in_specs = part * (members + 1) + [
        pl.BlockSpec((cols, depth_b.shape[1]), lambda i: (place(i), 0)),
        pl.BlockSpec((groups, 1, bias.shape[2]), lambda i: (place(i), 0, 0)),
        pl.BlockSpec(qkv_weight.shape, lambda i: (0, 0)),
        pl.BlockSpec(out_weight.shape, lambda i: (0, 0)),
    ]
    args = sum(normed, []) + mixed + [depth_b, bias, qkv_weight, out_weight]
    alias = {}
    if out is not None:
        in_specs.append(pl.BlockSpec(memory_space=pl.ANY))
        alias = {len(args): 0}
        args.append(out)
    tokens = lev * cols * nblocks
    return pl.pallas_call(
        functools.partial(attend_kernel, members, nparts),
        grid=(nblocks,),
        in_specs=in_specs,
        out_specs=pl.BlockSpec((1, lev, cols, width), lambda i: (0, 0, place(i), 0)),
        out_shape=jax.ShapeDtypeStruct(shape, BF16),
        scratch_shapes=[
            pltpu.VMEM((lev, cols, width), BF16),
            pltpu.VMEM((members * lev, cols, width), BF16),
            pltpu.VMEM((members * lev, cols, width), BF16),
            pltpu.VMEM((lev, cols, width), BF16),
        ],
        input_output_aliases=alias,
        compiler_params=params(),
        cost_estimate=cost(tokens * width * width * 8 * (members + 2), tokens * width * 2 * 5),
        name="attend",
    )(*args)


def body(
    atm_latent,
    ocean_state,
    depth,
    src_blocks,
    live,
    remap_weight,
    conv_weight,
    qkv_weight,
    out_weight,
):
    _, lev, cells, width = ocean_state.shape
    cols = remap_weight.shape[2]
    rows = cells // cols
    inner = cells - 2 * cols
    own = atm_latent.shape[1]
    atm_blk = own // cols
    tiles = lax.axis_size("tile")
    members = lax.axis_size("mem")
    depth_f = depth.astype(F32)
    depth_b = jnp.broadcast_to(depth_f[:, None], (cells, 128))
    levels = jnp.arange(lev, dtype=F32)
    bias = jnp.where(
        depth_f.reshape(-1, 1, GROUP) > levels[None, :, None], 0.0, NEG
    ).reshape(cells // GROUP, 1, lev * GROUP)

    grid = ocean_state[0].reshape(lev, rows, cols, width)
    dgrid = depth_f.reshape(rows, cols)

    def message(row):
        wet = (levels[:, None] < dgrid[row][None, :]).astype(BF16)
        edge = (grid[:, row] * wet[:, :, None]).reshape(lev * cols, width)
        return jnp.concatenate([edge, atm_latent[0]], axis=0)

    before = lax.ppermute(message(rows - 1), "tile", [(i, i + 1) for i in range(tiles - 1)])
    after = lax.ppermute(message(0), "tile", [(i + 1, i) for i in range(tiles - 1)])

    def exchange(x):
        out = []
        for k in range(1, members):
            out.append(lax.ppermute(x, "mem", [(i, (i + k) % members) for i in range(members)]))
        return out

    weight_spec = lambda nd: pl.BlockSpec(conv_weight.shape, lambda *i: (0, 0, 0, 0))
    depth_spec = pl.BlockSpec(depth_b.shape, lambda *i: (0, 0))
    tok = lambda n, c: jax.ShapeDtypeStruct((n, c, width), BF16)
    conv_flops = lambda n, c: 2 * 9 * n * c * width * width

    deep_mixed, deep_normed = pl.pallas_call(
        functools.partial(inner_kernel, cols, 1),
        grid=(lev - 1,),
        in_specs=[
            pl.BlockSpec((1, 1, cells, width), lambda l: (0, l + 1, 0, 0)),
            depth_spec,
            weight_spec(1),
        ],
        out_specs=[pl.BlockSpec((1, inner, width), lambda l: (l, 0, 0))] * 2,
        out_shape=[tok(lev - 1, inner)] * 2,
        compiler_params=params(),
        cost_estimate=cost(conv_flops(lev - 1, inner), lev * inner * width * 8),
        name="inner",
    )(ocean_state, depth_b, conv_weight)
    deep_other = exchange(deep_normed)

    first = (lax.axis_index("tile") - R) * atm_blk
    ids = jnp.clip(src_blocks - first, 0, 3 * atm_blk - 1)
    atm_at = lev * cols // own
    surf_mixed, surf_normed, edge_forcing = pl.pallas_call(
        functools.partial(surface_kernel, cols),
        grid_spec=pltpu.PrefetchScalarGridSpec(
            num_scalar_prefetch=2,
            grid=(1,),
            in_specs=[
                pl.BlockSpec((1, 1, cells, width), lambda i, *_: (0, 0, 0, 0)),
                depth_spec,
                weight_spec(1),
                pl.BlockSpec((own, width), lambda i, *_: (atm_at, 0)),
                pl.BlockSpec((1, own, width), lambda i, *_: (0, 0, 0)),
                pl.BlockSpec((own, width), lambda i, *_: (atm_at, 0)),
                pl.BlockSpec(remap_weight.shape, lambda i, *_: (0, 0, 0, 0)),
            ],
            out_specs=[
                pl.BlockSpec((1, inner, width), lambda i, *_: (0, 0, 0)),
                pl.BlockSpec((1, inner, width), lambda i, *_: (0, 0, 0)),
                pl.BlockSpec((2 * cols, width), lambda i, *_: (0, 0)),
            ],
            scratch_shapes=[pltpu.VMEM((3 * own, width), BF16), pltpu.VMEM((cells, width), F32)],
        ),
        out_shape=[tok(1, inner), tok(1, inner), jax.ShapeDtypeStruct((2 * cols, width), F32)],
        compiler_params=params(),
        cost_estimate=cost(conv_flops(1, inner) * 2, cells * width * 16),
        name="surface",
    )(ids, live, ocean_state, depth_b, conv_weight, before, atm_latent, after, remap_weight)
    surf_other = exchange(surf_normed)

    edge_mixed, edge_normed = pl.pallas_call(
        functools.partial(edge_kernel, cols),
        grid=(lev,),
        in_specs=[
            pl.BlockSpec((1, 1, cells, width), lambda l: (0, l, 0, 0)),
            depth_spec,
            weight_spec(1),
            pl.BlockSpec((cols, width), lambda l: (l, 0)),
            pl.BlockSpec((cols, width), lambda l: (l, 0)),
            pl.BlockSpec((2 * cols, width), lambda l: (0, 0)),
        ],
        out_specs=[pl.BlockSpec((1, 2 * cols, width), lambda l: (l, 0, 0))] * 2,
        out_shape=[tok(lev, 2 * cols)] * 2,
        compiler_params=params(),
        cost_estimate=cost(conv_flops(lev, 2 * cols), lev * cols * width * 16),
        name="edge",
    )(ocean_state, depth_b, conv_weight, before, after, edge_forcing)
    edge_other = exchange(edge_normed)

    shape = ocean_state.shape
    inner_normed = [[surf_normed, deep_normed]] + [list(p) for p in zip(surf_other, deep_other)]
    out = attend(
        inner_normed,
        [surf_mixed, deep_mixed],
        depth_b,
        bias,
        qkv_weight,
        out_weight,
        cols,
        lambda i: i + 1,
        None,
        shape,
    )
    return attend(
        [[edge_normed]] + [[p] for p in edge_other],
        [edge_mixed],
        depth_b,
        bias,
        qkv_weight,
        out_weight,
        cols,
        lambda i: i * (rows - 1),
        out,
        shape,
    )


def solution(mesh):
    return jax.shard_map(
        body,
        mesh=mesh,
        in_specs=(
            P("mem", "tile", None),
            P("mem", None, "tile", None),
            P("tile"),
            P("tile", None),
            P("tile"),
            P("tile", None, None, None),
            P(),
            P(),
            P(),
        ),
        out_specs=P("mem", None, "tile", None),
        check_vma=False,
    )
```

time: 175 us -> 84.5 us (0.48)
  local copies, waits for them, and re-layouts: 49 us -> 6.48 us
  Pallas kernels: 0 us -> 37.8 us
  matrix products: 32.4 us -> 0 us
  blocking collectives: 27.8 us -> 0 us
  other arithmetic: 20.5 us -> 2.36 us
  starting transfers between devices: 19 us -> 9.17 us
  waiting for transfers between devices: 24.6 us -> 28 us
    pallas_call x0 -> x5, Pallas kernels: none -> 37.8 us  [the longest x2 17.6 us: attend(): pl.pallas_call(functools.partial(attend_kernel, members, nparts), grid=(n...]
    dot_general x14 -> x0, matrix products: 32.4 us -> none  [the longest x1 10.3 us: attend_columns(): jnp.einsum('tnhd,snhd->nhts', query, keys, preferred_element_type=jnp.flo...]
    ppermute x4 -> x5, waiting for transfers between devices: 0.01 us -> 28 us  [the longest x3 22.3 us: exchange(): lax.ppermute(x, 'mem', [(i, (i + k) % members) for i in range(members)])]
    all_to_all x1 -> x0, blocking collectives: 27.8 us -> none  [body(): lax.all_to_all(relaid, 'mem', split_axis=0, concat_axis=2, tiled=True)]
    all_to_all x2 -> x0, waiting for transfers between devices: 24.6 us -> none  [the longest x1 24.6 us: body(): lax.all_to_all(tokens, 'mem', split_axis=2, concat_axis=0, tiled=True)]
    reshape x1 -> x0, local copies, waits for them, and re-layouts: 18.6 us -> none  [attend_columns(): qkv = qkv.reshape(mem_n * lev, count, 3, HEADS, head_size)]
    slice x3 -> x2, local copies, waits for them, and re-layouts: 16.1 us -> 1.28 us  [the longest x1 1.28 us: message(): edge = (grid[:, row] * wet[:, :, None]).reshape(lev * cols, width)]
    convert_element_type x12 -> x3, other arithmetic: 9.84 us -> 0.71 us  [the longest x1 0.68 us: body(): depth_f = depth.astype(F32)]
  transfers between devices with their start and end apart: 6 -> 5, of which waited for: 1 -> 2; matrix products, arithmetic and copies ran while one was open for 19% -> 3% of each run, Pallas kernels for 0% -> 35%
where the time goes in v1:
time: 84.5 us; the launch traced here: 83.9 us
  Pallas kernels  37.8 us (45%)
  waiting for transfers between devices  28 us (33%)
  starting transfers between devices  9.17 us (11%)
  local copies, waits for them, and re-layouts  6.48 us (8%)
  other arithmetic  2.36 us (3%)
    ppermute x3, waiting for transfers between devices, exchange(): lax.ppermute(x, 'mem', [(i, (i + k) % members) for i in range(members)])  22.3 us
    pallas_call x2, Pallas kernels, attend(): pl.pallas_call(functools.partial(attend_kernel, members, nparts), grid=(n...  17.6 us
    pallas_call x1, Pallas kernels, body(): pl.pallas_call(functools.partial(edge_kernel, cols), grid=(lev,), in_spec...  8.56 us
    pallas_call x1, Pallas kernels, body(): pl.pallas_call(functools.partial(inner_kernel, cols, 1), grid=(lev - 1,),...  7.51 us
    ppermute x1, waiting for transfers between devices, body(): lax.ppermute(message(rows - 1), 'tile', [(i, i + 1) for i in range(tiles...  5.68 us
    pallas_call x1, Pallas kernels, body(): pl.pallas_call(functools.partial(surface_kernel, cols), grid_spec=pltpu.P...  4.14 us
    unnamed x14, local copies, waits for them, and re-layouts  4.01 us
    ppermute x1, starting transfers between devices, body(): lax.ppermute(message(0), 'tile', [(i + 1, i) for i in range(tiles - 1)])  3.64 us
  transfers between devices with their start and end apart: 5, of which 2 were waited for; matrix products, arithmetic and copies ran while one was open for 3% of the time, Pallas kernels for 35%

profile of v1, /device:TPU:18, one launch (start us, length us, event | category | flops | bytes accessed | tf_op | source)
XLA Modules:
  0.0 83.9 jit_solution(7242583482302497472)
XLA Ops:
  0.0 0.7 convert_element_type.17
  0.7 1.3 %fusion.2 = (bf16[8,1,128,256]{3,2,1,0:T(8,128)(2,1)S(1)}, bf16[8,1,128,256]{3,2,1,0:T(8,128)(2,1)S(1)}) fusion(bf16[8,4,128,256]{3,2,1,0:T(8,128)(2,1)} %bitcast.20), kind=kLoop, calls=%fused_computation.10 | loop fusion | bytes 2097152 | tf_op jit(solution)/shard_map/slice | solution.py:258
  2.0 0.0 copy-start
  2.0 0.3 bitcast_multiply_fusion
  2.4 0.6 copy-done
  3.0 0.1 pad_maximum_fusion
  3.1 1.9 %collective-permute-start = (bf16[1536,256]{1,0:T(8,128)(2,1)S(1)}, bf16[1536,256]{1,0:T(8,128)(2,1)S(1)}, u32[]{:S(2)}, u32[]{:S(2)}) collective-permute-start(bf16[1536,256]{1,0:T(8,128)(2,1)S(1)} %get-tuple-element.22), channel_id=1, source_target_pairs={{0,2},{2,4},{4,6},{6,8},{8,10},{10,12},{12,14},{14,16},{16,18},{18... | collective-permute-start | bytes 2359304 | tf_op jit(solution)/shard_map/ppermute | solution.py:261
  5.0 3.6 %collective-permute-start.1 = (bf16[1536,256]{1,0:T(8,128)(2,1)S(1)}, bf16[1536,256]{1,0:T(8,128)(2,1)S(1)}, u32[]{:S(2)}, u32[]{:S(2)}) collective-permute-start(bf16[1536,256]{1,0:T(8,128)(2,1)S(1)} %get-tuple-element.21), channel_id=1, source_target_pairs={{2,0},{4,2},{6,4},{8,6},{10,8},{12,10},{14,12},{16,14},{18,16},{20... | collective-permute-start | bytes 2359304 | tf_op jit(solution)/shard_map/ppermute | solution.py:262
  8.7 0.8 %broadcast_in_dim.10.depth_ref.refs_6_.refs_3_ = f32[512,128]{1,0:T(8,128)} broadcast(f32[512]{0:T(512)S(1)} %convert_element_type.17), dimensions={0} | broadcast | bytes 264192 | tf_op jit(solution)/shard_map/broadcast_in_dim | solution.py:247
  9.5 7.5 %inner.1 = (bf16[7,256,256]{2,1,0:T(8,128)(2,1)}, bf16[7,256,256]{2,1,0:T(8,128)(2,1)}) custom-call(bf16[1,8,512,256]{3,2,1,0:T(8,128)(2,1)} %state_ref.5, f32[512,128]{1,0:T(8,128)} %broadcast_in_dim.10.depth_ref.refs_6_.refs_3_, bf16[3,3,256,256]{3,2,1,0:T(8,128)(2,1)} %weight_ref.5), custom_call_target="tpu_custom_call" | custom-call | flops 2113929216 | bytes 4194304 | tf_op jit(solution)/shard_map/inner/pallas_call | solution.py:275
  17.0 1.5 %collective-permute-start.4 = (bf16[7,256,256]{2,1,0:T(8,128)(2,1)}, bf16[7,256,256]{2,1,0:T(8,128)(2,1)}, u32[]{:S(2)}, u32[]{:S(2)}) collective-permute-start(bf16[7,256,256]{2,1,0:T(8,128)(2,1)} %get-tuple-element.16.refs_1_), channel_id=1, source_target_pairs={{0,1},{1,0},{2,3},{3,2},{4,5},{5,4},{6,7},{7,6},{8,9},{9,8},{10,11... | collective-permute-start | bytes 2752520 | tf_op jit(solution)/shard_map/ppermute | solution.py:267
  18.5 0.6 subtract_clamp_fusion.ids_ref
  19.1 5.7 %collective-permute-done.before_ref = bf16[1536,256]{1,0:T(8,128)(2,1)S(1)} collective-permute-done((bf16[1536,256]{1,0:T(8,128)(2,1)S(1)}, bf16[1536,256]{1,0:T(8,128)(2,1)S(1)}, u32[]{:S(2)}, u32[]{:S(2)}) %collective-permute-start) | collective-permute-done | bytes 786464 | tf_op jit(solution)/shard_map/ppermute | solution.py:261
  24.8 0.0 collective-permute-done.1.after_ref
  24.8 0.9 %copy-done.1 = bf16[1536,256]{1,0:T(8,128)(2,1)} copy-done((bf16[1536,256]{1,0:T(8,128)(2,1)}, bf16[1536,256]{1,0:T(8,128)(2,1)S(1)}, u32[]{:S(2)}) %copy-start.1) | copy-done | bytes 786456
  25.7 0.9 %copy-done.2 = bf16[1536,256]{1,0:T(8,128)(2,1)} copy-done((bf16[1536,256]{1,0:T(8,128)(2,1)}, bf16[1536,256]{1,0:T(8,128)(2,1)S(1)}, u32[]{:S(2)}) %copy-start.2) | copy-done | bytes 786456
  26.6 4.1 %surface.1 = (bf16[1,256,256]{2,1,0:T(8,128)(2,1)}, bf16[1,256,256]{2,1,0:T(8,128)(2,1)}, f32[256,256]{1,0:T(8,128)}) custom-call(s32[4,4]{1,0:T(4,128)} %subtract_clamp_fusion.ids_ref, s32[4]{0:T(128)} %live_ref.1, bf16[1,8,512,256]{3,2,1,0:T(8,128)(2,1)} %state_ref.5, f32[512,128]{1,0:T(8,128)} %broadcast_in_dim.10.depth_ref.refs_6_.refs_3_, ...), custom_call_target="tpu_custom_call" | custom-call | flops 603979776 | bytes 2097152 | tf_op jit(solution)/shard_map/surface/pallas_call | solution.py:294
  30.7 8.6 %edge.1 = (bf16[8,256,256]{2,1,0:T(8,128)(2,1)}, bf16[8,256,256]{2,1,0:T(8,128)(2,1)}) custom-call(bf16[1,8,512,256]{3,2,1,0:T(8,128)(2,1)} %state_ref.5, f32[512,128]{1,0:T(8,128)} %broadcast_in_dim.10.depth_ref.refs_6_.refs_3_, bf16[3,3,256,256]{3,2,1,0:T(8,128)(2,1)} %weight_ref.5, bf16[1536,256]{1,0:T(8,128)(2,1)} %copy-done.1, ...), custom_call_target="tpu_custom_call" | custom-call | flops 2415919104 | bytes 4194304 | tf_op jit(solution)/shard_map/edge/pallas_call | solution.py:322
  39.3 1.5 %collective-permute-start.2 = (bf16[8,256,256]{2,1,0:T(8,128)(2,1)}, bf16[8,256,256]{2,1,0:T(8,128)(2,1)S(1)}, u32[]{:S(2)}, u32[]{:S(2)}) collective-permute-start(bf16[8,256,256]{2,1,0:T(8,128)(2,1)} %get-tuple-element.13.refs_0_), channel_id=1, source_target_pairs={{0,1},{1,0},{2,3},{3,2},{4,5},{5,4},{6,7},{7,6},{8,9},{9,8},{10,11... | collective-permute-start | bytes 3145736 | tf_op jit(solution)/shard_map/ppermute | solution.py:267
  40.8 0.1 gt.28
  40.9 0.1 copy.15
  41.0 0.1 copy.16
  41.1 0.1 gt.32
  41.2 0.6 collective-permute-start.3
  41.7 0.6 compare_select_fusion.refs_7_.refs_4_
  42.3 22.3 %collective-permute-done.3.refs_2_ = bf16[1,256,256]{2,1,0:T(8,128)(2,1)S(1)} collective-permute-done((bf16[1,256,256]{2,1,0:T(8,128)(2,1)S(1)}, bf16[1,256,256]{2,1,0:T(8,128)(2,1)S(1)}, u32[]{:S(2)}, u32[]{:S(2)}) %collective-permute-start.3) | collective-permute-done | bytes 131104 | tf_op jit(solution)/shard_map/ppermute | solution.py:267
  64.7 0.0 collective-permute-done.4.refs_3_
  64.7 0.6 copy-done.6
  65.3 8.8 %attend.2.refs_7_ = bf16[1,8,512,256]{3,2,1,0:T(8,128)(2,1)} custom-call(bf16[1,256,256]{2,1,0:T(8,128)(2,1)} %get-tuple-element.15.refs_0_, bf16[7,256,256]{2,1,0:T(8,128)(2,1)} %get-tuple-element.16.refs_1_, bf16[1,256,256]{2,1,0:T(8,128)(2,1)} %copy-done.6, bf16[7,256,256]{2,1,0:T(8,128)(2,1)} %collective-permute-done.4.refs_3_, ...), custom_call_target="tpu_custom_call" | custom-call | flops 4294967296 | bytes 5242880 | tf_op jit(solution)/shard_map/attend/pallas_call | solution.py:208
  74.2 0.0 collective-permute-done.2.refs_1_
  74.2 1.0 %copy-done.4 = bf16[8,256,256]{2,1,0:T(8,128)(2,1)} copy-done((bf16[8,256,256]{2,1,0:T(8,128)(2,1)}, bf16[8,256,256]{2,1,0:T(8,128)(2,1)S(1)}, u32[]{:S(2)}) %copy-start.4) | copy-done | bytes 1048600
  75.1 8.8 %attend.3 = bf16[1,8,512,256]{3,2,1,0:T(8,128)(2,1)} custom-call(bf16[8,256,256]{2,1,0:T(8,128)(2,1)} %get-tuple-element.13.refs_0_, bf16[8,256,256]{2,1,0:T(8,128)(2,1)} %copy-done.4, bf16[8,256,256]{2,1,0:T(8,128)(2,1)} %get-tuple-element.14.refs_2_, f32[512,128]{1,0:T(8,128)} %broadcast_in_dim.10.depth_ref.refs_6_.refs_3_, ...), custom_call_target="tpu_custom_call", output_to_operand_aliasing={{}: (7, {})} | custom-call | flops 4294967296 | bytes 5242880 | tf_op jit(solution)/shard_map/attend/pallas_call | solution.py:208
  (15 shorter events, 0.1 us)
Async XLA Ops:
  2.0 1.0 %copy-start = (bf16[1,512,256]{2,1,0:T(8,128)(2,1)S(1)}, bf16[1,512,256]{2,1,0:T(8,128)(2,1)}, u32[]{:S(2)}) copy-start(bf16[1,512,256]{2,1,0:T(8,128)(2,1)} %atm_ref.1) | copy-start | bytes 786436
  3.1 21.7 %collective-permute-start = (bf16[1536,256]{1,0:T(8,128)(2,1)S(1)}, bf16[1536,256]{1,0:T(8,128)(2,1)S(1)}, u32[]{:S(2)}, u32[]{:S(2)}) collective-permute-start(bf16[1536,256]{1,0:T(8,128)(2,1)S(1)} %get-tuple-element.22), channel_id=1, source_target_pairs={{0,2},{2,4},{4,6},{6,8},{8,10},{10,12},{12,14},{14,16},{16,18},{18... | collective-permute-start | bytes 2359304 | tf_op jit(solution)/shard_map/ppermute | solution.py:261
  5.0 19.8 %collective-permute-start.1 = (bf16[1536,256]{1,0:T(8,128)(2,1)S(1)}, bf16[1536,256]{1,0:T(8,128)(2,1)S(1)}, u32[]{:S(2)}, u32[]{:S(2)}) collective-permute-start(bf16[1536,256]{1,0:T(8,128)(2,1)S(1)} %get-tuple-element.21), channel_id=1, source_target_pairs={{2,0},{4,2},{6,4},{8,6},{10,8},{12,10},{14,12},{16,14},{18,16},{20... | collective-permute-start | bytes 2359304 | tf_op jit(solution)/shard_map/ppermute | solution.py:262
  9.5 9.0 %copy-start.3 = (s32[4,4]{1,0:T(4,128)S(1)}, s32[4,4]{1,0:T(4,128)}, u32[]{:S(2)}) copy-start(s32[4,4]{1,0:T(4,128)} %param.12) | copy-start | bytes 196
  17.0 47.7 %collective-permute-start.4 = (bf16[7,256,256]{2,1,0:T(8,128)(2,1)}, bf16[7,256,256]{2,1,0:T(8,128)(2,1)}, u32[]{:S(2)}, u32[]{:S(2)}) collective-permute-start(bf16[7,256,256]{2,1,0:T(8,128)(2,1)} %get-tuple-element.16.refs_1_), channel_id=1, source_target_pairs={{0,1},{1,0},{2,3},{3,2},{4,5},{5,4},{6,7},{7,6},{8,9},{9,8},{10,11... | collective-permute-start | bytes 2752520 | tf_op jit(solution)/shard_map/ppermute | solution.py:267
  24.8 0.9 %copy-start.1 = (bf16[1536,256]{1,0:T(8,128)(2,1)}, bf16[1536,256]{1,0:T(8,128)(2,1)S(1)}, u32[]{:S(2)}) copy-start(bf16[1536,256]{1,0:T(8,128)(2,1)S(1)} %collective-permute-done.before_ref) | copy-start | bytes 2359300
  25.7 0.9 %copy-start.2 = (bf16[1536,256]{1,0:T(8,128)(2,1)}, bf16[1536,256]{1,0:T(8,128)(2,1)S(1)}, u32[]{:S(2)}) copy-start(bf16[1536,256]{1,0:T(8,128)(2,1)S(1)} %collective-permute-done.1.after_ref) | copy-start | bytes 2359300
  30.7 10.4 %copy-start.5 = (bf16[1,256,256]{2,1,0:T(8,128)(2,1)S(1)}, bf16[1,256,256]{2,1,0:T(8,128)(2,1)}, u32[]{:S(2)}) copy-start(bf16[1,256,256]{2,1,0:T(8,128)(2,1)} %get-tuple-element.15.refs_0_) | copy-start | bytes 393220
  39.3 34.9 %collective-permute-start.2 = (bf16[8,256,256]{2,1,0:T(8,128)(2,1)}, bf16[8,256,256]{2,1,0:T(8,128)(2,1)S(1)}, u32[]{:S(2)}, u32[]{:S(2)}) collective-permute-start(bf16[8,256,256]{2,1,0:T(8,128)(2,1)} %get-tuple-element.13.refs_0_), channel_id=1, source_target_pairs={{0,1},{1,0},{2,3},{3,2},{4,5},{5,4},{6,7},{7,6},{8,9},{9,8},{10,11... | collective-permute-start | bytes 3145736 | tf_op jit(solution)/shard_map/ppermute | solution.py:267
  41.2 23.5 %collective-permute-start.3 = (bf16[1,256,256]{2,1,0:T(8,128)(2,1)S(1)}, bf16[1,256,256]{2,1,0:T(8,128)(2,1)S(1)}, u32[]{:S(2)}, u32[]{:S(2)}) collective-permute-start(bf16[1,256,256]{2,1,0:T(8,128)(2,1)S(1)} %copy-done.5), channel_id=1, source_target_pairs={{0,1},{1,0},{2,3},{3,2},{4,5},{5,4},{6,7},{7,6},{8,9},{9,8},{10,11... | collective-permute-start | bytes 393224 | tf_op jit(solution)/shard_map/ppermute | solution.py:267
  64.7 0.7 copy-start.6
  74.2 1.0 %copy-start.4 = (bf16[8,256,256]{2,1,0:T(8,128)(2,1)}, bf16[8,256,256]{2,1,0:T(8,128)(2,1)S(1)}, u32[]{:S(2)}) copy-start(bf16[8,256,256]{2,1,0:T(8,128)(2,1)S(1)} %collective-permute-done.2.refs_1_) | copy-start | bytes 3145732

commit v2 on v1

v2 whole, which is shorter than its diff:
```python
import functools
import math

import jax
import jax.numpy as jnp
from jax import lax
from jax.experimental import pallas as pl
from jax.experimental.pallas import tpu as pltpu
from jax.sharding import PartitionSpec as P

HEADS = 4
R = 1
GROUP = 16
EPS = 1e-06
NEG = -1e30
F32 = jnp.float32
BF16 = jnp.bfloat16
MIB = 1024 * 1024


def params(mib, steps=0):
    return pltpu.CompilerParams(
        dimension_semantics=("arbitrary",) * steps if steps else None, vmem_limit_bytes=mib * MIB
    )


def cost(flops, nbytes):
    return pl.CostEstimate(flops=int(flops), bytes_accessed=int(nbytes), transcendentals=0)


def capacity(tokens, share):
    return -(-int(tokens * share) // 16) * 16


def row_plan(depth_row, lev):
    cols = depth_row.shape[1]
    level = lax.broadcasted_iota(jnp.int32, (lev, cols), 0).astype(F32)
    wet = (depth_row > level).astype(F32)
    upper = (
        lax.broadcasted_iota(jnp.int32, (cols, cols), 0)
        < lax.broadcasted_iota(jnp.int32, (cols, cols), 1)
    )
    upper = upper.astype(F32).astype(BF16)
    rank = jnp.dot(wet.astype(BF16), upper, preferred_element_type=F32)
    counts = [jnp.sum(wet[l : l + 1]).astype(jnp.int32) for l in range(lev)]
    return wet, rank, counts


def offsets(plans, first, lev):
    at, place = jnp.int32(0), {}
    for l in range(first, lev):
        for r, plan in enumerate(plans):
            place[l, r] = at
            at = at + plan[2][l]
    return place


def segment(wet, rank, offset, cap):
    cols = wet.shape[1]
    base = jnp.minimum((offset // 16) * 16, cap)
    target = jnp.where(wet > 0, rank + (offset - base).astype(F32), -1.0)
    slot = lax.broadcasted_iota(jnp.int32, (cols + 16, cols), 0).astype(F32)
    return pl.multiple_of(base, 16), (slot == target).astype(F32).astype(BF16)


def pack(buf_ref, wet, rank, offset, cap, tokens):
    base, hot = segment(wet, rank, offset, cap)
    rows = jnp.dot(hot, tokens, preferred_element_type=F32).astype(BF16)
    head = pl.ds(base, 16)
    buf_ref[head, :] = buf_ref[head, :] + rows[:16]
    buf_ref[pl.ds(pl.multiple_of(base + 16, 16), rows.shape[0] - 16), :] = rows[16:]


def unpack(buf_ref, wet, rank, offset, cap):
    base, hot = segment(wet, rank, offset, cap)
    rows = buf_ref[pl.ds(base, hot.shape[0]), :]
    return lax.dot_general(
        hot, rows, (((0,), (0,)), ((), ())), preferred_element_type=F32
    ).astype(BF16)


def column(depth_row, width):
    cols = depth_row.shape[1]
    turned = jnp.broadcast_to(depth_row, (cols, cols)).T
    return jnp.concatenate([turned] * (width // cols), axis=1)


def stencil(taps, weight_ref, cols):
    count, width = taps[0].shape
    x = jnp.concatenate(taps, axis=1)
    sums = [
        jnp.dot(x, weight_ref[:, dc].reshape(3 * width, -1), preferred_element_type=F32)
        for dc in range(3)
    ]
    col = lax.broadcasted_iota(jnp.int32, (count, 1), 0) % cols
    left = jnp.where(col == 0, 0.0, pltpu.roll(sums[0], 1, axis=0))
    right = jnp.where(col == cols - 1, 0.0, pltpu.roll(sums[2], count - 1, axis=0))
    return sums[1] + left + right


def normalise(mixed):
    mf = mixed.astype(F32)
    mean = jnp.mean(mf * mf, axis=-1, keepdims=True)
    return (mf * lax.rsqrt(mean + EPS)).astype(BF16)


def inner_kernel(
    cap,
    state_hbm,
    depth_ref,
    weight_hbm,
    mixed_hbm,
    normed_hbm,
    packed_hbm,
    base_ref,
    state,
    weight,
    mixed,
    normed,
    packed,
    in_sem,
    weight_sem,
    out_sem,
    packed_sem,
):
    _, lev, cells, width = state_hbm.shape
    rows, cols = depth_ref.shape
    order = list(range(1, lev)) + [0]
    load_w = pltpu.make_async_copy(weight_hbm, weight, weight_sem)
    loads = [pltpu.make_async_copy(state_hbm.at[0, l], state.at[l], in_sem.at[l]) for l in range(lev)]
    loads[1].start()
    load_w.start()
    for l in order[1:]:
        loads[l].start()
    packed[...] = jnp.zeros_like(packed)
    d = depth_ref[...].astype(F32)
    plans = [row_plan(d[r : r + 1], lev) for r in range(1, rows - 1)]
    place = offsets(plans, 1, lev)
    deep = jnp.concatenate([column(d[r : r + 1], width) for r in range(rows)], axis=0)
    count = cells - 2 * cols
    stores = []
    for l in order:
        wet = (deep > l).astype(F32)
        loads[l].wait()
        if l == 1:
            load_w.wait()
        x = state[l] * wet.astype(BF16)
        taps = [x[dr * cols : dr * cols + count] for dr in range(3)]
        total = stencil(taps, weight, cols)
        new = taps[1].astype(F32) + wet[cols : cols + count] * total
        if l == 0:
            base_ref[...] = new
            continue
        new = new.astype(BF16)
        mixed[l - 1] = new
        tokens = normalise(new)
        normed[l - 1] = tokens
        for k, (buf, out) in enumerate(((mixed, mixed_hbm), (normed, normed_hbm))):
            store = pltpu.make_async_copy(buf.at[l - 1], out.at[l - 1], out_sem.at[l - 1, k])
            store.start()
            stores.append(store)
        for r, plan in enumerate(plans):
            pack(
                packed,
                plan[0][l : l + 1],
                plan[1][l : l + 1],
                place[l, r],
                cap,
                tokens[r * cols : (r + 1) * cols],
            )
        if l == lev - 1:
            store = pltpu.make_async_copy(packed.at[pl.ds(0, cap)], packed_hbm, packed_sem)
            store.start()
            stores.append(store)
    for store in stores:
        store.wait()


def surface_kernel(
    ids_ref,
    live_ref,
    base_ref,
    depth_ref,
    before_ref,
    atm_ref,
    after_ref,
    remap_ref,
    mixed_ref,
    normed_ref,
    edge_ref,
    window_ref,
    forcing_ref,
):
    rows, cols = depth_ref.shape
    width = base_ref.shape[-1]
    own = atm_ref.shape[1]
    blocks, pairs = remap_ref.shape[0], remap_ref.shape[1]
    window_ref[0:own] = before_ref[0]
    window_ref[own : 2 * own] = atm_ref[0]
    window_ref[2 * own : 3 * own] = after_ref[0]
    for b in range(blocks):
        acc = jnp.zeros((cols, width), F32)
        for p in range(pairs):
            on = (p < live_ref[b]).astype(F32)
            start = pl.multiple_of(ids_ref[b, p] * cols, cols)
            acc = acc + on * jnp.dot(
                remap_ref[b, p], window_ref[pl.ds(start, cols), :], preferred_element_type=F32
            )
        forcing_ref[b * cols : (b + 1) * cols] = acc
    d = depth_ref[...].astype(F32)
    for r in range(1, rows - 1):
        at = slice((r - 1) * cols, r * cols)
        wet = (column(d[r : r + 1], width) > 0).astype(F32)
        new = (base_ref[at] + wet * forcing_ref[r * cols : (r + 1) * cols]).astype(BF16)
        mixed_ref[0, at] = new
        normed_ref[0, at] = normalise(new)
    edge_ref[0:cols] = forcing_ref[0:cols]
    edge_ref[cols : 2 * cols] = forcing_ref[(rows - 1) * cols :]


def edge_kernel(
    cap,
    state_hbm,
    depth_ref,
    weight_hbm,
    before_hbm,
    after_hbm,
    forcing_ref,
    mixed_hbm,
    normed_hbm,
    top_hbm,
    low_hbm,
    state,
    weight,
    before,
    after,
    mixed,
    normed,
    top,
    low,
    in_sem,
    weight_sem,
    out_sem,
    packed_sem,
):
    _, lev, cells, width = state_hbm.shape
    rows, cols = depth_ref.shape
    load_w = pltpu.make_async_copy(weight_hbm, weight, weight_sem)
    loads = []
    for l in range(lev):
        halo = pl.ds(l * cols, cols)
        loads.append(
            [
                pltpu.make_async_copy(state_hbm.at[0, l], state.at[l], in_sem.at[l, 0]),
                pltpu.make_async_copy(before_hbm.at[halo], before.at[halo], in_sem.at[l, 1]),
                pltpu.make_async_copy(after_hbm.at[halo], after.at[halo], in_sem.at[l, 2]),
            ]
        )
    for copy in loads[0]:
        copy.start()
    load_w.start()
    for l in range(1, lev):
        for copy in loads[l]:
            copy.start()
    top[...] = jnp.zeros_like(top)
    low[...] = jnp.zeros_like(low)
    d = depth_ref[...].astype(F32)
    ends = [d[0:1], d[rows - 1 : rows]]
    plans = [row_plan(e, lev) for e in ends]
    places = [offsets([plan], 0, lev) for plan in plans]
    deep = jnp.concatenate([column(d[r : r + 1], width) for r in range(rows)], axis=0)
    stores = []
    for l in range(lev):
        wet = (deep > l).astype(F32)
        for copy in loads[l]:
            copy.wait()
        if l == 0:
            load_w.wait()
        x = state[l] * wet.astype(BF16)
        halo = slice(l * cols, (l + 1) * cols)
        up = [before[halo], x[0:cols], x[cols : 2 * cols]]
        down = [x[cells - 2 * cols : cells - cols], x[cells - cols :], after[halo]]
        taps = [jnp.concatenate([a, b], axis=0) for a, b in zip(up, down)]
        total = stencil(taps, weight, cols)
        if l == 0:
            total = total + forcing_ref[...]
        edge_wet = jnp.concatenate([wet[0:cols], wet[cells - cols :]], axis=0)
        new = (taps[1].astype(F32) + edge_wet * total).astype(BF16)
        mixed[l] = new
        tokens = normalise(new)
        normed[l] = tokens
        for k, (buf, out) in enumerate(((mixed, mixed_hbm), (normed, normed_hbm))):
            store = pltpu.make_async_copy(buf.at[l], out.at[l], out_sem.at[l, k])
            store.start()
            stores.append(store)
        for r, buf in enumerate((top, low)):
            pack(
                buf,
                plans[r][0][l : l + 1],
                plans[r][1][l : l + 1],
                places[r][l, 0],
                cap,
                tokens[r * cols : (r + 1) * cols],
            )
    for k, (buf, out) in enumerate(((top, top_hbm), (low, low_hbm))):
        store = pltpu.make_async_copy(buf.at[pl.ds(0, cap)], out, packed_sem.at[k])
        store.start()
        stores.append(store)
    for store in stores:
        store.wait()


def attend_kernel(others, nparts, rows_of, first, cap, aliased, flag_ref, *refs):
    refs = list(refs)
    take = lambda k: [refs.pop(0) for _ in range(k)]
    own_normed = take(nparts)
    own_mixed = take(nparts)
    surf = take(others) if first else []
    packed = take(others)
    whole = take(others)
    depth_ref, qkv_ref, wo_ref = take(3)
    if aliased:
        take(1)
    out_ref, q_ref, k_ref, v_ref, att_ref, buf_ref, token_ref, sem = refs
    lev, count, width = q_ref.shape
    members = others + 1
    head = width // HEADS
    pair = 2 * head
    step = pl.program_id(0)

    def keys_values(x, m):
        rows = slice(m * lev, (m + 1) * lev)
        kv = jnp.dot(x, qkv_ref[:, width:], preferred_element_type=F32).astype(BF16)
        k_ref[rows] = kv[:, :width].reshape(lev, count, width)
        v_ref[rows] = kv[:, width:].reshape(lev, count, width)

    d = depth_ref[...].astype(F32)
    plans = [row_plan(d[r : r + 1], lev) for r in rows_of]
    place = offsets(plans, first, lev)
    two = len(rows_of) == 2
    pick = lambda a, b: jnp.where(step == 0, a, b)
    wet_row = pick(plans[0][0], plans[1][0]) if two else plans[0][0]
    rank = pick(plans[0][1], plans[1][1]) if two else plans[0][1]
    depth_row = d[rows_of[0] : rows_of[0] + 1]
    if two:
        depth_row = pick(depth_row, d[rows_of[1] : rows_of[1] + 1])

    x = jnp.concatenate([p[...].reshape(-1, width) for p in own_normed], axis=0)
    q = jnp.dot(x, qkv_ref[:, 0:width], preferred_element_type=F32).astype(BF16)
    q_ref[...] = (q * (1.0 / math.sqrt(head))).astype(BF16).reshape(lev, count, width)
    keys_values(x, 0)
    for o in range(others):
        if first:
            token_ref[0] = surf[o][0]

        @pl.when(flag_ref[0] == 0)
        def _():
            buf_ref[0:cap] = packed[o][...]
            buf_ref[cap:] = jnp.zeros((buf_ref.shape[0] - cap, width), BF16)
            for l in range(first, lev):
                at = pick(place[l, 0], place[l, 1]) if two else place[l, 0]
                token_ref[l] = unpack(
                    buf_ref, wet_row[l : l + 1], rank[l : l + 1], at, cap
                )

        @pl.when(flag_ref[0] != 0)
        def _():
            which = step if two else (0 if rows_of[0] == 0 else 1)
            copy = pltpu.make_async_copy(
                whole[o].at[:, pl.ds(which * count, count)], token_ref.at[pl.ds(first, lev - first)], sem
            )
            copy.start()
            copy.wait()

        keys_values(token_ref[...].reshape(-1, width), o + 1)

    nq, nk = lev * GROUP, members * lev * GROUP
    groups = count // GROUP
    lanes_n = lev * GROUP
    cell = lax.broadcasted_iota(jnp.int32, (groups, count), 1)
    mine = (cell // GROUP == lax.broadcasted_iota(jnp.int32, (groups, count), 0)).astype(F32)
    spread = lax.broadcasted_iota(jnp.int32, (count, lanes_n), 0) % GROUP
    spread = (spread == lax.broadcasted_iota(jnp.int32, (count, lanes_n), 1) % GROUP).astype(F32)
    key_depth = jnp.dot(
        (mine * depth_row).astype(BF16), spread.astype(BF16), preferred_element_type=F32
    )
    key_level = lax.broadcasted_iota(jnp.int32, (groups, lanes_n), 1) // GROUP
    key_bias = jnp.where(key_depth > key_level.astype(F32), 0.0, NEG)
    qc = lax.broadcasted_iota(jnp.int32, (nq, nk), 0) % GROUP
    kc = lax.broadcasted_iota(jnp.int32, (nq, nk), 1) % GROUP
    same = jnp.where(qc == kc, 0.0, NEG)
    lane = lax.broadcasted_iota(jnp.int32, (1, pair), 1)
    low = (lane < head).astype(F32).astype(BF16)
    high = (lane >= head).astype(F32).astype(BF16)
    for g in range(groups):
        cells = slice(g * GROUP, (g + 1) * GROUP)
        bias = same + jnp.concatenate([key_bias[g : g + 1]] * members, axis=1)
        bias = jnp.concatenate([bias, bias], axis=0)
        for h in range(HEADS // 2):
            lanes = slice(h * pair, (h + 1) * pair)
            q = q_ref[:, cells, lanes].reshape(nq, pair)
            q = jnp.concatenate([q * low, q * high], axis=0)
            k = k_ref[:, cells, lanes].reshape(nk, pair)
            v = v_ref[:, cells, lanes].reshape(nk, pair)
            s = lax.dot_general(q, k, (((1,), (1,)), ((), ())), preferred_element_type=F32) + bias
            p = jnp.exp(s - jnp.max(s, axis=-1, keepdims=True))
            norm = 1.0 / jnp.sum(p, axis=-1, keepdims=True)
            o = jnp.dot(p.astype(BF16), v, preferred_element_type=F32) * norm
            o = jnp.where(lane < head, o[:nq], o[nq:])
            att_ref[:, cells, lanes] = o.astype(BF16).reshape(lev, GROUP, pair)
    proj = jnp.dot(att_ref[...].reshape(-1, width), wo_ref[...], preferred_element_type=F32)
    base = jnp.concatenate([p[...].reshape(-1, width) for p in own_mixed], axis=0).astype(F32)
    deep = column(depth_row, width)
    for l in range(lev):
        rows = slice(l * count, (l + 1) * count)
        wet = (deep > l).astype(F32)
        out_ref[0, l] = (base[rows] + wet * proj[rows]).astype(BF16)


def attend(flag, normed, mixed, surf, packed, whole, depth, qkv_weight, out_weight, rows_of, out, shape):
    others, nparts = len(packed), len(mixed)
    lev = sum(p.shape[0] for p in mixed)
    width = shape[-1]
    rows, cols = depth.shape
    cap = packed[0].shape[0]
    first = 1 if surf else 0
    shift = 1 if rows_of[0] == rows - 1 else 0
    index = lambda i, *_: (0, i + shift, 0)
    full2 = lambda a: pl.BlockSpec(a.shape, lambda i, *_: (0, 0))
    part = [pl.BlockSpec((p.shape[0], cols, width), index) for p in mixed]
    hbm = pl.BlockSpec(memory_space=pl.ANY)
    in_specs = part * 2
    in_specs += [pl.BlockSpec((1, cols, width), index)] * len(surf)
    in_specs += [full2(p) for p in packed]
    in_specs += [hbm] * others
    in_specs += [full2(depth), full2(qkv_weight), full2(out_weight)]
    args = normed + mixed + surf + packed + whole + [depth, qkv_weight, out_weight]
    alias = {}
    if out is not None:
        in_specs.append(hbm)
        alias = {len(args) + 1: 0}
        args.append(out)
    tokens = lev * cols * len(rows_of)
    members = others + 1
    return pl.pallas_call(
        functools.partial(
            attend_kernel, others, nparts, tuple(rows_of), first, cap, out is not None
        ),
        grid_spec=pltpu.PrefetchScalarGridSpec(
            num_scalar_prefetch=1,
            grid=(len(rows_of),),
            in_specs=in_specs,
            out_specs=pl.BlockSpec(
                (1, lev, cols, width), lambda i, *_: (0, 0, i + rows_of[0], 0)
            ),
            scratch_shapes=[
                pltpu.VMEM((lev, cols, width), BF16),
                pltpu.VMEM((members * lev, cols, width), BF16),
                pltpu.VMEM((members * lev, cols, width), BF16),
                pltpu.VMEM((lev, cols, width), BF16),
                pltpu.VMEM((cap + cols + 16, width), BF16),
                pltpu.VMEM((lev, cols, width), BF16),
                pltpu.SemaphoreType.DMA,
            ],
        ),
        out_shape=jax.ShapeDtypeStruct(shape, BF16),
        input_output_aliases=alias,
        compiler_params=params(24 if members <= 2 else 48, 1),
        cost_estimate=cost(tokens * width * width * 8 * (members + 2), tokens * width * 2 * 5),
        name="attend",
    )(flag, *args)


def body(
    atm_latent,
    ocean_state,
    depth,
    src_blocks,
    live,
    remap_weight,
    conv_weight,
    qkv_weight,
    out_weight,
):
    _, lev, cells, width = ocean_state.shape
    cols = remap_weight.shape[2]
    rows = cells // cols
    inner = cells - 2 * cols
    own = atm_latent.shape[1]
    atm_blk = own // cols
    tiles = lax.axis_size("tile")
    members = lax.axis_size("mem")
    ups = [(i, i + 1) for i in range(tiles - 1)]
    downs = [(i + 1, i) for i in range(tiles - 1)]
    atm_before = lax.ppermute(atm_latent, "tile", ups)
    atm_after = lax.ppermute(atm_latent, "tile", downs)

    depth = depth.reshape(rows, cols)
    levels = jnp.arange(lev, dtype=jnp.int32)
    grid = ocean_state[0].reshape(lev, rows, cols, width)

    def edge(row):
        wet = (levels[:, None] < depth[row][None, :]).astype(BF16)
        return (grid[:, row] * wet[:, :, None]).reshape(lev * cols, width)

    before = lax.ppermute(edge(rows - 1), "tile", ups)
    after = lax.ppermute(edge(0), "tile", downs)

    def exchange(x):
        return [
            lax.ppermute(x, "mem", [(i, (i + k) % members) for i in range(members)])
            for k in range(1, members)
        ]

    deep_cap = capacity((lev - 1) * inner, 0.5625)
    edge_cap = capacity(lev * cols, 0.65625)
    wet_deep = jnp.sum(jnp.maximum(depth[1 : rows - 1] - 1, 0))
    wet_top = jnp.sum(jnp.maximum(depth[0], 0))
    wet_low = jnp.sum(jnp.maximum(depth[rows - 1], 0))
    over = (wet_deep > deep_cap) | (wet_top > edge_cap) | (wet_low > edge_cap)
    flag = over.astype(jnp.int32).reshape(1)

    hbm = pl.BlockSpec(memory_space=pl.ANY)
    vmem = pl.BlockSpec(memory_space=pltpu.VMEM)
    tok = lambda *s: jax.ShapeDtypeStruct((*s, width), BF16)
    conv_flops = lambda n, c: 2 * 9 * n * c * width * width
    dma = pltpu.SemaphoreType.DMA
    slack = cols + 16

    deep_mixed, deep_normed, deep_packed, base = pl.pallas_call(
        functools.partial(inner_kernel, deep_cap),
        in_specs=[hbm, vmem, hbm],
        out_specs=[hbm, hbm, hbm, vmem],
        out_shape=[
            tok(lev - 1, inner),
            tok(lev - 1, inner),
            tok(deep_cap),
            jax.ShapeDtypeStruct((inner, width), F32),
        ],
        scratch_shapes=[
            pltpu.VMEM((lev, cells, width), BF16),
            pltpu.VMEM(conv_weight.shape, BF16),
            pltpu.VMEM((lev - 1, inner, width), BF16),
            pltpu.VMEM((lev - 1, inner, width), BF16),
            pltpu.VMEM((deep_cap + slack, width), BF16),
            dma((lev,)),
            dma,
            dma((lev - 1, 2)),
            dma,
        ],
        compiler_params=params(24),
        cost_estimate=cost(conv_flops(lev, inner), lev * inner * width * 8),
        name="inner",
    )(ocean_state, depth, conv_weight)
    deep_others = exchange(deep_packed)

    first = (lax.axis_index("tile") - R) * atm_blk
    ids = jnp.clip(src_blocks - first, 0, 3 * atm_blk - 1)
    full = lambda a: pl.BlockSpec(a.shape, lambda i, *_: (0,) * a.ndim)
    surf_mixed, surf_normed, edge_forcing = pl.pallas_call(
        surface_kernel,
        grid_spec=pltpu.PrefetchScalarGridSpec(
            num_scalar_prefetch=2,
            grid=(1,),
            in_specs=[full(a) for a in (base, depth, atm_before, atm_latent, atm_after, remap_weight)],
            out_specs=[
                pl.BlockSpec((1, inner, width), lambda i, *_: (0, 0, 0)),
                pl.BlockSpec((1, inner, width), lambda i, *_: (0, 0, 0)),
                pl.BlockSpec((2 * cols, width), lambda i, *_: (0, 0)),
            ],
            scratch_shapes=[pltpu.VMEM((3 * own, width), BF16), pltpu.VMEM((cells, width), F32)],
        ),
        out_shape=[tok(1, inner), tok(1, inner), jax.ShapeDtypeStruct((2 * cols, width), F32)],
        compiler_params=params(24, 1),
        cost_estimate=cost(conv_flops(1, inner), cells * width * 16),
        name="surface",
    )(ids, live, base, depth, atm_before, atm_latent, atm_after, remap_weight)
    surf_others = exchange(surf_normed)

    edge_mixed, edge_normed, top_packed, low_packed = pl.pallas_call(
        functools.partial(edge_kernel, edge_cap),
        in_specs=[hbm, vmem, hbm, hbm, hbm, vmem],
        out_specs=[hbm] * 4,
        out_shape=[tok(lev, 2 * cols), tok(lev, 2 * cols), tok(edge_cap), tok(edge_cap)],
        scratch_shapes=[
            pltpu.VMEM((lev, cells, width), BF16),
            pltpu.VMEM(conv_weight.shape, BF16),
            pltpu.VMEM((lev * cols, width), BF16),
            pltpu.VMEM((lev * cols, width), BF16),
            pltpu.VMEM((lev, 2 * cols, width), BF16),
            pltpu.VMEM((lev, 2 * cols, width), BF16),
            pltpu.VMEM((edge_cap + slack, width), BF16),
            pltpu.VMEM((edge_cap + slack, width), BF16),
            dma((lev, 3)),
            dma,
            dma((lev, 2)),
            dma((2,)),
        ],
        compiler_params=params(24),
        cost_estimate=cost(conv_flops(lev, 2 * cols), lev * cols * width * 16),
        name="edge",
    )(ocean_state, depth, conv_weight, before, after, edge_forcing)
    top_others = exchange(top_packed)
    low_others = exchange(low_packed)

    deep_whole, edge_whole = lax.cond(
        over,
        lambda a, b: (exchange(a), exchange(b)),
        lambda a, b: ([a] * (members - 1), [b] * (members - 1)),
        deep_normed,
        edge_normed,
    )
    shape = ocean_state.shape
    weights = (depth, qkv_weight, out_weight)
    out = attend(
        flag,
        [surf_normed, deep_normed],
        [surf_mixed, deep_mixed],
        surf_others,
        deep_others,
        deep_whole,
        *weights,
        list(range(1, rows - 1)),
        None,
        shape,
    )
    for row, got in ((0, top_others), (rows - 1, low_others)):
        out = attend(
            flag, [edge_normed], [edge_mixed], [], got, edge_whole, *weights, [row], out, shape
        )
    return out


def solution(mesh):
    return jax.shard_map(
        body,
        mesh=mesh,
        in_specs=(
            P("mem", "tile", None),
            P("mem", None, "tile", None),
            P("tile"),
            P("tile", None),
            P("tile"),
            P("tile", None, None, None),
            P(),
            P(),
            P(),
        ),
        out_specs=P("mem", None, "tile", None),
        check_vma=False,
    )
```

time: 84.5 us -> 75.2 us (0.89)
  waiting for transfers between devices: 28 us -> 3.55 us
  starting transfers between devices: 9.17 us -> 15.6 us
  local copies, waits for them, and re-layouts: 6.48 us -> 9.13 us
  between operations: 0.08 us -> 2.26 us
  Pallas kernels: 37.8 us -> 39.7 us
  other arithmetic: 2.36 us -> 4.12 us
    ppermute x3 -> x4, waiting for transfers between devices: 22.3 us -> 3.54 us  [exchange(): lax.ppermute(x, 'mem', [(i, (i + k) % members) for i in range(members)])]
    ppermute x2 -> x4, waiting for transfers between devices: 5.68 us -> 0.01 us  [the longest x1 0.01 us: body(): atm_before = lax.ppermute(atm_latent, 'tile', ups)]
    ppermute x2 -> x4, starting transfers between devices: 5.56 us -> 11.1 us  [the longest x1 3.64 us: body(): atm_after = lax.ppermute(atm_latent, 'tile', downs)]
    reduce_sum x0 -> x2, other arithmetic: none -> 2.11 us  [the longest x1 1.48 us: body(): wet_low = jnp.sum(jnp.maximum(depth[rows - 1], 0))]
    cond x0 -> x2, local copies, waits for them, and re-layouts: none -> 1.92 us
    pallas_call x5 -> x6, Pallas kernels: 37.8 us -> 39.7 us  [the longest x3 16.9 us: attend(): pl.pallas_call(functools.partial(attend_kernel, others, nparts, tuple(row...]
    unnamed x14 -> x38, local copies, waits for them, and re-layouts: 4.01 us -> 5.78 us
    mul x1 -> x2, other arithmetic: 0.34 us -> 1.99 us  [edge(): return (grid[:, row] * wet[:, :, None]).reshape(lev * cols, width)]
  transfers between devices with their start and end apart: 5 -> 8, of which waited for: 2 -> 1; matrix products, arithmetic and copies ran while one was open for 3% -> 10% of each run, Pallas kernels for 35% -> 48%
where the time goes in v2:
time: 75.2 us; the launch traced here: 74.4 us
  Pallas kernels  39.7 us (53%)
  starting transfers between devices  15.6 us (21%)
  local copies, waits for them, and re-layouts  9.13 us (12%)
  other arithmetic  4.12 us (5%)
  waiting for transfers between devices  3.55 us (5%)
  between operations  2.26 us (3%)
    pallas_call x3, Pallas kernels, attend(): pl.pallas_call(functools.partial(attend_kernel, others, nparts, tuple(row...  16.9 us
    pallas_call x1, Pallas kernels, body(): pl.pallas_call(functools.partial(edge_kernel, edge_cap), in_specs=[hbm, v...  12 us
    pallas_call x1, Pallas kernels, body(): pl.pallas_call(functools.partial(inner_kernel, deep_cap), in_specs=[hbm,...  9.07 us
    unnamed x38, local copies, waits for them, and re-layouts  5.78 us
    ppermute x4, starting transfers between devices, exchange(): lax.ppermute(x, 'mem', [(i, (i + k) % members) for i in range(members)])  4.55 us
    ppermute x1, starting transfers between devices, body(): atm_after = lax.ppermute(atm_latent, 'tile', downs)  3.64 us
    ppermute x1, starting transfers between devices, body(): after = lax.ppermute(edge(0), 'tile', downs)  3.63 us
    ppermute x4, waiting for transfers between devices, exchange(): lax.ppermute(x, 'mem', [(i, (i + k) % members) for i in range(members)])  3.54 us
  transfers between devices with their start and end apart: 8, of which 1 were waited for; matrix products, arithmetic and copies ran while one was open for 10% of the time, Pallas kernels for 48%

profile of v2, /device:TPU:18, one launch (start us, length us, event | category | flops | bytes accessed | tf_op | source)
XLA Modules:
  0.0 74.4 jit_solution(894695017065854824)
XLA Ops:
  0.0 1.9 %collective-permute-start.4 = (bf16[1,512,256]{2,1,0:T(8,128)(2,1)}, bf16[1,512,256]{2,1,0:T(8,128)(2,1)S(1)}, u32[]{:S(2)}, u32[]{:S(2)}) collective-permute-start(bf16[1,512,256]{2,1,0:T(8,128)(2,1)} %atm_ref.1), channel_id=1, source_target_pairs={{0,2},{2,4},{4,6},{6,8},{8,10},{10,12},{12,14},{14,16},{16,18},{18... | collective-permute-start | bytes 786440 | tf_op jit(solution)/shard_map/ppermute | solution.py:495
  1.9 3.6 %collective-permute-start.5 = (bf16[1,512,256]{2,1,0:T(8,128)(2,1)}, bf16[1,512,256]{2,1,0:T(8,128)(2,1)S(1)}, u32[]{:S(2)}, u32[]{:S(2)}) collective-permute-start(bf16[1,512,256]{2,1,0:T(8,128)(2,1)} %atm_ref.1), channel_id=1, source_target_pairs={{2,0},{4,2},{6,4},{8,6},{10,8},{12,10},{14,12},{16,14},{18,16},{20... | collective-permute-start | bytes 786440 | tf_op jit(solution)/shard_map/ppermute | solution.py:496
  5.6 1.5 %maximum_reduce_fusion.1 = (s32[]{:T(128)}, s32[]{:T(128)}, s32[128]{0:T(128)S(1)}, s32[128]{0:T(128)S(1)}) fusion(s32[512]{0:T(512)} %param.13), kind=kLoop, calls=%fused_computation.8 | loop fusion | flops 510 | bytes 2056 | tf_op jit(solution)/shard_map/reduce_sum | solution.py:519
  7.1 0.0 copy-start.7
  7.1 0.0 copy-start.9
  7.1 1.4 %fusion.2 = (bf16[8,1,128,256]{3,2,1,0:T(8,128)(2,1)S(1)}, bf16[8,1,128,256]{3,2,1,0:T(8,128)(2,1)S(1)}) fusion(bf16[8,4,128,256]{3,2,1,0:T(8,128)(2,1)} %bitcast.20), kind=kLoop, calls=%fused_computation.10 | loop fusion | bytes 2097152 | tf_op jit(solution)/shard_map/slice | solution.py:504
  8.5 1.0 %bitcast_multiply_fusion.1 = bf16[1024,256]{1,0:T(8,128)(2,1)} fusion(bf16[8,1,128,256]{3,2,1,0:T(8,128)(2,1)S(1)} %get-tuple-element.44, bf16[1024]{0:T(1024)(128)(2,1)S(1)} %fusion), kind=kLoop, calls=%fused_computation.1 | loop fusion | flops 262144 | bytes 1050624 | tf_op jit(solution)/shard_map/mul | solution.py:504
  9.5 1.9 %collective-permute-start.2 = (bf16[1024,256]{1,0:T(8,128)(2,1)}, bf16[1024,256]{1,0:T(8,128)(2,1)}, u32[]{:S(2)}, u32[]{:S(2)}) collective-permute-start(bf16[1024,256]{1,0:T(8,128)(2,1)} %bitcast_multiply_fusion.1), channel_id=1, source_target_pairs={{0,2},{2,4},{4,6},{6,8},{8,10},{10,12},{12,14},{14,16},{16,18},{18... | collective-permute-start | bytes 1572872 | tf_op jit(solution)/shard_map/ppermute | solution.py:506
  11.5 1.0 %bitcast_multiply_fusion = bf16[1024,256]{1,0:T(8,128)(2,1)} fusion(bf16[8,1,128,256]{3,2,1,0:T(8,128)(2,1)S(1)} %get-tuple-element.43, bf16[1024]{0:T(1024)(128)(2,1)S(1)} %fusion.1), kind=kLoop, calls=%fused_computation | loop fusion | flops 262144 | bytes 1050624 | tf_op jit(solution)/shard_map/mul | solution.py:504
  12.4 3.6 %collective-permute-start.3 = (bf16[1024,256]{1,0:T(8,128)(2,1)}, bf16[1024,256]{1,0:T(8,128)(2,1)}, u32[]{:S(2)}, u32[]{:S(2)}) collective-permute-start(bf16[1024,256]{1,0:T(8,128)(2,1)} %bitcast_multiply_fusion), channel_id=1, source_target_pairs={{2,0},{4,2},{6,4},{8,6},{10,8},{12,10},{14,12},{16,14},{18,16},{20... | collective-permute-start | bytes 1572872 | tf_op jit(solution)/shard_map/ppermute | solution.py:507
  16.1 0.0 copy-start.18
  16.2 9.1 %inner.1 = (bf16[7,256,256]{2,1,0:T(8,128)(2,1)S(1)}, bf16[7,256,256]{2,1,0:T(8,128)(2,1)}, bf16[1008,256]{1,0:T(8,128)(2,1)}, f32[256,256]{1,0:T(8,128)S(1)}) custom-call(bf16[1,8,512,256]{3,2,1,0:T(8,128)(2,1)S(1)} %copy-done.2, s32[4,128]{1,0:T(4,128)S(1)} %bitcast.21, bf16[3,3,256,256]{3,2,1,0:T(8,128)(2,1)S(1)} %copy-done.9), custom_call_target="tpu_custom_call" | custom-call | flops 2415919104 | bytes 4194304 | tf_op jit(solution)/shard_map/inner/pallas_call | solution.py:530
  25.3 0.7 copy-done.5
  26.0 0.9 %copy-done.13 = bf16[7,256,256]{2,1,0:T(8,128)(2,1)} copy-done((bf16[7,256,256]{2,1,0:T(8,128)(2,1)}, bf16[7,256,256]{2,1,0:T(8,128)(2,1)S(1)}, u32[]{:S(2)}) %copy-start.13) | copy-done | bytes 917528
  26.9 1.5 %collective-permute-start.9 = (bf16[1008,256]{1,0:T(8,128)(2,1)}, bf16[1008,256]{1,0:T(8,128)(2,1)}, u32[]{:S(2)}, u32[]{:S(2)}) collective-permute-start(bf16[1008,256]{1,0:T(8,128)(2,1)} %get-tuple-element.39), channel_id=1, source_target_pairs={{0,1},{1,0},{2,3},{3,2},{4,5},{5,4},{6,7},{7,6},{8,9},{9,8},{10,11... | collective-permute-start | bytes 1548296 | tf_op jit(solution)/shard_map/ppermute | solution.py:511
  28.4 0.6 maximum_reduce_fusion
  30.9 0.9 %copy-done.6 = f32[256,256]{1,0:T(8,128)S(1)} copy-done((f32[256,256]{1,0:T(8,128)S(1)}, f32[256,256]{1,0:T(8,128)}, u32[]{:S(2)}) %copy-start.6) | copy-done | bytes 262168
  31.9 1.7 %surface.1 = (bf16[1,256,256]{2,1,0:T(8,128)(2,1)S(1)}, bf16[1,256,256]{2,1,0:T(8,128)(2,1)}, f32[256,256]{1,0:T(8,128)S(1)}) custom-call(s32[4,4]{1,0:T(4,128)S(1)} %subtract_clamp_fusion.ids_ref, s32[4]{0:T(128)S(1)} %copy-done.8, f32[256,256]{1,0:T(8,128)S(1)} %copy-done.6, s32[4,128]{1,0:T(4,128)S(1)} %bitcast.22, ...), custom_call_target="tpu_custom_call" | custom-call | flops 301989888 | bytes 2097152 | tf_op jit(solution)/shard_map/surface/pallas_call | solution.py:560
  33.6 0.5 collective-permute-start.8
  34.1 1.3 %copy-done.10 = bf16[3,3,256,256]{3,2,1,0:T(8,128)(2,1)S(1)} copy-done((bf16[3,3,256,256]{3,2,1,0:T(8,128)(2,1)S(1)}, bf16[3,3,256,256]{3,2,1,0:T(8,128)(2,1)}, u32[]{:S(2)}) %copy-start.10) | copy-done | bytes 1179672
  35.4 12.0 %edge.1 = (bf16[8,256,256]{2,1,0:T(8,128)(2,1)S(1)}, bf16[8,256,256]{2,1,0:T(8,128)(2,1)S(1)}, bf16[672,256]{1,0:T(8,128)(2,1)S(1)}, bf16[672,256]{1,0:T(8,128)(2,1)}) custom-call(bf16[1,8,512,256]{3,2,1,0:T(8,128)(2,1)S(1)} %copy-done.2, s32[4,128]{1,0:T(4,128)S(1)} %bitcast.23, bf16[3,3,256,256]{3,2,1,0:T(8,128)(2,1)S(1)} %copy-done.10, ...), custom_call_target="tpu_custom_call" | custom-call | flops 2415919104 | bytes 4194304 | tf_op jit(solution)/shard_map/edge/pallas_call | solution.py:580
  47.4 0.7 copy-done.11
  48.1 1.6 %collective-permute-start.6 = (bf16[672,256]{1,0:T(8,128)(2,1)}, bf16[672,256]{1,0:T(8,128)(2,1)S(1)}, u32[]{:S(2)}, u32[]{:S(2)}) collective-permute-start(bf16[672,256]{1,0:T(8,128)(2,1)} %get-tuple-element.32), channel_id=1, source_target_pairs={{0,1},{1,0},{2,3},{3,2},{4,5},{5,4},{6,7},{7,6},{8,9},{9,8},{10,11... | collective-permute-start | bytes 1032200 | tf_op jit(solution)/shard_map/ppermute | solution.py:511
  49.7 1.9 %conditional.1 = (bf16[7,256,256]{2,1,0:T(8,128)(2,1)}, bf16[8,256,256]{2,1,0:T(8,128)(2,1)}) conditional(s32[]{:T(128)} %convert_element_type.18, (bf16[7,256,256]{2,1,0:T(8,128)(2,1)S(1)}, bf16[8,256,256]{2,1,0:T(8,128)(2,1)S(1)}) %tuple.19, (bf16[7,256,256]{2,1,0:T(8,128)(2,1)S(1)}, bf16[8,256,256]{2,1,0:T(8,128)(2,1)S(1)}) %tuple.20), branch_computations={%region_3.4_spmd, %region_4.5_spmd} | conditional | bytes 7864416 | solution.py:606
  49.7 1.0 %copy.16 = bf16[7,256,256]{2,1,0:T(8,128)(2,1)} copy(bf16[7,256,256]{2,1,0:T(8,128)(2,1)S(1)} %get-tuple-element.47) | data formatting | bytes 1835008 | tf_op jit(solution)/shard_map/cond
  50.7 1.0 %copy.17 = bf16[8,256,256]{2,1,0:T(8,128)(2,1)} copy(bf16[8,256,256]{2,1,0:T(8,128)(2,1)S(1)} %get-tuple-element.48) | data formatting | bytes 2097152 | tf_op jit(solution)/shard_map/cond
  51.7 0.9 %collective-permute-start.7 = (bf16[672,256]{1,0:T(8,128)(2,1)S(1)}, bf16[672,256]{1,0:T(8,128)(2,1)S(1)}, u32[]{:S(2)}, u32[]{:S(2)}) collective-permute-start(bf16[672,256]{1,0:T(8,128)(2,1)S(1)} %copy-done.12), channel_id=1, source_target_pairs={{0,1},{1,0},{2,3},{3,2},{4,5},{5,4},{6,7},{7,6},{8,9},{9,8},{10,11... | collective-permute-start | bytes 1032200 | tf_op jit(solution)/shard_map/ppermute | solution.py:511
  52.6 1.2 %copy-done.14 = bf16[7,256,256]{2,1,0:T(8,128)(2,1)S(1)} copy-done((bf16[7,256,256]{2,1,0:T(8,128)(2,1)S(1)}, bf16[7,256,256]{2,1,0:T(8,128)(2,1)}, u32[]{:S(2)}) %copy-start.14) | copy-done | bytes 917528
  53.8 8.7 %attend.3.refs_7_ = bf16[1,8,512,256]{3,2,1,0:T(8,128)(2,1)} custom-call(s32[1]{0:T(128)} %bitcast.flag_ref, bf16[1,256,256]{2,1,0:T(8,128)(2,1)} %get-tuple-element.36.refs_0_, bf16[7,256,256]{2,1,0:T(8,128)(2,1)} %get-tuple-element.33.refs_1_, bf16[1,256,256]{2,1,0:T(8,128)(2,1)S(1)} %get-tuple-element.37.refs_2_, bf16[7,256,256]{2,1,0:T(8,128)(2,1)S(1)} %copy-done.14, ...), custom_call_target="tpu_custom_call" | custom-call | flops 4294967296 | bytes 5242880 | tf_op jit(solution)/shard_map/attend/pallas_call | solution.py:445
  62.5 3.5 %collective-permute-done.7.refs_2_ = bf16[672,256]{1,0:T(8,128)(2,1)S(1)} collective-permute-done((bf16[672,256]{1,0:T(8,128)(2,1)S(1)}, bf16[672,256]{1,0:T(8,128)(2,1)S(1)}, u32[]{:S(2)}, u32[]{:S(2)}) %collective-permute-start.7) | collective-permute-done | bytes 344096 | tf_op jit(solution)/shard_map/ppermute | solution.py:511
  66.0 4.1 %attend.4.refs_7_ = bf16[1,8,512,256]{3,2,1,0:T(8,128)(2,1)} custom-call(s32[1]{0:T(128)} %bitcast.flag_ref, bf16[8,256,256]{2,1,0:T(8,128)(2,1)S(1)} %copy-done.16, bf16[8,256,256]{2,1,0:T(8,128)(2,1)S(1)} %get-tuple-element.31.refs_1_, bf16[672,256]{1,0:T(8,128)(2,1)S(1)} %collective-permute-done.7.refs_2_, ...), custom_call_target="tpu_custom_call", output_to_operand_aliasing={{}: (8, {})} | custom-call | flops 2147483648 | bytes 2621440 | tf_op jit(solution)/shard_map/attend/pallas_call | solution.py:445
  70.2 4.1 %attend.5 = bf16[1,8,512,256]{3,2,1,0:T(8,128)(2,1)} custom-call(s32[1]{0:T(128)} %bitcast.flag_ref, bf16[8,256,256]{2,1,0:T(8,128)(2,1)S(1)} %copy-done.16, bf16[8,256,256]{2,1,0:T(8,128)(2,1)S(1)} %get-tuple-element.31.refs_1_, bf16[672,256]{1,0:T(8,128)(2,1)S(1)} %collective-permute-done.6.refs_2_, ...), custom_call_target="tpu_custom_call", output_to_operand_aliasing={{}: (8, {})} | custom-call | flops 2147483648 | bytes 2621440 | tf_op jit(solution)/shard_map/attend/pallas_call | solution.py:445
  (41 shorter events, 0.1 us)
Async XLA Ops:
  0.0 30.9 %collective-permute-start.4 = (bf16[1,512,256]{2,1,0:T(8,128)(2,1)}, bf16[1,512,256]{2,1,0:T(8,128)(2,1)S(1)}, u32[]{:S(2)}, u32[]{:S(2)}) collective-permute-start(bf16[1,512,256]{2,1,0:T(8,128)(2,1)} %atm_ref.1), channel_id=1, source_target_pairs={{0,2},{2,4},{4,6},{6,8},{8,10},{10,12},{12,14},{14,16},{16,18},{18... | collective-permute-start | bytes 786440 | tf_op jit(solution)/shard_map/ppermute | solution.py:495
  1.9 29.0 %collective-permute-start.5 = (bf16[1,512,256]{2,1,0:T(8,128)(2,1)}, bf16[1,512,256]{2,1,0:T(8,128)(2,1)S(1)}, u32[]{:S(2)}, u32[]{:S(2)}) collective-permute-start(bf16[1,512,256]{2,1,0:T(8,128)(2,1)} %atm_ref.1), channel_id=1, source_target_pairs={{2,0},{4,2},{6,4},{8,6},{10,8},{12,10},{14,12},{16,14},{18,16},{20... | collective-permute-start | bytes 786440 | tf_op jit(solution)/shard_map/ppermute | solution.py:496
  7.1 9.0 %copy-start.2 = (bf16[1,8,512,256]{3,2,1,0:T(8,128)(2,1)S(1)}, bf16[1,8,512,256]{3,2,1,0:T(8,128)(2,1)}, u32[]{:S(2)}) copy-start(bf16[1,8,512,256]{3,2,1,0:T(8,128)(2,1)} %state_hbm.3) | copy-start | bytes 6291460
  7.1 9.0 %copy-start.7 = (s32[512]{0:T(512)S(1)}, s32[512]{0:T(512)}, u32[]{:S(2)}) copy-start(s32[512]{0:T(512)} %param.13) | copy-start | bytes 6148
  7.1 9.0 %copy-start.9 = (bf16[3,3,256,256]{3,2,1,0:T(8,128)(2,1)S(1)}, bf16[3,3,256,256]{3,2,1,0:T(8,128)(2,1)}, u32[]{:S(2)}) copy-start(bf16[3,3,256,256]{3,2,1,0:T(8,128)(2,1)} %weight_hbm.3) | copy-start | bytes 3538948
  9.5 24.6 %collective-permute-start.2 = (bf16[1024,256]{1,0:T(8,128)(2,1)}, bf16[1024,256]{1,0:T(8,128)(2,1)}, u32[]{:S(2)}, u32[]{:S(2)}) collective-permute-start(bf16[1024,256]{1,0:T(8,128)(2,1)} %bitcast_multiply_fusion.1), channel_id=1, source_target_pairs={{0,2},{2,4},{4,6},{6,8},{8,10},{10,12},{12,14},{14,16},{16,18},{18... | collective-permute-start | bytes 1572872 | tf_op jit(solution)/shard_map/ppermute | solution.py:506
  12.4 21.7 %collective-permute-start.3 = (bf16[1024,256]{1,0:T(8,128)(2,1)}, bf16[1024,256]{1,0:T(8,128)(2,1)}, u32[]{:S(2)}, u32[]{:S(2)}) collective-permute-start(bf16[1024,256]{1,0:T(8,128)(2,1)} %bitcast_multiply_fusion), channel_id=1, source_target_pairs={{2,0},{4,2},{6,4},{8,6},{10,8},{12,10},{14,12},{16,14},{18,16},{20... | collective-permute-start | bytes 1572872 | tf_op jit(solution)/shard_map/ppermute | solution.py:507
  16.1 14.7 %copy-start.18 = (s32[4,4]{1,0:T(4,128)S(1)}, s32[4,4]{1,0:T(4,128)}, u32[]{:S(2)}) copy-start(s32[4,4]{1,0:T(4,128)} %param.14) | copy-start | bytes 196
  16.1 14.8 %copy-start.3 = (bf16[4,4,128,128]{3,2,1,0:T(8,128)(2,1)S(1)}, bf16[4,4,128,128]{3,2,1,0:T(8,128)(2,1)}, u32[]{:S(2)}) copy-start(bf16[4,4,128,128]{3,2,1,0:T(8,128)(2,1)} %remap_ref.1) | copy-start | bytes 1572868
  16.1 14.8 %copy-start.4 = (bf16[1,512,256]{2,1,0:T(8,128)(2,1)S(1)}, bf16[1,512,256]{2,1,0:T(8,128)(2,1)}, u32[]{:S(2)}) copy-start(bf16[1,512,256]{2,1,0:T(8,128)(2,1)} %atm_ref.1) | copy-start | bytes 786436
  16.2 14.8 %copy-start.8 = (s32[4]{0:T(128)S(1)}, s32[4]{0:T(128)}, u32[]{:S(2)}) copy-start(s32[4]{0:T(128)} %live_ref.1) | copy-start | bytes 52
  25.2 0.7 copy-start.5
  25.9 0.9 %copy-start.13 = (bf16[7,256,256]{2,1,0:T(8,128)(2,1)}, bf16[7,256,256]{2,1,0:T(8,128)(2,1)S(1)}, u32[]{:S(2)}) copy-start(bf16[7,256,256]{2,1,0:T(8,128)(2,1)S(1)} %get-tuple-element.38.refs_3_) | copy-start | bytes 2752516
  26.9 25.7 %collective-permute-start.9 = (bf16[1008,256]{1,0:T(8,128)(2,1)}, bf16[1008,256]{1,0:T(8,128)(2,1)}, u32[]{:S(2)}, u32[]{:S(2)}) collective-permute-start(bf16[1008,256]{1,0:T(8,128)(2,1)} %get-tuple-element.39), channel_id=1, source_target_pairs={{0,1},{1,0},{2,3},{3,2},{4,5},{5,4},{6,7},{7,6},{8,9},{9,8},{10,11... | collective-permute-start | bytes 1548296 | tf_op jit(solution)/shard_map/ppermute | solution.py:511
  30.9 1.0 %copy-start.6 = (f32[256,256]{1,0:T(8,128)S(1)}, f32[256,256]{1,0:T(8,128)}, u32[]{:S(2)}) copy-start(f32[256,256]{1,0:T(8,128)} %copy-done.5) | copy-start | bytes 786436
  33.6 19.0 %collective-permute-start.8 = (bf16[1,256,256]{2,1,0:T(8,128)(2,1)}, bf16[1,256,256]{2,1,0:T(8,128)(2,1)S(1)}, u32[]{:S(2)}, u32[]{:S(2)}) collective-permute-start(bf16[1,256,256]{2,1,0:T(8,128)(2,1)} %get-tuple-element.36.refs_0_), channel_id=1, source_target_pairs={{0,1},{1,0},{2,3},{3,2},{4,5},{5,4},{6,7},{7,6},{8,9},{9,8},{10,11... | collective-permute-start | bytes 393224 | tf_op jit(solution)/shard_map/ppermute | solution.py:511
  34.1 1.3 %copy-start.10 = (bf16[3,3,256,256]{3,2,1,0:T(8,128)(2,1)S(1)}, bf16[3,3,256,256]{3,2,1,0:T(8,128)(2,1)}, u32[]{:S(2)}) copy-start(bf16[3,3,256,256]{3,2,1,0:T(8,128)(2,1)} %weight_hbm.3) | copy-start | bytes 3538948
  35.4 14.3 %copy-start.17 = (bf16[7,256,256]{2,1,0:T(8,128)(2,1)S(1)}, bf16[7,256,256]{2,1,0:T(8,128)(2,1)}, u32[]{:S(2)}) copy-start(bf16[7,256,256]{2,1,0:T(8,128)(2,1)} %get-tuple-element.33.refs_1_) | copy-start | bytes 2752516
  47.4 0.7 copy-start.11
  48.1 1.6 %copy-start.15 = (bf16[8,256,256]{2,1,0:T(8,128)(2,1)}, bf16[8,256,256]{2,1,0:T(8,128)(2,1)S(1)}, u32[]{:S(2)}) copy-start(bf16[8,256,256]{2,1,0:T(8,128)(2,1)S(1)} %get-tuple-element.30.refs_0_) | copy-start | bytes 3145732
  48.1 4.5 %copy-start = (bf16[256,768]{1,0:T(8,128)(2,1)S(1)}, bf16[256,768]{1,0:T(8,128)(2,1)}, u32[]{:S(2)}) copy-start(bf16[256,768]{1,0:T(8,128)(2,1)} %refs_5_.3) | copy-start | bytes 1179652
  48.1 4.5 %copy-start.1 = (bf16[256,256]{1,0:T(8,128)(2,1)S(1)}, bf16[256,256]{1,0:T(8,128)(2,1)}, u32[]{:S(2)}) copy-start(bf16[256,256]{1,0:T(8,128)(2,1)} %refs_6_.3) | copy-start | bytes 393220
  48.1 3.5 %copy-start.12 = (bf16[672,256]{1,0:T(8,128)(2,1)S(1)}, bf16[672,256]{1,0:T(8,128)(2,1)}, u32[]{:S(2)}) copy-start(bf16[672,256]{1,0:T(8,128)(2,1)} %copy-done.11) | copy-start | bytes 1032196
  48.1 22.0 %collective-permute-start.6 = (bf16[672,256]{1,0:T(8,128)(2,1)}, bf16[672,256]{1,0:T(8,128)(2,1)S(1)}, u32[]{:S(2)}, u32[]{:S(2)}) collective-permute-start(bf16[672,256]{1,0:T(8,128)(2,1)} %get-tuple-element.32), channel_id=1, source_target_pairs={{0,1},{1,0},{2,3},{3,2},{4,5},{5,4},{6,7},{7,6},{8,9},{9,8},{10,11... | collective-permute-start | bytes 1032200 | tf_op jit(solution)/shard_map/ppermute | solution.py:511
  51.7 14.4 %collective-permute-start.7 = (bf16[672,256]{1,0:T(8,128)(2,1)S(1)}, bf16[672,256]{1,0:T(8,128)(2,1)S(1)}, u32[]{:S(2)}, u32[]{:S(2)}) collective-permute-start(bf16[672,256]{1,0:T(8,128)(2,1)S(1)} %copy-done.12), channel_id=1, source_target_pairs={{0,1},{1,0},{2,3},{3,2},{4,5},{5,4},{6,7},{7,6},{8,9},{9,8},{10,11... | collective-permute-start | bytes 1032200 | tf_op jit(solution)/shard_map/ppermute | solution.py:511
  52.6 1.2 %copy-start.14 = (bf16[7,256,256]{2,1,0:T(8,128)(2,1)S(1)}, bf16[7,256,256]{2,1,0:T(8,128)(2,1)}, u32[]{:S(2)}) copy-start(bf16[7,256,256]{2,1,0:T(8,128)(2,1)} %copy-done.13) | copy-start | bytes 2752516
  53.8 12.2 %copy-start.16 = (bf16[8,256,256]{2,1,0:T(8,128)(2,1)S(1)}, bf16[8,256,256]{2,1,0:T(8,128)(2,1)}, u32[]{:S(2)}) copy-start(bf16[8,256,256]{2,1,0:T(8,128)(2,1)} %copy-done.15) | copy-start | bytes 3145732

commit v3 on v2

v3 whole, which is shorter than its diff:
```python
import functools
import math

import jax
import jax.numpy as jnp
from jax import lax
from jax.experimental import pallas as pl
from jax.experimental.pallas import tpu as pltpu
from jax.sharding import PartitionSpec as P

HEADS = 4
R = 1
GROUP = 16
EPS = 1e-06
NEG = -1e30
F32 = jnp.float32
BF16 = jnp.bfloat16
MIB = 1024 * 1024


def params(mib, steps=0):
    return pltpu.CompilerParams(
        dimension_semantics=("arbitrary",) * steps if steps else None, vmem_limit_bytes=mib * MIB
    )


def cost(flops, nbytes):
    return pl.CostEstimate(flops=int(flops), bytes_accessed=int(nbytes), transcendentals=0)


def capacity(tokens, share):
    return -(-int(tokens * share) // 16) * 16


def row_plan(depth_row, lev):
    cols = depth_row.shape[1]
    level = lax.broadcasted_iota(jnp.int32, (lev, cols), 0).astype(F32)
    wet = (depth_row > level).astype(F32)
    upper = (
        lax.broadcasted_iota(jnp.int32, (cols, cols), 0)
        < lax.broadcasted_iota(jnp.int32, (cols, cols), 1)
    )
    upper = upper.astype(F32).astype(BF16)
    rank = jnp.dot(wet.astype(BF16), upper, preferred_element_type=F32)
    counts = [jnp.sum(wet[l : l + 1]).astype(jnp.int32) for l in range(lev)]
    return wet, rank, counts


def offsets(plans, first, lev):
    at, place = jnp.int32(0), {}
    for l in range(first, lev):
        for r, plan in enumerate(plans):
            place[l, r] = at
            at = at + plan[2][l]
    return place


def segment(wet, rank, offset, cap):
    cols = wet.shape[1]
    base = jnp.minimum((offset // 16) * 16, cap)
    target = jnp.where(wet > 0, rank + (offset - base).astype(F32), -1.0)
    slot = lax.broadcasted_iota(jnp.int32, (cols + 16, cols), 0).astype(F32)
    return pl.multiple_of(base, 16), (slot == target).astype(F32).astype(BF16)


def pack(buf_ref, wet, rank, offset, cap, tokens):
    base, hot = segment(wet, rank, offset, cap)
    rows = jnp.dot(hot, tokens, preferred_element_type=F32).astype(BF16)
    head = pl.ds(base, 16)
    buf_ref[head, :] = buf_ref[head, :] + rows[:16]
    buf_ref[pl.ds(pl.multiple_of(base + 16, 16), rows.shape[0] - 16), :] = rows[16:]


def unpack(buf_ref, wet, rank, offset, cap):
    base, hot = segment(wet, rank, offset, cap)
    rows = buf_ref[pl.ds(base, hot.shape[0]), :]
    return lax.dot_general(
        hot, rows, (((0,), (0,)), ((), ())), preferred_element_type=F32
    ).astype(BF16)


def column(depth_row):
    cols = depth_row.shape[1]
    return jnp.broadcast_to(depth_row, (cols, cols)).T


def widen(x, width):
    return jnp.concatenate([x] * (width // x.shape[1]), axis=1)


def stencil(taps, weight_ref, cols):
    count, width = taps[0].shape
    x = jnp.concatenate(taps, axis=1)
    sums = [
        jnp.dot(x, weight_ref[:, dc].reshape(3 * width, -1), preferred_element_type=F32)
        for dc in range(3)
    ]
    col = lax.broadcasted_iota(jnp.int32, (count, 1), 0) % cols
    left = jnp.where(col == 0, 0.0, pltpu.roll(sums[0], 1, axis=0))
    right = jnp.where(col == cols - 1, 0.0, pltpu.roll(sums[2], count - 1, axis=0))
    return sums[1] + left + right


def normalise(mixed):
    mf = mixed.astype(F32)
    mean = jnp.mean(mf * mf, axis=-1, keepdims=True)
    return (mf * lax.rsqrt(mean + EPS)).astype(BF16)


def prep_kernel(caps, side_ref, near_ref, far_ref, atm_ref, depth_ref, on_ref, off_ref, flag_ref):
    _, lev, cols, width = near_ref.shape
    rows = depth_ref.shape[0]
    for block, row, out in ((near_ref, 0, on_ref), (far_ref, 1, off_ref)):
        deep = column(depth_ref[pl.ds(side_ref[row], 1), :].astype(F32))
        for l in range(lev):
            wet = (deep > l).astype(F32).astype(BF16)
            out[l * cols : (l + 1) * cols] = block[0, l] * widen(wet, width)
    on_ref[lev * cols :] = atm_ref[0]
    d = depth_ref[...].astype(F32)
    near = depth_ref[pl.ds(side_ref[0], 1), :].astype(F32)
    far = depth_ref[pl.ds(side_ref[1], 1), :].astype(F32)
    counts = [
        jnp.sum(jnp.maximum(d[1 : rows - 1] - 1.0, 0.0)),
        jnp.sum(jnp.maximum(near - 1.0, 0.0)),
        jnp.sum(far),
    ]
    over = jnp.int32(0)
    for count, cap in zip(counts, caps):
        over = over | (count > cap).astype(jnp.int32)
    flag_ref[0] = over


def inner_kernel(
    cap,
    state,
    depth_ref,
    weight,
    mixed_hbm,
    normed_hbm,
    packed_hbm,
    base_ref,
    mixed,
    normed,
    packed,
    out_sem,
    packed_sem,
):
    _, lev, cells, width = state.shape
    rows, cols = depth_ref.shape
    packed[...] = jnp.zeros_like(packed)
    d = depth_ref[...].astype(F32)
    plans = [row_plan(d[r : r + 1], lev) for r in range(1, rows - 1)]
    place = offsets(plans, 1, lev)
    deep = jnp.concatenate([column(d[r : r + 1]) for r in range(rows)], axis=0)
    count = cells - 2 * cols
    stores = []
    for l in list(range(1, lev)) + [0]:
        wet = (deep > l).astype(F32)
        x = state[0, l] * widen(wet.astype(BF16), width)
        taps = [x[dr * cols : dr * cols + count] for dr in range(3)]
        total = stencil(taps, weight, cols)
        new = taps[1].astype(F32) + widen(wet[cols : cols + count], width) * total
        if l == 0:
            base_ref[...] = new
            continue
        new = new.astype(BF16)
        mixed[l - 1] = new
        tokens = normalise(new)
        normed[l - 1] = tokens
        for k, (buf, out) in enumerate(((mixed, mixed_hbm), (normed, normed_hbm))):
            store = pltpu.make_async_copy(buf.at[l - 1], out.at[l - 1], out_sem.at[l - 1, k])
            store.start()
            stores.append(store)
        for r, plan in enumerate(plans):
            pack(
                packed,
                plan[0][l : l + 1],
                plan[1][l : l + 1],
                place[l, r],
                cap,
                tokens[r * cols : (r + 1) * cols],
            )
        if l == lev - 1:
            store = pltpu.make_async_copy(packed.at[pl.ds(0, cap)], packed_hbm, packed_sem)
            store.start()
            stores.append(store)
    for store in stores:
        store.wait()


def surface_kernel(
    ids_ref,
    live_ref,
    side_ref,
    base_ref,
    near_base_ref,
    depth_ref,
    on_ref,
    off_ref,
    atm_ref,
    remap_ref,
    mixed_ref,
    normed_ref,
    far_ref,
    window_ref,
    forcing_ref,
):
    rows, cols = depth_ref.shape
    width = base_ref.shape[-1]
    own = atm_ref.shape[1]
    blocks, pairs = remap_ref.shape[0], remap_ref.shape[1]
    near, far = side_ref[0], side_ref[1]
    on_at = jnp.where(near == 0, 0, 2 * own)
    window_ref[pl.ds(pl.multiple_of(on_at, own), own)] = on_ref[on_ref.shape[0] - own :]
    window_ref[pl.ds(pl.multiple_of(2 * own - on_at, own), own)] = off_ref[0]
    window_ref[own : 2 * own] = atm_ref[0]
    for b in range(blocks):
        acc = jnp.zeros((cols, width), F32)
        for p in range(pairs):
            on = (p < live_ref[b]).astype(F32)
            start = pl.multiple_of(ids_ref[b, p] * cols, cols)
            acc = acc + on * jnp.dot(
                remap_ref[b, p], window_ref[pl.ds(start, cols), :], preferred_element_type=F32
            )
        forcing_ref[b] = acc
    d = depth_ref[...].astype(F32)
    near_row = depth_ref[pl.ds(near, 1), :].astype(F32)
    for k in range(rows - 1):
        at = slice(k * cols, (k + 1) * cols)
        last = k == rows - 2
        wet = (column(near_row if last else d[k + 1 : k + 2]) > 0).astype(F32)
        part = near_base_ref[...] if last else base_ref[at]
        forcing = forcing_ref[near] if last else forcing_ref[k + 1]
        new = (part + widen(wet, width) * forcing).astype(BF16)
        mixed_ref[0, at] = new
        normed_ref[0, at] = normalise(new)
    far_ref[...] = forcing_ref[far]


def row_kernel(cap, first, which, side_ref, state, depth_ref, weight, halo, *refs):
    refs = list(refs)
    forcing_ref = None if first else refs.pop(0)
    mixed_hbm, normed_hbm, packed_hbm = refs[:3]
    refs = refs[3:]
    base_ref = refs.pop(0) if first else None
    tap, mixed, normed, packed, out_sem, packed_sem = refs
    _, lev, cells, width = state.shape
    rows, cols = depth_ref.shape
    row = side_ref[which]
    top = row == 0
    beside = jnp.where(top, 1, rows - 2)
    outer = jnp.where(top, 0, 2)
    packed[...] = jnp.zeros_like(packed)
    own_depth = depth_ref[pl.ds(row, 1), :].astype(F32)
    plan = row_plan(own_depth, lev)
    place = offsets([plan], first, lev)
    deep, deep_beside = column(own_depth), column(depth_ref[pl.ds(beside, 1), :].astype(F32))
    at = pl.multiple_of(row * cols, cols)
    at_beside = pl.multiple_of(beside * cols, cols)
    wets = []
    for l in range(lev):
        rows_l = slice(l * cols, (l + 1) * cols)
        wet = (deep > l).astype(F32)
        wets.append(wet)
        wet_beside = (deep_beside > l).astype(F32)
        tap[1, rows_l] = state[0, l, pl.ds(at, cols)] * widen(wet.astype(BF16), width)
        tap[2 - outer, rows_l] = state[0, l, pl.ds(at_beside, cols)] * widen(
            wet_beside.astype(BF16), width
        )
        tap[outer, rows_l] = halo[rows_l]
    stores = []
    half = lev // 2
    for start in range(0, lev, half):
        rows_b = slice(start * cols, (start + half) * cols)
        taps = [tap[dr, rows_b] for dr in range(3)]
        total = stencil(taps, weight, cols)
        for k in range(half):
            l = start + k
            rows_k = slice(k * cols, (k + 1) * cols)
            part = total[rows_k]
            if l == 0 and not first:
                part = part + forcing_ref[...]
            new = taps[1][rows_k].astype(F32) + widen(wets[l], width) * part
            if l < first:
                base_ref[...] = new
                continue
            new = new.astype(BF16)
            mixed[l - first] = new
            tokens = normalise(new)
            normed[l - first] = tokens
            pack(packed, plan[0][l : l + 1], plan[1][l : l + 1], place[l, 0], cap, tokens)
    for k, (buf, out) in enumerate(((mixed, mixed_hbm), (normed, normed_hbm))):
        store = pltpu.make_async_copy(buf, out, out_sem.at[k])
        store.start()
        stores.append(store)
    store = pltpu.make_async_copy(packed.at[pl.ds(0, cap)], packed_hbm, packed_sem)
    store.start()
    stores.append(store)
    for store in stores:
        store.wait()


def attend_kernel(others, nparts, which, first, cap, aliased, flag_ref, side_ref, *refs):
    refs = list(refs)
    take = lambda k: [refs.pop(0) for _ in range(k)]
    own_normed = take(nparts)
    own_mixed = take(nparts)
    surf = take(others) if first else []
    packed = take(others)
    whole = take(others)
    depth_ref, qkv_ref, wo_ref = take(3)
    if aliased:
        take(1)
    out_ref, q_ref, k_ref, v_ref, att_ref, buf_ref, token_ref, sem = refs
    lev, count, width = q_ref.shape
    members = others + 1
    head = width // HEADS
    pair = 2 * head
    step = pl.program_id(0)

    def keys_values(x, m):
        rows = slice(m * lev, (m + 1) * lev)
        kv = jnp.dot(x, qkv_ref[:, width:], preferred_element_type=F32).astype(BF16)
        k_ref[rows] = kv[:, :width].reshape(lev, count, width)
        v_ref[rows] = kv[:, width:].reshape(lev, count, width)

    two = which is None
    pick = lambda a, b: jnp.where(step == 0, a, b)
    if two:
        rows_d = [depth_ref[r : r + 1, :].astype(F32) for r in range(1, depth_ref.shape[0] - 1)]
        plans = [row_plan(row, lev) for row in rows_d]
        place = offsets(plans, first, lev)
        wet_row = pick(plans[0][0], plans[1][0])
        rank = pick(plans[0][1], plans[1][1])
        depth_row = pick(*rows_d)
    else:
        depth_row = depth_ref[pl.ds(side_ref[which], 1), :].astype(F32)
        plan = row_plan(depth_row, lev)
        place = offsets([plan], first, lev)
        wet_row, rank, _ = plan

    x = jnp.concatenate([p[...].reshape(-1, width) for p in own_normed], axis=0)
    q = jnp.dot(x, qkv_ref[:, 0:width], preferred_element_type=F32).astype(BF16)
    q_ref[...] = (q * (1.0 / math.sqrt(head))).astype(BF16).reshape(lev, count, width)
    keys_values(x, 0)
    for o in range(others):
        if first:
            token_ref[0] = surf[o][0]

        @pl.when(flag_ref[0] == 0)
        def _():
            buf_ref[0:cap] = packed[o][...]
            buf_ref[cap:] = jnp.zeros((buf_ref.shape[0] - cap, width), BF16)
            for l in range(first, lev):
                at = pick(place[l, 0], place[l, 1]) if two else place[l, 0]
                token_ref[l] = unpack(
                    buf_ref, wet_row[l : l + 1], rank[l : l + 1], at, cap
                )

        @pl.when(flag_ref[0] != 0)
        def _():
            copy = pltpu.make_async_copy(
                whole[o].at[:, pl.ds(pl.multiple_of(step * count, count), count)], token_ref.at[pl.ds(first, lev - first)], sem
            )
            copy.start()
            copy.wait()

        keys_values(token_ref[...].reshape(-1, width), o + 1)

    nq, nk = lev * GROUP, members * lev * GROUP
    groups = count // GROUP
    lanes_n = lev * GROUP
    cell = lax.broadcasted_iota(jnp.int32, (groups, count), 1)
    mine = (cell // GROUP == lax.broadcasted_iota(jnp.int32, (groups, count), 0)).astype(F32)
    spread = lax.broadcasted_iota(jnp.int32, (count, lanes_n), 0) % GROUP
    spread = (spread == lax.broadcasted_iota(jnp.int32, (count, lanes_n), 1) % GROUP).astype(F32)
    key_depth = jnp.dot(
        (mine * depth_row).astype(BF16), spread.astype(BF16), preferred_element_type=F32
    )
    key_level = lax.broadcasted_iota(jnp.int32, (groups, lanes_n), 1) // GROUP
    key_bias = jnp.where(key_depth > key_level.astype(F32), 0.0, NEG)
    qc = lax.broadcasted_iota(jnp.int32, (nq, nk), 0) % GROUP
    kc = lax.broadcasted_iota(jnp.int32, (nq, nk), 1) % GROUP
    same = jnp.where(qc == kc, 0.0, NEG)
    lane = lax.broadcasted_iota(jnp.int32, (1, pair), 1)
    low = (lane < head).astype(F32).astype(BF16)
    high = (lane >= head).astype(F32).astype(BF16)
    for g in range(groups):
        cells = slice(g * GROUP, (g + 1) * GROUP)
        bias = same + jnp.concatenate([key_bias[g : g + 1]] * members, axis=1)
        bias = jnp.concatenate([bias, bias], axis=0)
        for h in range(HEADS // 2):
            lanes = slice(h * pair, (h + 1) * pair)
            q = q_ref[:, cells, lanes].reshape(nq, pair)
            q = jnp.concatenate([q * low, q * high], axis=0)
            k = k_ref[:, cells, lanes].reshape(nk, pair)
            v = v_ref[:, cells, lanes].reshape(nk, pair)
            s = lax.dot_general(q, k, (((1,), (1,)), ((), ())), preferred_element_type=F32) + bias
            p = jnp.exp(s - jnp.max(s, axis=-1, keepdims=True))
            norm = 1.0 / jnp.sum(p, axis=-1, keepdims=True)
            o = jnp.dot(p.astype(BF16), v, preferred_element_type=F32) * norm
            o = jnp.where(lane < head, o[:nq], o[nq:])
            att_ref[:, cells, lanes] = o.astype(BF16).reshape(lev, GROUP, pair)
    proj = jnp.dot(att_ref[...].reshape(-1, width), wo_ref[...], preferred_element_type=F32)
    base = jnp.concatenate([p[...].reshape(-1, width) for p in own_mixed], axis=0).astype(F32)
    deep = column(depth_row)
    for l in range(lev):
        rows = slice(l * count, (l + 1) * count)
        wet = widen((deep > l).astype(F32), width)
        out_ref[0, l] = (base[rows] + wet * proj[rows]).astype(BF16)


def attend(
    flag, side, normed, mixed, surf, packed, whole, depth, qkv_weight, out_weight, which, out, shape
):
    others, nparts = len(packed), len(mixed)
    lev = sum(p.shape[0] for p in mixed)
    width = shape[-1]
    rows, cols = depth.shape
    cap = packed[0].shape[0]
    first = 1 if surf else 0
    steps = rows - 2 if which is None else 1
    row_of = lambda i, s: i + 1 if which is None else s[which]
    surf_at = 0 if which is None else rows - 2
    full2 = lambda a: pl.BlockSpec(a.shape, lambda i, *_: (0, 0))
    block = lambda n, at: pl.BlockSpec((n, cols, width), lambda i, *_: (0, i + at, 0))
    part = [block(p.shape[0], surf_at if first and k == 0 else 0) for k, p in enumerate(mixed)]
    hbm = pl.BlockSpec(memory_space=pl.ANY)
    in_specs = part * 2
    in_specs += [block(1, surf_at)] * len(surf)
    in_specs += [full2(p) for p in packed]
    in_specs += [hbm] * others
    in_specs += [full2(depth), full2(qkv_weight), full2(out_weight)]
    args = normed + mixed + surf + packed + whole + [depth, qkv_weight, out_weight]
    alias = {}
    if out is not None:
        in_specs.append(hbm)
        alias = {len(args) + 2: 0}
        args.append(out)
    tokens = lev * cols * steps
    members = others + 1
    return pl.pallas_call(
        functools.partial(attend_kernel, others, nparts, which, first, cap, out is not None),
        grid_spec=pltpu.PrefetchScalarGridSpec(
            num_scalar_prefetch=2,
            grid=(steps,),
            in_specs=in_specs,
            out_specs=pl.BlockSpec(
                (1, lev, cols, width), lambda i, f, s: (0, 0, row_of(i, s), 0)
            ),
            scratch_shapes=[
                pltpu.VMEM((lev, cols, width), BF16),
                pltpu.VMEM((members * lev, cols, width), BF16),
                pltpu.VMEM((members * lev, cols, width), BF16),
                pltpu.VMEM((lev, cols, width), BF16),
                pltpu.VMEM((cap + cols + 16, width), BF16),
                pltpu.VMEM((lev, cols, width), BF16),
                pltpu.SemaphoreType.DMA,
            ],
        ),
        out_shape=jax.ShapeDtypeStruct(shape, BF16),
        input_output_aliases=alias,
        compiler_params=params(20 if members <= 2 else 48, 1),
        cost_estimate=cost(tokens * width * width * 8 * (members + 2), tokens * width * 2 * 5),
        name="attend",
    )(flag, side, *args)


def body(
    atm_latent,
    ocean_state,
    depth,
    src_blocks,
    live,
    remap_weight,
    conv_weight,
    qkv_weight,
    out_weight,
):
    _, lev, cells, width = ocean_state.shape
    cols = remap_weight.shape[2]
    rows = cells // cols
    inner = cells - 2 * cols
    own = atm_latent.shape[1]
    atm_blk = own // cols
    tiles = lax.axis_size("tile")
    members = lax.axis_size("mem")
    tile = lax.axis_index("tile")

    def swap(x, first):
        pairs = [(i, i + 1) for i in range(first, tiles - 1, 2)]
        return lax.ppermute(x, "tile", pairs + [(b, a) for a, b in pairs])

    def exchange(x):
        return [
            lax.ppermute(x, "mem", [(i, (i + k) % members) for i in range(members)])
            for k in range(1, members)
        ]

    odd = tile % 2
    side = jnp.stack([(1 - odd) * (rows - 1), odd * (rows - 1)]).astype(jnp.int32)
    depth = depth.reshape(rows, cols)
    deep_cap = capacity((lev - 1) * inner, 0.5625)
    near_cap = capacity((lev - 1) * cols, 0.605)
    far_cap = capacity(lev * cols, 0.65625)

    hbm = pl.BlockSpec(memory_space=pltpu.HBM)
    vmem = pl.BlockSpec(memory_space=pltpu.VMEM)
    smem = pl.BlockSpec(memory_space=pltpu.SMEM)
    tok = lambda *s: jax.ShapeDtypeStruct((*s, width), BF16)
    row_f32 = jax.ShapeDtypeStruct((cols, width), F32)
    conv_flops = lambda n, c: 2 * 9 * n * c * width * width
    dma = pltpu.SemaphoreType.DMA
    slack = cols + 16
    full = lambda a: pl.BlockSpec(a.shape, lambda i, *_: (0,) * a.ndim)
    state_row = lambda k: pl.BlockSpec((1, lev, cols, width), lambda i, s: (0, 0, s[k], 0))

    off_atm = swap(atm_latent, 1)
    on_msg, off_msg, flag = pl.pallas_call(
        functools.partial(prep_kernel, (deep_cap, near_cap, far_cap)),
        grid_spec=pltpu.PrefetchScalarGridSpec(
            num_scalar_prefetch=1,
            grid=(1,),
            in_specs=[state_row(0), state_row(1), full(atm_latent), full(depth)],
            out_specs=[
                pl.BlockSpec((lev * cols + own, width), lambda i, s: (0, 0)),
                pl.BlockSpec((lev * cols, width), lambda i, s: (0, 0)),
                smem,
            ],
        ),
        out_shape=[
            tok(lev * cols + own),
            tok(lev * cols),
            jax.ShapeDtypeStruct((1,), jnp.int32),
        ],
        compiler_params=params(16, 1),
        cost_estimate=cost(lev * cols * width * 4, lev * cols * width * 10),
        name="prep",
    )(side, ocean_state, ocean_state, atm_latent, depth)
    off_halo = swap(off_msg, 1)
    on_halo = swap(on_msg, 0)

    deep_mixed, deep_normed, deep_packed, base = pl.pallas_call(
        functools.partial(inner_kernel, deep_cap),
        in_specs=[vmem, vmem, vmem],
        out_specs=[hbm, hbm, hbm, vmem],
        out_shape=[
            tok(lev - 1, inner),
            tok(lev - 1, inner),
            tok(deep_cap),
            jax.ShapeDtypeStruct((inner, width), F32),
        ],
        scratch_shapes=[
            pltpu.VMEM((lev - 1, inner, width), BF16),
            pltpu.VMEM((lev - 1, inner, width), BF16),
            pltpu.VMEM((deep_cap + slack, width), BF16),
            dma((lev - 1, 2)),
            dma,
        ],
        compiler_params=params(20),
        cost_estimate=cost(conv_flops(lev, inner), lev * inner * width * 8),
        name="inner",
    )(ocean_state, depth, conv_weight)
    deep_others = exchange(deep_packed)

    def row_conv(which, first, cap, halo, forcing):
        n = lev - first
        extra = [] if forcing is None else [forcing]
        return pl.pallas_call(
            functools.partial(row_kernel, cap, first, which),
            in_specs=[smem] + [vmem] * (4 + len(extra)),
            out_specs=[hbm] * 3 + [vmem] * first,
            out_shape=[tok(n, cols), tok(n, cols), tok(cap)] + [row_f32] * first,
            scratch_shapes=[
                pltpu.VMEM((3, lev * cols, width), BF16),
                pltpu.VMEM((n, cols, width), BF16),
                pltpu.VMEM((n, cols, width), BF16),
                pltpu.VMEM((cap + slack, width), BF16),
                dma((2,)),
                dma,
            ],
            compiler_params=params(20),
            cost_estimate=cost(conv_flops(lev, cols), lev * cols * width * 16),
            name="row",
        )(side, ocean_state, depth, conv_weight, halo, *extra)

    near_mixed, near_normed, near_packed, near_base = row_conv(0, 1, near_cap, on_halo, None)

    ids = jnp.clip(src_blocks - (tile - R) * atm_blk, 0, 3 * atm_blk - 1)
    surf_mixed, surf_normed, far_forcing = pl.pallas_call(
        surface_kernel,
        in_specs=[smem] * 3 + [vmem] * 7,
        out_specs=[pl.BlockSpec((1, inner + cols, width), lambda *_: (0, 0, 0))] * 2 + [vmem],
        out_shape=[tok(1, inner + cols), tok(1, inner + cols), row_f32],
        scratch_shapes=[pltpu.VMEM((3 * own, width), BF16), pltpu.VMEM((rows, cols, width), F32)],
        compiler_params=params(20),
        cost_estimate=cost(conv_flops(1, inner), cells * width * 16),
        name="surface",
    )(ids, live, side, base, near_base, depth, on_halo, off_atm, atm_latent, remap_weight)
    surf_others = exchange(surf_normed)
    near_others = exchange(near_packed)

    far_mixed, far_normed, far_packed = row_conv(1, 0, far_cap, off_halo, far_forcing)
    far_others = exchange(far_packed)

    deep_whole, near_whole, far_whole = lax.cond(
        flag[0] > 0,
        lambda *a: tuple(exchange(x) for x in a),
        lambda *a: tuple([x] * (members - 1) for x in a),
        deep_normed,
        near_normed,
        far_normed,
    )
    shape = ocean_state.shape
    weights = (depth, qkv_weight, out_weight)
    out = None
    for which, normed, mixed, surf, packed, whole in (
        (
            None,
            [surf_normed, deep_normed],
            [surf_mixed, deep_mixed],
            surf_others,
            deep_others,
            deep_whole,
        ),
        (
            0,
            [surf_normed, near_normed],
            [surf_mixed, near_mixed],
            surf_others,
            near_others,
            near_whole,
        ),
        (1, [far_normed], [far_mixed], [], far_others, far_whole),
    ):
        out = attend(
            flag, side, normed, mixed, surf, packed, whole, *weights, which, out, shape
        )
    return out


def solution(mesh):
    return jax.shard_map(
        body,
        mesh=mesh,
        in_specs=(
            P("mem", "tile", None),
            P("mem", None, "tile", None),
            P("tile"),
            P("tile", None),
            P("tile"),
            P("tile", None, None, None),
            P(),
            P(),
            P(),
        ),
        out_specs=P("mem", None, "tile", None),
        check_vma=False,
    )
```

time: 75.2 us -> 70.3 us (0.935)
  starting transfers between devices: 15.6 us -> 9.68 us
  other arithmetic: 4.12 us -> 0.08 us
  Pallas kernels: 39.7 us -> 43.5 us
  waiting for transfers between devices: 3.55 us -> 4.92 us
  local copies, waits for them, and re-layouts: 9.13 us -> 10.5 us
  between operations: 2.26 us -> 1.02 us
    ppermute x4 -> x3, starting transfers between devices: 11.1 us -> 5.64 us  [swap(): return lax.ppermute(x, 'tile', pairs + [(b, a) for a, b in pairs])]
    pallas_call x6 -> x8, Pallas kernels: 39.7 us -> 43.5 us  [the longest x3 22 us: attend(): pl.pallas_call(functools.partial(attend_kernel, others, nparts, which, fi...]
    reduce_sum x2 -> x0, other arithmetic: 2.11 us -> none  [the longest x1 1.48 us: body(): wet_low = jnp.sum(jnp.maximum(depth[rows - 1], 0))]
    mul x2 -> x0, other arithmetic: 1.99 us -> none  [edge(): return (grid[:, row] * wet[:, :, None]).reshape(lev * cols, width)]
    cond x2 -> x3, local copies, waits for them, and re-layouts: 1.92 us -> 3.58 us
    slice x1 -> x0, local copies, waits for them, and re-layouts: 1.42 us -> none  [edge(): return (grid[:, row] * wet[:, :, None]).reshape(lev * cols, width)]
    ppermute x4, waiting for transfers between devices: 3.54 us -> 4.92 us  [exchange(): lax.ppermute(x, 'mem', [(i, (i + k) % members) for i in range(members)])]
    unnamed x38 -> x50, local copies, waits for them, and re-layouts: 5.78 us -> 6.88 us
  transfers between devices with their start and end apart: 8 -> 7, of which waited for: 1 -> 1; matrix products, arithmetic and copies ran while one was open for 10% -> 5% of each run, Pallas kernels for 48% -> 49%
where the time goes in v3:
time: 70.3 us; the launch traced here: 69.7 us
  Pallas kernels  43.5 us (62%)
  local copies, waits for them, and re-layouts  10.5 us (15%)
  starting transfers between devices  9.68 us (14%)
  waiting for transfers between devices  4.92 us (7%)
  between operations  1.02 us (1%)
    pallas_call x3, Pallas kernels, attend(): pl.pallas_call(functools.partial(attend_kernel, others, nparts, which, fi...  22 us
    pallas_call x2, Pallas kernels, row_conv(): pl.pallas_call(functools.partial(row_kernel, cap, first, which), in_specs...  8.3 us
    pallas_call x1, Pallas kernels, body(): pl.pallas_call(functools.partial(inner_kernel, deep_cap), in_specs=[vmem,...  7.69 us
    unnamed x50, local copies, waits for them, and re-layouts  6.88 us
    ppermute x3, starting transfers between devices, swap(): return lax.ppermute(x, 'tile', pairs + [(b, a) for a, b in pairs])  5.64 us
    ppermute x4, waiting for transfers between devices, exchange(): lax.ppermute(x, 'mem', [(i, (i + k) % members) for i in range(members)])  4.92 us
    ppermute x4, starting transfers between devices, exchange(): lax.ppermute(x, 'mem', [(i, (i + k) % members) for i in range(members)])  4.05 us
    cond x3, local copies, waits for them, and re-layouts  3.58 us
  transfers between devices with their start and end apart: 7, of which 1 were waited for; matrix products, arithmetic and copies ran while one was open for 5% of the time, Pallas kernels for 49%

profile of v3, /device:TPU:18, one launch (start us, length us, event | category | flops | bytes accessed | tf_op | source)
XLA Modules:
  0.0 69.7 jit_solution(9694400060076857036)
XLA Ops:
  0.0 0.1 pad_add_fusion.side_ref
  0.1 1.6 %copy-done = bf16[1,8,512,256]{3,2,1,0:T(8,128)(2,1)S(1)} copy-done((bf16[1,8,512,256]{3,2,1,0:T(8,128)(2,1)S(1)}, bf16[1,8,512,256]{3,2,1,0:T(8,128)(2,1)}, u32[]{:S(2)}) %copy-start) | copy-done | bytes 2097176
  1.7 0.7 copy-done.3
  2.4 3.1 %prep.1 = (bf16[1536,256]{1,0:T(8,128)(2,1)}, bf16[1024,256]{1,0:T(8,128)(2,1)}, s32[1]{0:T(128)}) custom-call(s32[2]{0:T(128)S(1)} %pad_add_fusion.side_ref, bf16[1,8,512,256]{3,2,1,0:T(8,128)(2,1)S(1)} %copy-done, bf16[1,8,512,256]{3,2,1,0:T(8,128)(2,1)S(1)} %copy-done, bf16[1,512,256]{2,1,0:T(8,128)(2,1)} %atm_ref.3, s32[4,128]{1,0:T(4,128)S(1)} %bitcast.4), custom_call_target="tpu_custom_call" | custom-call | flops 1048576 | bytes 2621440 | tf_op jit(solution)/shard_map/prep/pallas_call | solution.py:519
  5.5 0.1 collective-permute-start.4
  5.5 2.5 %collective-permute-start.5 = (bf16[1,512,256]{2,1,0:T(8,128)(2,1)}, bf16[1,512,256]{2,1,0:T(8,128)(2,1)S(1)}, u32[]{:S(2)}, u32[]{:S(2)}) collective-permute-start(bf16[1,512,256]{2,1,0:T(8,128)(2,1)} %atm_ref.3), channel_id=1, source_target_pairs={{2,4},{6,8},{10,12},{14,16},{18,20},{22,24},{26,28},{4,2},{8,6},{1... | collective-permute-start | bytes 786440 | tf_op jit(solution)/shard_map/ppermute | solution.py:492
  8.1 0.0 copy-start.24
  8.1 3.0 %collective-permute-start.3 = (bf16[1024,256]{1,0:T(8,128)(2,1)}, bf16[1024,256]{1,0:T(8,128)(2,1)}, u32[]{:S(2)}, u32[]{:S(2)}) collective-permute-start(bf16[1024,256]{1,0:T(8,128)(2,1)} %get-tuple-element.41), channel_id=1, source_target_pairs={{2,4},{6,8},{10,12},{14,16},{18,20},{22,24},{26,28},{4,2},{8,6},{1... | collective-permute-start | bytes 1572872 | tf_op jit(solution)/shard_map/ppermute | solution.py:492
  11.2 7.7 %inner.1 = (bf16[7,256,256]{2,1,0:T(8,128)(2,1)S(1)}, bf16[7,256,256]{2,1,0:T(8,128)(2,1)}, bf16[1008,256]{1,0:T(8,128)(2,1)}, f32[256,256]{1,0:T(8,128)S(1)}) custom-call(bf16[1,8,512,256]{3,2,1,0:T(8,128)(2,1)S(1)} %copy-done.1, s32[4,128]{1,0:T(4,128)S(1)} %bitcast.5, bf16[3,3,256,256]{3,2,1,0:T(8,128)(2,1)S(1)} %copy-done.6), custom_call_target="tpu_custom_call" | custom-call | flops 2415919104 | bytes 4194304 | tf_op jit(solution)/shard_map/inner/pallas_call | solution.py:543
  18.9 0.9 %copy-done.18 = bf16[7,256,256]{2,1,0:T(8,128)(2,1)} copy-done((bf16[7,256,256]{2,1,0:T(8,128)(2,1)}, bf16[7,256,256]{2,1,0:T(8,128)(2,1)S(1)}, u32[]{:S(2)}) %copy-start.18) | copy-done | bytes 917528
  19.8 1.5 %collective-permute-start.9 = (bf16[1008,256]{1,0:T(8,128)(2,1)}, bf16[1008,256]{1,0:T(8,128)(2,1)}, u32[]{:S(2)}, u32[]{:S(2)}) collective-permute-start(bf16[1008,256]{1,0:T(8,128)(2,1)} %get-tuple-element.58), channel_id=1, source_target_pairs={{0,1},{1,0},{2,3},{3,2},{4,5},{5,4},{6,7},{7,6},{8,9},{9,8},{10,11... | collective-permute-start | bytes 1548296 | tf_op jit(solution)/shard_map/ppermute | solution.py:496
  21.4 0.0 copy-start.7
  21.4 1.3 %copy-done.7 = bf16[3,3,256,256]{3,2,1,0:T(8,128)(2,1)S(1)} copy-done((bf16[3,3,256,256]{3,2,1,0:T(8,128)(2,1)S(1)}, bf16[3,3,256,256]{3,2,1,0:T(8,128)(2,1)}, u32[]{:S(2)}) %copy-start.7) | copy-done | bytes 1179672
  22.7 3.7 %row.2 = (bf16[7,128,256]{2,1,0:T(8,128)(2,1)S(1)}, bf16[7,128,256]{2,1,0:T(8,128)(2,1)S(1)}, bf16[544,256]{1,0:T(8,128)(2,1)S(1)}, f32[128,256]{1,0:T(8,128)S(1)}) custom-call(s32[2]{0:T(128)S(1)} %pad_add_fusion.side_ref, bf16[1,8,512,256]{3,2,1,0:T(8,128)(2,1)S(1)} %copy-done.1, s32[4,128]{1,0:T(4,128)S(1)} %bitcast.6, ...), custom_call_target="tpu_custom_call" | custom-call | flops 1207959552 | bytes 4194304 | tf_op jit(solution)/shard_map/row/pallas_call | solution.py:569
  26.4 0.7 %copy-done.9 = bf16[544,256]{1,0:T(8,128)(2,1)} copy-done((bf16[544,256]{1,0:T(8,128)(2,1)}, bf16[544,256]{1,0:T(8,128)(2,1)S(1)}, u32[]{:S(2)}) %copy-start.9) | copy-done | bytes 278552
  27.1 0.8 %copy-done.14 = bf16[7,128,256]{2,1,0:T(8,128)(2,1)} copy-done((bf16[7,128,256]{2,1,0:T(8,128)(2,1)}, bf16[7,128,256]{2,1,0:T(8,128)(2,1)S(1)}, u32[]{:S(2)}) %copy-start.14) | copy-done | bytes 458776
  27.9 2.4 %surface.1 = (bf16[1,384,256]{2,1,0:T(8,128)(2,1)S(1)}, bf16[1,384,256]{2,1,0:T(8,128)(2,1)}, f32[128,256]{1,0:T(8,128)S(1)}) custom-call(s32[4,4]{1,0:T(4,128)S(1)} %subtract_clamp_fusion.ids_ref, s32[4]{0:T(128)S(1)} %copy-done.5, s32[2]{0:T(128)S(1)} %pad_add_fusion.side_ref, f32[256,256]{1,0:T(8,128)S(1)} %get-tuple-element.42.base_ref, ...), custom_call_target="tpu_custom_call" | custom-call | flops 301989888 | bytes 2097152 | tf_op jit(solution)/shard_map/surface/pallas_call | solution.py:590
  30.3 0.5 collective-permute-start.7
  31.4 0.0 copy-start.20
  31.4 4.6 %row.3 = (bf16[8,128,256]{2,1,0:T(8,128)(2,1)S(1)}, bf16[8,128,256]{2,1,0:T(8,128)(2,1)}, bf16[672,256]{1,0:T(8,128)(2,1)S(1)}) custom-call(s32[2]{0:T(128)S(1)} %pad_add_fusion.side_ref, bf16[1,8,512,256]{3,2,1,0:T(8,128)(2,1)S(1)} %copy-done.1, s32[4,128]{1,0:T(4,128)S(1)} %bitcast.8, bf16[3,3,256,256]{3,2,1,0:T(8,128)(2,1)S(1)} %copy-done.7, ...), custom_call_target="tpu_custom_call" | custom-call | flops 1207959552 | bytes 4194304 | tf_op jit(solution)/shard_map/row/pallas_call | solution.py:569
  36.0 0.8 %copy-done.16 = bf16[8,128,256]{2,1,0:T(8,128)(2,1)} copy-done((bf16[8,128,256]{2,1,0:T(8,128)(2,1)}, bf16[8,128,256]{2,1,0:T(8,128)(2,1)S(1)}, u32[]{:S(2)}) %copy-start.16) | copy-done | bytes 524312
  36.8 0.0 copy-start.21
  36.9 3.6 %conditional.1 = (bf16[7,256,256]{2,1,0:T(8,128)(2,1)}, bf16[7,128,256]{2,1,0:T(8,128)(2,1)}, bf16[8,128,256]{2,1,0:T(8,128)(2,1)}) conditional(s32[]{:T(128)} %bitcast.3, (bf16[7,256,256]{2,1,0:T(8,128)(2,1)S(1)}, bf16[7,128,256]{2,1,0:T(8,128)(2,1)S(1)}, bf16[8,128,256]{2,1,0:T(8,128)(2,1)}) %tuple.15, (bf16[7,256,256]{2,1,0:T(8,128)(2,1)S(1)}, ...), branch_computations={%region_0.1_spmd, %region_1.2_spmd} | conditional | bytes 7602320 | solution.py:606
  36.9 0.9 %copy.12 = bf16[7,256,256]{2,1,0:T(8,128)(2,1)} copy(bf16[7,256,256]{2,1,0:T(8,128)(2,1)S(1)} %get-tuple-element.60) | data formatting | bytes 1835008 | tf_op jit(solution)/shard_map/cond
  37.8 0.8 %copy.13 = bf16[7,128,256]{2,1,0:T(8,128)(2,1)} copy(bf16[7,128,256]{2,1,0:T(8,128)(2,1)S(1)} %get-tuple-element.61) | data formatting | bytes 917504 | tf_op jit(solution)/shard_map/cond
  38.6 1.9 %copy.14 = bf16[8,128,256]{2,1,0:T(8,128)(2,1)} copy(bf16[8,128,256]{2,1,0:T(8,128)(2,1)} %get-tuple-element.62) | data formatting | bytes 1048576 | tf_op jit(solution)/shard_map/cond
  40.5 1.5 %collective-permute-start.6 = (bf16[672,256]{1,0:T(8,128)(2,1)S(1)}, bf16[672,256]{1,0:T(8,128)(2,1)S(1)}, u32[]{:S(2)}, u32[]{:S(2)}) collective-permute-start(bf16[672,256]{1,0:T(8,128)(2,1)S(1)} %get-tuple-element.48), channel_id=1, source_target_pairs={{0,1},{1,0},{2,3},{3,2},{4,5},{5,4},{6,7},{7,6},{8,9},{9,8},{10,11... | collective-permute-start | bytes 1032200 | tf_op jit(solution)/shard_map/ppermute | solution.py:496
  42.0 0.5 collective-permute-start.8
  42.6 9.7 %attend.3.refs_10_ = bf16[1,8,512,256]{3,2,1,0:T(8,128)(2,1)} custom-call(s32[1]{0:T(128)} %get-tuple-element.40.flag_ref, s32[2]{0:T(128)S(1)} %pad_add_fusion.side_ref, bf16[1,384,256]{2,1,0:T(8,128)(2,1)} %get-tuple-element.52.refs_0_, bf16[7,256,256]{2,1,0:T(8,128)(2,1)S(1)} %copy-done.21, bf16[1,384,256]{2,1,0:T(8,128)(2,1)S(1)} %copy-done.12, ...), custom_call_target="tpu_custom_call" | custom-call | flops 4294967296 | bytes 5242880 | tf_op jit(solution)/shard_map/attend/pallas_call | solution.py:442
  52.3 4.9 %collective-permute-done.8.refs_5_ = bf16[544,256]{1,0:T(8,128)(2,1)S(1)} collective-permute-done((bf16[544,256]{1,0:T(8,128)(2,1)S(1)}, bf16[544,256]{1,0:T(8,128)(2,1)S(1)}, u32[]{:S(2)}, u32[]{:S(2)}) %collective-permute-start.8) | collective-permute-done | bytes 278560 | tf_op jit(solution)/shard_map/ppermute | solution.py:496
  57.2 6.1 %attend.4.refs_7_ = bf16[1,8,512,256]{3,2,1,0:T(8,128)(2,1)} custom-call(s32[1]{0:T(128)} %get-tuple-element.40.flag_ref, s32[2]{0:T(128)S(1)} %pad_add_fusion.side_ref, bf16[1,384,256]{2,1,0:T(8,128)(2,1)} %get-tuple-element.52.refs_0_, bf16[7,128,256]{2,1,0:T(8,128)(2,1)S(1)} %copy-done.23, ...), custom_call_target="tpu_custom_call", output_to_operand_aliasing={{}: (12, {})} | custom-call | flops 2147483648 | bytes 2621440 | tf_op jit(solution)/shard_map/attend/pallas_call | solution.py:442
  63.3 6.2 %attend.5 = bf16[1,8,512,256]{3,2,1,0:T(8,128)(2,1)} custom-call(s32[1]{0:T(128)} %get-tuple-element.40.flag_ref, s32[2]{0:T(128)S(1)} %pad_add_fusion.side_ref, bf16[8,128,256]{2,1,0:T(8,128)(2,1)} %get-tuple-element.46.refs_0_, bf16[8,128,256]{2,1,0:T(8,128)(2,1)S(1)} %copy-done.17, ...), custom_call_target="tpu_custom_call", output_to_operand_aliasing={{}: (9, {})} | custom-call | flops 2147483648 | bytes 2621440 | tf_op jit(solution)/shard_map/attend/pallas_call | solution.py:442
  (46 shorter events, 0.1 us)
Async XLA Ops:
  0.1 1.6 %copy-start = (bf16[1,8,512,256]{3,2,1,0:T(8,128)(2,1)S(1)}, bf16[1,8,512,256]{3,2,1,0:T(8,128)(2,1)}, u32[]{:S(2)}) copy-start(bf16[1,8,512,256]{3,2,1,0:T(8,128)(2,1)} %state.5) | copy-start | bytes 6291460
  1.7 0.7 copy-start.3
  2.3 8.8 %copy-start.1 = (bf16[1,8,512,256]{3,2,1,0:T(8,128)(2,1)S(1)}, bf16[1,8,512,256]{3,2,1,0:T(8,128)(2,1)}, u32[]{:S(2)}) copy-start(bf16[1,8,512,256]{3,2,1,0:T(8,128)(2,1)} %state.5) | copy-start | bytes 6291460
  2.4 8.8 %copy-start.4 = (s32[512]{0:T(512)S(1)}, s32[512]{0:T(512)}, u32[]{:S(2)}) copy-start(s32[512]{0:T(512)} %param.13) | copy-start | bytes 6148
  2.4 8.8 %copy-start.6 = (bf16[3,3,256,256]{3,2,1,0:T(8,128)(2,1)S(1)}, bf16[3,3,256,256]{3,2,1,0:T(8,128)(2,1)}, u32[]{:S(2)}) copy-start(bf16[3,3,256,256]{3,2,1,0:T(8,128)(2,1)} %weight.5) | copy-start | bytes 3538948
  5.5 15.9 %collective-permute-start.4 = (bf16[1536,256]{1,0:T(8,128)(2,1)}, bf16[1536,256]{1,0:T(8,128)(2,1)S(1)}, u32[]{:S(2)}, u32[]{:S(2)}) collective-permute-start(bf16[1536,256]{1,0:T(8,128)(2,1)} %get-tuple-element.43), channel_id=1, source_target_pairs={{0,2},{4,6},{8,10},{12,14},{16,18},{20,22},{24,26},{28,30},{2,0},{... | collective-permute-start | bytes 2359304 | tf_op jit(solution)/shard_map/ppermute | solution.py:492
  5.5 22.4 %collective-permute-start.5 = (bf16[1,512,256]{2,1,0:T(8,128)(2,1)}, bf16[1,512,256]{2,1,0:T(8,128)(2,1)S(1)}, u32[]{:S(2)}, u32[]{:S(2)}) collective-permute-start(bf16[1,512,256]{2,1,0:T(8,128)(2,1)} %atm_ref.3), channel_id=1, source_target_pairs={{2,4},{6,8},{10,12},{14,16},{18,20},{22,24},{26,28},{4,2},{8,6},{1... | collective-permute-start | bytes 786440 | tf_op jit(solution)/shard_map/ppermute | solution.py:492
  8.1 13.2 %copy-start.24 = (s32[4,4]{1,0:T(4,128)S(1)}, s32[4,4]{1,0:T(4,128)}, u32[]{:S(2)}) copy-start(s32[4,4]{1,0:T(4,128)} %param.14) | copy-start | bytes 196
  8.1 23.3 %collective-permute-start.3 = (bf16[1024,256]{1,0:T(8,128)(2,1)}, bf16[1024,256]{1,0:T(8,128)(2,1)}, u32[]{:S(2)}, u32[]{:S(2)}) collective-permute-start(bf16[1024,256]{1,0:T(8,128)(2,1)} %get-tuple-element.41), channel_id=1, source_target_pairs={{2,4},{6,8},{10,12},{14,16},{18,20},{22,24},{26,28},{4,2},{8,6},{1... | collective-permute-start | bytes 1572872 | tf_op jit(solution)/shard_map/ppermute | solution.py:492
  18.9 0.9 %copy-start.18 = (bf16[7,256,256]{2,1,0:T(8,128)(2,1)}, bf16[7,256,256]{2,1,0:T(8,128)(2,1)S(1)}, u32[]{:S(2)}) copy-start(bf16[7,256,256]{2,1,0:T(8,128)(2,1)S(1)} %get-tuple-element.57.refs_3_) | copy-start | bytes 2752516
  19.8 22.7 %collective-permute-start.9 = (bf16[1008,256]{1,0:T(8,128)(2,1)}, bf16[1008,256]{1,0:T(8,128)(2,1)}, u32[]{:S(2)}, u32[]{:S(2)}) collective-permute-start(bf16[1008,256]{1,0:T(8,128)(2,1)} %get-tuple-element.58), channel_id=1, source_target_pairs={{0,1},{1,0},{2,3},{3,2},{4,5},{5,4},{6,7},{7,6},{8,9},{9,8},{10,11... | collective-permute-start | bytes 1548296 | tf_op jit(solution)/shard_map/ppermute | solution.py:496
  21.3 6.6 %copy-start.2 = (bf16[4,4,128,128]{3,2,1,0:T(8,128)(2,1)S(1)}, bf16[4,4,128,128]{3,2,1,0:T(8,128)(2,1)}, u32[]{:S(2)}) copy-start(bf16[4,4,128,128]{3,2,1,0:T(8,128)(2,1)} %remap_ref.1) | copy-start | bytes 1572868
  21.3 6.6 %copy-start.5 = (s32[4]{0:T(128)S(1)}, s32[4]{0:T(128)}, u32[]{:S(2)}) copy-start(s32[4]{0:T(128)} %live_ref.1) | copy-start | bytes 52
  21.4 1.3 %copy-start.7 = (bf16[3,3,256,256]{3,2,1,0:T(8,128)(2,1)S(1)}, bf16[3,3,256,256]{3,2,1,0:T(8,128)(2,1)}, u32[]{:S(2)}) copy-start(bf16[3,3,256,256]{3,2,1,0:T(8,128)(2,1)} %weight.5) | copy-start | bytes 3538948
  26.4 0.7 %copy-start.9 = (bf16[544,256]{1,0:T(8,128)(2,1)}, bf16[544,256]{1,0:T(8,128)(2,1)S(1)}, u32[]{:S(2)}) copy-start(bf16[544,256]{1,0:T(8,128)(2,1)S(1)} %get-tuple-element.55) | copy-start | bytes 835588
  27.1 0.8 %copy-start.14 = (bf16[7,128,256]{2,1,0:T(8,128)(2,1)}, bf16[7,128,256]{2,1,0:T(8,128)(2,1)S(1)}, u32[]{:S(2)}) copy-start(bf16[7,128,256]{2,1,0:T(8,128)(2,1)S(1)} %get-tuple-element.54.refs_3_) | copy-start | bytes 1376260
  27.9 9.0 %copy-start.22 = (bf16[7,128,256]{2,1,0:T(8,128)(2,1)}, bf16[7,128,256]{2,1,0:T(8,128)(2,1)S(1)}, u32[]{:S(2)}) copy-start(bf16[7,128,256]{2,1,0:T(8,128)(2,1)S(1)} %get-tuple-element.50.refs_1_) | copy-start | bytes 1376260
  30.3 5.7 %copy-start.11 = (bf16[1,384,256]{2,1,0:T(8,128)(2,1)}, bf16[1,384,256]{2,1,0:T(8,128)(2,1)S(1)}, u32[]{:S(2)}) copy-start(bf16[1,384,256]{2,1,0:T(8,128)(2,1)S(1)} %get-tuple-element.53.refs_2_) | copy-start | bytes 589828
  30.3 12.2 %collective-permute-start.7 = (bf16[1,384,256]{2,1,0:T(8,128)(2,1)}, bf16[1,384,256]{2,1,0:T(8,128)(2,1)S(1)}, u32[]{:S(2)}, u32[]{:S(2)}) collective-permute-start(bf16[1,384,256]{2,1,0:T(8,128)(2,1)} %get-tuple-element.52.refs_0_), channel_id=1, source_target_pairs={{0,1},{1,0},{2,3},{3,2},{4,5},{5,4},{6,7},{7,6},{8,9},{9,8},{10,11... | collective-permute-start | bytes 589832 | tf_op jit(solution)/shard_map/ppermute | solution.py:496
  31.4 5.5 %copy-start.20 = (bf16[7,256,256]{2,1,0:T(8,128)(2,1)S(1)}, bf16[7,256,256]{2,1,0:T(8,128)(2,1)}, u32[]{:S(2)}) copy-start(bf16[7,256,256]{2,1,0:T(8,128)(2,1)} %get-tuple-element.49.refs_1_) | copy-start | bytes 2752516
  36.0 0.8 %copy-start.16 = (bf16[8,128,256]{2,1,0:T(8,128)(2,1)}, bf16[8,128,256]{2,1,0:T(8,128)(2,1)S(1)}, u32[]{:S(2)}) copy-start(bf16[8,128,256]{2,1,0:T(8,128)(2,1)S(1)} %get-tuple-element.47.refs_1_) | copy-start | bytes 1572868
  36.8 5.2 %copy-start.10 = (bf16[544,256]{1,0:T(8,128)(2,1)S(1)}, bf16[544,256]{1,0:T(8,128)(2,1)}, u32[]{:S(2)}) copy-start(bf16[544,256]{1,0:T(8,128)(2,1)} %copy-done.9) | copy-start | bytes 835588
  36.8 5.7 %copy-start.8 = (bf16[256,768]{1,0:T(8,128)(2,1)S(1)}, bf16[256,768]{1,0:T(8,128)(2,1)}, u32[]{:S(2)}) copy-start(bf16[256,768]{1,0:T(8,128)(2,1)} %refs_5_.1) | copy-start | bytes 1179652
  36.8 5.7 %copy-start.13 = (bf16[256,256]{1,0:T(8,128)(2,1)S(1)}, bf16[256,256]{1,0:T(8,128)(2,1)}, u32[]{:S(2)}) copy-start(bf16[256,256]{1,0:T(8,128)(2,1)} %refs_6_.1) | copy-start | bytes 393220
  36.8 5.7 %copy-start.19 = (bf16[7,256,256]{2,1,0:T(8,128)(2,1)S(1)}, bf16[7,256,256]{2,1,0:T(8,128)(2,1)}, u32[]{:S(2)}) copy-start(bf16[7,256,256]{2,1,0:T(8,128)(2,1)} %copy-done.18) | copy-start | bytes 2752516
  36.8 5.7 %copy-start.21 = (bf16[7,256,256]{2,1,0:T(8,128)(2,1)S(1)}, bf16[7,256,256]{2,1,0:T(8,128)(2,1)}, u32[]{:S(2)}) copy-start(bf16[7,256,256]{2,1,0:T(8,128)(2,1)} %get-tuple-element.49.refs_1_) | copy-start | bytes 2752516
  36.9 5.7 %copy-start.12 = (bf16[1,384,256]{2,1,0:T(8,128)(2,1)S(1)}, bf16[1,384,256]{2,1,0:T(8,128)(2,1)}, u32[]{:S(2)}) copy-start(bf16[1,384,256]{2,1,0:T(8,128)(2,1)} %copy-done.11) | copy-start | bytes 589828
  40.5 22.8 %collective-permute-start.6 = (bf16[672,256]{1,0:T(8,128)(2,1)S(1)}, bf16[672,256]{1,0:T(8,128)(2,1)S(1)}, u32[]{:S(2)}, u32[]{:S(2)}) collective-permute-start(bf16[672,256]{1,0:T(8,128)(2,1)S(1)} %get-tuple-element.48), channel_id=1, source_target_pairs={{0,1},{1,0},{2,3},{3,2},{4,5},{5,4},{6,7},{7,6},{8,9},{9,8},{10,11... | collective-permute-start | bytes 1032200 | tf_op jit(solution)/shard_map/ppermute | solution.py:496
  42.0 15.2 %collective-permute-start.8 = (bf16[544,256]{1,0:T(8,128)(2,1)S(1)}, bf16[544,256]{1,0:T(8,128)(2,1)S(1)}, u32[]{:S(2)}, u32[]{:S(2)}) collective-permute-start(bf16[544,256]{1,0:T(8,128)(2,1)S(1)} %copy-done.10), channel_id=1, source_target_pairs={{0,1},{1,0},{2,3},{3,2},{4,5},{5,4},{6,7},{7,6},{8,9},{9,8},{10,11... | collective-permute-start | bytes 835592 | tf_op jit(solution)/shard_map/ppermute | solution.py:496
  42.6 14.7 %copy-start.15 = (bf16[7,128,256]{2,1,0:T(8,128)(2,1)S(1)}, bf16[7,128,256]{2,1,0:T(8,128)(2,1)}, u32[]{:S(2)}) copy-start(bf16[7,128,256]{2,1,0:T(8,128)(2,1)} %copy-done.14) | copy-start | bytes 1376260
  42.6 14.7 %copy-start.23 = (bf16[7,128,256]{2,1,0:T(8,128)(2,1)S(1)}, bf16[7,128,256]{2,1,0:T(8,128)(2,1)}, u32[]{:S(2)}) copy-start(bf16[7,128,256]{2,1,0:T(8,128)(2,1)} %copy-done.22) | copy-start | bytes 1376260
  57.2 6.1 %copy-start.17 = (bf16[8,128,256]{2,1,0:T(8,128)(2,1)S(1)}, bf16[8,128,256]{2,1,0:T(8,128)(2,1)}, u32[]{:S(2)}) copy-start(bf16[8,128,256]{2,1,0:T(8,128)(2,1)} %copy-done.16) | copy-start | bytes 1572868

commit v4 on v2

--- a/solution.py
+++ b/solution.py
@@ -79,10 +79,13 @@
     ).astype(BF16)
 
 
-def column(depth_row, width):
+def column(depth_row):
     cols = depth_row.shape[1]
-    turned = jnp.broadcast_to(depth_row, (cols, cols)).T
-    return jnp.concatenate([turned] * (width // cols), axis=1)
+    return jnp.broadcast_to(depth_row, (cols, cols)).T
+
+
+def widen(x, width):
+    return jnp.concatenate([x] * (width // x.shape[1]), axis=1)
 
 
 def stencil(taps, weight_ref, cols):
@@ -104,53 +107,56 @@
     return (mf * lax.rsqrt(mean + EPS)).astype(BF16)
 
 
+def prep_kernel(caps, side_ref, near_ref, far_ref, atm_ref, depth_ref, on_ref, off_ref, flag_ref):
+    _, lev, cols, width = near_ref.shape
+    rows = depth_ref.shape[0]
+    for block, row, out in ((near_ref, 0, on_ref), (far_ref, 1, off_ref)):
+        deep = column(depth_ref[pl.ds(side_ref[row], 1), :].astype(F32))
+        for l in range(lev):
+            wet = (deep > l).astype(F32).astype(BF16)
+            out[l * cols : (l + 1) * cols] = block[0, l] * widen(wet, width)
+    on_ref[lev * cols :] = atm_ref[0]
+    d = depth_ref[...].astype(F32)
+    counts = [
+        jnp.sum(jnp.maximum(d[1 : rows - 1] - 1.0, 0.0)),
+        jnp.sum(d[0:1]),
+        jnp.sum(d[rows - 1 :]),
+    ]
+    over = jnp.int32(0)
+    for count, cap in zip(counts, caps):
+        over = over | (count > cap).astype(jnp.int32)
+    flag_ref[0] = over
+
+
 def inner_kernel(
     cap,
-    state_hbm,
+    state,
     depth_ref,
-    weight_hbm,
+    weight,
     mixed_hbm,
     normed_hbm,
     packed_hbm,
-    base_ref,
-    state,
-    weight,
     mixed,
     normed,
     packed,
-    in_sem,
-    weight_sem,
     out_sem,
     packed_sem,
 ):
-    _, lev, cells, width = state_hbm.shape
+    _, lev, cells, width = state.shape
     rows, cols = depth_ref.shape
-    order = list(range(1, lev)) + [0]
-    load_w = pltpu.make_async_copy(weight_hbm, weight, weight_sem)
-    loads = [pltpu.make_async_copy(state_hbm.at[0, l], state.at[l], in_sem.at[l]) for l in range(lev)]
-    loads[1].start()
-    load_w.start()
-    for l in order[1:]:
-        loads[l].start()
     packed[...] = jnp.zeros_like(packed)
     d = depth_ref[...].astype(F32)
     plans = [row_plan(d[r : r + 1], lev) for r in range(1, rows - 1)]
     place = offsets(plans, 1, lev)
-    deep = jnp.concatenate([column(d[r : r + 1], width) for r in range(rows)], axis=0)
+    deep = jnp.concatenate([column(d[r : r + 1]) for r in range(rows)], axis=0)
     count = cells - 2 * cols
     stores = []
-    for l in order:
+    for l in range(1, lev):
         wet = (deep > l).astype(F32)
-        loads[l].wait()
-        if l == 1:
-            load_w.wait()
-        x = state[l] * wet.astype(BF16)
+        x = state[0, l] * widen(wet.astype(BF16), width)
         taps = [x[dr * cols : dr * cols + count] for dr in range(3)]
         total = stencil(taps, weight, cols)
-        new = taps[1].astype(F32) + wet[cols : cols + count] * total
-        if l == 0:
-            base_ref[...] = new
-            continue
+        new = taps[1].astype(F32) + widen(wet[cols : cols + count], width) * total
         new = new.astype(BF16)
         mixed[l - 1] = new
         tokens = normalise(new)
@@ -179,113 +185,122 @@
 def surface_kernel(
     ids_ref,
     live_ref,
-    base_ref,
+    side_ref,
+    state,
     depth_ref,
-    before_ref,
-    atm_ref,
-    after_ref,
-    remap_ref,
+    weight,
+    on_hbm,
+    off_hbm,
+    atm_hbm,
+    remap_hbm,
     mixed_ref,
     normed_ref,
     edge_ref,
-    window_ref,
+    window,
+    remap,
     forcing_ref,
+    sem,
 ):
     rows, cols = depth_ref.shape
-    width = base_ref.shape[-1]
-    own = atm_ref.shape[1]
-    blocks, pairs = remap_ref.shape[0], remap_ref.shape[1]
-    window_ref[0:own] = before_ref[0]
-    window_ref[own : 2 * own] = atm_ref[0]
-    window_ref[2 * own : 3 * own] = after_ref[0]
+    _, own, width = atm_hbm.shape
+    cells = state.shape[2]
+    blocks, pairs = remap_hbm.shape[0], remap_hbm.shape[1]
+    on_at = jnp.where(side_ref[0] == 0, 0, 2 * own)
+    copies = [
+        pltpu.make_async_copy(
+            on_hbm.at[pl.ds(on_hbm.shape[0] - own, own)],
+            window.at[pl.ds(pl.multiple_of(on_at, own), own)],
+            sem.at[0],
+        ),
+        pltpu.make_async_copy(
+            off_hbm.at[0], window.at[pl.ds(pl.multiple_of(2 * own - on_at, own), own)], sem.at[1]
+        ),
+        pltpu.make_async_copy(atm_hbm.at[0], window.at[pl.ds(own, own)], sem.at[2]),
+        pltpu.make_async_copy(remap_hbm, remap, sem.at[3]),
+    ]
+    for copy in copies:
+        copy.start()
+    d = depth_ref[...].astype(F32)
+    wet = (jnp.concatenate([column(d[r : r + 1]) for r in range(rows)], axis=0) > 0).astype(F32)
+    x = state[0, 0] * widen(wet.astype(BF16), width)
+    count = cells - 2 * cols
+    taps = [x[dr * cols : dr * cols + count] for dr in range(3)]
+    total = stencil(taps, weight, cols)
+    for copy in copies:
+        copy.wait()
     for b in range(blocks):
         acc = jnp.zeros((cols, width), F32)
         for p in range(pairs):
             on = (p < live_ref[b]).astype(F32)
             start = pl.multiple_of(ids_ref[b, p] * cols, cols)
             acc = acc + on * jnp.dot(
-                remap_ref[b, p], window_ref[pl.ds(start, cols), :], preferred_element_type=F32
+                remap[b, p], window[pl.ds(start, cols), :], preferred_element_type=F32
             )
         forcing_ref[b * cols : (b + 1) * cols] = acc
-    d = depth_ref[...].astype(F32)
-    for r in range(1, rows - 1):
-        at = slice((r - 1) * cols, r * cols)
-        wet = (column(d[r : r + 1], width) > 0).astype(F32)
-        new = (base_ref[at] + wet * forcing_ref[r * cols : (r + 1) * cols]).astype(BF16)
-        mixed_ref[0, at] = new
-        normed_ref[0, at] = normalise(new)
+    total = total + forcing_ref[cols : cols + count]
+    new = (taps[1].astype(F32) + widen(wet[cols : cols + count], width) * total).astype(BF16)
+    mixed_ref[0] = new
+    normed_ref[0] = normalise(new)
     edge_ref[0:cols] = forcing_ref[0:cols]
-    edge_ref[cols : 2 * cols] = forcing_ref[(rows - 1) * cols :]
+    edge_ref[cols : 2 * cols] = forcing_ref[cols + count :]
 
 
 def edge_kernel(
     cap,
-    state_hbm,
+    side_ref,
+    state,
     depth_ref,
     weight_hbm,
-    before_hbm,
-    after_hbm,
-    forcing_ref,
+    on_hbm,
+    off_hbm,
+    forcing_hbm,
     mixed_hbm,
     normed_hbm,
     top_hbm,
     low_hbm,
-    state,
     weight,
-    before,
-    after,
+    halos,
+    forcing,
     mixed,
     normed,
     top,
     low,
     in_sem,
-    weight_sem,
     out_sem,
     packed_sem,
 ):
-    _, lev, cells, width = state_hbm.shape
+    _, lev, cells, width = state.shape
     rows, cols = depth_ref.shape
-    load_w = pltpu.make_async_copy(weight_hbm, weight, weight_sem)
-    loads = []
-    for l in range(lev):
-        halo = pl.ds(l * cols, cols)
-        loads.append(
-            [
-                pltpu.make_async_copy(state_hbm.at[0, l], state.at[l], in_sem.at[l, 0]),
-                pltpu.make_async_copy(before_hbm.at[halo], before.at[halo], in_sem.at[l, 1]),
-                pltpu.make_async_copy(after_hbm.at[halo], after.at[halo], in_sem.at[l, 2]),
-            ]
-        )
-    for copy in loads[0]:
+    on_at = jnp.where(side_ref[0] == 0, 0, 1)
+    copies = [
+        pltpu.make_async_copy(weight_hbm, weight, in_sem.at[0]),
+        pltpu.make_async_copy(on_hbm.at[pl.ds(0, lev * cols)], halos.at[on_at], in_sem.at[1]),
+        pltpu.make_async_copy(off_hbm, halos.at[1 - on_at], in_sem.at[2]),
+        pltpu.make_async_copy(forcing_hbm, forcing, in_sem.at[3]),
+    ]
+    for copy in copies:
         copy.start()
-    load_w.start()
-    for l in range(1, lev):
-        for copy in loads[l]:
-            copy.start()
     top[...] = jnp.zeros_like(top)
     low[...] = jnp.zeros_like(low)
     d = depth_ref[...].astype(F32)
-    ends = [d[0:1], d[rows - 1 : rows]]
-    plans = [row_plan(e, lev) for e in ends]
+    plans = [row_plan(d[r : r + 1], lev) for r in (0, rows - 1)]
     places = [offsets([plan], 0, lev) for plan in plans]
-    deep = jnp.concatenate([column(d[r : r + 1], width) for r in range(rows)], axis=0)
+    deep = jnp.concatenate([column(d[r : r + 1]) for r in range(rows)], axis=0)
+    for copy in copies:
+        copy.wait()
     stores = []
     for l in range(lev):
         wet = (deep > l).astype(F32)
-        for copy in loads[l]:
-            copy.wait()
-        if l == 0:
-            load_w.wait()
-        x = state[l] * wet.astype(BF16)
+        x = state[0, l] * widen(wet.astype(BF16), width)
         halo = slice(l * cols, (l + 1) * cols)
-        up = [before[halo], x[0:cols], x[cols : 2 * cols]]
-        down = [x[cells - 2 * cols : cells - cols], x[cells - cols :], after[halo]]
+        up = [halos[0, halo], x[0:cols], x[cols : 2 * cols]]
+        down = [x[cells - 2 * cols : cells - cols], x[cells - cols :], halos[1, halo]]
         taps = [jnp.concatenate([a, b], axis=0) for a, b in zip(up, down)]
         total = stencil(taps, weight, cols)
         if l == 0:
-            total = total + forcing_ref[...]
+            total = total + forcing[...]
         edge_wet = jnp.concatenate([wet[0:cols], wet[cells - cols :]], axis=0)
-        new = (taps[1].astype(F32) + edge_wet * total).astype(BF16)
+        new = (taps[1].astype(F32) + widen(edge_wet, width) * total).astype(BF16)
         mixed[l] = new
         tokens = normalise(new)
         normed[l] = tokens
@@ -334,16 +349,17 @@
         k_ref[rows] = kv[:, :width].reshape(lev, count, width)
         v_ref[rows] = kv[:, width:].reshape(lev, count, width)
 
-    d = depth_ref[...].astype(F32)
-    plans = [row_plan(d[r : r + 1], lev) for r in rows_of]
-    place = offsets(plans, first, lev)
     two = len(rows_of) == 2
     pick = lambda a, b: jnp.where(step == 0, a, b)
-    wet_row = pick(plans[0][0], plans[1][0]) if two else plans[0][0]
-    rank = pick(plans[0][1], plans[1][1]) if two else plans[0][1]
-    depth_row = d[rows_of[0] : rows_of[0] + 1]
+    d = depth_ref[...].astype(F32)
+    rows_d = [d[r : r + 1] for r in rows_of]
+    plans = [row_plan(row, lev) for row in rows_d]
+    place = offsets(plans, first, lev)
+    wet_row, rank, _ = plans[0]
+    depth_row = rows_d[0]
     if two:
-        depth_row = pick(depth_row, d[rows_of[1] : rows_of[1] + 1])
+        wet_row, rank = pick(wet_row, plans[1][0]), pick(rank, plans[1][1])
+        depth_row = pick(*rows_d)
 
     x = jnp.concatenate([p[...].reshape(-1, width) for p in own_normed], axis=0)
     q = jnp.dot(x, qkv_ref[:, 0:width], preferred_element_type=F32).astype(BF16)
@@ -410,10 +426,10 @@
             att_ref[:, cells, lanes] = o.astype(BF16).reshape(lev, GROUP, pair)
     proj = jnp.dot(att_ref[...].reshape(-1, width), wo_ref[...], preferred_element_type=F32)
     base = jnp.concatenate([p[...].reshape(-1, width) for p in own_mixed], axis=0).astype(F32)
-    deep = column(depth_row, width)
+    deep = column(depth_row)
     for l in range(lev):
         rows = slice(l * count, (l + 1) * count)
-        wet = (deep > l).astype(F32)
+        wet = widen((deep > l).astype(F32), width)
         out_ref[0, l] = (base[rows] + wet * proj[rows]).astype(BF16)
 
 
@@ -465,7 +481,7 @@
         ),
         out_shape=jax.ShapeDtypeStruct(shape, BF16),
         input_output_aliases=alias,
-        compiler_params=params(24 if members <= 2 else 48, 1),
+        compiler_params=params(20 if members <= 2 else 48, 1),
         cost_estimate=cost(tokens * width * width * 8 * (members + 2), tokens * width * 2 * 5),
         name="attend",
     )(flag, *args)
@@ -490,21 +506,11 @@
     atm_blk = own // cols
     tiles = lax.axis_size("tile")
     members = lax.axis_size("mem")
-    ups = [(i, i + 1) for i in range(tiles - 1)]
-    downs = [(i + 1, i) for i in range(tiles - 1)]
-    atm_before = lax.ppermute(atm_latent, "tile", ups)
-    atm_after = lax.ppermute(atm_latent, "tile", downs)
-
-    depth = depth.reshape(rows, cols)
-    levels = jnp.arange(lev, dtype=jnp.int32)
-    grid = ocean_state[0].reshape(lev, rows, cols, width)
-
-    def edge(row):
-        wet = (levels[:, None] < depth[row][None, :]).astype(BF16)
-        return (grid[:, row] * wet[:, :, None]).reshape(lev * cols, width)
-
-    before = lax.ppermute(edge(rows - 1), "tile", ups)
-    after = lax.ppermute(edge(0), "tile", downs)
+    tile = lax.axis_index("tile")
+
+    def swap(x, first):
+        pairs = [(i, i + 1) for i in range(first, tiles - 1, 2)]
+        return lax.ppermute(x, "tile", pairs + [(b, a) for a, b in pairs])
 
     def exchange(x):
         return [
@@ -512,101 +518,133 @@
             for k in range(1, members)
         ]
 
+    odd = tile % 2
+    side = jnp.stack([(1 - odd) * (rows - 1), odd * (rows - 1)]).astype(jnp.int32)
+    depth = depth.reshape(rows, cols)
     deep_cap = capacity((lev - 1) * inner, 0.5625)
     edge_cap = capacity(lev * cols, 0.65625)
-    wet_deep = jnp.sum(jnp.maximum(depth[1 : rows - 1] - 1, 0))
-    wet_top = jnp.sum(jnp.maximum(depth[0], 0))
-    wet_low = jnp.sum(jnp.maximum(depth[rows - 1], 0))
-    over = (wet_deep > deep_cap) | (wet_top > edge_cap) | (wet_low > edge_cap)
-    flag = over.astype(jnp.int32).reshape(1)
-
-    hbm = pl.BlockSpec(memory_space=pl.ANY)
+
+    hbm = pl.BlockSpec(memory_space=pltpu.HBM)
+    anywhere = pl.BlockSpec(memory_space=pl.ANY)
     vmem = pl.BlockSpec(memory_space=pltpu.VMEM)
-    tok = lambda *s: jax.ShapeDtypeStruct((*s, width), BF16)
+    smem = pl.BlockSpec(memory_space=pltpu.SMEM)
+    tok = lambda *s: pltpu.HBM((*s, width), BF16)
+    stay = lambda x: pltpu.with_memory_space_constraint(x, pltpu.HBM)
     conv_flops = lambda n, c: 2 * 9 * n * c * width * width
     dma = pltpu.SemaphoreType.DMA
     slack = cols + 16
-
-    deep_mixed, deep_normed, deep_packed, base = pl.pallas_call(
+    full = lambda a: pl.BlockSpec(a.shape, lambda i, *_: (0,) * a.ndim)
+    state_row = lambda k: pl.BlockSpec((1, lev, cols, width), lambda i, s: (0, 0, s[k], 0))
+
+    off_atm = swap(atm_latent, 1)
+    on_msg, off_msg, flag = pl.pallas_call(
+        functools.partial(prep_kernel, (deep_cap, edge_cap, edge_cap)),
+        grid_spec=pltpu.PrefetchScalarGridSpec(
+            num_scalar_prefetch=1,
+            grid=(1,),
+            in_specs=[state_row(0), state_row(1), full(atm_latent), full(depth)],
+            out_specs=[
+                pl.BlockSpec((lev * cols + own, width), lambda i, s: (0, 0)),
+                pl.BlockSpec((lev * cols, width), lambda i, s: (0, 0)),
+                smem,
+            ],
+        ),
+        out_shape=[
+            tok(lev * cols + own),
+            tok(lev * cols),
+            jax.ShapeDtypeStruct((1,), jnp.int32),
+        ],
+        compiler_params=params(16, 1),
+        cost_estimate=cost(lev * cols * width * 4, lev * cols * width * 10),
+        name="prep",
+    )(side, stay(ocean_state), stay(ocean_state), stay(atm_latent), stay(depth))
+    off_halo = swap(off_msg, 1)
+    on_halo = swap(on_msg, 0)
+
+    deep_mixed, deep_normed, deep_packed = pl.pallas_call(
         functools.partial(inner_kernel, deep_cap),
-        in_specs=[hbm, vmem, hbm],
-        out_specs=[hbm, hbm, hbm, vmem],
-        out_shape=[
-            tok(lev - 1, inner),
-            tok(lev - 1, inner),
-            tok(deep_cap),
-            jax.ShapeDtypeStruct((inner, width), F32),
-        ],
+        in_specs=[vmem, vmem, vmem],
+        out_specs=[hbm] * 3,
+        out_shape=[tok(lev - 1, inner), tok(lev - 1, inner), tok(deep_cap)],
         scratch_shapes=[
-            pltpu.VMEM((lev, cells, width), BF16),
-            pltpu.VMEM(conv_weight.shape, BF16),
             pltpu.VMEM((lev - 1, inner, width), BF16),
             pltpu.VMEM((lev - 1, inner, width), BF16),
             pltpu.VMEM((deep_cap + slack, width), BF16),
-            dma((lev,)),
-            dma,
             dma((lev - 1, 2)),
             dma,
         ],
-        compiler_params=params(24),
+        compiler_params=params(20),
         cost_estimate=cost(conv_flops(lev, inner), lev * inner * width * 8),
         name="inner",
     )(ocean_state, depth, conv_weight)
     deep_others = exchange(deep_packed)
 
-    first = (lax.axis_index("tile") - R) * atm_blk
-    ids = jnp.clip(src_blocks - first, 0, 3 * atm_blk - 1)
-    full = lambda a: pl.BlockSpec(a.shape, lambda i, *_: (0,) * a.ndim)
+    ids = jnp.clip(src_blocks - (tile - R) * atm_blk, 0, 3 * atm_blk - 1)
+    whole_spec = lambda *sh: pl.BlockSpec(sh, lambda *_: (0,) * len(sh))
     surf_mixed, surf_normed, edge_forcing = pl.pallas_call(
         surface_kernel,
-        grid_spec=pltpu.PrefetchScalarGridSpec(
-            num_scalar_prefetch=2,
-            grid=(1,),
-            in_specs=[full(a) for a in (base, depth, atm_before, atm_latent, atm_after, remap_weight)],
-            out_specs=[
-                pl.BlockSpec((1, inner, width), lambda i, *_: (0, 0, 0)),
-                pl.BlockSpec((1, inner, width), lambda i, *_: (0, 0, 0)),
-                pl.BlockSpec((2 * cols, width), lambda i, *_: (0, 0)),
-            ],
-            scratch_shapes=[pltpu.VMEM((3 * own, width), BF16), pltpu.VMEM((cells, width), F32)],
-        ),
-        out_shape=[tok(1, inner), tok(1, inner), jax.ShapeDtypeStruct((2 * cols, width), F32)],
-        compiler_params=params(24, 1),
+        in_specs=[smem] * 3 + [vmem] * 3 + [anywhere] * 2 + [hbm] * 2,
+        out_specs=[whole_spec(1, inner, width)] * 2 + [whole_spec(2 * cols, width)],
+        out_shape=[tok(1, inner), tok(1, inner), pltpu.HBM((2 * cols, width), F32)],
+        scratch_shapes=[
+            pltpu.VMEM((3 * own, width), BF16),
+            pltpu.VMEM(remap_weight.shape, BF16),
+            pltpu.VMEM((cells, width), F32),
+            dma((4,)),
+        ],
+        compiler_params=params(20),
         cost_estimate=cost(conv_flops(1, inner), cells * width * 16),
         name="surface",
-    )(ids, live, base, depth, atm_before, atm_latent, atm_after, remap_weight)
+    )(
+        ids,
+        live,
+        side,
+        ocean_state,
+        depth,
+        conv_weight,
+        on_halo,
+        off_atm,
+        stay(atm_latent),
+        stay(remap_weight),
+    )
     surf_others = exchange(surf_normed)
 
     edge_mixed, edge_normed, top_packed, low_packed = pl.pallas_call(
         functools.partial(edge_kernel, edge_cap),
-        in_specs=[hbm, vmem, hbm, hbm, hbm, vmem],
+        in_specs=[smem, vmem, vmem, hbm, anywhere, anywhere, hbm],
         out_specs=[hbm] * 4,
         out_shape=[tok(lev, 2 * cols), tok(lev, 2 * cols), tok(edge_cap), tok(edge_cap)],
         scratch_shapes=[
-            pltpu.VMEM((lev, cells, width), BF16),
             pltpu.VMEM(conv_weight.shape, BF16),
-            pltpu.VMEM((lev * cols, width), BF16),
-            pltpu.VMEM((lev * cols, width), BF16),
+            pltpu.VMEM((2, lev * cols, width), BF16),
+            pltpu.VMEM((2 * cols, width), F32),
             pltpu.VMEM((lev, 2 * cols, width), BF16),
             pltpu.VMEM((lev, 2 * cols, width), BF16),
             pltpu.VMEM((edge_cap + slack, width), BF16),
             pltpu.VMEM((edge_cap + slack, width), BF16),
-            dma((lev, 3)),
-            dma,
+            dma((4,)),
             dma((lev, 2)),
             dma((2,)),
         ],
-        compiler_params=params(24),
+        compiler_params=params(20),
         cost_estimate=cost(conv_flops(lev, 2 * cols), lev * cols * width * 16),
         name="edge",
-    )(ocean_state, depth, conv_weight, before, after, edge_forcing)
+    )(side, ocean_state, depth, stay(conv_weight), on_halo, off_halo, edge_forcing)
     top_others = exchange(top_packed)
     low_others = exchange(low_packed)
 
+    def unread(shape):
+        return pl.pallas_call(
+            lambda out_ref: None,
+            out_specs=hbm,
+            out_shape=pltpu.HBM(shape, BF16),
+            name="unread",
+        )()
+
     deep_whole, edge_whole = lax.cond(
-        over,
-        lambda a, b: (exchange(a), exchange(b)),
-        lambda a, b: ([a] * (members - 1), [b] * (members - 1)),
+        flag[0] > 0,
+        lambda *a: tuple(exchange(x) for x in a),
+        lambda *a: tuple([unread(x.shape) for _ in range(members - 1)] for x in a),
         deep_normed,
         edge_normed,
     )

time: 75.2 us -> 63.4 us (0.84)
  local copies, waits for them, and re-layouts: 9.13 us -> 2.17 us
  starting transfers between devices: 15.6 us -> 10.9 us
  waiting for transfers between devices: 3.55 us -> 8.23 us
  other arithmetic: 4.12 us -> 0.08 us
  between operations: 2.26 us -> 1 us
    ppermute x4 -> x3, waiting for transfers between devices: 0.01 us -> 8.22 us  [swap(): return lax.ppermute(x, 'tile', pairs + [(b, a) for a, b in pairs])]
    ppermute x4 -> x3, starting transfers between devices: 11.1 us -> 5.64 us  [swap(): return lax.ppermute(x, 'tile', pairs + [(b, a) for a, b in pairs])]
    unnamed x38 -> x26, local copies, waits for them, and re-layouts: 5.78 us -> 2.17 us
    ppermute x4, waiting for transfers between devices: 3.54 us -> 0.01 us  [exchange(): lax.ppermute(x, 'mem', [(i, (i + k) % members) for i in range(members)])]
    reduce_sum x2 -> x0, other arithmetic: 2.11 us -> none  [the longest x1 1.48 us: body(): wet_low = jnp.sum(jnp.maximum(depth[rows - 1], 0))]
    mul x2 -> x0, other arithmetic: 1.99 us -> none  [edge(): return (grid[:, row] * wet[:, :, None]).reshape(lev * cols, width)]
    pallas_call x3, Pallas kernels: 16.9 us -> 18.8 us  [attend(): pl.pallas_call(functools.partial(attend_kernel, others, nparts, tuple(row...]
    cond x2 -> x0, local copies, waits for them, and re-layouts: 1.92 us -> none
  transfers between devices with their start and end apart: 8 -> 7, of which waited for: 1 -> 1; matrix products, arithmetic and copies ran while one was open for 10% -> 0% of each run, Pallas kernels for 48% -> 51%
where the time goes in v4:
time: 63.4 us; the launch traced here: 62.7 us
  Pallas kernels  40.3 us (64%)
  starting transfers between devices  10.9 us (17%)
  waiting for transfers between devices  8.23 us (13%)
  local copies, waits for them, and re-layouts  2.17 us (3%)
  between operations  1 us (2%)
    pallas_call x3, Pallas kernels, attend(): pl.pallas_call(functools.partial(attend_kernel, others, nparts, tuple(row...  18.8 us
    pallas_call x1, Pallas kernels, body(): pl.pallas_call(functools.partial(edge_kernel, edge_cap), in_specs=[smem,...  8.72 us
    ppermute x3, waiting for transfers between devices, swap(): return lax.ppermute(x, 'tile', pairs + [(b, a) for a, b in pairs])  8.22 us
    pallas_call x1, Pallas kernels, body(): pl.pallas_call(functools.partial(inner_kernel, deep_cap), in_specs=[vmem,...  5.86 us
    ppermute x3, starting transfers between devices, swap(): return lax.ppermute(x, 'tile', pairs + [(b, a) for a, b in pairs])  5.64 us
    ppermute x4, starting transfers between devices, exchange(): lax.ppermute(x, 'mem', [(i, (i + k) % members) for i in range(members)])  5.26 us
    pallas_call x1, Pallas kernels, body(): pl.pallas_call(surface_kernel, in_specs=[smem] * 3 + [vmem] * 3 + [anywhe...  3.49 us
    pallas_call x1, Pallas kernels, body(): pl.pallas_call(functools.partial(prep_kernel, (deep_cap, edge_cap, edge_c...  3.44 us
  transfers between devices with their start and end apart: 7, of which 1 were waited for; matrix products, arithmetic and copies ran while one was open for 0% of the time, Pallas kernels for 51%

profile of v4, /device:TPU:18, one launch (start us, length us, event | category | flops | bytes accessed | tf_op | source)
XLA Modules:
  0.0 62.7 jit_solution(10630556960898341949)
XLA Ops:
  0.0 0.1 pad_add_fusion.side_ref
  0.1 3.4 %prep.1 = (bf16[1536,256]{1,0:T(8,128)(2,1)}, bf16[1024,256]{1,0:T(8,128)(2,1)}, s32[1]{0:T(128)}) custom-call(s32[2]{0:T(128)S(1)} %pad_add_fusion.side_ref, bf16[1,8,512,256]{3,2,1,0:T(8,128)(2,1)} %state.5, bf16[1,8,512,256]{3,2,1,0:T(8,128)(2,1)} %state.5, bf16[1,512,256]{2,1,0:T(8,128)(2,1)} %atm_hbm.1, s32[4,128]{1,0:T(4,128)} %bitcast.4), custom_call_target="tpu_custom_call" | custom-call | flops 1048576 | bytes 2621440 | tf_op jit(solution)/shard_map/prep/pallas_call | solution.py:540
  3.5 0.1 collective-permute-start.2
  3.6 0.0 copy-start.12
  3.6 0.0 copy-start.6
  3.6 2.6 %collective-permute-start.3 = (bf16[1024,256]{1,0:T(8,128)(2,1)}, bf16[1024,256]{1,0:T(8,128)(2,1)}, u32[]{:S(2)}, u32[]{:S(2)}) collective-permute-start(bf16[1024,256]{1,0:T(8,128)(2,1)} %get-tuple-element.28), channel_id=1, source_target_pairs={{2,4},{6,8},{10,12},{14,16},{18,20},{22,24},{26,28},{4,2},{8,6},{1... | collective-permute-start | bytes 1572872 | tf_op jit(solution)/shard_map/ppermute | solution.py:513
  6.3 2.9 %collective-permute-start.4 = (bf16[1,512,256]{2,1,0:T(8,128)(2,1)}, bf16[1,512,256]{2,1,0:T(8,128)(2,1)S(1)}, u32[]{:S(2)}, u32[]{:S(2)}) collective-permute-start(bf16[1,512,256]{2,1,0:T(8,128)(2,1)} %atm_hbm.1), channel_id=1, source_target_pairs={{2,4},{6,8},{10,12},{14,16},{18,20},{22,24},{26,28},{4,2},{8,6},{1... | collective-permute-start | bytes 786440 | tf_op jit(solution)/shard_map/ppermute | solution.py:513
  9.2 0.0 copy-done
  9.2 0.0 copy-done.3
  9.2 0.0 copy-done.5
  9.2 5.9 %inner.1 = (bf16[7,256,256]{2,1,0:T(8,128)(2,1)}, bf16[7,256,256]{2,1,0:T(8,128)(2,1)}, bf16[1008,256]{1,0:T(8,128)(2,1)}) custom-call(bf16[1,8,512,256]{3,2,1,0:T(8,128)(2,1)S(1)} %copy-done, s32[4,128]{1,0:T(4,128)S(1)} %bitcast.5, bf16[3,3,256,256]{3,2,1,0:T(8,128)(2,1)S(1)} %copy-done.3), custom_call_target="tpu_custom_call" | custom-call | flops 2415919104 | bytes 4194304 | tf_op jit(solution)/shard_map/inner/pallas_call | solution.py:564
  15.1 1.6 %collective-permute-start.8 = (bf16[1008,256]{1,0:T(8,128)(2,1)}, bf16[1008,256]{1,0:T(8,128)(2,1)}, u32[]{:S(2)}, u32[]{:S(2)}) collective-permute-start(bf16[1008,256]{1,0:T(8,128)(2,1)} %get-tuple-element.39), channel_id=1, source_target_pairs={{0,1},{1,0},{2,3},{3,2},{4,5},{5,4},{6,7},{7,6},{8,9},{9,8},{10,11... | collective-permute-start | bytes 1548296 | tf_op jit(solution)/shard_map/ppermute | solution.py:517
  17.3 0.0 copy-done.12
  17.4 8.2 %collective-permute-done.4.off_hbm = bf16[1,512,256]{2,1,0:T(8,128)(2,1)S(1)} collective-permute-done((bf16[1,512,256]{2,1,0:T(8,128)(2,1)}, bf16[1,512,256]{2,1,0:T(8,128)(2,1)S(1)}, u32[]{:S(2)}, u32[]{:S(2)}) %collective-permute-start.4) | collective-permute-done | bytes 262176 | tf_op jit(solution)/shard_map/ppermute | solution.py:513
  25.6 0.0 collective-permute-done.2.on_hbm
  25.6 0.0 copy-done.6
  25.6 3.5 %surface.1 = (bf16[1,256,256]{2,1,0:T(8,128)(2,1)}, bf16[1,256,256]{2,1,0:T(8,128)(2,1)}, f32[256,256]{1,0:T(8,128)}) custom-call(s32[4,4]{1,0:T(4,128)S(1)} %subtract_clamp_fusion.ids_ref, s32[4]{0:T(128)S(1)} %copy-done.6, s32[2]{0:T(128)S(1)} %pad_add_fusion.side_ref, bf16[1,8,512,256]{3,2,1,0:T(8,128)(2,1)S(1)} %copy-done, s32[4,128]{1,0:T(4,128)S(1)} %bitcast.6, ...), custom_call_target="tpu_custom_call" | custom-call | flops 301989888 | bytes 2097152 | tf_op jit(solution)/shard_map/surface/pallas_call | solution.py:584
  29.1 1.6 %collective-permute-start.7 = (bf16[1,256,256]{2,1,0:T(8,128)(2,1)}, bf16[1,256,256]{2,1,0:T(8,128)(2,1)S(1)}, u32[]{:S(2)}, u32[]{:S(2)}) collective-permute-start(bf16[1,256,256]{2,1,0:T(8,128)(2,1)} %get-tuple-element.36.refs_0_), channel_id=1, source_target_pairs={{0,1},{1,0},{2,3},{3,2},{4,5},{5,4},{6,7},{7,6},{8,9},{9,8},{10,11... | collective-permute-start | bytes 393224 | tf_op jit(solution)/shard_map/ppermute | solution.py:517
  30.7 0.0 collective-permute-done.3.off_hbm
  30.7 0.9 %copy-done.7 = f32[256,256]{1,0:T(8,128)S(1)} copy-done((f32[256,256]{1,0:T(8,128)S(1)}, f32[256,256]{1,0:T(8,128)}, u32[]{:S(2)}) %copy-start.7) | copy-done | bytes 262168
  31.6 8.7 %edge.1 = (bf16[8,256,256]{2,1,0:T(8,128)(2,1)}, bf16[8,256,256]{2,1,0:T(8,128)(2,1)}, bf16[672,256]{1,0:T(8,128)(2,1)}, bf16[672,256]{1,0:T(8,128)(2,1)}) custom-call(s32[2]{0:T(128)S(1)} %pad_add_fusion.side_ref, bf16[1,8,512,256]{3,2,1,0:T(8,128)(2,1)S(1)} %copy-done, s32[4,128]{1,0:T(4,128)S(1)} %bitcast.7, bf16[3,3,256,256]{3,2,1,0:T(8,128)(2,1)} %weight.3, ...), custom_call_target="tpu_custom_call" | custom-call | flops 2415919104 | bytes 4194304 | tf_op jit(solution)/shard_map/edge/pallas_call | solution.py:612
  40.3 0.6 collective-permute-start.5
  40.9 1.5 %collective-permute-start.6 = (bf16[672,256]{1,0:T(8,128)(2,1)}, bf16[672,256]{1,0:T(8,128)(2,1)S(1)}, u32[]{:S(2)}, u32[]{:S(2)}) collective-permute-start(bf16[672,256]{1,0:T(8,128)(2,1)} %get-tuple-element.35), channel_id=1, source_target_pairs={{0,1},{1,0},{2,3},{3,2},{4,5},{5,4},{6,7},{7,6},{8,9},{9,8},{10,11... | collective-permute-start | bytes 1032200 | tf_op jit(solution)/shard_map/ppermute | solution.py:517
  42.4 0.0 collective-permute-done.8.refs_5_
  42.4 0.0 collective-permute-done.7.refs_4_
  42.5 0.0 copy-start.10
  42.5 1.2 %copy-done.10 = bf16[7,256,256]{2,1,0:T(8,128)(2,1)S(1)} copy-done((bf16[7,256,256]{2,1,0:T(8,128)(2,1)S(1)}, bf16[7,256,256]{2,1,0:T(8,128)(2,1)}, u32[]{:S(2)}) %copy-start.10) | copy-done | bytes 917528
  43.7 9.4 %attend.3.refs_7_ = bf16[1,8,512,256]{3,2,1,0:T(8,128)(2,1)} custom-call(s32[1]{0:T(128)} %get-tuple-element.26.flag_ref, bf16[1,256,256]{2,1,0:T(8,128)(2,1)S(1)} %copy-done.9, bf16[7,256,256]{2,1,0:T(8,128)(2,1)} %get-tuple-element.33.refs_1_, bf16[1,256,256]{2,1,0:T(8,128)(2,1)S(1)} %copy-done.8, bf16[7,256,256]{2,1,0:T(8,128)(2,1)S(1)} %copy-done.10, ...), custom_call_target="tpu_custom_call" | custom-call | flops 4294967296 | bytes 5242880 | tf_op jit(solution)/shard_map/attend/pallas_call | solution.py:461
  53.1 0.0 collective-permute-done.6.refs_2_
  53.1 4.7 %attend.4.refs_7_ = bf16[1,8,512,256]{3,2,1,0:T(8,128)(2,1)} custom-call(s32[1]{0:T(128)} %get-tuple-element.26.flag_ref, bf16[8,256,256]{2,1,0:T(8,128)(2,1)S(1)} %copy-done.11, bf16[8,256,256]{2,1,0:T(8,128)(2,1)S(1)} %copy-done.1, bf16[672,256]{1,0:T(8,128)(2,1)S(1)} %collective-permute-done.6.refs_2_, ...), custom_call_target="tpu_custom_call", output_to_operand_aliasing={{}: (8, {})} | custom-call | flops 2147483648 | bytes 2621440 | tf_op jit(solution)/shard_map/attend/pallas_call | solution.py:461
  57.8 0.0 collective-permute-done.5.refs_2_
  57.8 4.7 %attend.5 = bf16[1,8,512,256]{3,2,1,0:T(8,128)(2,1)} custom-call(s32[1]{0:T(128)} %get-tuple-element.26.flag_ref, bf16[8,256,256]{2,1,0:T(8,128)(2,1)S(1)} %copy-done.11, bf16[8,256,256]{2,1,0:T(8,128)(2,1)S(1)} %copy-done.1, bf16[672,256]{1,0:T(8,128)(2,1)S(1)} %collective-permute-done.5.refs_2_, ...), custom_call_target="tpu_custom_call", output_to_operand_aliasing={{}: (8, {})} | custom-call | flops 2147483648 | bytes 2621440 | tf_op jit(solution)/shard_map/attend/pallas_call | solution.py:461
  (20 shorter events, 0.0 us)
Async XLA Ops:
  0.1 9.1 %copy-start = (bf16[1,8,512,256]{3,2,1,0:T(8,128)(2,1)S(1)}, bf16[1,8,512,256]{3,2,1,0:T(8,128)(2,1)}, u32[]{:S(2)}) copy-start(bf16[1,8,512,256]{3,2,1,0:T(8,128)(2,1)} %state.5) | copy-start | bytes 6291460
  0.1 9.1 %copy-start.3 = (bf16[3,3,256,256]{3,2,1,0:T(8,128)(2,1)S(1)}, bf16[3,3,256,256]{3,2,1,0:T(8,128)(2,1)}, u32[]{:S(2)}) copy-start(bf16[3,3,256,256]{3,2,1,0:T(8,128)(2,1)} %weight.3) | copy-start | bytes 3538948
  0.1 9.2 %copy-start.5 = (s32[512]{0:T(512)S(1)}, s32[512]{0:T(512)}, u32[]{:S(2)}) copy-start(s32[512]{0:T(512)} %param.13) | copy-start | bytes 6148
  3.5 22.1 %collective-permute-start.2 = (bf16[1536,256]{1,0:T(8,128)(2,1)}, bf16[1536,256]{1,0:T(8,128)(2,1)}, u32[]{:S(2)}, u32[]{:S(2)}) collective-permute-start(bf16[1536,256]{1,0:T(8,128)(2,1)} %get-tuple-element.27), channel_id=1, source_target_pairs={{0,2},{4,6},{8,10},{12,14},{16,18},{20,22},{24,26},{28,30},{2,0},{... | collective-permute-start | bytes 2359304 | tf_op jit(solution)/shard_map/ppermute | solution.py:513
  3.6 13.7 %copy-start.12 = (s32[4,4]{1,0:T(4,128)S(1)}, s32[4,4]{1,0:T(4,128)}, u32[]{:S(2)}) copy-start(s32[4,4]{1,0:T(4,128)} %param.14) | copy-start | bytes 196
  3.6 22.0 %copy-start.6 = (s32[4]{0:T(128)S(1)}, s32[4]{0:T(128)}, u32[]{:S(2)}) copy-start(s32[4]{0:T(128)} %live_ref.1) | copy-start | bytes 52
  3.6 27.0 %collective-permute-start.3 = (bf16[1024,256]{1,0:T(8,128)(2,1)}, bf16[1024,256]{1,0:T(8,128)(2,1)}, u32[]{:S(2)}, u32[]{:S(2)}) collective-permute-start(bf16[1024,256]{1,0:T(8,128)(2,1)} %get-tuple-element.28), channel_id=1, source_target_pairs={{2,4},{6,8},{10,12},{14,16},{18,20},{22,24},{26,28},{4,2},{8,6},{1... | collective-permute-start | bytes 1572872 | tf_op jit(solution)/shard_map/ppermute | solution.py:513
  6.3 19.3 %collective-permute-start.4 = (bf16[1,512,256]{2,1,0:T(8,128)(2,1)}, bf16[1,512,256]{2,1,0:T(8,128)(2,1)S(1)}, u32[]{:S(2)}, u32[]{:S(2)}) collective-permute-start(bf16[1,512,256]{2,1,0:T(8,128)(2,1)} %atm_hbm.1), channel_id=1, source_target_pairs={{2,4},{6,8},{10,12},{14,16},{18,20},{22,24},{26,28},{4,2},{8,6},{1... | collective-permute-start | bytes 786440 | tf_op jit(solution)/shard_map/ppermute | solution.py:513
  15.1 27.3 %collective-permute-start.8 = (bf16[1008,256]{1,0:T(8,128)(2,1)}, bf16[1008,256]{1,0:T(8,128)(2,1)}, u32[]{:S(2)}, u32[]{:S(2)}) collective-permute-start(bf16[1008,256]{1,0:T(8,128)(2,1)} %get-tuple-element.39), channel_id=1, source_target_pairs={{0,1},{1,0},{2,3},{3,2},{4,5},{5,4},{6,7},{7,6},{8,9},{9,8},{10,11... | collective-permute-start | bytes 1548296 | tf_op jit(solution)/shard_map/ppermute | solution.py:517
  29.1 13.4 %collective-permute-start.7 = (bf16[1,256,256]{2,1,0:T(8,128)(2,1)}, bf16[1,256,256]{2,1,0:T(8,128)(2,1)S(1)}, u32[]{:S(2)}, u32[]{:S(2)}) collective-permute-start(bf16[1,256,256]{2,1,0:T(8,128)(2,1)} %get-tuple-element.36.refs_0_), channel_id=1, source_target_pairs={{0,1},{1,0},{2,3},{3,2},{4,5},{5,4},{6,7},{7,6},{8,9},{9,8},{10,11... | collective-permute-start | bytes 393224 | tf_op jit(solution)/shard_map/ppermute | solution.py:517
  30.7 1.0 %copy-start.7 = (f32[256,256]{1,0:T(8,128)S(1)}, f32[256,256]{1,0:T(8,128)}, u32[]{:S(2)}) copy-start(f32[256,256]{1,0:T(8,128)} %get-tuple-element.29.forcing_hbm) | copy-start | bytes 786436
  31.6 10.8 %copy-start.2 = (bf16[256,768]{1,0:T(8,128)(2,1)S(1)}, bf16[256,768]{1,0:T(8,128)(2,1)}, u32[]{:S(2)}) copy-start(bf16[256,768]{1,0:T(8,128)(2,1)} %refs_5_.3) | copy-start | bytes 1179652
  31.6 10.8 %copy-start.4 = (bf16[256,256]{1,0:T(8,128)(2,1)S(1)}, bf16[256,256]{1,0:T(8,128)(2,1)}, u32[]{:S(2)}) copy-start(bf16[256,256]{1,0:T(8,128)(2,1)} %refs_6_.3) | copy-start | bytes 393220
  31.6 10.9 %copy-start.8 = (bf16[1,256,256]{2,1,0:T(8,128)(2,1)S(1)}, bf16[1,256,256]{2,1,0:T(8,128)(2,1)}, u32[]{:S(2)}) copy-start(bf16[1,256,256]{2,1,0:T(8,128)(2,1)} %get-tuple-element.37.refs_2_) | copy-start | bytes 393220
  31.6 10.9 %copy-start.9 = (bf16[1,256,256]{2,1,0:T(8,128)(2,1)S(1)}, bf16[1,256,256]{2,1,0:T(8,128)(2,1)}, u32[]{:S(2)}) copy-start(bf16[1,256,256]{2,1,0:T(8,128)(2,1)} %get-tuple-element.36.refs_0_) | copy-start | bytes 393220
  40.3 17.5 %collective-permute-start.5 = (bf16[672,256]{1,0:T(8,128)(2,1)}, bf16[672,256]{1,0:T(8,128)(2,1)S(1)}, u32[]{:S(2)}, u32[]{:S(2)}) collective-permute-start(bf16[672,256]{1,0:T(8,128)(2,1)} %get-tuple-element.32), channel_id=1, source_target_pairs={{0,1},{1,0},{2,3},{3,2},{4,5},{5,4},{6,7},{7,6},{8,9},{9,8},{10,11... | collective-permute-start | bytes 1032200 | tf_op jit(solution)/shard_map/ppermute | solution.py:517
  40.9 12.1 %collective-permute-start.6 = (bf16[672,256]{1,0:T(8,128)(2,1)}, bf16[672,256]{1,0:T(8,128)(2,1)S(1)}, u32[]{:S(2)}, u32[]{:S(2)}) collective-permute-start(bf16[672,256]{1,0:T(8,128)(2,1)} %get-tuple-element.35), channel_id=1, source_target_pairs={{0,1},{1,0},{2,3},{3,2},{4,5},{5,4},{6,7},{7,6},{8,9},{9,8},{10,11... | collective-permute-start | bytes 1032200 | tf_op jit(solution)/shard_map/ppermute | solution.py:517
  42.5 1.2 %copy-start.10 = (bf16[7,256,256]{2,1,0:T(8,128)(2,1)S(1)}, bf16[7,256,256]{2,1,0:T(8,128)(2,1)}, u32[]{:S(2)}) copy-start(bf16[7,256,256]{2,1,0:T(8,128)(2,1)} %get-tuple-element.38.refs_3_) | copy-start | bytes 2752516
  43.7 9.4 %copy-start.1 = (bf16[8,256,256]{2,1,0:T(8,128)(2,1)S(1)}, bf16[8,256,256]{2,1,0:T(8,128)(2,1)}, u32[]{:S(2)}) copy-start(bf16[8,256,256]{2,1,0:T(8,128)(2,1)} %get-tuple-element.31.refs_1_) | copy-start | bytes 3145732
  43.7 9.4 %copy-start.11 = (bf16[8,256,256]{2,1,0:T(8,128)(2,1)S(1)}, bf16[8,256,256]{2,1,0:T(8,128)(2,1)}, u32[]{:S(2)}) copy-start(bf16[8,256,256]{2,1,0:T(8,128)(2,1)} %get-tuple-element.30.refs_0_) | copy-start | bytes 3145732

commit v5 on v4

--- a/solution.py
+++ b/solution.py
@@ -107,16 +107,39 @@
     return (mf * lax.rsqrt(mean + EPS)).astype(BF16)
 
 
-def prep_kernel(caps, side_ref, near_ref, far_ref, atm_ref, depth_ref, on_ref, off_ref, flag_ref):
-    _, lev, cols, width = near_ref.shape
-    rows = depth_ref.shape[0]
-    for block, row, out in ((near_ref, 0, on_ref), (far_ref, 1, off_ref)):
-        deep = column(depth_ref[pl.ds(side_ref[row], 1), :].astype(F32))
+def prep_kernel(
+    caps, side_ref, state_hbm, atm_hbm, depth_ref, on_hbm, off_hbm, flag_ref, rows_in, in_sem, out_sem, atm_sem
+):
+    _, lev, cells, width = state_hbm.shape
+    rows, cols = depth_ref.shape
+    own = atm_hbm.shape[1]
+    sides = (on_hbm, off_hbm)
+    loads, stores = [], []
+    for k in (1, 0):
+        at = pl.multiple_of(side_ref[k] * cols, cols)
         for l in range(lev):
-            wet = (deep > l).astype(F32).astype(BF16)
-            out[l * cols : (l + 1) * cols] = block[0, l] * widen(wet, width)
-    on_ref[lev * cols :] = atm_ref[0]
+            load = pltpu.make_async_copy(
+                state_hbm.at[0, l, pl.ds(at, cols)], rows_in.at[k, l], in_sem.at[k, l]
+            )
+            load.start()
+            loads.append((k, l, load))
+    for k, out in enumerate(sides):
+        store = pltpu.make_async_copy(
+            atm_hbm.at[0], out.at[pl.ds(lev * cols, own)], atm_sem.at[k]
+        )
+        store.start()
+        stores.append(store)
     d = depth_ref[...].astype(F32)
+    deep = [column(jnp.where(side_ref[k] == 0, d[0:1], d[rows - 1 :])) for k in range(2)]
+    for k, l, load in loads:
+        wet = widen((deep[k] > l).astype(F32).astype(BF16), width)
+        load.wait()
+        rows_in[k, l] = rows_in[k, l] * wet
+        store = pltpu.make_async_copy(
+            rows_in.at[k, l], sides[k].at[pl.ds(l * cols, cols)], out_sem.at[k, l]
+        )
+        store.start()
+        stores.append(store)
     counts = [
         jnp.sum(jnp.maximum(d[1 : rows - 1] - 1.0, 0.0)),
         jnp.sum(d[0:1]),
@@ -126,6 +149,8 @@
     for count, cap in zip(counts, caps):
         over = over | (count > cap).astype(jnp.int32)
     flag_ref[0] = over
+    for store in stores:
+        store.wait()
 
 
 def inner_kernel(
@@ -213,7 +238,9 @@
             sem.at[0],
         ),
         pltpu.make_async_copy(
-            off_hbm.at[0], window.at[pl.ds(pl.multiple_of(2 * own - on_at, own), own)], sem.at[1]
+            off_hbm.at[pl.ds(off_hbm.shape[0] - own, own)],
+            window.at[pl.ds(pl.multiple_of(2 * own - on_at, own), own)],
+            sem.at[1],
         ),
         pltpu.make_async_copy(atm_hbm.at[0], window.at[pl.ds(own, own)], sem.at[2]),
         pltpu.make_async_copy(remap_hbm, remap, sem.at[3]),
@@ -275,7 +302,7 @@
     copies = [
         pltpu.make_async_copy(weight_hbm, weight, in_sem.at[0]),
         pltpu.make_async_copy(on_hbm.at[pl.ds(0, lev * cols)], halos.at[on_at], in_sem.at[1]),
-        pltpu.make_async_copy(off_hbm, halos.at[1 - on_at], in_sem.at[2]),
+        pltpu.make_async_copy(off_hbm.at[pl.ds(0, lev * cols)], halos.at[1 - on_at], in_sem.at[2]),
         pltpu.make_async_copy(forcing_hbm, forcing, in_sem.at[3]),
     ]
     for copy in copies:
@@ -533,31 +560,22 @@
     conv_flops = lambda n, c: 2 * 9 * n * c * width * width
     dma = pltpu.SemaphoreType.DMA
     slack = cols + 16
-    full = lambda a: pl.BlockSpec(a.shape, lambda i, *_: (0,) * a.ndim)
-    state_row = lambda k: pl.BlockSpec((1, lev, cols, width), lambda i, s: (0, 0, s[k], 0))
-
-    off_atm = swap(atm_latent, 1)
+    message = lev * cols + own
     on_msg, off_msg, flag = pl.pallas_call(
         functools.partial(prep_kernel, (deep_cap, edge_cap, edge_cap)),
-        grid_spec=pltpu.PrefetchScalarGridSpec(
-            num_scalar_prefetch=1,
-            grid=(1,),
-            in_specs=[state_row(0), state_row(1), full(atm_latent), full(depth)],
-            out_specs=[
-                pl.BlockSpec((lev * cols + own, width), lambda i, s: (0, 0)),
-                pl.BlockSpec((lev * cols, width), lambda i, s: (0, 0)),
-                smem,
-            ],
-        ),
-        out_shape=[
-            tok(lev * cols + own),
-            tok(lev * cols),
-            jax.ShapeDtypeStruct((1,), jnp.int32),
+        in_specs=[smem, hbm, hbm, vmem],
+        out_specs=[hbm, hbm, smem],
+        out_shape=[tok(message), tok(message), jax.ShapeDtypeStruct((1,), jnp.int32)],
+        scratch_shapes=[
+            pltpu.VMEM((2, lev, cols, width), BF16),
+            dma((2, lev)),
+            dma((2, lev)),
+            dma((2,)),
         ],
-        compiler_params=params(16, 1),
+        compiler_params=params(16),
         cost_estimate=cost(lev * cols * width * 4, lev * cols * width * 10),
         name="prep",
-    )(side, stay(ocean_state), stay(ocean_state), stay(atm_latent), stay(depth))
+    )(side, stay(ocean_state), stay(atm_latent), depth)
     off_halo = swap(off_msg, 1)
     on_halo = swap(on_msg, 0)
 
@@ -603,7 +621,7 @@
         depth,
         conv_weight,
         on_halo,
-        off_atm,
+        off_halo,
         stay(atm_latent),
         stay(remap_weight),
     )
@@ -629,7 +647,7 @@
         compiler_params=params(20),
         cost_estimate=cost(conv_flops(lev, 2 * cols), lev * cols * width * 16),
         name="edge",
-    )(side, ocean_state, depth, stay(conv_weight), on_halo, off_halo, edge_forcing)
+    )(side, ocean_state, depth, stay(conv_weight), on_halo, off_halo, stay(edge_forcing))
     top_others = exchange(top_packed)
     low_others = exchange(low_packed)
 

time: 63.4 us -> 78.3 us (1.24)
  Pallas kernels: 40.3 us -> 55.5 us
  starting transfers between devices: 10.9 us -> 7.86 us
  waiting for transfers between devices: 8.23 us -> 10.1 us
  local copies, waits for them, and re-layouts: 2.17 us -> 3.3 us
    pallas_call x1, Pallas kernels: 3.44 us -> 18.4 us  [body(): pl.pallas_call(functools.partial(prep_kernel, (deep_cap, edge_cap, edge_c...]
    ppermute x3 -> x2, starting transfers between devices: 5.64 us -> 2.6 us  [swap(): return lax.ppermute(x, 'tile', pairs + [(b, a) for a, b in pairs])]
    ppermute x3 -> x2, waiting for transfers between devices: 8.22 us -> 10.1 us  [swap(): return lax.ppermute(x, 'tile', pairs + [(b, a) for a, b in pairs])]
    unnamed x26 -> x28, local copies, waits for them, and re-layouts: 2.17 us -> 3.3 us
  transfers between devices with their start and end apart: 7 -> 6, of which waited for: 1 -> 1; matrix products, arithmetic and copies ran while one was open for 0% -> 0% of each run, Pallas kernels for 51% -> 42%
where the time goes in v5:
time: 78.3 us; the launch traced here: 77.8 us
  Pallas kernels  55.5 us (71%)
  waiting for transfers between devices  10.1 us (13%)
  starting transfers between devices  7.86 us (10%)
  local copies, waits for them, and re-layouts  3.3 us (4%)
  between operations  0.99 us (1%)
    pallas_call x3, Pallas kernels, attend(): pl.pallas_call(functools.partial(attend_kernel, others, nparts, tuple(row...  18.8 us
    pallas_call x1, Pallas kernels, body(): pl.pallas_call(functools.partial(prep_kernel, (deep_cap, edge_cap, edge_c...  18.4 us
    ppermute x2, waiting for transfers between devices, swap(): return lax.ppermute(x, 'tile', pairs + [(b, a) for a, b in pairs])  10.1 us
    pallas_call x1, Pallas kernels, body(): pl.pallas_call(functools.partial(edge_kernel, edge_cap), in_specs=[smem,...  8.81 us
    pallas_call x1, Pallas kernels, body(): pl.pallas_call(functools.partial(inner_kernel, deep_cap), in_specs=[vmem,...  5.86 us
    ppermute x4, starting transfers between devices, exchange(): lax.ppermute(x, 'mem', [(i, (i + k) % members) for i in range(members)])  5.26 us
    pallas_call x1, Pallas kernels, body(): pl.pallas_call(surface_kernel, in_specs=[smem] * 3 + [vmem] * 3 + [anywhe...  3.6 us
    unnamed x28, local copies, waits for them, and re-layouts  3.3 us
  transfers between devices with their start and end apart: 6, of which 1 were waited for; matrix products, arithmetic and copies ran while one was open for 0% of the time, Pallas kernels for 42%

profile of v5, /device:TPU:18, one launch (start us, length us, event | category | flops | bytes accessed | tf_op | source)
XLA Modules:
  0.0 77.8 jit_solution(11980368031751233614)
XLA Ops:
  0.0 0.1 pad_add_fusion.side_ref
  0.1 0.8 %copy-done.6 = s32[512]{0:T(512)S(1)} copy-done((s32[512]{0:T(512)S(1)}, s32[512]{0:T(512)}, u32[]{:S(2)}) %copy-start.6) | copy-done | bytes 2072
  0.9 18.4 %prep.1 = (bf16[1536,256]{1,0:T(8,128)(2,1)}, bf16[1536,256]{1,0:T(8,128)(2,1)}, s32[1]{0:T(128)}) custom-call(s32[2]{0:T(128)S(1)} %pad_add_fusion.side_ref, bf16[1,8,512,256]{3,2,1,0:T(8,128)(2,1)} %state.5, bf16[1,512,256]{2,1,0:T(8,128)(2,1)} %atm_hbm.3, s32[4,128]{1,0:T(4,128)S(1)} %bitcast.4), custom_call_target="tpu_custom_call" | custom-call | flops 1048576 | bytes 2621440 | tf_op jit(solution)/shard_map/prep/pallas_call | solution.py:564
  19.3 0.1 collective-permute-start.2
  19.4 2.5 %collective-permute-start.3 = (bf16[1536,256]{1,0:T(8,128)(2,1)}, bf16[1536,256]{1,0:T(8,128)(2,1)}, u32[]{:S(2)}, u32[]{:S(2)}) collective-permute-start(bf16[1536,256]{1,0:T(8,128)(2,1)} %get-tuple-element.28), channel_id=1, source_target_pairs={{2,4},{6,8},{10,12},{14,16},{18,20},{22,24},{26,28},{4,2},{8,6},{1... | collective-permute-start | bytes 2359304 | tf_op jit(solution)/shard_map/ppermute | solution.py:540
  21.9 0.0 copy-done
  21.9 0.0 copy-done.7
  21.9 0.0 copy-start.3
  21.9 1.3 %copy-done.3 = bf16[3,3,256,256]{3,2,1,0:T(8,128)(2,1)S(1)} copy-done((bf16[3,3,256,256]{3,2,1,0:T(8,128)(2,1)S(1)}, bf16[3,3,256,256]{3,2,1,0:T(8,128)(2,1)}, u32[]{:S(2)}) %copy-start.3) | copy-done | bytes 1179672
  23.2 5.9 %inner.1 = (bf16[7,256,256]{2,1,0:T(8,128)(2,1)}, bf16[7,256,256]{2,1,0:T(8,128)(2,1)}, bf16[1008,256]{1,0:T(8,128)(2,1)}) custom-call(bf16[1,8,512,256]{3,2,1,0:T(8,128)(2,1)S(1)} %copy-done, s32[4,128]{1,0:T(4,128)S(1)} %bitcast.5, bf16[3,3,256,256]{3,2,1,0:T(8,128)(2,1)S(1)} %copy-done.3), custom_call_target="tpu_custom_call" | custom-call | flops 2415919104 | bytes 4194304 | tf_op jit(solution)/shard_map/inner/pallas_call | solution.py:582
  29.1 1.6 %collective-permute-start.7 = (bf16[1008,256]{1,0:T(8,128)(2,1)}, bf16[1008,256]{1,0:T(8,128)(2,1)}, u32[]{:S(2)}, u32[]{:S(2)}) collective-permute-start(bf16[1008,256]{1,0:T(8,128)(2,1)} %get-tuple-element.39), channel_id=1, source_target_pairs={{0,1},{1,0},{2,3},{3,2},{4,5},{5,4},{6,7},{7,6},{8,9},{9,8},{10,11... | collective-permute-start | bytes 1548296 | tf_op jit(solution)/shard_map/ppermute | solution.py:544
  31.3 0.0 copy-done.13
  31.3 0.0 collective-permute-done.2.on_hbm
  31.3 10.1 %collective-permute-done.3.off_hbm = bf16[1536,256]{1,0:T(8,128)(2,1)} collective-permute-done((bf16[1536,256]{1,0:T(8,128)(2,1)}, bf16[1536,256]{1,0:T(8,128)(2,1)}, u32[]{:S(2)}, u32[]{:S(2)}) %collective-permute-start.3) | collective-permute-done | bytes 786464 | tf_op jit(solution)/shard_map/ppermute | solution.py:540
  41.4 0.0 copy-done.4
  41.4 0.0 copy-done.8
  41.4 3.6 %surface.1 = (bf16[1,256,256]{2,1,0:T(8,128)(2,1)}, bf16[1,256,256]{2,1,0:T(8,128)(2,1)}, f32[256,256]{1,0:T(8,128)}) custom-call(s32[4,4]{1,0:T(4,128)S(1)} %subtract_clamp_fusion.ids_ref, s32[4]{0:T(128)S(1)} %copy-done.8, s32[2]{0:T(128)S(1)} %pad_add_fusion.side_ref, bf16[1,8,512,256]{3,2,1,0:T(8,128)(2,1)S(1)} %copy-done, s32[4,128]{1,0:T(4,128)S(1)} %bitcast.6, ...), custom_call_target="tpu_custom_call" | custom-call | flops 301989888 | bytes 2097152 | tf_op jit(solution)/shard_map/surface/pallas_call | solution.py:602
  45.0 1.6 %collective-permute-start.6 = (bf16[1,256,256]{2,1,0:T(8,128)(2,1)}, bf16[1,256,256]{2,1,0:T(8,128)(2,1)S(1)}, u32[]{:S(2)}, u32[]{:S(2)}) collective-permute-start(bf16[1,256,256]{2,1,0:T(8,128)(2,1)} %get-tuple-element.36.refs_0_), channel_id=1, source_target_pairs={{0,1},{1,0},{2,3},{3,2},{4,5},{5,4},{6,7},{7,6},{8,9},{9,8},{10,11... | collective-permute-start | bytes 393224 | tf_op jit(solution)/shard_map/ppermute | solution.py:544
  46.6 8.8 %edge.1 = (bf16[8,256,256]{2,1,0:T(8,128)(2,1)}, bf16[8,256,256]{2,1,0:T(8,128)(2,1)}, bf16[672,256]{1,0:T(8,128)(2,1)}, bf16[672,256]{1,0:T(8,128)(2,1)}) custom-call(s32[2]{0:T(128)S(1)} %pad_add_fusion.side_ref, bf16[1,8,512,256]{3,2,1,0:T(8,128)(2,1)S(1)} %copy-done, s32[4,128]{1,0:T(4,128)S(1)} %bitcast.7, bf16[3,3,256,256]{3,2,1,0:T(8,128)(2,1)} %weight.3, ...), custom_call_target="tpu_custom_call" | custom-call | flops 2415919104 | bytes 4194304 | tf_op jit(solution)/shard_map/edge/pallas_call | solution.py:630
  55.5 0.6 collective-permute-start.4
  56.0 1.5 %collective-permute-start.5 = (bf16[672,256]{1,0:T(8,128)(2,1)}, bf16[672,256]{1,0:T(8,128)(2,1)S(1)}, u32[]{:S(2)}, u32[]{:S(2)}) collective-permute-start(bf16[672,256]{1,0:T(8,128)(2,1)} %get-tuple-element.35), channel_id=1, source_target_pairs={{0,1},{1,0},{2,3},{3,2},{4,5},{5,4},{6,7},{7,6},{8,9},{9,8},{10,11... | collective-permute-start | bytes 1032200 | tf_op jit(solution)/shard_map/ppermute | solution.py:544
  57.6 0.0 collective-permute-done.7.refs_5_
  57.6 0.0 collective-permute-done.6.refs_4_
  57.6 0.0 copy-done.2
  57.6 0.0 copy-done.5
  57.6 0.0 copy-start.11
  57.6 1.2 %copy-done.11 = bf16[7,256,256]{2,1,0:T(8,128)(2,1)S(1)} copy-done((bf16[7,256,256]{2,1,0:T(8,128)(2,1)S(1)}, bf16[7,256,256]{2,1,0:T(8,128)(2,1)}, u32[]{:S(2)}) %copy-start.11) | copy-done | bytes 917528
  58.8 9.4 %attend.3.refs_7_ = bf16[1,8,512,256]{3,2,1,0:T(8,128)(2,1)} custom-call(s32[1]{0:T(128)} %get-tuple-element.26.flag_ref, bf16[1,256,256]{2,1,0:T(8,128)(2,1)S(1)} %copy-done.10, bf16[7,256,256]{2,1,0:T(8,128)(2,1)} %get-tuple-element.33.refs_1_, bf16[1,256,256]{2,1,0:T(8,128)(2,1)S(1)} %copy-done.9, bf16[7,256,256]{2,1,0:T(8,128)(2,1)S(1)} %copy-done.11, ...), custom_call_target="tpu_custom_call" | custom-call | flops 4294967296 | bytes 5242880 | tf_op jit(solution)/shard_map/attend/pallas_call | solution.py:488
  68.2 0.0 collective-permute-done.5.refs_2_
  68.2 4.7 %attend.4.refs_7_ = bf16[1,8,512,256]{3,2,1,0:T(8,128)(2,1)} custom-call(s32[1]{0:T(128)} %get-tuple-element.26.flag_ref, bf16[8,256,256]{2,1,0:T(8,128)(2,1)S(1)} %copy-done.12, bf16[8,256,256]{2,1,0:T(8,128)(2,1)S(1)} %copy-done.1, bf16[672,256]{1,0:T(8,128)(2,1)S(1)} %collective-permute-done.5.refs_2_, ...), custom_call_target="tpu_custom_call", output_to_operand_aliasing={{}: (8, {})} | custom-call | flops 2147483648 | bytes 2621440 | tf_op jit(solution)/shard_map/attend/pallas_call | solution.py:488
  72.9 0.0 collective-permute-done.4.refs_2_
  72.9 4.7 %attend.5 = bf16[1,8,512,256]{3,2,1,0:T(8,128)(2,1)} custom-call(s32[1]{0:T(128)} %get-tuple-element.26.flag_ref, bf16[8,256,256]{2,1,0:T(8,128)(2,1)S(1)} %copy-done.12, bf16[8,256,256]{2,1,0:T(8,128)(2,1)S(1)} %copy-done.1, bf16[672,256]{1,0:T(8,128)(2,1)S(1)} %collective-permute-done.4.refs_2_, ...), custom_call_target="tpu_custom_call", output_to_operand_aliasing={{}: (8, {})} | custom-call | flops 2147483648 | bytes 2621440 | tf_op jit(solution)/shard_map/attend/pallas_call | solution.py:488
  (20 shorter events, 0.0 us)
Async XLA Ops:
  0.0 21.9 %copy-start = (bf16[1,8,512,256]{3,2,1,0:T(8,128)(2,1)S(1)}, bf16[1,8,512,256]{3,2,1,0:T(8,128)(2,1)}, u32[]{:S(2)}) copy-start(bf16[1,8,512,256]{3,2,1,0:T(8,128)(2,1)} %state.5) | copy-start | bytes 6291460
  0.1 0.8 %copy-start.6 = (s32[512]{0:T(512)S(1)}, s32[512]{0:T(512)}, u32[]{:S(2)}) copy-start(s32[512]{0:T(512)} %param.13) | copy-start | bytes 6148
  0.9 21.0 %copy-start.7 = (s32[512]{0:T(512)S(1)}, s32[512]{0:T(512)}, u32[]{:S(2)}) copy-start(s32[512]{0:T(512)} %param.13) | copy-start | bytes 6148
  19.3 12.0 %collective-permute-start.2 = (bf16[1536,256]{1,0:T(8,128)(2,1)}, bf16[1536,256]{1,0:T(8,128)(2,1)}, u32[]{:S(2)}, u32[]{:S(2)}) collective-permute-start(bf16[1536,256]{1,0:T(8,128)(2,1)} %get-tuple-element.27), channel_id=1, source_target_pairs={{0,2},{4,6},{8,10},{12,14},{16,18},{20,22},{24,26},{28,30},{2,0},{... | collective-permute-start | bytes 2359304 | tf_op jit(solution)/shard_map/ppermute | solution.py:540
  19.4 22.1 %collective-permute-start.3 = (bf16[1536,256]{1,0:T(8,128)(2,1)}, bf16[1536,256]{1,0:T(8,128)(2,1)}, u32[]{:S(2)}, u32[]{:S(2)}) collective-permute-start(bf16[1536,256]{1,0:T(8,128)(2,1)} %get-tuple-element.28), channel_id=1, source_target_pairs={{2,4},{6,8},{10,12},{14,16},{18,20},{22,24},{26,28},{4,2},{8,6},{1... | collective-permute-start | bytes 2359304 | tf_op jit(solution)/shard_map/ppermute | solution.py:540
  21.9 1.3 %copy-start.3 = (bf16[3,3,256,256]{3,2,1,0:T(8,128)(2,1)S(1)}, bf16[3,3,256,256]{3,2,1,0:T(8,128)(2,1)}, u32[]{:S(2)}) copy-start(bf16[3,3,256,256]{3,2,1,0:T(8,128)(2,1)} %weight.3) | copy-start | bytes 3538948
  23.2 8.1 %copy-start.13 = (s32[4,4]{1,0:T(4,128)S(1)}, s32[4,4]{1,0:T(4,128)}, u32[]{:S(2)}) copy-start(s32[4,4]{1,0:T(4,128)} %param.14) | copy-start | bytes 196
  23.2 18.2 %copy-start.4 = (bf16[3,3,256,256]{3,2,1,0:T(8,128)(2,1)S(1)}, bf16[3,3,256,256]{3,2,1,0:T(8,128)(2,1)}, u32[]{:S(2)}) copy-start(bf16[3,3,256,256]{3,2,1,0:T(8,128)(2,1)} %weight.3) | copy-start | bytes 3538948
  23.2 18.2 %copy-start.8 = (s32[4]{0:T(128)S(1)}, s32[4]{0:T(128)}, u32[]{:S(2)}) copy-start(s32[4]{0:T(128)} %live_ref.1) | copy-start | bytes 52
  29.1 28.5 %collective-permute-start.7 = (bf16[1008,256]{1,0:T(8,128)(2,1)}, bf16[1008,256]{1,0:T(8,128)(2,1)}, u32[]{:S(2)}, u32[]{:S(2)}) collective-permute-start(bf16[1008,256]{1,0:T(8,128)(2,1)} %get-tuple-element.39), channel_id=1, source_target_pairs={{0,1},{1,0},{2,3},{3,2},{4,5},{5,4},{6,7},{7,6},{8,9},{9,8},{10,11... | collective-permute-start | bytes 1548296 | tf_op jit(solution)/shard_map/ppermute | solution.py:544
  45.0 12.5 %collective-permute-start.6 = (bf16[1,256,256]{2,1,0:T(8,128)(2,1)}, bf16[1,256,256]{2,1,0:T(8,128)(2,1)S(1)}, u32[]{:S(2)}, u32[]{:S(2)}) collective-permute-start(bf16[1,256,256]{2,1,0:T(8,128)(2,1)} %get-tuple-element.36.refs_0_), channel_id=1, source_target_pairs={{0,1},{1,0},{2,3},{3,2},{4,5},{5,4},{6,7},{7,6},{8,9},{9,8},{10,11... | collective-permute-start | bytes 393224 | tf_op jit(solution)/shard_map/ppermute | solution.py:544
  46.6 10.9 %copy-start.2 = (bf16[256,768]{1,0:T(8,128)(2,1)S(1)}, bf16[256,768]{1,0:T(8,128)(2,1)}, u32[]{:S(2)}) copy-start(bf16[256,768]{1,0:T(8,128)(2,1)} %refs_5_.3) | copy-start | bytes 1179652
  46.6 10.9 %copy-start.5 = (bf16[256,256]{1,0:T(8,128)(2,1)S(1)}, bf16[256,256]{1,0:T(8,128)(2,1)}, u32[]{:S(2)}) copy-start(bf16[256,256]{1,0:T(8,128)(2,1)} %refs_6_.3) | copy-start | bytes 393220
  46.6 10.9 %copy-start.9 = (bf16[1,256,256]{2,1,0:T(8,128)(2,1)S(1)}, bf16[1,256,256]{2,1,0:T(8,128)(2,1)}, u32[]{:S(2)}) copy-start(bf16[1,256,256]{2,1,0:T(8,128)(2,1)} %get-tuple-element.37.refs_2_) | copy-start | bytes 393220
  46.6 11.0 %copy-start.10 = (bf16[1,256,256]{2,1,0:T(8,128)(2,1)S(1)}, bf16[1,256,256]{2,1,0:T(8,128)(2,1)}, u32[]{:S(2)}) copy-start(bf16[1,256,256]{2,1,0:T(8,128)(2,1)} %get-tuple-element.36.refs_0_) | copy-start | bytes 393220
  55.5 17.5 %collective-permute-start.4 = (bf16[672,256]{1,0:T(8,128)(2,1)}, bf16[672,256]{1,0:T(8,128)(2,1)S(1)}, u32[]{:S(2)}, u32[]{:S(2)}) collective-permute-start(bf16[672,256]{1,0:T(8,128)(2,1)} %get-tuple-element.32), channel_id=1, source_target_pairs={{0,1},{1,0},{2,3},{3,2},{4,5},{5,4},{6,7},{7,6},{8,9},{9,8},{10,11... | collective-permute-start | bytes 1032200 | tf_op jit(solution)/shard_map/ppermute | solution.py:544
  56.0 12.1 %collective-permute-start.5 = (bf16[672,256]{1,0:T(8,128)(2,1)}, bf16[672,256]{1,0:T(8,128)(2,1)S(1)}, u32[]{:S(2)}, u32[]{:S(2)}) collective-permute-start(bf16[672,256]{1,0:T(8,128)(2,1)} %get-tuple-element.35), channel_id=1, source_target_pairs={{0,1},{1,0},{2,3},{3,2},{4,5},{5,4},{6,7},{7,6},{8,9},{9,8},{10,11... | collective-permute-start | bytes 1032200 | tf_op jit(solution)/shard_map/ppermute | solution.py:544
  57.6 1.2 %copy-start.11 = (bf16[7,256,256]{2,1,0:T(8,128)(2,1)S(1)}, bf16[7,256,256]{2,1,0:T(8,128)(2,1)}, u32[]{:S(2)}) copy-start(bf16[7,256,256]{2,1,0:T(8,128)(2,1)} %get-tuple-element.38.refs_3_) | copy-start | bytes 2752516
  58.8 9.4 %copy-start.1 = (bf16[8,256,256]{2,1,0:T(8,128)(2,1)S(1)}, bf16[8,256,256]{2,1,0:T(8,128)(2,1)}, u32[]{:S(2)}) copy-start(bf16[8,256,256]{2,1,0:T(8,128)(2,1)} %get-tuple-element.31.refs_1_) | copy-start | bytes 3145732
  58.8 9.4 %copy-start.12 = (bf16[8,256,256]{2,1,0:T(8,128)(2,1)S(1)}, bf16[8,256,256]{2,1,0:T(8,128)(2,1)}, u32[]{:S(2)}) copy-start(bf16[8,256,256]{2,1,0:T(8,128)(2,1)} %get-tuple-element.30.refs_0_) | copy-start | bytes 3145732

commit v6 on v3

--- a/solution.py
+++ b/solution.py
@@ -107,27 +107,51 @@
     return (mf * lax.rsqrt(mean + EPS)).astype(BF16)
 
 
-def prep_kernel(caps, side_ref, near_ref, far_ref, atm_ref, depth_ref, on_ref, off_ref, flag_ref):
-    _, lev, cols, width = near_ref.shape
-    rows = depth_ref.shape[0]
-    for block, row, out in ((near_ref, 0, on_ref), (far_ref, 1, off_ref)):
-        deep = column(depth_ref[pl.ds(side_ref[row], 1), :].astype(F32))
+def prep_kernel(
+    caps, side_ref, state_hbm, atm_ref, depth_ref, on_hbm, off_hbm, flag_ref, rows_in, in_sem, out_sem, atm_sem
+):
+    _, lev, cells, width = state_hbm.shape
+    rows, cols = depth_ref.shape
+    own = atm_ref.shape[1]
+    sides = (on_hbm, off_hbm)
+    loads, stores = [], []
+    for k in (1, 0):
+        at = pl.multiple_of(side_ref[k] * cols, cols)
         for l in range(lev):
-            wet = (deep > l).astype(F32).astype(BF16)
-            out[l * cols : (l + 1) * cols] = block[0, l] * widen(wet, width)
-    on_ref[lev * cols :] = atm_ref[0]
+            load = pltpu.make_async_copy(
+                state_hbm.at[0, l, pl.ds(at, cols)], rows_in.at[k, l], in_sem.at[k, l]
+            )
+            load.start()
+            loads.append((k, l, load))
+    for k, out in enumerate(sides):
+        store = pltpu.make_async_copy(
+            atm_ref.at[0], out.at[pl.ds(lev * cols, own)], atm_sem.at[k]
+        )
+        store.start()
+        stores.append(store)
     d = depth_ref[...].astype(F32)
-    near = depth_ref[pl.ds(side_ref[0], 1), :].astype(F32)
-    far = depth_ref[pl.ds(side_ref[1], 1), :].astype(F32)
+    pick = lambda k: jnp.where(side_ref[k] == 0, d[0:1], d[rows - 1 :])
+    deep = [column(pick(k)) for k in range(2)]
+    for k, l, load in loads:
+        wet = widen((deep[k] > l).astype(F32).astype(BF16), width)
+        load.wait()
+        rows_in[k, l] = rows_in[k, l] * wet
+        store = pltpu.make_async_copy(
+            rows_in.at[k, l], sides[k].at[pl.ds(l * cols, cols)], out_sem.at[k, l]
+        )
+        store.start()
+        stores.append(store)
     counts = [
         jnp.sum(jnp.maximum(d[1 : rows - 1] - 1.0, 0.0)),
-        jnp.sum(jnp.maximum(near - 1.0, 0.0)),
-        jnp.sum(far),
+        jnp.sum(jnp.maximum(pick(0) - 1.0, 0.0)),
+        jnp.sum(pick(1)),
     ]
     over = jnp.int32(0)
     for count, cap in zip(counts, caps):
         over = over | (count > cap).astype(jnp.int32)
     flag_ref[0] = over
+    for store in stores:
+        store.wait()
 
 
 def inner_kernel(
@@ -138,7 +162,6 @@
     mixed_hbm,
     normed_hbm,
     packed_hbm,
-    base_ref,
     mixed,
     normed,
     packed,
@@ -154,15 +177,12 @@
     deep = jnp.concatenate([column(d[r : r + 1]) for r in range(rows)], axis=0)
     count = cells - 2 * cols
     stores = []
-    for l in list(range(1, lev)) + [0]:
+    for l in range(1, lev):
         wet = (deep > l).astype(F32)
         x = state[0, l] * widen(wet.astype(BF16), width)
         taps = [x[dr * cols : dr * cols + count] for dr in range(3)]
         total = stencil(taps, weight, cols)
         new = taps[1].astype(F32) + widen(wet[cols : cols + count], width) * total
-        if l == 0:
-            base_ref[...] = new
-            continue
         new = new.astype(BF16)
         mixed[l - 1] = new
         tokens = normalise(new)
@@ -192,69 +212,105 @@
     ids_ref,
     live_ref,
     side_ref,
-    base_ref,
-    near_base_ref,
+    state,
     depth_ref,
-    on_ref,
-    off_ref,
-    atm_ref,
-    remap_ref,
+    weight,
+    on_hbm,
+    off_hbm,
+    atm_hbm,
+    remap_hbm,
+    near_base,
     mixed_ref,
     normed_ref,
     far_ref,
-    window_ref,
+    window,
+    remap,
     forcing_ref,
+    sem,
 ):
     rows, cols = depth_ref.shape
-    width = base_ref.shape[-1]
-    own = atm_ref.shape[1]
-    blocks, pairs = remap_ref.shape[0], remap_ref.shape[1]
-    near, far = side_ref[0], side_ref[1]
-    on_at = jnp.where(near == 0, 0, 2 * own)
-    window_ref[pl.ds(pl.multiple_of(on_at, own), own)] = on_ref[on_ref.shape[0] - own :]
-    window_ref[pl.ds(pl.multiple_of(2 * own - on_at, own), own)] = off_ref[0]
-    window_ref[own : 2 * own] = atm_ref[0]
+    _, own, width = atm_hbm.shape
+    cells = state.shape[2]
+    blocks, pairs = remap_hbm.shape[0], remap_hbm.shape[1]
+    on_at = jnp.where(side_ref[0] == 0, 0, 2 * own)
+    copies = [
+        pltpu.make_async_copy(
+            on_hbm.at[pl.ds(on_hbm.shape[0] - own, own)],
+            window.at[pl.ds(pl.multiple_of(on_at, own), own)],
+            sem.at[0],
+        ),
+        pltpu.make_async_copy(
+            off_hbm.at[pl.ds(off_hbm.shape[0] - own, own)],
+            window.at[pl.ds(pl.multiple_of(2 * own - on_at, own), own)],
+            sem.at[1],
+        ),
+        pltpu.make_async_copy(atm_hbm.at[0], window.at[pl.ds(own, own)], sem.at[2]),
+        pltpu.make_async_copy(remap_hbm, remap, sem.at[3]),
+    ]
+    for copy in copies:
+        copy.start()
+    d = depth_ref[...].astype(F32)
+    wet = (jnp.concatenate([column(d[r : r + 1]) for r in range(rows)], axis=0) > 0).astype(F32)
+    x = state[0, 0] * widen(wet.astype(BF16), width)
+    count = cells - 2 * cols
+    taps = [x[dr * cols : dr * cols + count] for dr in range(3)]
+    total = stencil(taps, weight, cols)
+    for copy in copies:
+        copy.wait()
     for b in range(blocks):
         acc = jnp.zeros((cols, width), F32)
         for p in range(pairs):
             on = (p < live_ref[b]).astype(F32)
             start = pl.multiple_of(ids_ref[b, p] * cols, cols)
             acc = acc + on * jnp.dot(
-                remap_ref[b, p], window_ref[pl.ds(start, cols), :], preferred_element_type=F32
+                remap[b, p], window[pl.ds(start, cols), :], preferred_element_type=F32
             )
         forcing_ref[b] = acc
-    d = depth_ref[...].astype(F32)
-    near_row = depth_ref[pl.ds(near, 1), :].astype(F32)
-    for k in range(rows - 1):
+    near = side_ref[0]
+    parts = [
+        (taps[1][r * cols : (r + 1) * cols].astype(F32), total[r * cols : (r + 1) * cols], r + 1)
+        for r in range(rows - 2)
+    ]
+    for k, (base, conv, r) in enumerate(parts):
         at = slice(k * cols, (k + 1) * cols)
-        last = k == rows - 2
-        wet = (column(near_row if last else d[k + 1 : k + 2]) > 0).astype(F32)
-        part = near_base_ref[...] if last else base_ref[at]
-        forcing = forcing_ref[near] if last else forcing_ref[k + 1]
-        new = (part + widen(wet, width) * forcing).astype(BF16)
+        wet_k = widen(wet[r * cols : (r + 1) * cols], width)
+        new = (base + wet_k * (conv + forcing_ref[r])).astype(BF16)
         mixed_ref[0, at] = new
         normed_ref[0, at] = normalise(new)
-    far_ref[...] = forcing_ref[far]
-
-
-def row_kernel(cap, first, which, side_ref, state, depth_ref, weight, halo, *refs):
+    at = slice((rows - 2) * cols, (rows - 1) * cols)
+    wet_near = jnp.where(near == 0, wet[0:cols], wet[cells - cols :])
+    new = (near_base[...] + widen(wet_near, width) * forcing_ref[near]).astype(BF16)
+    mixed_ref[0, at] = new
+    normed_ref[0, at] = normalise(new)
+    far_ref[...] = forcing_ref[side_ref[1]]
+
+
+def row_kernel(cap, first, which, side_ref, state, depth_ref, weight_hbm, halo_hbm, *refs):
     refs = list(refs)
     forcing_ref = None if first else refs.pop(0)
     mixed_hbm, normed_hbm, packed_hbm = refs[:3]
     refs = refs[3:]
     base_ref = refs.pop(0) if first else None
-    tap, mixed, normed, packed, out_sem, packed_sem = refs
+    weight, tap, mixed, normed, packed, weight_sem, halo_sem, out_sem, packed_sem = refs
+    load = pltpu.make_async_copy(weight_hbm, weight, weight_sem)
+    load.start()
     _, lev, cells, width = state.shape
     rows, cols = depth_ref.shape
     row = side_ref[which]
     top = row == 0
     beside = jnp.where(top, 1, rows - 2)
     outer = jnp.where(top, 0, 2)
+    halo = pltpu.make_async_copy(
+        halo_hbm.at[pl.ds(0, lev * cols)], tap.at[outer], halo_sem
+    )
+    halo.start()
     packed[...] = jnp.zeros_like(packed)
-    own_depth = depth_ref[pl.ds(row, 1), :].astype(F32)
+    d = depth_ref[...].astype(F32)
+    own_depth = jnp.where(top, d[0:1], d[rows - 1 :])
     plan = row_plan(own_depth, lev)
     place = offsets([plan], first, lev)
-    deep, deep_beside = column(own_depth), column(depth_ref[pl.ds(beside, 1), :].astype(F32))
+    deep = column(own_depth)
+    deep_beside = column(jnp.where(top, d[1:2], d[rows - 2 : rows - 1]))
     at = pl.multiple_of(row * cols, cols)
     at_beside = pl.multiple_of(beside * cols, cols)
     wets = []
@@ -267,9 +323,10 @@
         tap[2 - outer, rows_l] = state[0, l, pl.ds(at_beside, cols)] * widen(
             wet_beside.astype(BF16), width
         )
-        tap[outer, rows_l] = halo[rows_l]
     stores = []
     half = lev // 2
+    load.wait()
+    halo.wait()
     for start in range(0, lev, half):
         rows_b = slice(start * cols, (start + half) * cols)
         taps = [tap[dr, rows_b] for dr in range(3)]
@@ -326,18 +383,19 @@
 
     two = which is None
     pick = lambda a, b: jnp.where(step == 0, a, b)
+    d = depth_ref[...].astype(F32)
+    last = d.shape[0] - 1
     if two:
-        rows_d = [depth_ref[r : r + 1, :].astype(F32) for r in range(1, depth_ref.shape[0] - 1)]
-        plans = [row_plan(row, lev) for row in rows_d]
-        place = offsets(plans, first, lev)
-        wet_row = pick(plans[0][0], plans[1][0])
-        rank = pick(plans[0][1], plans[1][1])
+        rows_d = [d[r : r + 1] for r in range(1, last)]
+    else:
+        rows_d = [jnp.where(side_ref[which] == 0, d[0:1], d[last:])]
+    plans = [row_plan(row, lev) for row in rows_d]
+    place = offsets(plans, first, lev)
+    wet_row, rank, _ = plans[0]
+    depth_row = rows_d[0]
+    if two:
+        wet_row, rank = pick(wet_row, plans[1][0]), pick(rank, plans[1][1])
         depth_row = pick(*rows_d)
-    else:
-        depth_row = depth_ref[pl.ds(side_ref[which], 1), :].astype(F32)
-        plan = row_plan(depth_row, lev)
-        place = offsets([plan], first, lev)
-        wet_row, rank, _ = plan
 
     x = jnp.concatenate([p[...].reshape(-1, width) for p in own_normed], axis=0)
     q = jnp.dot(x, qkv_ref[:, 0:width], preferred_element_type=F32).astype(BF16)
@@ -382,24 +440,25 @@
     qc = lax.broadcasted_iota(jnp.int32, (nq, nk), 0) % GROUP
     kc = lax.broadcasted_iota(jnp.int32, (nq, nk), 1) % GROUP
     same = jnp.where(qc == kc, 0.0, NEG)
-    lane = lax.broadcasted_iota(jnp.int32, (1, pair), 1)
-    low = (lane < head).astype(F32).astype(BF16)
-    high = (lane >= head).astype(F32).astype(BF16)
+    lane = lax.broadcasted_iota(jnp.int32, (1, width), 1)
+    masks = [(lane // head == h).astype(F32).astype(BF16) for h in range(HEADS)]
     for g in range(groups):
         cells = slice(g * GROUP, (g + 1) * GROUP)
         bias = same + jnp.concatenate([key_bias[g : g + 1]] * members, axis=1)
-        bias = jnp.concatenate([bias, bias], axis=0)
+        bias = jnp.concatenate([bias] * HEADS, axis=0)
+        q = q_ref[:, cells].reshape(nq, width)
+        q = jnp.concatenate([q * mask for mask in masks], axis=0)
+        k = k_ref[:, cells].reshape(nk, width)
+        v = v_ref[:, cells].reshape(nk, width)
+        s = lax.dot_general(q, k, (((1,), (1,)), ((), ())), preferred_element_type=F32) + bias
+        p = jnp.exp(s - jnp.max(s, axis=-1, keepdims=True))
+        norm = 1.0 / jnp.sum(p, axis=-1, keepdims=True)
+        p = p.astype(BF16)
         for h in range(HEADS // 2):
             lanes = slice(h * pair, (h + 1) * pair)
-            q = q_ref[:, cells, lanes].reshape(nq, pair)
-            q = jnp.concatenate([q * low, q * high], axis=0)
-            k = k_ref[:, cells, lanes].reshape(nk, pair)
-            v = v_ref[:, cells, lanes].reshape(nk, pair)
-            s = lax.dot_general(q, k, (((1,), (1,)), ((), ())), preferred_element_type=F32) + bias
-            p = jnp.exp(s - jnp.max(s, axis=-1, keepdims=True))
-            norm = 1.0 / jnp.sum(p, axis=-1, keepdims=True)
-            o = jnp.dot(p.astype(BF16), v, preferred_element_type=F32) * norm
-            o = jnp.where(lane < head, o[:nq], o[nq:])
+            mine = slice(h * 2 * nq, (h + 1) * 2 * nq)
+            o = jnp.dot(p[mine], v[:, lanes], preferred_element_type=F32) * norm[mine]
+            o = jnp.where(lane[:, :pair] < head, o[:nq], o[nq:])
             att_ref[:, cells, lanes] = o.astype(BF16).reshape(lev, GROUP, pair)
     proj = jnp.dot(att_ref[...].reshape(-1, width), wo_ref[...], preferred_element_type=F32)
     base = jnp.concatenate([p[...].reshape(-1, width) for p in own_mixed], axis=0).astype(F32)
@@ -505,51 +564,38 @@
     far_cap = capacity(lev * cols, 0.65625)
 
     hbm = pl.BlockSpec(memory_space=pltpu.HBM)
+    anywhere = pl.BlockSpec(memory_space=pl.ANY)
     vmem = pl.BlockSpec(memory_space=pltpu.VMEM)
     smem = pl.BlockSpec(memory_space=pltpu.SMEM)
-    tok = lambda *s: jax.ShapeDtypeStruct((*s, width), BF16)
-    row_f32 = jax.ShapeDtypeStruct((cols, width), F32)
+    tok = lambda *s: pltpu.HBM((*s, width), BF16)
+    stay = lambda x: pltpu.with_memory_space_constraint(x, pltpu.HBM)
     conv_flops = lambda n, c: 2 * 9 * n * c * width * width
     dma = pltpu.SemaphoreType.DMA
     slack = cols + 16
-    full = lambda a: pl.BlockSpec(a.shape, lambda i, *_: (0,) * a.ndim)
-    state_row = lambda k: pl.BlockSpec((1, lev, cols, width), lambda i, s: (0, 0, s[k], 0))
-
-    off_atm = swap(atm_latent, 1)
+    message = lev * cols + own
     on_msg, off_msg, flag = pl.pallas_call(
         functools.partial(prep_kernel, (deep_cap, near_cap, far_cap)),
-        grid_spec=pltpu.PrefetchScalarGridSpec(
-            num_scalar_prefetch=1,
-            grid=(1,),
-            in_specs=[state_row(0), state_row(1), full(atm_latent), full(depth)],
-            out_specs=[
-                pl.BlockSpec((lev * cols + own, width), lambda i, s: (0, 0)),
-                pl.BlockSpec((lev * cols, width), lambda i, s: (0, 0)),
-                smem,
-            ],
-        ),
-        out_shape=[
-            tok(lev * cols + own),
-            tok(lev * cols),
-            jax.ShapeDtypeStruct((1,), jnp.int32),
+        in_specs=[smem, hbm, vmem, vmem],
+        out_specs=[hbm, hbm, smem],
+        out_shape=[tok(message), tok(message), jax.ShapeDtypeStruct((1,), jnp.int32)],
+        scratch_shapes=[
+            pltpu.VMEM((2, lev, cols, width), BF16),
+            dma((2, lev)),
+            dma((2, lev)),
+            dma((2,)),
         ],
-        compiler_params=params(16, 1),
+        compiler_params=params(16),
         cost_estimate=cost(lev * cols * width * 4, lev * cols * width * 10),
         name="prep",
-    )(side, ocean_state, ocean_state, atm_latent, depth)
+    )(side, stay(ocean_state), atm_latent, depth)
     off_halo = swap(off_msg, 1)
     on_halo = swap(on_msg, 0)
 
-    deep_mixed, deep_normed, deep_packed, base = pl.pallas_call(
+    deep_mixed, deep_normed, deep_packed = pl.pallas_call(
         functools.partial(inner_kernel, deep_cap),
         in_specs=[vmem, vmem, vmem],
-        out_specs=[hbm, hbm, hbm, vmem],
-        out_shape=[
-            tok(lev - 1, inner),
-            tok(lev - 1, inner),
-            tok(deep_cap),
-            jax.ShapeDtypeStruct((inner, width), F32),
-        ],
+        out_specs=[hbm] * 3,
+        out_shape=[tok(lev - 1, inner), tok(lev - 1, inner), tok(deep_cap)],
         scratch_shapes=[
             pltpu.VMEM((lev - 1, inner, width), BF16),
             pltpu.VMEM((lev - 1, inner, width), BF16),
@@ -563,50 +609,92 @@
     )(ocean_state, depth, conv_weight)
     deep_others = exchange(deep_packed)
 
+    whole_spec = lambda *sh: pl.BlockSpec(sh, lambda *_: (0,) * len(sh))
+    row_f32 = pltpu.HBM((cols, width), F32)
+
     def row_conv(which, first, cap, halo, forcing):
         n = lev - first
         extra = [] if forcing is None else [forcing]
         return pl.pallas_call(
             functools.partial(row_kernel, cap, first, which),
-            in_specs=[smem] + [vmem] * (4 + len(extra)),
-            out_specs=[hbm] * 3 + [vmem] * first,
+            in_specs=[smem, vmem, vmem, hbm, anywhere] + [vmem] * len(extra),
+            out_specs=[hbm] * 3 + [whole_spec(cols, width)] * first,
             out_shape=[tok(n, cols), tok(n, cols), tok(cap)] + [row_f32] * first,
             scratch_shapes=[
+                pltpu.VMEM(conv_weight.shape, BF16),
                 pltpu.VMEM((3, lev * cols, width), BF16),
                 pltpu.VMEM((n, cols, width), BF16),
                 pltpu.VMEM((n, cols, width), BF16),
                 pltpu.VMEM((cap + slack, width), BF16),
+                dma,
+                dma,
                 dma((2,)),
                 dma,
             ],
             compiler_params=params(20),
             cost_estimate=cost(conv_flops(lev, cols), lev * cols * width * 16),
             name="row",
-        )(side, ocean_state, depth, conv_weight, halo, *extra)
+        )(side, ocean_state, depth, stay(conv_weight), halo, *extra)
 
     near_mixed, near_normed, near_packed, near_base = row_conv(0, 1, near_cap, on_halo, None)
 
     ids = jnp.clip(src_blocks - (tile - R) * atm_blk, 0, 3 * atm_blk - 1)
     surf_mixed, surf_normed, far_forcing = pl.pallas_call(
         surface_kernel,
-        in_specs=[smem] * 3 + [vmem] * 7,
-        out_specs=[pl.BlockSpec((1, inner + cols, width), lambda *_: (0, 0, 0))] * 2 + [vmem],
+        in_specs=[smem] * 3 + [vmem] * 3 + [anywhere] * 2 + [hbm] * 2 + [vmem],
+        out_specs=[whole_spec(1, inner + cols, width)] * 2 + [whole_spec(cols, width)],
         out_shape=[tok(1, inner + cols), tok(1, inner + cols), row_f32],
-        scratch_shapes=[pltpu.VMEM((3 * own, width), BF16), pltpu.VMEM((rows, cols, width), F32)],
+        scratch_shapes=[
+            pltpu.VMEM((3 * own, width), BF16),
+            pltpu.VMEM(remap_weight.shape, BF16),
+            pltpu.VMEM((rows, cols, width), F32),
+            dma((4,)),
+        ],
         compiler_params=params(20),
         cost_estimate=cost(conv_flops(1, inner), cells * width * 16),
         name="surface",
-    )(ids, live, side, base, near_base, depth, on_halo, off_atm, atm_latent, remap_weight)
+    )(
+        ids,
+        live,
+        side,
+        ocean_state,
+        depth,
+        conv_weight,
+        on_halo,
+        off_halo,
+        stay(atm_latent),
+        stay(remap_weight),
+        near_base,
+    )
     surf_others = exchange(surf_normed)
     near_others = exchange(near_packed)
 
     far_mixed, far_normed, far_packed = row_conv(1, 0, far_cap, off_halo, far_forcing)
     far_others = exchange(far_packed)
 
+    def unread(shape):
+        return pl.pallas_call(
+            lambda out_ref: None,
+            out_specs=hbm,
+            out_shape=pltpu.HBM(shape, BF16),
+            name="unread",
+        )()
+
+    def send_all(*arrays):
+        sizes = [x.shape[0] * x.shape[1] for x in arrays]
+        joined = jnp.concatenate([x.reshape(-1, width) for x in arrays], axis=0)
+        got = [[] for _ in arrays]
+        for part in exchange(joined):
+            at = 0
+            for k, (x, size) in enumerate(zip(arrays, sizes)):
+                got[k].append(part[at : at + size].reshape(x.shape))
+                at += size
+        return tuple(got)
+
     deep_whole, near_whole, far_whole = lax.cond(
         flag[0] > 0,
-        lambda *a: tuple(exchange(x) for x in a),
-        lambda *a: tuple([x] * (members - 1) for x in a),
+        send_all,
+        lambda *a: tuple([unread(x.shape) for _ in range(members - 1)] for x in a),
         deep_normed,
         near_normed,
         far_normed,

time: 70.3 us -> 66.5 us (0.946)
  local copies, waits for them, and re-layouts: 10.5 us -> 6.97 us
  starting transfers between devices: 9.68 us -> 7.86 us
  Pallas kernels: 43.5 us -> 45 us
    ppermute x4, waiting for transfers between devices: 4.92 us -> 0.01 us  [exchange(): lax.ppermute(x, 'mem', [(i, (i + k) % members) for i in range(members)])]
    ppermute x3 -> x2, waiting for transfers between devices: 0.01 us -> 4.69 us  [swap(): return lax.ppermute(x, 'tile', pairs + [(b, a) for a, b in pairs])]
    cond x3 -> x0, local copies, waits for them, and re-layouts: 3.58 us -> none
    ppermute x3 -> x2, starting transfers between devices: 5.64 us -> 2.6 us  [swap(): return lax.ppermute(x, 'tile', pairs + [(b, a) for a, b in pairs])]
    pallas_call x2, Pallas kernels: 8.3 us -> 10.9 us  [row_conv(): pl.pallas_call(functools.partial(row_kernel, cap, first, which), in_specs...]
    pallas_call x1, Pallas kernels: 7.69 us -> 5.97 us  [body(): pl.pallas_call(functools.partial(inner_kernel, deep_cap), in_specs=[vmem,...]
    ppermute x4, starting transfers between devices: 4.05 us -> 5.26 us  [exchange(): lax.ppermute(x, 'mem', [(i, (i + k) % members) for i in range(members)])]
    pallas_call x1 -> x4, Pallas kernels: 2.42 us -> 3.61 us  [the longest x1 3.61 us: body(): pl.pallas_call(surface_kernel, in_specs=[smem] * 3 + [vmem] * 3 + [anywhe...]
  transfers between devices with their start and end apart: 7 -> 6, of which waited for: 1 -> 1; matrix products, arithmetic and copies ran while one was open for 5% -> 0% of each run, Pallas kernels for 49% -> 55%
where the time goes in v6:
time: 66.5 us; the launch traced here: 65.8 us
  Pallas kernels  45 us (68%)
  starting transfers between devices  7.86 us (12%)
  local copies, waits for them, and re-layouts  6.97 us (10%)
  waiting for transfers between devices  4.7 us (7%)
  between operations  1.03 us (2%)
    pallas_call x3, Pallas kernels, attend(): pl.pallas_call(functools.partial(attend_kernel, others, nparts, which, fi...  21 us
    pallas_call x2, Pallas kernels, row_conv(): pl.pallas_call(functools.partial(row_kernel, cap, first, which), in_specs...  10.9 us
    unnamed x42, local copies, waits for them, and re-layouts  6.97 us
    pallas_call x1, Pallas kernels, body(): pl.pallas_call(functools.partial(inner_kernel, deep_cap), in_specs=[vmem,...  5.97 us
    ppermute x4, starting transfers between devices, exchange(): lax.ppermute(x, 'mem', [(i, (i + k) % members) for i in range(members)])  5.26 us
    ppermute x2, waiting for transfers between devices, swap(): return lax.ppermute(x, 'tile', pairs + [(b, a) for a, b in pairs])  4.69 us
    pallas_call x1, Pallas kernels, body(): pl.pallas_call(surface_kernel, in_specs=[smem] * 3 + [vmem] * 3 + [anywhe...  3.61 us
    pallas_call x1, Pallas kernels, body(): pl.pallas_call(functools.partial(prep_kernel, (deep_cap, near_cap, far_ca...  3.45 us
  transfers between devices with their start and end apart: 6, of which 1 were waited for; matrix products, arithmetic and copies ran while one was open for 0% of the time, Pallas kernels for 55%

profile of v6, /device:TPU:18, one launch (start us, length us, event | category | flops | bytes accessed | tf_op | source)
XLA Modules:
  0.0 65.8 jit_solution(11892001488171775405)
XLA Ops:
  0.0 0.1 pad_add_fusion.side_ref
  0.1 1.1 %copy-done.3 = bf16[1,512,256]{2,1,0:T(8,128)(2,1)S(1)} copy-done((bf16[1,512,256]{2,1,0:T(8,128)(2,1)S(1)}, bf16[1,512,256]{2,1,0:T(8,128)(2,1)}, u32[]{:S(2)}) %copy-start.3) | copy-done | bytes 262168
  1.2 0.7 %copy-done.5 = s32[512]{0:T(512)S(1)} copy-done((s32[512]{0:T(512)S(1)}, s32[512]{0:T(512)}, u32[]{:S(2)}) %copy-start.5) | copy-done | bytes 2072
  1.8 3.5 %prep.1 = (bf16[1536,256]{1,0:T(8,128)(2,1)}, bf16[1536,256]{1,0:T(8,128)(2,1)}, s32[1]{0:T(128)}) custom-call(s32[2]{0:T(128)S(1)} %pad_add_fusion.side_ref, bf16[1,8,512,256]{3,2,1,0:T(8,128)(2,1)} %state.7, bf16[1,512,256]{2,1,0:T(8,128)(2,1)S(1)} %copy-done.3, s32[4,128]{1,0:T(4,128)S(1)} %bitcast.10), custom_call_target="tpu_custom_call" | custom-call | flops 1048576 | bytes 2621440 | tf_op jit(solution)/shard_map/prep/pallas_call | solution.py:576
  5.3 0.1 collective-permute-start.2
  5.4 2.5 %collective-permute-start.1 = (bf16[1536,256]{1,0:T(8,128)(2,1)}, bf16[1536,256]{1,0:T(8,128)(2,1)S(1)}, u32[]{:S(2)}, u32[]{:S(2)}) collective-permute-start(bf16[1536,256]{1,0:T(8,128)(2,1)} %get-tuple-element.34), channel_id=1, source_target_pairs={{2,4},{6,8},{10,12},{14,16},{18,20},{22,24},{26,28},{4,2},{8,6},{1... | collective-permute-start | bytes 2359304 | tf_op jit(solution)/shard_map/ppermute | solution.py:551
  7.9 0.0 copy-start.1
  8.0 1.3 %copy-done.1 = bf16[3,3,256,256]{3,2,1,0:T(8,128)(2,1)S(1)} copy-done((bf16[3,3,256,256]{3,2,1,0:T(8,128)(2,1)S(1)}, bf16[3,3,256,256]{3,2,1,0:T(8,128)(2,1)}, u32[]{:S(2)}) %copy-start.1) | copy-done | bytes 1179672
  9.2 6.0 %inner.1 = (bf16[7,256,256]{2,1,0:T(8,128)(2,1)}, bf16[7,256,256]{2,1,0:T(8,128)(2,1)}, bf16[1008,256]{1,0:T(8,128)(2,1)}) custom-call(bf16[1,8,512,256]{3,2,1,0:T(8,128)(2,1)S(1)} %copy-done, s32[4,128]{1,0:T(4,128)S(1)} %bitcast.11, bf16[3,3,256,256]{3,2,1,0:T(8,128)(2,1)S(1)} %copy-done.1), custom_call_target="tpu_custom_call" | custom-call | flops 2415919104 | bytes 4194304 | tf_op jit(solution)/shard_map/inner/pallas_call | solution.py:594
  15.2 1.6 %collective-permute-start.6 = (bf16[1008,256]{1,0:T(8,128)(2,1)}, bf16[1008,256]{1,0:T(8,128)(2,1)S(1)}, u32[]{:S(2)}, u32[]{:S(2)}) collective-permute-start(bf16[1008,256]{1,0:T(8,128)(2,1)} %get-tuple-element.50), channel_id=1, source_target_pairs={{0,1},{1,0},{2,3},{3,2},{4,5},{5,4},{6,7},{7,6},{8,9},{9,8},{10,11... | collective-permute-start | bytes 1548296 | tf_op jit(solution)/shard_map/ppermute | solution.py:555
  16.8 0.0 copy-start.7
  16.8 0.0 collective-permute-done.2.halo_hbm.on_hbm
  16.8 5.8 %row.2 = (bf16[7,128,256]{2,1,0:T(8,128)(2,1)}, bf16[7,128,256]{2,1,0:T(8,128)(2,1)}, bf16[544,256]{1,0:T(8,128)(2,1)}, f32[128,256]{1,0:T(8,128)}) custom-call(s32[2]{0:T(128)S(1)} %pad_add_fusion.side_ref, bf16[1,8,512,256]{3,2,1,0:T(8,128)(2,1)S(1)} %copy-done, s32[4,128]{1,0:T(4,128)S(1)} %bitcast.12, bf16[3,3,256,256]{3,2,1,0:T(8,128)(2,1)} %weight.3, ...), custom_call_target="tpu_custom_call" | custom-call | flops 1207959552 | bytes 4194304 | tf_op jit(solution)/shard_map/row/pallas_call | solution.py:618
  22.6 4.7 %collective-permute-done.1.off_hbm.halo_hbm = bf16[1536,256]{1,0:T(8,128)(2,1)S(1)} collective-permute-done((bf16[1536,256]{1,0:T(8,128)(2,1)}, bf16[1536,256]{1,0:T(8,128)(2,1)S(1)}, u32[]{:S(2)}, u32[]{:S(2)}) %collective-permute-start.1) | collective-permute-done | bytes 786464 | tf_op jit(solution)/shard_map/ppermute | solution.py:551
  27.3 0.9 %copy-done.4 = f32[128,256]{1,0:T(8,128)S(1)} copy-done((f32[128,256]{1,0:T(8,128)S(1)}, f32[128,256]{1,0:T(8,128)}, u32[]{:S(2)}) %copy-start.4) | copy-done | bytes 131096
  28.2 3.6 %surface.1 = (bf16[1,384,256]{2,1,0:T(8,128)(2,1)}, bf16[1,384,256]{2,1,0:T(8,128)(2,1)}, f32[128,256]{1,0:T(8,128)}) custom-call(s32[4,4]{1,0:T(4,128)S(1)} %subtract_clamp_fusion.ids_ref, s32[4]{0:T(128)S(1)} %copy-done.7, s32[2]{0:T(128)S(1)} %pad_add_fusion.side_ref, bf16[1,8,512,256]{3,2,1,0:T(8,128)(2,1)S(1)} %copy-done, s32[4,128]{1,0:T(4,128)S(1)} %bitcast.13, ...), custom_call_target="tpu_custom_call" | custom-call | flops 301989888 | bytes 2097152 | tf_op jit(solution)/shard_map/surface/pallas_call | solution.py:642
  31.9 1.6 %collective-permute-start.4 = (bf16[1,384,256]{2,1,0:T(8,128)(2,1)}, bf16[1,384,256]{2,1,0:T(8,128)(2,1)}, u32[]{:S(2)}, u32[]{:S(2)}) collective-permute-start(bf16[1,384,256]{2,1,0:T(8,128)(2,1)} %get-tuple-element.44.refs_0_), channel_id=1, source_target_pairs={{0,1},{1,0},{2,3},{3,2},{4,5},{5,4},{6,7},{7,6},{8,9},{9,8},{10,11... | collective-permute-start | bytes 589832 | tf_op jit(solution)/shard_map/ppermute | solution.py:555
  34.1 0.9 %copy-done.12 = f32[128,256]{1,0:T(8,128)S(1)} copy-done((f32[128,256]{1,0:T(8,128)S(1)}, f32[128,256]{1,0:T(8,128)}, u32[]{:S(2)}) %copy-start.12) | copy-done | bytes 131096
  35.0 5.1 %row.3 = (bf16[8,128,256]{2,1,0:T(8,128)(2,1)}, bf16[8,128,256]{2,1,0:T(8,128)(2,1)}, bf16[672,256]{1,0:T(8,128)(2,1)}) custom-call(s32[2]{0:T(128)S(1)} %pad_add_fusion.side_ref, bf16[1,8,512,256]{3,2,1,0:T(8,128)(2,1)S(1)} %copy-done, s32[4,128]{1,0:T(4,128)S(1)} %bitcast.14, bf16[3,3,256,256]{3,2,1,0:T(8,128)(2,1)} %weight.3, ...), custom_call_target="tpu_custom_call" | custom-call | flops 1207959552 | bytes 4194304 | tf_op jit(solution)/shard_map/row/pallas_call | solution.py:618
  40.1 0.6 collective-permute-start.3
  40.6 1.5 %collective-permute-start.5 = (bf16[544,256]{1,0:T(8,128)(2,1)}, bf16[544,256]{1,0:T(8,128)(2,1)S(1)}, u32[]{:S(2)}, u32[]{:S(2)}) collective-permute-start(bf16[544,256]{1,0:T(8,128)(2,1)} %get-tuple-element.47), channel_id=1, source_target_pairs={{0,1},{1,0},{2,3},{3,2},{4,5},{5,4},{6,7},{7,6},{8,9},{9,8},{10,11... | collective-permute-start | bytes 835592 | tf_op jit(solution)/shard_map/ppermute | solution.py:555
  42.2 0.2 conditional.1
  42.4 0.7 %copy-done.8 = bf16[256,768]{1,0:T(8,128)(2,1)S(1)} copy-done((bf16[256,768]{1,0:T(8,128)(2,1)S(1)}, bf16[256,768]{1,0:T(8,128)(2,1)}, u32[]{:S(2)}) %copy-start.8) | copy-done | bytes 393240
  43.1 0.0 copy-done.9
  43.2 0.1 copy-done.10
  43.3 0.0 copy-done.11
  43.3 1.2 %copy-done.15 = bf16[7,256,256]{2,1,0:T(8,128)(2,1)S(1)} copy-done((bf16[7,256,256]{2,1,0:T(8,128)(2,1)S(1)}, bf16[7,256,256]{2,1,0:T(8,128)(2,1)}, u32[]{:S(2)}) %copy-start.15) | copy-done | bytes 917528
  44.5 9.7 %attend.3.refs_10_ = bf16[1,8,512,256]{3,2,1,0:T(8,128)(2,1)} custom-call(s32[1]{0:T(128)} %get-tuple-element.33.flag_ref, s32[2]{0:T(128)S(1)} %pad_add_fusion.side_ref, bf16[1,384,256]{2,1,0:T(8,128)(2,1)S(1)} %copy-done.10, bf16[7,256,256]{2,1,0:T(8,128)(2,1)} %get-tuple-element.41.refs_1_, bf16[1,384,256]{2,1,0:T(8,128)(2,1)S(1)} %copy-done.9, ...), custom_call_target="tpu_custom_call" | custom-call | flops 4294967296 | bytes 5242880 | tf_op jit(solution)/shard_map/attend/pallas_call | solution.py:501
  54.2 0.0 collective-permute-done.5.refs_5_
  54.3 6.1 %attend.4.refs_7_ = bf16[1,8,512,256]{3,2,1,0:T(8,128)(2,1)} custom-call(s32[1]{0:T(128)} %get-tuple-element.33.flag_ref, s32[2]{0:T(128)S(1)} %pad_add_fusion.side_ref, bf16[1,384,256]{2,1,0:T(8,128)(2,1)S(1)} %copy-done.10, bf16[7,128,256]{2,1,0:T(8,128)(2,1)S(1)} %copy-done.19, ...), custom_call_target="tpu_custom_call", output_to_operand_aliasing={{}: (12, {})} | custom-call | flops 2147483648 | bytes 2621440 | tf_op jit(solution)/shard_map/attend/pallas_call | solution.py:501
  60.4 0.0 collective-permute-done.3.refs_2_
  60.5 5.2 %attend.5 = bf16[1,8,512,256]{3,2,1,0:T(8,128)(2,1)} custom-call(s32[1]{0:T(128)} %get-tuple-element.33.flag_ref, s32[2]{0:T(128)S(1)} %pad_add_fusion.side_ref, bf16[8,128,256]{2,1,0:T(8,128)(2,1)S(1)} %copy-done.17, bf16[8,128,256]{2,1,0:T(8,128)(2,1)S(1)} %copy-done.13, ...), custom_call_target="tpu_custom_call", output_to_operand_aliasing={{}: (9, {})} | custom-call | flops 2147483648 | bytes 2621440 | tf_op jit(solution)/shard_map/attend/pallas_call | solution.py:501
  (36 shorter events, 0.1 us)
Async XLA Ops:
  0.0 7.9 %copy-start = (bf16[1,8,512,256]{3,2,1,0:T(8,128)(2,1)S(1)}, bf16[1,8,512,256]{3,2,1,0:T(8,128)(2,1)}, u32[]{:S(2)}) copy-start(bf16[1,8,512,256]{3,2,1,0:T(8,128)(2,1)} %state.7) | copy-start | bytes 6291460
  0.1 1.1 %copy-start.3 = (bf16[1,512,256]{2,1,0:T(8,128)(2,1)S(1)}, bf16[1,512,256]{2,1,0:T(8,128)(2,1)}, u32[]{:S(2)}) copy-start(bf16[1,512,256]{2,1,0:T(8,128)(2,1)} %atm_hbm.1) | copy-start | bytes 786436
  1.2 0.7 %copy-start.5 = (s32[512]{0:T(512)S(1)}, s32[512]{0:T(512)}, u32[]{:S(2)}) copy-start(s32[512]{0:T(512)} %param.13) | copy-start | bytes 6148
  1.8 6.1 %copy-start.6 = (s32[512]{0:T(512)S(1)}, s32[512]{0:T(512)}, u32[]{:S(2)}) copy-start(s32[512]{0:T(512)} %param.13) | copy-start | bytes 6148
  5.3 11.5 %collective-permute-start.2 = (bf16[1536,256]{1,0:T(8,128)(2,1)}, bf16[1536,256]{1,0:T(8,128)(2,1)}, u32[]{:S(2)}, u32[]{:S(2)}) collective-permute-start(bf16[1536,256]{1,0:T(8,128)(2,1)} %get-tuple-element.35), channel_id=1, source_target_pairs={{0,2},{4,6},{8,10},{12,14},{16,18},{20,22},{24,26},{28,30},{2,0},{... | collective-permute-start | bytes 2359304 | tf_op jit(solution)/shard_map/ppermute | solution.py:551
  5.4 21.9 %collective-permute-start.1 = (bf16[1536,256]{1,0:T(8,128)(2,1)}, bf16[1536,256]{1,0:T(8,128)(2,1)S(1)}, u32[]{:S(2)}, u32[]{:S(2)}) collective-permute-start(bf16[1536,256]{1,0:T(8,128)(2,1)} %get-tuple-element.34), channel_id=1, source_target_pairs={{2,4},{6,8},{10,12},{14,16},{18,20},{22,24},{26,28},{4,2},{8,6},{1... | collective-permute-start | bytes 2359304 | tf_op jit(solution)/shard_map/ppermute | solution.py:551
  7.9 1.3 %copy-start.1 = (bf16[3,3,256,256]{3,2,1,0:T(8,128)(2,1)S(1)}, bf16[3,3,256,256]{3,2,1,0:T(8,128)(2,1)}, u32[]{:S(2)}) copy-start(bf16[3,3,256,256]{3,2,1,0:T(8,128)(2,1)} %weight.3) | copy-start | bytes 3538948
  9.2 7.6 %copy-start.20 = (s32[4,4]{1,0:T(4,128)S(1)}, s32[4,4]{1,0:T(4,128)}, u32[]{:S(2)}) copy-start(s32[4,4]{1,0:T(4,128)} %param.14) | copy-start | bytes 196
  15.2 27.2 %collective-permute-start.6 = (bf16[1008,256]{1,0:T(8,128)(2,1)}, bf16[1008,256]{1,0:T(8,128)(2,1)S(1)}, u32[]{:S(2)}, u32[]{:S(2)}) collective-permute-start(bf16[1008,256]{1,0:T(8,128)(2,1)} %get-tuple-element.50), channel_id=1, source_target_pairs={{0,1},{1,0},{2,3},{3,2},{4,5},{5,4},{6,7},{7,6},{8,9},{9,8},{10,11... | collective-permute-start | bytes 1548296 | tf_op jit(solution)/shard_map/ppermute | solution.py:555
  16.8 10.5 %copy-start.2 = (bf16[3,3,256,256]{3,2,1,0:T(8,128)(2,1)S(1)}, bf16[3,3,256,256]{3,2,1,0:T(8,128)(2,1)}, u32[]{:S(2)}) copy-start(bf16[3,3,256,256]{3,2,1,0:T(8,128)(2,1)} %weight.3) | copy-start | bytes 3538948
  16.8 10.5 %copy-start.7 = (s32[4]{0:T(128)S(1)}, s32[4]{0:T(128)}, u32[]{:S(2)}) copy-start(s32[4]{0:T(128)} %live_ref.1) | copy-start | bytes 52
  27.3 0.9 %copy-start.4 = (f32[128,256]{1,0:T(8,128)S(1)}, f32[128,256]{1,0:T(8,128)}, u32[]{:S(2)}) copy-start(f32[128,256]{1,0:T(8,128)} %get-tuple-element.36.near_base) | copy-start | bytes 393220
  31.9 10.5 %collective-permute-start.4 = (bf16[1,384,256]{2,1,0:T(8,128)(2,1)}, bf16[1,384,256]{2,1,0:T(8,128)(2,1)}, u32[]{:S(2)}, u32[]{:S(2)}) collective-permute-start(bf16[1,384,256]{2,1,0:T(8,128)(2,1)} %get-tuple-element.44.refs_0_), channel_id=1, source_target_pairs={{0,1},{1,0},{2,3},{3,2},{4,5},{5,4},{6,7},{7,6},{8,9},{9,8},{10,11... | collective-permute-start | bytes 589832 | tf_op jit(solution)/shard_map/ppermute | solution.py:555
  34.1 0.9 %copy-start.12 = (f32[128,256]{1,0:T(8,128)S(1)}, f32[128,256]{1,0:T(8,128)}, u32[]{:S(2)}) copy-start(f32[128,256]{1,0:T(8,128)} %get-tuple-element.37.refs_0_) | copy-start | bytes 393220
  40.1 20.4 %collective-permute-start.3 = (bf16[672,256]{1,0:T(8,128)(2,1)}, bf16[672,256]{1,0:T(8,128)(2,1)S(1)}, u32[]{:S(2)}, u32[]{:S(2)}) collective-permute-start(bf16[672,256]{1,0:T(8,128)(2,1)} %get-tuple-element.40), channel_id=1, source_target_pairs={{0,1},{1,0},{2,3},{3,2},{4,5},{5,4},{6,7},{7,6},{8,9},{9,8},{10,11... | collective-permute-start | bytes 1032200 | tf_op jit(solution)/shard_map/ppermute | solution.py:555
  40.6 13.6 %collective-permute-start.5 = (bf16[544,256]{1,0:T(8,128)(2,1)}, bf16[544,256]{1,0:T(8,128)(2,1)S(1)}, u32[]{:S(2)}, u32[]{:S(2)}) collective-permute-start(bf16[544,256]{1,0:T(8,128)(2,1)} %get-tuple-element.47), channel_id=1, source_target_pairs={{0,1},{1,0},{2,3},{3,2},{4,5},{5,4},{6,7},{7,6},{8,9},{9,8},{10,11... | collective-permute-start | bytes 835592 | tf_op jit(solution)/shard_map/ppermute | solution.py:555
  42.1 1.0 %copy-start.8 = (bf16[256,768]{1,0:T(8,128)(2,1)S(1)}, bf16[256,768]{1,0:T(8,128)(2,1)}, u32[]{:S(2)}) copy-start(bf16[256,768]{1,0:T(8,128)(2,1)} %refs_5_.1) | copy-start | bytes 1179652
  42.2 1.0 %copy-start.9 = (bf16[1,384,256]{2,1,0:T(8,128)(2,1)S(1)}, bf16[1,384,256]{2,1,0:T(8,128)(2,1)}, u32[]{:S(2)}) copy-start(bf16[1,384,256]{2,1,0:T(8,128)(2,1)} %get-tuple-element.45.refs_2_) | copy-start | bytes 589828
  42.2 1.1 %copy-start.10 = (bf16[1,384,256]{2,1,0:T(8,128)(2,1)S(1)}, bf16[1,384,256]{2,1,0:T(8,128)(2,1)}, u32[]{:S(2)}) copy-start(bf16[1,384,256]{2,1,0:T(8,128)(2,1)} %get-tuple-element.44.refs_0_) | copy-start | bytes 589828
  42.2 1.2 %copy-start.11 = (bf16[256,256]{1,0:T(8,128)(2,1)S(1)}, bf16[256,256]{1,0:T(8,128)(2,1)}, u32[]{:S(2)}) copy-start(bf16[256,256]{1,0:T(8,128)(2,1)} %refs_6_.1) | copy-start | bytes 393220
  43.3 1.2 %copy-start.15 = (bf16[7,256,256]{2,1,0:T(8,128)(2,1)S(1)}, bf16[7,256,256]{2,1,0:T(8,128)(2,1)}, u32[]{:S(2)}) copy-start(bf16[7,256,256]{2,1,0:T(8,128)(2,1)} %get-tuple-element.49.refs_3_) | copy-start | bytes 2752516
  44.5 9.7 %copy-start.14 = (bf16[7,128,256]{2,1,0:T(8,128)(2,1)S(1)}, bf16[7,128,256]{2,1,0:T(8,128)(2,1)}, u32[]{:S(2)}) copy-start(bf16[7,128,256]{2,1,0:T(8,128)(2,1)} %get-tuple-element.46.refs_3_) | copy-start | bytes 1376260
  44.5 9.7 %copy-start.18 = (bf16[7,128,256]{2,1,0:T(8,128)(2,1)S(1)}, bf16[7,128,256]{2,1,0:T(8,128)(2,1)}, u32[]{:S(2)}) copy-start(bf16[7,128,256]{2,1,0:T(8,128)(2,1)} %get-tuple-element.48.refs_6_) | copy-start | bytes 1376260
  44.5 9.7 %copy-start.19 = (bf16[7,128,256]{2,1,0:T(8,128)(2,1)S(1)}, bf16[7,128,256]{2,1,0:T(8,128)(2,1)}, u32[]{:S(2)}) copy-start(bf16[7,128,256]{2,1,0:T(8,128)(2,1)} %get-tuple-element.42.refs_1_) | copy-start | bytes 1376260
  54.2 6.2 %copy-start.13 = (bf16[8,128,256]{2,1,0:T(8,128)(2,1)S(1)}, bf16[8,128,256]{2,1,0:T(8,128)(2,1)}, u32[]{:S(2)}) copy-start(bf16[8,128,256]{2,1,0:T(8,128)(2,1)} %get-tuple-element.39.refs_1_) | copy-start | bytes 1572868
  54.2 6.2 %copy-start.16 = (bf16[8,128,256]{2,1,0:T(8,128)(2,1)S(1)}, bf16[8,128,256]{2,1,0:T(8,128)(2,1)}, u32[]{:S(2)}) copy-start(bf16[8,128,256]{2,1,0:T(8,128)(2,1)} %get-tuple-element.43.refs_3_) | copy-start | bytes 1572868
  54.3 6.2 %copy-start.17 = (bf16[8,128,256]{2,1,0:T(8,128)(2,1)S(1)}, bf16[8,128,256]{2,1,0:T(8,128)(2,1)}, u32[]{:S(2)}) copy-start(bf16[8,128,256]{2,1,0:T(8,128)(2,1)} %get-tuple-element.38.refs_0_) | copy-start | bytes 1572868

commit v7 on v6

--- a/solution.py
+++ b/solution.py
@@ -108,12 +108,28 @@
 
 
 def prep_kernel(
-    caps, side_ref, state_hbm, atm_ref, depth_ref, on_hbm, off_hbm, flag_ref, rows_in, in_sem, out_sem, atm_sem
+    caps,
+    side_ref,
+    state_hbm,
+    atm_hbm,
+    depth_hbm,
+    on_hbm,
+    off_hbm,
+    flag_ref,
+    depth_ref,
+    atm,
+    rows_in,
+    in_sem,
+    out_sem,
+    atm_sem,
+    own_sem,
 ):
     _, lev, cells, width = state_hbm.shape
     rows, cols = depth_ref.shape
-    own = atm_ref.shape[1]
+    own = atm_hbm.shape[1]
     sides = (on_hbm, off_hbm)
+    load_depth = pltpu.make_async_copy(depth_hbm, depth_ref, own_sem.at[0])
+    load_depth.start()
     loads, stores = [], []
     for k in (1, 0):
         at = pl.multiple_of(side_ref[k] * cols, cols)
@@ -123,12 +139,9 @@
             )
             load.start()
             loads.append((k, l, load))
-    for k, out in enumerate(sides):
-        store = pltpu.make_async_copy(
-            atm_ref.at[0], out.at[pl.ds(lev * cols, own)], atm_sem.at[k]
-        )
-        store.start()
-        stores.append(store)
+    load_atm = pltpu.make_async_copy(atm_hbm.at[0], atm, own_sem.at[1])
+    load_atm.start()
+    load_depth.wait()
     d = depth_ref[...].astype(F32)
     pick = lambda k: jnp.where(side_ref[k] == 0, d[0:1], d[rows - 1 :])
     deep = [column(pick(k)) for k in range(2)]
@@ -138,6 +151,13 @@
         rows_in[k, l] = rows_in[k, l] * wet
         store = pltpu.make_async_copy(
             rows_in.at[k, l], sides[k].at[pl.ds(l * cols, cols)], out_sem.at[k, l]
+        )
+        store.start()
+        stores.append(store)
+    load_atm.wait()
+    for k in (1, 0):
+        store = pltpu.make_async_copy(
+            atm, sides[k].at[pl.ds(lev * cols, own)], atm_sem.at[k]
         )
         store.start()
         stores.append(store)
@@ -158,18 +178,22 @@
     cap,
     state,
     depth_ref,
-    weight,
+    weight_hbm,
     mixed_hbm,
     normed_hbm,
     packed_hbm,
+    weight,
     mixed,
     normed,
     packed,
+    weight_sem,
     out_sem,
     packed_sem,
 ):
     _, lev, cells, width = state.shape
     rows, cols = depth_ref.shape
+    load = pltpu.make_async_copy(weight_hbm, weight, weight_sem)
+    load.start()
     packed[...] = jnp.zeros_like(packed)
     d = depth_ref[...].astype(F32)
     plans = [row_plan(d[r : r + 1], lev) for r in range(1, rows - 1)]
@@ -181,6 +205,8 @@
         wet = (deep > l).astype(F32)
         x = state[0, l] * widen(wet.astype(BF16), width)
         taps = [x[dr * cols : dr * cols + count] for dr in range(3)]
+        if l == 1:
+            load.wait()
         total = stencil(taps, weight, cols)
         new = taps[1].astype(F32) + widen(wet[cols : cols + count], width) * total
         new = new.astype(BF16)
@@ -214,15 +240,17 @@
     side_ref,
     state,
     depth_ref,
-    weight,
+    weight_hbm,
     on_hbm,
     off_hbm,
     atm_hbm,
     remap_hbm,
-    near_base,
+    base_hbm,
     mixed_ref,
     normed_ref,
     far_ref,
+    weight,
+    near_base,
     window,
     remap,
     forcing_ref,
@@ -233,6 +261,8 @@
     cells = state.shape[2]
     blocks, pairs = remap_hbm.shape[0], remap_hbm.shape[1]
     on_at = jnp.where(side_ref[0] == 0, 0, 2 * own)
+    load = pltpu.make_async_copy(weight_hbm, weight, sem.at[4])
+    load.start()
     copies = [
         pltpu.make_async_copy(
             on_hbm.at[pl.ds(on_hbm.shape[0] - own, own)],
@@ -246,6 +276,7 @@
         ),
         pltpu.make_async_copy(atm_hbm.at[0], window.at[pl.ds(own, own)], sem.at[2]),
         pltpu.make_async_copy(remap_hbm, remap, sem.at[3]),
+        pltpu.make_async_copy(base_hbm, near_base, sem.at[5]),
     ]
     for copy in copies:
         copy.start()
@@ -254,7 +285,6 @@
     x = state[0, 0] * widen(wet.astype(BF16), width)
     count = cells - 2 * cols
     taps = [x[dr * cols : dr * cols + count] for dr in range(3)]
-    total = stencil(taps, weight, cols)
     for copy in copies:
         copy.wait()
     for b in range(blocks):
@@ -266,6 +296,8 @@
                 remap[b, p], window[pl.ds(start, cols), :], preferred_element_type=F32
             )
         forcing_ref[b] = acc
+    load.wait()
+    total = stencil(taps, weight, cols)
     near = side_ref[0]
     parts = [
         (taps[1][r * cols : (r + 1) * cols].astype(F32), total[r * cols : (r + 1) * cols], r + 1)
@@ -287,11 +319,11 @@
 
 def row_kernel(cap, first, which, side_ref, state, depth_ref, weight_hbm, halo_hbm, *refs):
     refs = list(refs)
-    forcing_ref = None if first else refs.pop(0)
+    forcing_hbm = None if first else refs.pop(0)
     mixed_hbm, normed_hbm, packed_hbm = refs[:3]
     refs = refs[3:]
     base_ref = refs.pop(0) if first else None
-    weight, tap, mixed, normed, packed, weight_sem, halo_sem, out_sem, packed_sem = refs
+    forcing_ref, weight, tap, mixed, normed, packed, weight_sem, halo_sem, out_sem, packed_sem = refs
     load = pltpu.make_async_copy(weight_hbm, weight, weight_sem)
     load.start()
     _, lev, cells, width = state.shape
@@ -304,6 +336,9 @@
         halo_hbm.at[pl.ds(0, lev * cols)], tap.at[outer], halo_sem
     )
     halo.start()
+    if not first:
+        forcing = pltpu.make_async_copy(forcing_hbm, forcing_ref, packed_sem)
+        forcing.start()
     packed[...] = jnp.zeros_like(packed)
     d = depth_ref[...].astype(F32)
     own_depth = jnp.where(top, d[0:1], d[rows - 1 :])
@@ -327,6 +362,8 @@
     half = lev // 2
     load.wait()
     halo.wait()
+    if not first:
+        forcing.wait()
     for start in range(0, lev, half):
         rows_b = slice(start * cols, (start + half) * cols)
         taps = [tap[dr, rows_b] for dr in range(3)]
@@ -490,7 +527,9 @@
     in_specs += [full2(p) for p in packed]
     in_specs += [hbm] * others
     in_specs += [full2(depth), full2(qkv_weight), full2(out_weight)]
-    args = normed + mixed + surf + packed + whole + [depth, qkv_weight, out_weight]
+    stay = lambda x: pltpu.with_memory_space_constraint(x, pltpu.HBM)
+    args = [stay(x) for x in normed + mixed] + surf + packed + whole
+    args += [depth, qkv_weight, out_weight]
     alias = {}
     if out is not None:
         in_specs.append(hbm)
@@ -519,7 +558,7 @@
         ),
         out_shape=jax.ShapeDtypeStruct(shape, BF16),
         input_output_aliases=alias,
-        compiler_params=params(20 if members <= 2 else 48, 1),
+        compiler_params=params(16 if members <= 2 else 48, 1),
         cost_estimate=cost(tokens * width * width * 8 * (members + 2), tokens * width * 2 * 5),
         name="attend",
     )(flag, side, *args)
@@ -575,38 +614,43 @@
     message = lev * cols + own
     on_msg, off_msg, flag = pl.pallas_call(
         functools.partial(prep_kernel, (deep_cap, near_cap, far_cap)),
-        in_specs=[smem, hbm, vmem, vmem],
+        in_specs=[smem, hbm, hbm, hbm],
         out_specs=[hbm, hbm, smem],
         out_shape=[tok(message), tok(message), jax.ShapeDtypeStruct((1,), jnp.int32)],
         scratch_shapes=[
+            pltpu.VMEM((rows, cols), jnp.int32),
+            pltpu.VMEM((own, width), BF16),
             pltpu.VMEM((2, lev, cols, width), BF16),
             dma((2, lev)),
             dma((2, lev)),
+            dma((2,)),
             dma((2,)),
         ],
         compiler_params=params(16),
         cost_estimate=cost(lev * cols * width * 4, lev * cols * width * 10),
         name="prep",
-    )(side, stay(ocean_state), atm_latent, depth)
+    )(side, stay(ocean_state), stay(atm_latent), stay(depth))
     off_halo = swap(off_msg, 1)
     on_halo = swap(on_msg, 0)
 
     deep_mixed, deep_normed, deep_packed = pl.pallas_call(
         functools.partial(inner_kernel, deep_cap),
-        in_specs=[vmem, vmem, vmem],
+        in_specs=[vmem, vmem, hbm],
         out_specs=[hbm] * 3,
         out_shape=[tok(lev - 1, inner), tok(lev - 1, inner), tok(deep_cap)],
         scratch_shapes=[
+            pltpu.VMEM(conv_weight.shape, BF16),
             pltpu.VMEM((lev - 1, inner, width), BF16),
             pltpu.VMEM((lev - 1, inner, width), BF16),
             pltpu.VMEM((deep_cap + slack, width), BF16),
+            dma,
             dma((lev - 1, 2)),
             dma,
         ],
-        compiler_params=params(20),
+        compiler_params=params(12),
         cost_estimate=cost(conv_flops(lev, inner), lev * inner * width * 8),
         name="inner",
-    )(ocean_state, depth, conv_weight)
+    )(ocean_state, depth, stay(conv_weight))
     deep_others = exchange(deep_packed)
 
     whole_spec = lambda *sh: pl.BlockSpec(sh, lambda *_: (0,) * len(sh))
@@ -614,13 +658,14 @@
 
     def row_conv(which, first, cap, halo, forcing):
         n = lev - first
-        extra = [] if forcing is None else [forcing]
+        extra = [] if forcing is None else [stay(forcing)]
         return pl.pallas_call(
             functools.partial(row_kernel, cap, first, which),
-            in_specs=[smem, vmem, vmem, hbm, anywhere] + [vmem] * len(extra),
+            in_specs=[smem, vmem, vmem, hbm, anywhere] + [hbm] * len(extra),
             out_specs=[hbm] * 3 + [whole_spec(cols, width)] * first,
             out_shape=[tok(n, cols), tok(n, cols), tok(cap)] + [row_f32] * first,
             scratch_shapes=[
+                pltpu.VMEM((cols, width), F32),
                 pltpu.VMEM(conv_weight.shape, BF16),
                 pltpu.VMEM((3, lev * cols, width), BF16),
                 pltpu.VMEM((n, cols, width), BF16),
@@ -631,7 +676,7 @@
                 dma((2,)),
                 dma,
             ],
-            compiler_params=params(20),
+            compiler_params=params(12),
             cost_estimate=cost(conv_flops(lev, cols), lev * cols * width * 16),
             name="row",
         )(side, ocean_state, depth, stay(conv_weight), halo, *extra)
@@ -641,16 +686,18 @@
     ids = jnp.clip(src_blocks - (tile - R) * atm_blk, 0, 3 * atm_blk - 1)
     surf_mixed, surf_normed, far_forcing = pl.pallas_call(
         surface_kernel,
-        in_specs=[smem] * 3 + [vmem] * 3 + [anywhere] * 2 + [hbm] * 2 + [vmem],
+        in_specs=[smem] * 3 + [vmem] * 2 + [hbm] + [anywhere] * 2 + [hbm] * 3,
         out_specs=[whole_spec(1, inner + cols, width)] * 2 + [whole_spec(cols, width)],
         out_shape=[tok(1, inner + cols), tok(1, inner + cols), row_f32],
         scratch_shapes=[
+            pltpu.VMEM(conv_weight.shape, BF16),
+            pltpu.VMEM((cols, width), F32),
             pltpu.VMEM((3 * own, width), BF16),
             pltpu.VMEM(remap_weight.shape, BF16),
             pltpu.VMEM((rows, cols, width), F32),
-            dma((4,)),
+            dma((6,)),
         ],
-        compiler_params=params(20),
+        compiler_params=params(12),
         cost_estimate=cost(conv_flops(1, inner), cells * width * 16),
         name="surface",
     )(
@@ -659,12 +706,12 @@
         side,
         ocean_state,
         depth,
-        conv_weight,
+        stay(conv_weight),
         on_halo,
         off_halo,
         stay(atm_latent),
         stay(remap_weight),
-        near_base,
+        stay(near_base),
     )
     surf_others = exchange(surf_normed)
     near_others = exchange(near_packed)

time: 66.5 us -> 64 us (0.962)
  local copies, waits for them, and re-layouts: 6.97 us -> 1.02 us
  Pallas kernels: 45 us -> 48.6 us
    unnamed x42 -> x16, local copies, waits for them, and re-layouts: 6.97 us -> 1.02 us
    pallas_call x3, Pallas kernels: 21 us -> 22.8 us  [attend(): pl.pallas_call(functools.partial(attend_kernel, others, nparts, which, fi...]
    pallas_call x1, Pallas kernels: 5.97 us -> 7.13 us  [body(): pl.pallas_call(functools.partial(inner_kernel, deep_cap), in_specs=[vmem,...]
  transfers between devices with their start and end apart: 6 -> 6, of which waited for: 1 -> 1; matrix products, arithmetic and copies ran while one was open for 0% -> 0% of each run, Pallas kernels for 55% -> 61%
where the time goes in v7:
time: 64 us; the launch traced here: 63.4 us
  Pallas kernels  48.6 us (76%)
  starting transfers between devices  7.98 us (12%)
  waiting for transfers between devices  4.7 us (7%)
  local copies, waits for them, and re-layouts  1.02 us (2%)
  between operations  1.02 us (2%)
    pallas_call x3, Pallas kernels, attend(): pl.pallas_call(functools.partial(attend_kernel, others, nparts, which, fi...  22.8 us
    pallas_call x2, Pallas kernels, row_conv(): pl.pallas_call(functools.partial(row_kernel, cap, first, which), in_specs...  10.9 us
    pallas_call x1, Pallas kernels, body(): pl.pallas_call(functools.partial(inner_kernel, deep_cap), in_specs=[vmem,...  7.13 us
    ppermute x4, starting transfers between devices, exchange(): lax.ppermute(x, 'mem', [(i, (i + k) % members) for i in range(members)])  5.26 us
    ppermute x2, waiting for transfers between devices, swap(): return lax.ppermute(x, 'tile', pairs + [(b, a) for a, b in pairs])  4.69 us
    pallas_call x1, Pallas kernels, body(): pl.pallas_call(surface_kernel, in_specs=[smem] * 3 + [vmem] * 2 + [hbm] +...  4.02 us
    pallas_call x1, Pallas kernels, body(): pl.pallas_call(functools.partial(prep_kernel, (deep_cap, near_cap, far_ca...  3.7 us
    ppermute x2, starting transfers between devices, swap(): return lax.ppermute(x, 'tile', pairs + [(b, a) for a, b in pairs])  2.72 us
  transfers between devices with their start and end apart: 6, of which 1 were waited for; matrix products, arithmetic and copies ran while one was open for 0% of the time, Pallas kernels for 61%

profile of v7, /device:TPU:18, one launch (start us, length us, event | category | flops | bytes accessed | tf_op | source)
XLA Modules:
  0.0 63.4 jit_solution(2678801864843675458)
XLA Ops:
  0.0 0.0 copy-start
  0.0 0.1 pad_add_fusion.side_ref
  0.1 3.7 %prep.1 = (bf16[1536,256]{1,0:T(8,128)(2,1)}, bf16[1536,256]{1,0:T(8,128)(2,1)}, s32[1]{0:T(128)}) custom-call(s32[2]{0:T(128)S(1)} %pad_add_fusion.side_ref, bf16[1,8,512,256]{3,2,1,0:T(8,128)(2,1)} %state.7, bf16[1,512,256]{2,1,0:T(8,128)(2,1)} %atm_hbm.3, s32[4,128]{1,0:T(4,128)} %bitcast.10), custom_call_target="tpu_custom_call" | custom-call | flops 1048576 | bytes 2621440 | tf_op jit(solution)/shard_map/prep/pallas_call | solution.py:615
  3.8 0.1 collective-permute-start.2
  3.9 0.0 copy-start.7
  3.9 2.7 %collective-permute-start.1 = (bf16[1536,256]{1,0:T(8,128)(2,1)}, bf16[1536,256]{1,0:T(8,128)(2,1)S(1)}, u32[]{:S(2)}, u32[]{:S(2)}) collective-permute-start(bf16[1536,256]{1,0:T(8,128)(2,1)} %get-tuple-element.34), channel_id=1, source_target_pairs={{2,4},{6,8},{10,12},{14,16},{18,20},{22,24},{26,28},{4,2},{8,6},{1... | collective-permute-start | bytes 2359304 | tf_op jit(solution)/shard_map/ppermute | solution.py:590
  6.5 0.0 copy-done
  6.5 0.0 copy-done.1
  6.6 7.1 %inner.1 = (bf16[7,256,256]{2,1,0:T(8,128)(2,1)}, bf16[7,256,256]{2,1,0:T(8,128)(2,1)}, bf16[1008,256]{1,0:T(8,128)(2,1)}) custom-call(bf16[1,8,512,256]{3,2,1,0:T(8,128)(2,1)S(1)} %copy-done, s32[4,128]{1,0:T(4,128)S(1)} %bitcast.11, bf16[3,3,256,256]{3,2,1,0:T(8,128)(2,1)} %weight_hbm.7), custom_call_target="tpu_custom_call" | custom-call | flops 2415919104 | bytes 4194304 | tf_op jit(solution)/shard_map/inner/pallas_call | solution.py:636
  13.7 1.6 %collective-permute-start.6 = (bf16[1008,256]{1,0:T(8,128)(2,1)}, bf16[1008,256]{1,0:T(8,128)(2,1)S(1)}, u32[]{:S(2)}, u32[]{:S(2)}) collective-permute-start(bf16[1008,256]{1,0:T(8,128)(2,1)} %get-tuple-element.50), channel_id=1, source_target_pairs={{0,1},{1,0},{2,3},{3,2},{4,5},{5,4},{6,7},{7,6},{8,9},{9,8},{10,11... | collective-permute-start | bytes 1548296 | tf_op jit(solution)/shard_map/ppermute | solution.py:594
  15.3 0.0 copy-done.7
  15.3 0.0 collective-permute-done.2.halo_hbm.on_hbm
  15.3 5.8 %row.2 = (bf16[7,128,256]{2,1,0:T(8,128)(2,1)}, bf16[7,128,256]{2,1,0:T(8,128)(2,1)}, bf16[544,256]{1,0:T(8,128)(2,1)}, f32[128,256]{1,0:T(8,128)}) custom-call(s32[2]{0:T(128)S(1)} %pad_add_fusion.side_ref, bf16[1,8,512,256]{3,2,1,0:T(8,128)(2,1)S(1)} %copy-done, s32[4,128]{1,0:T(4,128)S(1)} %bitcast.12, bf16[3,3,256,256]{3,2,1,0:T(8,128)(2,1)} %weight_hbm.7, ...), custom_call_target="tpu_custom_call" | custom-call | flops 1207959552 | bytes 4194304 | tf_op jit(solution)/shard_map/row/pallas_call | solution.py:662
  21.1 4.7 %collective-permute-done.1.off_hbm.halo_hbm = bf16[1536,256]{1,0:T(8,128)(2,1)S(1)} collective-permute-done((bf16[1536,256]{1,0:T(8,128)(2,1)}, bf16[1536,256]{1,0:T(8,128)(2,1)S(1)}, u32[]{:S(2)}, u32[]{:S(2)}) %collective-permute-start.1) | collective-permute-done | bytes 786464 | tf_op jit(solution)/shard_map/ppermute | solution.py:590
  25.8 0.0 copy-done.2
  25.8 4.0 %surface.1 = (bf16[1,384,256]{2,1,0:T(8,128)(2,1)}, bf16[1,384,256]{2,1,0:T(8,128)(2,1)}, f32[128,256]{1,0:T(8,128)}) custom-call(s32[4,4]{1,0:T(4,128)S(1)} %subtract_clamp_fusion.ids_ref, s32[4]{0:T(128)S(1)} %copy-done.2, s32[2]{0:T(128)S(1)} %pad_add_fusion.side_ref, bf16[1,8,512,256]{3,2,1,0:T(8,128)(2,1)S(1)} %copy-done, s32[4,128]{1,0:T(4,128)S(1)} %bitcast.13, ...), custom_call_target="tpu_custom_call" | custom-call | flops 301989888 | bytes 2097152 | tf_op jit(solution)/shard_map/surface/pallas_call | solution.py:687
  29.9 1.6 %collective-permute-start.4 = (bf16[1,384,256]{2,1,0:T(8,128)(2,1)}, bf16[1,384,256]{2,1,0:T(8,128)(2,1)}, u32[]{:S(2)}, u32[]{:S(2)}) collective-permute-start(bf16[1,384,256]{2,1,0:T(8,128)(2,1)} %get-tuple-element.44.refs_0_), channel_id=1, source_target_pairs={{0,1},{1,0},{2,3},{3,2},{4,5},{5,4},{6,7},{7,6},{8,9},{9,8},{10,11... | collective-permute-start | bytes 589832 | tf_op jit(solution)/shard_map/ppermute | solution.py:594
  32.1 5.1 %row.3 = (bf16[8,128,256]{2,1,0:T(8,128)(2,1)}, bf16[8,128,256]{2,1,0:T(8,128)(2,1)}, bf16[672,256]{1,0:T(8,128)(2,1)}) custom-call(s32[2]{0:T(128)S(1)} %pad_add_fusion.side_ref, bf16[1,8,512,256]{3,2,1,0:T(8,128)(2,1)S(1)} %copy-done, s32[4,128]{1,0:T(4,128)S(1)} %bitcast.14, bf16[3,3,256,256]{3,2,1,0:T(8,128)(2,1)} %weight_hbm.7, ...), custom_call_target="tpu_custom_call" | custom-call | flops 1207959552 | bytes 4194304 | tf_op jit(solution)/shard_map/row/pallas_call | solution.py:662
  37.2 0.6 collective-permute-start.3
  37.8 1.5 %collective-permute-start.5 = (bf16[544,256]{1,0:T(8,128)(2,1)}, bf16[544,256]{1,0:T(8,128)(2,1)S(1)}, u32[]{:S(2)}, u32[]{:S(2)}) collective-permute-start(bf16[544,256]{1,0:T(8,128)(2,1)} %get-tuple-element.47), channel_id=1, source_target_pairs={{0,1},{1,0},{2,3},{3,2},{4,5},{5,4},{6,7},{7,6},{8,9},{9,8},{10,11... | collective-permute-start | bytes 835592 | tf_op jit(solution)/shard_map/ppermute | solution.py:594
  39.3 0.0 collective-permute-done.6.refs_5_
  39.3 0.0 collective-permute-done.4.refs_4_
  39.3 1.0 %copy-done.3 = bf16[256,768]{1,0:T(8,128)(2,1)S(1)} copy-done((bf16[256,768]{1,0:T(8,128)(2,1)S(1)}, bf16[256,768]{1,0:T(8,128)(2,1)}, u32[]{:S(2)}) %copy-start.3) | copy-done | bytes 393240
  40.3 0.0 copy-done.4
  40.3 9.9 %attend.3.refs_10_ = bf16[1,8,512,256]{3,2,1,0:T(8,128)(2,1)} custom-call(s32[1]{0:T(128)} %get-tuple-element.33.flag_ref, s32[2]{0:T(128)S(1)} %pad_add_fusion.side_ref, bf16[1,384,256]{2,1,0:T(8,128)(2,1)} %get-tuple-element.44.refs_0_, bf16[7,256,256]{2,1,0:T(8,128)(2,1)} %get-tuple-element.41.refs_1_, bf16[1,384,256]{2,1,0:T(8,128)(2,1)} %get-tuple-element.45.refs_2_, ...), custom_call_target="tpu_custom_call" | custom-call | flops 4294967296 | bytes 5242880 | tf_op jit(solution)/shard_map/attend/pallas_call | solution.py:540
  50.2 0.0 collective-permute-done.5.refs_5_
  50.2 0.0 copy-done.6
  50.2 0.0 copy-start.5
  50.2 6.5 %attend.4.refs_7_ = bf16[1,8,512,256]{3,2,1,0:T(8,128)(2,1)} custom-call(s32[1]{0:T(128)} %get-tuple-element.33.flag_ref, s32[2]{0:T(128)S(1)} %pad_add_fusion.side_ref, bf16[1,384,256]{2,1,0:T(8,128)(2,1)} %get-tuple-element.44.refs_0_, bf16[7,128,256]{2,1,0:T(8,128)(2,1)} %get-tuple-element.42.refs_1_, ...), custom_call_target="tpu_custom_call", output_to_operand_aliasing={{}: (12, {})} | custom-call | flops 2147483648 | bytes 2621440 | tf_op jit(solution)/shard_map/attend/pallas_call | solution.py:540
  56.7 0.0 collective-permute-done.3.refs_2_
  56.7 0.0 copy-done.5
  56.7 6.5 %attend.5 = bf16[1,8,512,256]{3,2,1,0:T(8,128)(2,1)} custom-call(s32[1]{0:T(128)} %get-tuple-element.33.flag_ref, s32[2]{0:T(128)S(1)} %pad_add_fusion.side_ref, bf16[8,128,256]{2,1,0:T(8,128)(2,1)} %get-tuple-element.38.refs_0_, bf16[8,128,256]{2,1,0:T(8,128)(2,1)} %get-tuple-element.39.refs_1_, ...), custom_call_target="tpu_custom_call", output_to_operand_aliasing={{}: (9, {})} | custom-call | flops 2147483648 | bytes 2621440 | tf_op jit(solution)/shard_map/attend/pallas_call | solution.py:540
  (10 shorter events, 0.0 us)
Async XLA Ops:
  0.0 6.5 %copy-start = (bf16[1,8,512,256]{3,2,1,0:T(8,128)(2,1)S(1)}, bf16[1,8,512,256]{3,2,1,0:T(8,128)(2,1)}, u32[]{:S(2)}) copy-start(bf16[1,8,512,256]{3,2,1,0:T(8,128)(2,1)} %state.7) | copy-start | bytes 6291460
  0.0 6.5 %copy-start.1 = (s32[512]{0:T(512)S(1)}, s32[512]{0:T(512)}, u32[]{:S(2)}) copy-start(s32[512]{0:T(512)} %param.13) | copy-start | bytes 6148
  3.8 11.5 %collective-permute-start.2 = (bf16[1536,256]{1,0:T(8,128)(2,1)}, bf16[1536,256]{1,0:T(8,128)(2,1)}, u32[]{:S(2)}, u32[]{:S(2)}) collective-permute-start(bf16[1536,256]{1,0:T(8,128)(2,1)} %get-tuple-element.35), channel_id=1, source_target_pairs={{0,2},{4,6},{8,10},{12,14},{16,18},{20,22},{24,26},{28,30},{2,0},{... | collective-permute-start | bytes 2359304 | tf_op jit(solution)/shard_map/ppermute | solution.py:590
  3.9 11.4 %copy-start.7 = (s32[4,4]{1,0:T(4,128)S(1)}, s32[4,4]{1,0:T(4,128)}, u32[]{:S(2)}) copy-start(s32[4,4]{1,0:T(4,128)} %param.14) | copy-start | bytes 196
  3.9 21.9 %collective-permute-start.1 = (bf16[1536,256]{1,0:T(8,128)(2,1)}, bf16[1536,256]{1,0:T(8,128)(2,1)S(1)}, u32[]{:S(2)}, u32[]{:S(2)}) collective-permute-start(bf16[1536,256]{1,0:T(8,128)(2,1)} %get-tuple-element.34), channel_id=1, source_target_pairs={{2,4},{6,8},{10,12},{14,16},{18,20},{22,24},{26,28},{4,2},{8,6},{1... | collective-permute-start | bytes 2359304 | tf_op jit(solution)/shard_map/ppermute | solution.py:590
  13.7 25.6 %collective-permute-start.6 = (bf16[1008,256]{1,0:T(8,128)(2,1)}, bf16[1008,256]{1,0:T(8,128)(2,1)S(1)}, u32[]{:S(2)}, u32[]{:S(2)}) collective-permute-start(bf16[1008,256]{1,0:T(8,128)(2,1)} %get-tuple-element.50), channel_id=1, source_target_pairs={{0,1},{1,0},{2,3},{3,2},{4,5},{5,4},{6,7},{7,6},{8,9},{9,8},{10,11... | collective-permute-start | bytes 1548296 | tf_op jit(solution)/shard_map/ppermute | solution.py:594
  15.3 10.5 %copy-start.2 = (s32[4]{0:T(128)S(1)}, s32[4]{0:T(128)}, u32[]{:S(2)}) copy-start(s32[4]{0:T(128)} %live_ref.1) | copy-start | bytes 52
  29.9 9.5 %collective-permute-start.4 = (bf16[1,384,256]{2,1,0:T(8,128)(2,1)}, bf16[1,384,256]{2,1,0:T(8,128)(2,1)}, u32[]{:S(2)}, u32[]{:S(2)}) collective-permute-start(bf16[1,384,256]{2,1,0:T(8,128)(2,1)} %get-tuple-element.44.refs_0_), channel_id=1, source_target_pairs={{0,1},{1,0},{2,3},{3,2},{4,5},{5,4},{6,7},{7,6},{8,9},{9,8},{10,11... | collective-permute-start | bytes 589832 | tf_op jit(solution)/shard_map/ppermute | solution.py:594
  37.2 19.5 %collective-permute-start.3 = (bf16[672,256]{1,0:T(8,128)(2,1)}, bf16[672,256]{1,0:T(8,128)(2,1)S(1)}, u32[]{:S(2)}, u32[]{:S(2)}) collective-permute-start(bf16[672,256]{1,0:T(8,128)(2,1)} %get-tuple-element.40), channel_id=1, source_target_pairs={{0,1},{1,0},{2,3},{3,2},{4,5},{5,4},{6,7},{7,6},{8,9},{9,8},{10,11... | collective-permute-start | bytes 1032200 | tf_op jit(solution)/shard_map/ppermute | solution.py:594
  37.8 12.4 %collective-permute-start.5 = (bf16[544,256]{1,0:T(8,128)(2,1)}, bf16[544,256]{1,0:T(8,128)(2,1)S(1)}, u32[]{:S(2)}, u32[]{:S(2)}) collective-permute-start(bf16[544,256]{1,0:T(8,128)(2,1)} %get-tuple-element.47), channel_id=1, source_target_pairs={{0,1},{1,0},{2,3},{3,2},{4,5},{5,4},{6,7},{7,6},{8,9},{9,8},{10,11... | collective-permute-start | bytes 835592 | tf_op jit(solution)/shard_map/ppermute | solution.py:594
  39.3 1.0 %copy-start.3 = (bf16[256,768]{1,0:T(8,128)(2,1)S(1)}, bf16[256,768]{1,0:T(8,128)(2,1)}, u32[]{:S(2)}) copy-start(bf16[256,768]{1,0:T(8,128)(2,1)} %refs_5_.1) | copy-start | bytes 1179652
  39.3 1.0 %copy-start.4 = (bf16[256,256]{1,0:T(8,128)(2,1)S(1)}, bf16[256,256]{1,0:T(8,128)(2,1)}, u32[]{:S(2)}) copy-start(bf16[256,256]{1,0:T(8,128)(2,1)} %refs_6_.1) | copy-start | bytes 393220
  40.3 9.9 %copy-start.6 = (bf16[7,128,256]{2,1,0:T(8,128)(2,1)S(1)}, bf16[7,128,256]{2,1,0:T(8,128)(2,1)}, u32[]{:S(2)}) copy-start(bf16[7,128,256]{2,1,0:T(8,128)(2,1)} %get-tuple-element.48.refs_6_) | copy-start | bytes 1376260
  50.2 6.5 %copy-start.5 = (bf16[8,128,256]{2,1,0:T(8,128)(2,1)S(1)}, bf16[8,128,256]{2,1,0:T(8,128)(2,1)}, u32[]{:S(2)}) copy-start(bf16[8,128,256]{2,1,0:T(8,128)(2,1)} %get-tuple-element.43.refs_3_) | copy-start | bytes 1572868

commit v8 on v7

--- a/solution.py
+++ b/solution.py
@@ -238,19 +238,20 @@
     ids_ref,
     live_ref,
     side_ref,
-    state,
     depth_ref,
-    weight_hbm,
     on_hbm,
     off_hbm,
     atm_hbm,
     remap_hbm,
     base_hbm,
+    edge_mixed_in,
+    edge_normed_in,
     mixed_ref,
     normed_ref,
     far_ref,
-    weight,
-    near_base,
+    edge_mixed_hbm,
+    edge_normed_hbm,
+    base,
     window,
     remap,
     forcing_ref,
@@ -258,11 +259,8 @@
 ):
     rows, cols = depth_ref.shape
     _, own, width = atm_hbm.shape
-    cells = state.shape[2]
     blocks, pairs = remap_hbm.shape[0], remap_hbm.shape[1]
     on_at = jnp.where(side_ref[0] == 0, 0, 2 * own)
-    load = pltpu.make_async_copy(weight_hbm, weight, sem.at[4])
-    load.start()
     copies = [
         pltpu.make_async_copy(
             on_hbm.at[pl.ds(on_hbm.shape[0] - own, own)],
@@ -276,15 +274,15 @@
         ),
         pltpu.make_async_copy(atm_hbm.at[0], window.at[pl.ds(own, own)], sem.at[2]),
         pltpu.make_async_copy(remap_hbm, remap, sem.at[3]),
-        pltpu.make_async_copy(base_hbm, near_base, sem.at[5]),
+        pltpu.make_async_copy(base_hbm, base, sem.at[4]),
     ]
     for copy in copies:
         copy.start()
     d = depth_ref[...].astype(F32)
-    wet = (jnp.concatenate([column(d[r : r + 1]) for r in range(rows)], axis=0) > 0).astype(F32)
-    x = state[0, 0] * widen(wet.astype(BF16), width)
-    count = cells - 2 * cols
-    taps = [x[dr * cols : dr * cols + count] for dr in range(3)]
+    near, far = side_ref[0], side_ref[1]
+    rows_d = [d[r : r + 1] for r in range(1, rows - 1)]
+    rows_d.append(jnp.where(near == 0, d[0:1], d[rows - 1 :]))
+    wets = [widen((column(row) > 0).astype(F32), width) for row in rows_d]
     for copy in copies:
         copy.wait()
     for b in range(blocks):
@@ -296,30 +294,30 @@
                 remap[b, p], window[pl.ds(start, cols), :], preferred_element_type=F32
             )
         forcing_ref[b] = acc
-    load.wait()
-    total = stencil(taps, weight, cols)
-    near = side_ref[0]
-    parts = [
-        (taps[1][r * cols : (r + 1) * cols].astype(F32), total[r * cols : (r + 1) * cols], r + 1)
-        for r in range(rows - 2)
-    ]
-    for k, (base, conv, r) in enumerate(parts):
+    for k, wet in enumerate(wets):
         at = slice(k * cols, (k + 1) * cols)
-        wet_k = widen(wet[r * cols : (r + 1) * cols], width)
-        new = (base + wet_k * (conv + forcing_ref[r])).astype(BF16)
+        forcing = forcing_ref[near] if k == rows - 2 else forcing_ref[k + 1]
+        new = (base[at] + wet * forcing).astype(BF16)
         mixed_ref[0, at] = new
         normed_ref[0, at] = normalise(new)
-    at = slice((rows - 2) * cols, (rows - 1) * cols)
-    wet_near = jnp.where(near == 0, wet[0:cols], wet[cells - cols :])
-    new = (near_base[...] + widen(wet_near, width) * forcing_ref[near]).astype(BF16)
-    mixed_ref[0, at] = new
-    normed_ref[0, at] = normalise(new)
-    far_ref[...] = forcing_ref[side_ref[1]]
+    far_ref[...] = forcing_ref[far]
+    at = pl.ds((rows - 2) * cols, cols)
+    stores = [
+        pltpu.make_async_copy(mixed_ref.at[0, at], edge_mixed_hbm.at[0, pl.ds(0, cols)], sem.at[5]),
+        pltpu.make_async_copy(normed_ref.at[0, at], edge_normed_hbm.at[0, pl.ds(0, cols)], sem.at[6]),
+    ]
+    for store in stores:
+        store.start()
+    for store in stores:
+        store.wait()
 
 
 def row_kernel(cap, first, which, side_ref, state, depth_ref, weight_hbm, halo_hbm, *refs):
     refs = list(refs)
-    forcing_hbm = None if first else refs.pop(0)
+    forcing_hbm = None
+    if not first:
+        forcing_hbm = refs[0]
+        refs = refs[3:]
     mixed_hbm, normed_hbm, packed_hbm = refs[:3]
     refs = refs[3:]
     base_ref = refs.pop(0) if first else None
@@ -376,15 +374,22 @@
                 part = part + forcing_ref[...]
             new = taps[1][rows_k].astype(F32) + widen(wets[l], width) * part
             if l < first:
-                base_ref[...] = new
+                base_ref[cells - 2 * cols :] = new
                 continue
             new = new.astype(BF16)
             mixed[l - first] = new
             tokens = normalise(new)
             normed[l - first] = tokens
             pack(packed, plan[0][l : l + 1], plan[1][l : l + 1], place[l, 0], cap, tokens)
+    if first:
+        wet = (jnp.concatenate([column(d[r : r + 1]) for r in range(rows)], axis=0) > 0).astype(F32)
+        x = state[0, 0] * widen(wet.astype(BF16), width)
+        taps = [x[dr * cols : dr * cols + cells - 2 * cols] for dr in range(3)]
+        inside = widen(wet[cols : cells - cols], width)
+        base_ref[0 : cells - 2 * cols] = taps[1].astype(F32) + inside * stencil(taps, weight, cols)
+    block = (pl.ds(first, lev - first), pl.ds(which * cols, cols))
     for k, (buf, out) in enumerate(((mixed, mixed_hbm), (normed, normed_hbm))):
-        store = pltpu.make_async_copy(buf, out, out_sem.at[k])
+        store = pltpu.make_async_copy(buf, out.at[block], out_sem.at[k])
         store.start()
         stores.append(store)
     store = pltpu.make_async_copy(packed.at[pl.ds(0, cap)], packed_hbm, packed_sem)
@@ -394,16 +399,16 @@
         store.wait()
 
 
-def attend_kernel(others, nparts, which, first, cap, aliased, flag_ref, side_ref, *refs):
+def attend_kernel(others, nparts, edges, flag_ref, side_ref, *refs):
     refs = list(refs)
     take = lambda k: [refs.pop(0) for _ in range(k)]
     own_normed = take(nparts)
     own_mixed = take(nparts)
-    surf = take(others) if first else []
-    packed = take(others)
+    surf = take(others)
+    packed = [take(others) for _ in range(1 + edges)]
     whole = take(others)
     depth_ref, qkv_ref, wo_ref = take(3)
-    if aliased:
+    if edges:
         take(1)
     out_ref, q_ref, k_ref, v_ref, att_ref, buf_ref, token_ref, sem = refs
     lev, count, width = q_ref.shape
@@ -411,6 +416,7 @@
     head = width // HEADS
     pair = 2 * head
     step = pl.program_id(0)
+    cap = max(p[0].shape[0] for p in packed)
 
     def keys_values(x, m):
         rows = slice(m * lev, (m + 1) * lev)
@@ -418,44 +424,65 @@
         k_ref[rows] = kv[:, :width].reshape(lev, count, width)
         v_ref[rows] = kv[:, width:].reshape(lev, count, width)
 
-    two = which is None
     pick = lambda a, b: jnp.where(step == 0, a, b)
     d = depth_ref[...].astype(F32)
     last = d.shape[0] - 1
-    if two:
+    if edges:
+        rows_d = [jnp.where(side_ref[k] == 0, d[0:1], d[last:]) for k in range(2)]
+        plans = [row_plan(row, lev) for row in rows_d]
+        near, far = offsets(plans[:1], 1, lev), offsets(plans[1:], 0, lev)
+        place = [far[0, 0]] + [pick(near[l, 0], far[l, 0]) for l in range(1, lev)]
+    else:
         rows_d = [d[r : r + 1] for r in range(1, last)]
-    else:
-        rows_d = [jnp.where(side_ref[which] == 0, d[0:1], d[last:])]
-    plans = [row_plan(row, lev) for row in rows_d]
-    place = offsets(plans, first, lev)
-    wet_row, rank, _ = plans[0]
-    depth_row = rows_d[0]
-    if two:
-        wet_row, rank = pick(wet_row, plans[1][0]), pick(rank, plans[1][1])
-        depth_row = pick(*rows_d)
+        plans = [row_plan(row, lev) for row in rows_d]
+        both = offsets(plans, 1, lev)
+        place = [None] + [pick(both[l, 0], both[l, 1]) for l in range(1, lev)]
+    wet_row, rank = pick(plans[0][0], plans[1][0]), pick(plans[0][1], plans[1][1])
+    depth_row = pick(*rows_d)
+
+    def fill(packed_ref):
+        size = packed_ref.shape[0]
+        buf_ref[0:size] = packed_ref[...]
+        buf_ref[size : size + count + 16] = jnp.zeros((count + 16, width), BF16)
+
+    def restore(l):
+        token_ref[l] = unpack(buf_ref, wet_row[l : l + 1], rank[l : l + 1], place[l], cap)
 
     x = jnp.concatenate([p[...].reshape(-1, width) for p in own_normed], axis=0)
     q = jnp.dot(x, qkv_ref[:, 0:width], preferred_element_type=F32).astype(BF16)
     q_ref[...] = (q * (1.0 / math.sqrt(head))).astype(BF16).reshape(lev, count, width)
     keys_values(x, 0)
     for o in range(others):
-        if first:
-            token_ref[0] = surf[o][0]
 
         @pl.when(flag_ref[0] == 0)
         def _():
-            buf_ref[0:cap] = packed[o][...]
-            buf_ref[cap:] = jnp.zeros((buf_ref.shape[0] - cap, width), BF16)
-            for l in range(first, lev):
-                at = pick(place[l, 0], place[l, 1]) if two else place[l, 0]
-                token_ref[l] = unpack(
-                    buf_ref, wet_row[l : l + 1], rank[l : l + 1], at, cap
-                )
+            if edges:
+
+                @pl.when(step == 0)
+                def _():
+                    token_ref[0] = surf[o][0]
+                    fill(packed[0][o])
+
+                @pl.when(step == 1)
+                def _():
+                    fill(packed[1][o])
+                    restore(0)
+
+            else:
+                token_ref[0] = surf[o][0]
+                fill(packed[0][o])
+            for l in range(1, lev):
+                restore(l)
 
         @pl.when(flag_ref[0] != 0)
         def _():
+            if not edges:
+                token_ref[0] = surf[o][0]
+            first = lev - whole[o].shape[0]
             copy = pltpu.make_async_copy(
-                whole[o].at[:, pl.ds(pl.multiple_of(step * count, count), count)], token_ref.at[pl.ds(first, lev - first)], sem
+                whole[o].at[:, pl.ds(pl.multiple_of(step * count, count), count)],
+                token_ref.at[pl.ds(first, lev - first)],
+                sem,
             )
             copy.start()
             copy.wait()
@@ -507,41 +534,40 @@
 
 
 def attend(
-    flag, side, normed, mixed, surf, packed, whole, depth, qkv_weight, out_weight, which, out, shape
+    flag, side, normed, mixed, surf, packed, whole, depth, qkv_weight, out_weight, out, shape
 ):
-    others, nparts = len(packed), len(mixed)
+    edges = out is not None
+    others, nparts = len(whole), len(mixed)
     lev = sum(p.shape[0] for p in mixed)
     width = shape[-1]
     rows, cols = depth.shape
-    cap = packed[0].shape[0]
-    first = 1 if surf else 0
-    steps = rows - 2 if which is None else 1
-    row_of = lambda i, s: i + 1 if which is None else s[which]
-    surf_at = 0 if which is None else rows - 2
+    cap = max(p.shape[0] for p in packed)
+    row_of = lambda i, s: s[i] if edges else i + 1
     full2 = lambda a: pl.BlockSpec(a.shape, lambda i, *_: (0, 0))
-    block = lambda n, at: pl.BlockSpec((n, cols, width), lambda i, *_: (0, i + at, 0))
-    part = [block(p.shape[0], surf_at if first and k == 0 else 0) for k, p in enumerate(mixed)]
+    block = lambda n: pl.BlockSpec((n, cols, width), lambda i, *_: (0, i, 0))
+    near = pl.BlockSpec((1, cols, width), lambda i, *_: (0, rows - 2, 0))
+    part = [block(p.shape[0]) for p in mixed]
     hbm = pl.BlockSpec(memory_space=pl.ANY)
     in_specs = part * 2
-    in_specs += [block(1, surf_at)] * len(surf)
+    in_specs += [near if edges else block(1)] * others
     in_specs += [full2(p) for p in packed]
     in_specs += [hbm] * others
     in_specs += [full2(depth), full2(qkv_weight), full2(out_weight)]
     stay = lambda x: pltpu.with_memory_space_constraint(x, pltpu.HBM)
-    args = [stay(x) for x in normed + mixed] + surf + packed + whole
-    args += [depth, qkv_weight, out_weight]
+    args = [x if edges else stay(x) for x in normed + mixed]
+    args += surf + packed + whole + [depth, qkv_weight, out_weight]
     alias = {}
-    if out is not None:
+    if edges:
         in_specs.append(hbm)
         alias = {len(args) + 2: 0}
         args.append(out)
-    tokens = lev * cols * steps
+    tokens = lev * cols * 2
     members = others + 1
     return pl.pallas_call(
-        functools.partial(attend_kernel, others, nparts, which, first, cap, out is not None),
+        functools.partial(attend_kernel, others, nparts, edges),
         grid_spec=pltpu.PrefetchScalarGridSpec(
             num_scalar_prefetch=2,
-            grid=(steps,),
+            grid=(2,),
             in_specs=in_specs,
             out_specs=pl.BlockSpec(
                 (1, lev, cols, width), lambda i, f, s: (0, 0, row_of(i, s), 0)
@@ -656,14 +682,14 @@
     whole_spec = lambda *sh: pl.BlockSpec(sh, lambda *_: (0,) * len(sh))
     row_f32 = pltpu.HBM((cols, width), F32)
 
-    def row_conv(which, first, cap, halo, forcing):
+    def row_conv(which, first, cap, halo, extra):
         n = lev - first
-        extra = [] if forcing is None else [stay(forcing)]
+        base = pltpu.HBM((inner + cols, width), F32)
         return pl.pallas_call(
             functools.partial(row_kernel, cap, first, which),
             in_specs=[smem, vmem, vmem, hbm, anywhere] + [hbm] * len(extra),
-            out_specs=[hbm] * 3 + [whole_spec(cols, width)] * first,
-            out_shape=[tok(n, cols), tok(n, cols), tok(cap)] + [row_f32] * first,
+            out_specs=[hbm] * 3 + [whole_spec(inner + cols, width)] * first,
+            out_shape=[tok(lev, 2 * cols), tok(lev, 2 * cols), tok(cap)] + [base] * first,
             scratch_shapes=[
                 pltpu.VMEM((cols, width), F32),
                 pltpu.VMEM(conv_weight.shape, BF16),
@@ -676,27 +702,29 @@
                 dma((2,)),
                 dma,
             ],
+            input_output_aliases={6: 0, 7: 1} if extra else {},
             compiler_params=params(12),
             cost_estimate=cost(conv_flops(lev, cols), lev * cols * width * 16),
             name="row",
-        )(side, ocean_state, depth, stay(conv_weight), halo, *extra)
-
-    near_mixed, near_normed, near_packed, near_base = row_conv(0, 1, near_cap, on_halo, None)
+        )(side, ocean_state, depth, stay(conv_weight), halo, *[stay(x) for x in extra])
+
+    edge_mixed, edge_normed, near_packed, base = row_conv(0, 1, near_cap, on_halo, [])
 
     ids = jnp.clip(src_blocks - (tile - R) * atm_blk, 0, 3 * atm_blk - 1)
-    surf_mixed, surf_normed, far_forcing = pl.pallas_call(
+    surf_mixed, surf_normed, far_forcing, edge_mixed, edge_normed = pl.pallas_call(
         surface_kernel,
-        in_specs=[smem] * 3 + [vmem] * 2 + [hbm] + [anywhere] * 2 + [hbm] * 3,
-        out_specs=[whole_spec(1, inner + cols, width)] * 2 + [whole_spec(cols, width)],
-        out_shape=[tok(1, inner + cols), tok(1, inner + cols), row_f32],
+        in_specs=[smem] * 3 + [vmem] + [anywhere] * 2 + [hbm] * 5,
+        out_specs=[whole_spec(1, inner + cols, width)] * 2 + [whole_spec(cols, width)] + [hbm] * 2,
+        out_shape=[tok(1, inner + cols), tok(1, inner + cols), row_f32]
+        + [tok(lev, 2 * cols)] * 2,
         scratch_shapes=[
-            pltpu.VMEM(conv_weight.shape, BF16),
-            pltpu.VMEM((cols, width), F32),
+            pltpu.VMEM((inner + cols, width), F32),
             pltpu.VMEM((3 * own, width), BF16),
             pltpu.VMEM(remap_weight.shape, BF16),
             pltpu.VMEM((rows, cols, width), F32),
-            dma((6,)),
+            dma((7,)),
         ],
+        input_output_aliases={9: 3, 10: 4},
         compiler_params=params(12),
         cost_estimate=cost(conv_flops(1, inner), cells * width * 16),
         name="surface",
@@ -704,19 +732,21 @@
         ids,
         live,
         side,
-        ocean_state,
         depth,
-        stay(conv_weight),
         on_halo,
         off_halo,
         stay(atm_latent),
         stay(remap_weight),
-        stay(near_base),
+        stay(base),
+        stay(edge_mixed),
+        stay(edge_normed),
     )
     surf_others = exchange(surf_normed)
     near_others = exchange(near_packed)
 
-    far_mixed, far_normed, far_packed = row_conv(1, 0, far_cap, off_halo, far_forcing)
+    edge_mixed, edge_normed, far_packed = row_conv(
+        1, 0, far_cap, off_halo, [far_forcing, edge_mixed, edge_normed]
+    )
     far_others = exchange(far_packed)
 
     def unread(shape):
@@ -738,40 +768,39 @@
                 at += size
         return tuple(got)
 
-    deep_whole, near_whole, far_whole = lax.cond(
+    deep_whole, edge_whole = lax.cond(
         flag[0] > 0,
         send_all,
         lambda *a: tuple([unread(x.shape) for _ in range(members - 1)] for x in a),
         deep_normed,
-        near_normed,
-        far_normed,
+        edge_normed,
     )
     shape = ocean_state.shape
     weights = (depth, qkv_weight, out_weight)
-    out = None
-    for which, normed, mixed, surf, packed, whole in (
-        (
-            None,
-            [surf_normed, deep_normed],
-            [surf_mixed, deep_mixed],
-            surf_others,
-            deep_others,
-            deep_whole,
-        ),
-        (
-            0,
-            [surf_normed, near_normed],
-            [surf_mixed, near_mixed],
-            surf_others,
-            near_others,
-            near_whole,
-        ),
-        (1, [far_normed], [far_mixed], [], far_others, far_whole),
-    ):
-        out = attend(
-            flag, side, normed, mixed, surf, packed, whole, *weights, which, out, shape
-        )
-    return out
+    out = attend(
+        flag,
+        side,
+        [surf_normed, deep_normed],
+        [surf_mixed, deep_mixed],
+        surf_others,
+        deep_others,
+        deep_whole,
+        *weights,
+        None,
+        shape,
+    )
+    return attend(
+        flag,
+        side,
+        [edge_normed],
+        [edge_mixed],
+        surf_others,
+        near_others + far_others,
+        edge_whole,
+        *weights,
+        out,
+        shape,
+    )
 
 
 def solution(mesh):

time: 64 us -> 61 us (0.953)
  Pallas kernels: 48.6 us -> 46.1 us
    pallas_call x4 -> x3, Pallas kernels: 26.8 us -> 23.8 us  [the longest x2 19.9 us: attend(): pl.pallas_call(functools.partial(attend_kernel, others, nparts, edges), g...]
  transfers between devices with their start and end apart: 6 -> 6, of which waited for: 1 -> 1; matrix products, arithmetic and copies ran while one was open for 0% -> 0% of each run, Pallas kernels for 61% -> 54%
where the time goes in v8:
time: 61 us; the launch traced here: 60.4 us
  Pallas kernels  46.1 us (76%)
  starting transfers between devices  8.05 us (13%)
  waiting for transfers between devices  4.26 us (7%)
  local copies, waits for them, and re-layouts  1.03 us (2%)
  between operations  0.95 us (2%)
    pallas_call x2, Pallas kernels, attend(): pl.pallas_call(functools.partial(attend_kernel, others, nparts, edges), g...  19.9 us
    pallas_call x2, Pallas kernels, row_conv(): pl.pallas_call(functools.partial(row_kernel, cap, first, which), in_specs...  11.4 us
    pallas_call x1, Pallas kernels, body(): pl.pallas_call(functools.partial(inner_kernel, deep_cap), in_specs=[vmem,...  7.16 us
    ppermute x4, starting transfers between devices, exchange(): lax.ppermute(x, 'mem', [(i, (i + k) % members) for i in range(members)])  5.32 us
    ppermute x2, waiting for transfers between devices, swap(): return lax.ppermute(x, 'tile', pairs + [(b, a) for a, b in pairs])  4.25 us
    pallas_call x1, Pallas kernels, body(): pl.pallas_call(surface_kernel, in_specs=[smem] * 3 + [vmem] + [anywhere]...  3.94 us
    pallas_call x1, Pallas kernels, body(): pl.pallas_call(functools.partial(prep_kernel, (deep_cap, near_cap, far_ca...  3.7 us
    ppermute x2, starting transfers between devices, swap(): return lax.ppermute(x, 'tile', pairs + [(b, a) for a, b in pairs])  2.72 us
  transfers between devices with their start and end apart: 6, of which 1 were waited for; matrix products, arithmetic and copies ran while one was open for 0% of the time, Pallas kernels for 54%

profile of v8, /device:TPU:18, one launch (start us, length us, event | category | flops | bytes accessed | tf_op | source)
XLA Modules:
  0.0 60.4 jit_solution(6737948070187720925)
XLA Ops:
  0.0 0.0 copy-start
  0.0 0.0 copy-start.2
  0.0 0.1 pad_add_fusion.side_ref
  0.1 3.7 %prep.1 = (bf16[1536,256]{1,0:T(8,128)(2,1)}, bf16[1536,256]{1,0:T(8,128)(2,1)}, s32[1]{0:T(128)}) custom-call(s32[2]{0:T(128)S(1)} %pad_add_fusion.side_ref, bf16[1,8,512,256]{3,2,1,0:T(8,128)(2,1)} %state.5, bf16[1,512,256]{2,1,0:T(8,128)(2,1)} %atm_hbm.3, s32[4,128]{1,0:T(4,128)} %bitcast.8), custom_call_target="tpu_custom_call" | custom-call | flops 1048576 | bytes 2621440 | tf_op jit(solution)/shard_map/prep/pallas_call | solution.py:641
  3.8 0.1 collective-permute-start.2
  3.9 0.0 copy-start.8
  3.9 2.7 %collective-permute-start.1 = (bf16[1536,256]{1,0:T(8,128)(2,1)}, bf16[1536,256]{1,0:T(8,128)(2,1)S(1)}, u32[]{:S(2)}, u32[]{:S(2)}) collective-permute-start(bf16[1536,256]{1,0:T(8,128)(2,1)} %get-tuple-element.32), channel_id=1, source_target_pairs={{2,4},{6,8},{10,12},{14,16},{18,20},{22,24},{26,28},{4,2},{8,6},{1... | collective-permute-start | bytes 2359304 | tf_op jit(solution)/shard_map/ppermute | solution.py:616
  6.5 0.0 copy-done
  6.5 0.0 copy-done.2
  6.6 7.2 %inner.1 = (bf16[7,256,256]{2,1,0:T(8,128)(2,1)}, bf16[7,256,256]{2,1,0:T(8,128)(2,1)}, bf16[1008,256]{1,0:T(8,128)(2,1)}) custom-call(bf16[1,8,512,256]{3,2,1,0:T(8,128)(2,1)S(1)} %copy-done, s32[4,128]{1,0:T(4,128)S(1)} %bitcast.9, bf16[3,3,256,256]{3,2,1,0:T(8,128)(2,1)} %weight_hbm.5), custom_call_target="tpu_custom_call" | custom-call | flops 2415919104 | bytes 4194304 | tf_op jit(solution)/shard_map/inner/pallas_call | solution.py:662
  13.7 1.6 %collective-permute-start.6 = (bf16[1008,256]{1,0:T(8,128)(2,1)}, bf16[1008,256]{1,0:T(8,128)(2,1)S(1)}, u32[]{:S(2)}, u32[]{:S(2)}) collective-permute-start(bf16[1008,256]{1,0:T(8,128)(2,1)} %get-tuple-element.49), channel_id=1, source_target_pairs={{0,1},{1,0},{2,3},{3,2},{4,5},{5,4},{6,7},{7,6},{8,9},{9,8},{10,11... | collective-permute-start | bytes 1548296 | tf_op jit(solution)/shard_map/ppermute | solution.py:620
  15.3 0.0 copy-done.8
  15.3 0.0 collective-permute-done.2.halo_hbm.on_hbm
  15.3 6.2 %row.2 = (bf16[8,256,256]{2,1,0:T(8,128)(2,1)}, bf16[8,256,256]{2,1,0:T(8,128)(2,1)}, bf16[544,256]{1,0:T(8,128)(2,1)}, f32[384,256]{1,0:T(8,128)}) custom-call(s32[2]{0:T(128)S(1)} %pad_add_fusion.side_ref, bf16[1,8,512,256]{3,2,1,0:T(8,128)(2,1)S(1)} %copy-done, s32[4,128]{1,0:T(4,128)S(1)} %bitcast.10, bf16[3,3,256,256]{3,2,1,0:T(8,128)(2,1)} %weight_hbm.5, ...), custom_call_target="tpu_custom_call" | custom-call | flops 1207959552 | bytes 4194304 | tf_op jit(solution)/shard_map/row/pallas_call | solution.py:688
  21.6 4.2 %collective-permute-done.1.off_hbm.halo_hbm = bf16[1536,256]{1,0:T(8,128)(2,1)S(1)} collective-permute-done((bf16[1536,256]{1,0:T(8,128)(2,1)}, bf16[1536,256]{1,0:T(8,128)(2,1)S(1)}, u32[]{:S(2)}, u32[]{:S(2)}) %collective-permute-start.1) | collective-permute-done | bytes 786464 | tf_op jit(solution)/shard_map/ppermute | solution.py:616
  25.8 0.0 copy-done.3
  25.8 3.9 %surface.1 = (bf16[1,384,256]{2,1,0:T(8,128)(2,1)}, bf16[1,384,256]{2,1,0:T(8,128)(2,1)}, f32[128,256]{1,0:T(8,128)}, bf16[8,256,256]{2,1,0:T(8,128)(2,1)}, bf16[8,256,256]{2,1,0:T(8,128)(2,1)}) custom-call(s32[4,4]{1,0:T(4,128)S(1)} %subtract_clamp_fusion.ids_ref, s32[4]{0:T(128)S(1)} %copy-done.3, ...), custom_call_target="tpu_custom_call", output_to_operand_aliasing={{3}: (9, {}), {4}: (10, {})} | custom-call | flops 301989888 | bytes 2097152 | tf_op jit(solution)/shard_map/surface/pallas_call | solution.py:714
  29.8 1.6 %collective-permute-start.3 = (bf16[1,384,256]{2,1,0:T(8,128)(2,1)}, bf16[1,384,256]{2,1,0:T(8,128)(2,1)}, u32[]{:S(2)}, u32[]{:S(2)}) collective-permute-start(bf16[1,384,256]{2,1,0:T(8,128)(2,1)} %get-tuple-element.42.refs_0_), channel_id=1, source_target_pairs={{0,1},{1,0},{2,3},{3,2},{4,5},{5,4},{6,7},{7,6},{8,9},{9,8},{10,11... | collective-permute-start | bytes 589832 | tf_op jit(solution)/shard_map/ppermute | solution.py:620
  32.0 0.6 collective-permute-start.4
  32.6 5.2 %row.3 = (bf16[8,256,256]{2,1,0:T(8,128)(2,1)}, bf16[8,256,256]{2,1,0:T(8,128)(2,1)}, bf16[672,256]{1,0:T(8,128)(2,1)}) custom-call(s32[2]{0:T(128)S(1)} %pad_add_fusion.side_ref, bf16[1,8,512,256]{3,2,1,0:T(8,128)(2,1)S(1)} %copy-done, s32[4,128]{1,0:T(4,128)S(1)} %bitcast.12, ...), custom_call_target="tpu_custom_call", output_to_operand_aliasing={{0}: (6, {}), {1}: (7, {})} | custom-call | flops 1207959552 | bytes 4194304 | tf_op jit(solution)/shard_map/row/pallas_call | solution.py:688
  37.8 1.6 %collective-permute-start.5 = (bf16[672,256]{1,0:T(8,128)(2,1)}, bf16[672,256]{1,0:T(8,128)(2,1)S(1)}, u32[]{:S(2)}, u32[]{:S(2)}) collective-permute-start(bf16[672,256]{1,0:T(8,128)(2,1)} %get-tuple-element.44), channel_id=1, source_target_pairs={{0,1},{1,0},{2,3},{3,2},{4,5},{5,4},{6,7},{7,6},{8,9},{9,8},{10,11... | collective-permute-start | bytes 1032200 | tf_op jit(solution)/shard_map/ppermute | solution.py:620
  39.4 0.0 collective-permute-done.6.refs_5_
  39.4 0.0 collective-permute-done.3.refs_4_.refs_2_
  39.4 1.0 %copy-done.4 = bf16[256,768]{1,0:T(8,128)(2,1)S(1)} copy-done((bf16[256,768]{1,0:T(8,128)(2,1)S(1)}, bf16[256,768]{1,0:T(8,128)(2,1)}, u32[]{:S(2)}) %copy-start.4) | copy-done | bytes 393240
  40.3 0.0 copy-done.5
  40.4 9.9 %attend.2.refs_9_ = bf16[1,8,512,256]{3,2,1,0:T(8,128)(2,1)} custom-call(s32[1]{0:T(128)} %get-tuple-element.31.flag_ref, s32[2]{0:T(128)S(1)} %pad_add_fusion.side_ref, bf16[1,384,256]{2,1,0:T(8,128)(2,1)} %get-tuple-element.42.refs_0_, bf16[7,256,256]{2,1,0:T(8,128)(2,1)} %get-tuple-element.45.refs_1_, bf16[1,384,256]{2,1,0:T(8,128)(2,1)} %get-tuple-element.47.refs_2_, ...), custom_call_target="tpu_custom_call" | custom-call | flops 4294967296 | bytes 5242880 | tf_op jit(solution)/shard_map/attend/pallas_call | solution.py:566
  50.3 0.0 collective-permute-done.4.refs_3_
  50.3 0.0 collective-permute-done.5.refs_4_
  50.3 0.0 copy-done.1
  50.3 0.0 copy-done.6
  50.4 0.0 copy-done.7
  50.4 9.9 %attend.3 = bf16[1,8,512,256]{3,2,1,0:T(8,128)(2,1)} custom-call(s32[1]{0:T(128)} %get-tuple-element.31.flag_ref, s32[2]{0:T(128)S(1)} %pad_add_fusion.side_ref, bf16[8,256,256]{2,1,0:T(8,128)(2,1)S(1)} %copy-done.6, bf16[8,256,256]{2,1,0:T(8,128)(2,1)S(1)} %copy-done.1, ...), custom_call_target="tpu_custom_call", output_to_operand_aliasing={{}: (11, {})} | custom-call | flops 4294967296 | bytes 5242880 | tf_op jit(solution)/shard_map/attend/pallas_call | solution.py:566
  (10 shorter events, 0.0 us)
Async XLA Ops:
  0.0 6.5 %copy-start = (bf16[1,8,512,256]{3,2,1,0:T(8,128)(2,1)S(1)}, bf16[1,8,512,256]{3,2,1,0:T(8,128)(2,1)}, u32[]{:S(2)}) copy-start(bf16[1,8,512,256]{3,2,1,0:T(8,128)(2,1)} %state.5) | copy-start | bytes 6291460
  0.0 6.5 %copy-start.2 = (s32[512]{0:T(512)S(1)}, s32[512]{0:T(512)}, u32[]{:S(2)}) copy-start(s32[512]{0:T(512)} %param.13) | copy-start | bytes 6148
  3.8 11.5 %collective-permute-start.2 = (bf16[1536,256]{1,0:T(8,128)(2,1)}, bf16[1536,256]{1,0:T(8,128)(2,1)}, u32[]{:S(2)}, u32[]{:S(2)}) collective-permute-start(bf16[1536,256]{1,0:T(8,128)(2,1)} %get-tuple-element.33), channel_id=1, source_target_pairs={{0,2},{4,6},{8,10},{12,14},{16,18},{20,22},{24,26},{28,30},{2,0},{... | collective-permute-start | bytes 2359304 | tf_op jit(solution)/shard_map/ppermute | solution.py:616
  3.9 11.4 %copy-start.8 = (s32[4,4]{1,0:T(4,128)S(1)}, s32[4,4]{1,0:T(4,128)}, u32[]{:S(2)}) copy-start(s32[4,4]{1,0:T(4,128)} %param.14) | copy-start | bytes 196
  3.9 21.9 %collective-permute-start.1 = (bf16[1536,256]{1,0:T(8,128)(2,1)}, bf16[1536,256]{1,0:T(8,128)(2,1)S(1)}, u32[]{:S(2)}, u32[]{:S(2)}) collective-permute-start(bf16[1536,256]{1,0:T(8,128)(2,1)} %get-tuple-element.32), channel_id=1, source_target_pairs={{2,4},{6,8},{10,12},{14,16},{18,20},{22,24},{26,28},{4,2},{8,6},{1... | collective-permute-start | bytes 2359304 | tf_op jit(solution)/shard_map/ppermute | solution.py:616
  13.7 25.6 %collective-permute-start.6 = (bf16[1008,256]{1,0:T(8,128)(2,1)}, bf16[1008,256]{1,0:T(8,128)(2,1)S(1)}, u32[]{:S(2)}, u32[]{:S(2)}) collective-permute-start(bf16[1008,256]{1,0:T(8,128)(2,1)} %get-tuple-element.49), channel_id=1, source_target_pairs={{0,1},{1,0},{2,3},{3,2},{4,5},{5,4},{6,7},{7,6},{8,9},{9,8},{10,11... | collective-permute-start | bytes 1548296 | tf_op jit(solution)/shard_map/ppermute | solution.py:620
  15.3 10.5 %copy-start.3 = (s32[4]{0:T(128)S(1)}, s32[4]{0:T(128)}, u32[]{:S(2)}) copy-start(s32[4]{0:T(128)} %live_ref.1) | copy-start | bytes 52
  29.8 9.6 %collective-permute-start.3 = (bf16[1,384,256]{2,1,0:T(8,128)(2,1)}, bf16[1,384,256]{2,1,0:T(8,128)(2,1)}, u32[]{:S(2)}, u32[]{:S(2)}) collective-permute-start(bf16[1,384,256]{2,1,0:T(8,128)(2,1)} %get-tuple-element.42.refs_0_), channel_id=1, source_target_pairs={{0,1},{1,0},{2,3},{3,2},{4,5},{5,4},{6,7},{7,6},{8,9},{9,8},{10,11... | collective-permute-start | bytes 589832 | tf_op jit(solution)/shard_map/ppermute | solution.py:620
  32.0 18.3 %collective-permute-start.4 = (bf16[544,256]{1,0:T(8,128)(2,1)}, bf16[544,256]{1,0:T(8,128)(2,1)}, u32[]{:S(2)}, u32[]{:S(2)}) collective-permute-start(bf16[544,256]{1,0:T(8,128)(2,1)} %get-tuple-element.43), channel_id=1, source_target_pairs={{0,1},{1,0},{2,3},{3,2},{4,5},{5,4},{6,7},{7,6},{8,9},{9,8},{10,11... | collective-permute-start | bytes 835592 | tf_op jit(solution)/shard_map/ppermute | solution.py:620
  37.8 12.6 %collective-permute-start.5 = (bf16[672,256]{1,0:T(8,128)(2,1)}, bf16[672,256]{1,0:T(8,128)(2,1)S(1)}, u32[]{:S(2)}, u32[]{:S(2)}) collective-permute-start(bf16[672,256]{1,0:T(8,128)(2,1)} %get-tuple-element.44), channel_id=1, source_target_pairs={{0,1},{1,0},{2,3},{3,2},{4,5},{5,4},{6,7},{7,6},{8,9},{9,8},{10,11... | collective-permute-start | bytes 1032200 | tf_op jit(solution)/shard_map/ppermute | solution.py:620
  39.3 1.0 %copy-start.4 = (bf16[256,768]{1,0:T(8,128)(2,1)S(1)}, bf16[256,768]{1,0:T(8,128)(2,1)}, u32[]{:S(2)}) copy-start(bf16[256,768]{1,0:T(8,128)(2,1)} %refs_7_.1) | copy-start | bytes 1179652
  39.3 1.0 %copy-start.5 = (bf16[256,256]{1,0:T(8,128)(2,1)S(1)}, bf16[256,256]{1,0:T(8,128)(2,1)}, u32[]{:S(2)}) copy-start(bf16[256,256]{1,0:T(8,128)(2,1)} %refs_8_.3) | copy-start | bytes 393220
  40.4 10.0 %copy-start.1 = (bf16[8,256,256]{2,1,0:T(8,128)(2,1)S(1)}, bf16[8,256,256]{2,1,0:T(8,128)(2,1)}, u32[]{:S(2)}) copy-start(bf16[8,256,256]{2,1,0:T(8,128)(2,1)} %get-tuple-element.41.refs_1_) | copy-start | bytes 3145732
  40.4 10.0 %copy-start.6 = (bf16[8,256,256]{2,1,0:T(8,128)(2,1)S(1)}, bf16[8,256,256]{2,1,0:T(8,128)(2,1)}, u32[]{:S(2)}) copy-start(bf16[8,256,256]{2,1,0:T(8,128)(2,1)} %get-tuple-element.40.refs_0_) | copy-start | bytes 3145732
  40.4 10.0 %copy-start.7 = (bf16[8,256,256]{2,1,0:T(8,128)(2,1)S(1)}, bf16[8,256,256]{2,1,0:T(8,128)(2,1)}, u32[]{:S(2)}) copy-start(bf16[8,256,256]{2,1,0:T(8,128)(2,1)} %get-tuple-element.46.refs_5_) | copy-start | bytes 3145732

commit v9 on v8

--- a/solution.py
+++ b/solution.py
@@ -55,9 +55,9 @@
     return place
 
 
-def segment(wet, rank, offset, cap):
+def segment(wet, rank, offset, limit):
     cols = wet.shape[1]
-    base = jnp.minimum((offset // 16) * 16, cap)
+    base = jnp.minimum((offset // 16) * 16, limit)
     target = jnp.where(wet > 0, rank + (offset - base).astype(F32), -1.0)
     slot = lax.broadcasted_iota(jnp.int32, (cols + 16, cols), 0).astype(F32)
     return pl.multiple_of(base, 16), (slot == target).astype(F32).astype(BF16)
@@ -71,11 +71,10 @@
     buf_ref[pl.ds(pl.multiple_of(base + 16, 16), rows.shape[0] - 16), :] = rows[16:]
 
 
-def unpack(buf_ref, wet, rank, offset, cap):
-    base, hot = segment(wet, rank, offset, cap)
-    rows = buf_ref[pl.ds(base, hot.shape[0]), :]
+def unpack(rows_of, wet, rank, offset, limit):
+    base, hot = segment(wet, rank, offset, limit)
     return lax.dot_general(
-        hot, rows, (((0,), (0,)), ((), ())), preferred_element_type=F32
+        hot, rows_of(base, hot.shape[0]), (((0,), (0,)), ((), ())), preferred_element_type=F32
     ).astype(BF16)
 
 
@@ -241,8 +240,8 @@
     depth_ref,
     on_hbm,
     off_hbm,
-    atm_hbm,
-    remap_hbm,
+    atm_ref,
+    remap,
     base_hbm,
     edge_mixed_in,
     edge_normed_in,
@@ -253,13 +252,12 @@
     edge_normed_hbm,
     base,
     window,
-    remap,
     forcing_ref,
     sem,
 ):
     rows, cols = depth_ref.shape
-    _, own, width = atm_hbm.shape
-    blocks, pairs = remap_hbm.shape[0], remap_hbm.shape[1]
+    _, own, width = atm_ref.shape
+    blocks, pairs = remap.shape[0], remap.shape[1]
     on_at = jnp.where(side_ref[0] == 0, 0, 2 * own)
     copies = [
         pltpu.make_async_copy(
@@ -272,12 +270,11 @@
             window.at[pl.ds(pl.multiple_of(2 * own - on_at, own), own)],
             sem.at[1],
         ),
-        pltpu.make_async_copy(atm_hbm.at[0], window.at[pl.ds(own, own)], sem.at[2]),
-        pltpu.make_async_copy(remap_hbm, remap, sem.at[3]),
         pltpu.make_async_copy(base_hbm, base, sem.at[4]),
     ]
     for copy in copies:
         copy.start()
+    window[own : 2 * own] = atm_ref[0]
     d = depth_ref[...].astype(F32)
     near, far = side_ref[0], side_ref[1]
     rows_d = [d[r : r + 1] for r in range(1, rows - 1)]
@@ -303,8 +300,8 @@
     far_ref[...] = forcing_ref[far]
     at = pl.ds((rows - 2) * cols, cols)
     stores = [
-        pltpu.make_async_copy(mixed_ref.at[0, at], edge_mixed_hbm.at[0, pl.ds(0, cols)], sem.at[5]),
-        pltpu.make_async_copy(normed_ref.at[0, at], edge_normed_hbm.at[0, pl.ds(0, cols)], sem.at[6]),
+        pltpu.make_async_copy(mixed_ref.at[0, at], edge_mixed_hbm.at[0, pl.ds(0, cols)], sem.at[2]),
+        pltpu.make_async_copy(normed_ref.at[0, at], edge_normed_hbm.at[0, pl.ds(0, cols)], sem.at[3]),
     ]
     for store in stores:
         store.start()
@@ -410,13 +407,12 @@
     depth_ref, qkv_ref, wo_ref = take(3)
     if edges:
         take(1)
-    out_ref, q_ref, k_ref, v_ref, att_ref, buf_ref, token_ref, sem = refs
+    out_ref, q_ref, k_ref, v_ref, att_ref, token_ref, sem = refs
     lev, count, width = q_ref.shape
     members = others + 1
     head = width // HEADS
     pair = 2 * head
     step = pl.program_id(0)
-    cap = max(p[0].shape[0] for p in packed)
 
     def keys_values(x, m):
         rows = slice(m * lev, (m + 1) * lev)
@@ -440,44 +436,30 @@
     wet_row, rank = pick(plans[0][0], plans[1][0]), pick(plans[0][1], plans[1][1])
     depth_row = pick(*rows_d)
 
-    def fill(packed_ref):
-        size = packed_ref.shape[0]
-        buf_ref[0:size] = packed_ref[...]
-        buf_ref[size : size + count + 16] = jnp.zeros((count + 16, width), BF16)
-
-    def restore(l):
-        token_ref[l] = unpack(buf_ref, wet_row[l : l + 1], rank[l : l + 1], place[l], cap)
+    window = count + 16
+    limits = [p[0].shape[0] - window for p in packed]
+    limit = pick(*limits) if edges else limits[0]
+
+    def restore(l, o):
+        def rows_of(base, size):
+            if not edges:
+                return packed[0][o][pl.ds(base, size), :]
+            near_at, far_at = (pl.multiple_of(jnp.minimum(base, at), 16) for at in limits)
+            return pick(packed[0][o][pl.ds(near_at, size), :], packed[1][o][pl.ds(far_at, size), :])
+
+        return unpack(rows_of, wet_row[l : l + 1], rank[l : l + 1], place[l], limit)
 
     x = jnp.concatenate([p[...].reshape(-1, width) for p in own_normed], axis=0)
     q = jnp.dot(x, qkv_ref[:, 0:width], preferred_element_type=F32).astype(BF16)
     q_ref[...] = (q * (1.0 / math.sqrt(head))).astype(BF16).reshape(lev, count, width)
     keys_values(x, 0)
     for o in range(others):
-
-        @pl.when(flag_ref[0] == 0)
-        def _():
-            if edges:
-
-                @pl.when(step == 0)
-                def _():
-                    token_ref[0] = surf[o][0]
-                    fill(packed[0][o])
-
-                @pl.when(step == 1)
-                def _():
-                    fill(packed[1][o])
-                    restore(0)
-
-            else:
-                token_ref[0] = surf[o][0]
-                fill(packed[0][o])
-            for l in range(1, lev):
-                restore(l)
+        token_ref[0] = pick(surf[o][0], restore(0, o)) if edges else surf[o][0]
+        for l in range(1, lev):
+            token_ref[l] = restore(l, o)
 
         @pl.when(flag_ref[0] != 0)
         def _():
-            if not edges:
-                token_ref[0] = surf[o][0]
             first = lev - whole[o].shape[0]
             copy = pltpu.make_async_copy(
                 whole[o].at[:, pl.ds(pl.multiple_of(step * count, count), count)],
@@ -541,7 +523,6 @@
     lev = sum(p.shape[0] for p in mixed)
     width = shape[-1]
     rows, cols = depth.shape
-    cap = max(p.shape[0] for p in packed)
     row_of = lambda i, s: s[i] if edges else i + 1
     full2 = lambda a: pl.BlockSpec(a.shape, lambda i, *_: (0, 0))
     block = lambda n: pl.BlockSpec((n, cols, width), lambda i, *_: (0, i, 0))
@@ -577,7 +558,6 @@
                 pltpu.VMEM((members * lev, cols, width), BF16),
                 pltpu.VMEM((members * lev, cols, width), BF16),
                 pltpu.VMEM((lev, cols, width), BF16),
-                pltpu.VMEM((cap + cols + 16, width), BF16),
                 pltpu.VMEM((lev, cols, width), BF16),
                 pltpu.SemaphoreType.DMA,
             ],
@@ -713,16 +693,15 @@
     ids = jnp.clip(src_blocks - (tile - R) * atm_blk, 0, 3 * atm_blk - 1)
     surf_mixed, surf_normed, far_forcing, edge_mixed, edge_normed = pl.pallas_call(
         surface_kernel,
-        in_specs=[smem] * 3 + [vmem] + [anywhere] * 2 + [hbm] * 5,
+        in_specs=[smem] * 3 + [vmem] + [anywhere] * 2 + [vmem] * 2 + [hbm] * 3,
         out_specs=[whole_spec(1, inner + cols, width)] * 2 + [whole_spec(cols, width)] + [hbm] * 2,
         out_shape=[tok(1, inner + cols), tok(1, inner + cols), row_f32]
         + [tok(lev, 2 * cols)] * 2,
         scratch_shapes=[
             pltpu.VMEM((inner + cols, width), F32),
             pltpu.VMEM((3 * own, width), BF16),
-            pltpu.VMEM(remap_weight.shape, BF16),
             pltpu.VMEM((rows, cols, width), F32),
-            dma((7,)),
+            dma((5,)),
         ],
         input_output_aliases={9: 3, 10: 4},
         compiler_params=params(12),
@@ -735,8 +714,8 @@
         depth,
         on_halo,
         off_halo,
-        stay(atm_latent),
-        stay(remap_weight),
+        atm_latent,
+        remap_weight,
         stay(base),
         stay(edge_mixed),
         stay(edge_normed),

time: 61 us -> 60.5 us (level)
  no operation moved by 1% of the time
where the time goes in v9:
time: 60.5 us; the launch traced here: 59.9 us
  Pallas kernels  45.6 us (75%)
  starting transfers between devices  8.05 us (13%)
  waiting for transfers between devices  4.21 us (7%)
  local copies, waits for them, and re-layouts  1.04 us (2%)
  between operations  0.92 us (2%)
    pallas_call x2, Pallas kernels, attend(): pl.pallas_call(functools.partial(attend_kernel, others, nparts, edges), g...  19.6 us
    pallas_call x2, Pallas kernels, row_conv(): pl.pallas_call(functools.partial(row_kernel, cap, first, which), in_specs...  11.4 us
    pallas_call x1, Pallas kernels, body(): pl.pallas_call(functools.partial(inner_kernel, deep_cap), in_specs=[vmem,...  7.17 us
    ppermute x4, starting transfers between devices, exchange(): lax.ppermute(x, 'mem', [(i, (i + k) % members) for i in range(members)])  5.32 us
    ppermute x2, waiting for transfers between devices, swap(): return lax.ppermute(x, 'tile', pairs + [(b, a) for a, b in pairs])  4.2 us
    pallas_call x1, Pallas kernels, body(): pl.pallas_call(surface_kernel, in_specs=[smem] * 3 + [vmem] + [anywhere]...  3.7 us
    pallas_call x1, Pallas kernels, body(): pl.pallas_call(functools.partial(prep_kernel, (deep_cap, near_cap, far_ca...  3.7 us
    ppermute x2, starting transfers between devices, swap(): return lax.ppermute(x, 'tile', pairs + [(b, a) for a, b in pairs])  2.72 us
  transfers between devices with their start and end apart: 6, of which 1 were waited for; matrix products, arithmetic and copies ran while one was open for 0% of the time, Pallas kernels for 54%

profile of v9, /device:TPU:18, one launch (start us, length us, event | category | flops | bytes accessed | tf_op | source)
XLA Modules:
  0.0 59.9 jit_solution(15120309647271948345)
XLA Ops:
  0.0 0.1 pad_add_fusion.side_ref
  0.1 3.7 %prep.1 = (bf16[1536,256]{1,0:T(8,128)(2,1)}, bf16[1536,256]{1,0:T(8,128)(2,1)}, s32[1]{0:T(128)}) custom-call(s32[2]{0:T(128)S(1)} %pad_add_fusion.side_ref, bf16[1,8,512,256]{3,2,1,0:T(8,128)(2,1)} %state.5, bf16[1,512,256]{2,1,0:T(8,128)(2,1)} %atm_ref.1, s32[4,128]{1,0:T(4,128)} %bitcast.8), custom_call_target="tpu_custom_call" | custom-call | flops 1048576 | bytes 2621440 | tf_op jit(solution)/shard_map/prep/pallas_call | solution.py:621
  3.8 0.1 collective-permute-start.2
  3.9 0.0 copy-start.10
  3.9 2.7 %collective-permute-start.1 = (bf16[1536,256]{1,0:T(8,128)(2,1)}, bf16[1536,256]{1,0:T(8,128)(2,1)S(1)}, u32[]{:S(2)}, u32[]{:S(2)}) collective-permute-start(bf16[1536,256]{1,0:T(8,128)(2,1)} %get-tuple-element.32), channel_id=1, source_target_pairs={{2,4},{6,8},{10,12},{14,16},{18,20},{22,24},{26,28},{4,2},{8,6},{1... | collective-permute-start | bytes 2359304 | tf_op jit(solution)/shard_map/ppermute | solution.py:596
  6.5 0.0 copy-done
  6.5 0.0 copy-done.4
  6.6 7.2 %inner.1 = (bf16[7,256,256]{2,1,0:T(8,128)(2,1)}, bf16[7,256,256]{2,1,0:T(8,128)(2,1)}, bf16[1008,256]{1,0:T(8,128)(2,1)}) custom-call(bf16[1,8,512,256]{3,2,1,0:T(8,128)(2,1)S(1)} %copy-done, s32[4,128]{1,0:T(4,128)S(1)} %bitcast.9, bf16[3,3,256,256]{3,2,1,0:T(8,128)(2,1)} %weight_hbm.5), custom_call_target="tpu_custom_call" | custom-call | flops 2415919104 | bytes 4194304 | tf_op jit(solution)/shard_map/inner/pallas_call | solution.py:642
  13.7 1.6 %collective-permute-start.6 = (bf16[1008,256]{1,0:T(8,128)(2,1)}, bf16[1008,256]{1,0:T(8,128)(2,1)S(1)}, u32[]{:S(2)}, u32[]{:S(2)}) collective-permute-start(bf16[1008,256]{1,0:T(8,128)(2,1)} %get-tuple-element.49), channel_id=1, source_target_pairs={{0,1},{1,0},{2,3},{3,2},{4,5},{5,4},{6,7},{7,6},{8,9},{9,8},{10,11... | collective-permute-start | bytes 1548296 | tf_op jit(solution)/shard_map/ppermute | solution.py:600
  15.3 0.0 copy-done.10
  15.3 0.0 copy-start.3
  15.3 0.0 copy-start.5
  15.4 0.0 collective-permute-done.2.halo_hbm.on_hbm
  15.4 6.3 %row.2 = (bf16[8,256,256]{2,1,0:T(8,128)(2,1)}, bf16[8,256,256]{2,1,0:T(8,128)(2,1)}, bf16[544,256]{1,0:T(8,128)(2,1)}, f32[384,256]{1,0:T(8,128)}) custom-call(s32[2]{0:T(128)S(1)} %pad_add_fusion.side_ref, bf16[1,8,512,256]{3,2,1,0:T(8,128)(2,1)S(1)} %copy-done, s32[4,128]{1,0:T(4,128)S(1)} %bitcast.10, bf16[3,3,256,256]{3,2,1,0:T(8,128)(2,1)} %weight_hbm.5, ...), custom_call_target="tpu_custom_call" | custom-call | flops 1207959552 | bytes 4194304 | tf_op jit(solution)/shard_map/row/pallas_call | solution.py:668
  21.6 4.2 %collective-permute-done.1.off_hbm.halo_hbm = bf16[1536,256]{1,0:T(8,128)(2,1)S(1)} collective-permute-done((bf16[1536,256]{1,0:T(8,128)(2,1)}, bf16[1536,256]{1,0:T(8,128)(2,1)S(1)}, u32[]{:S(2)}, u32[]{:S(2)}) %collective-permute-start.1) | collective-permute-done | bytes 786464 | tf_op jit(solution)/shard_map/ppermute | solution.py:596
  25.8 0.0 copy-done.5
  25.8 3.7 %surface.1 = (bf16[1,384,256]{2,1,0:T(8,128)(2,1)}, bf16[1,384,256]{2,1,0:T(8,128)(2,1)}, f32[128,256]{1,0:T(8,128)}, bf16[8,256,256]{2,1,0:T(8,128)(2,1)}, bf16[8,256,256]{2,1,0:T(8,128)(2,1)}) custom-call(s32[4,4]{1,0:T(4,128)S(1)} %subtract_clamp_fusion.ids_ref, s32[4]{0:T(128)S(1)} %copy-done.5, ...), custom_call_target="tpu_custom_call", output_to_operand_aliasing={{3}: (9, {}), {4}: (10, {})} | custom-call | flops 301989888 | bytes 2097152 | tf_op jit(solution)/shard_map/surface/pallas_call | solution.py:694
  29.5 1.6 %collective-permute-start.3 = (bf16[1,384,256]{2,1,0:T(8,128)(2,1)}, bf16[1,384,256]{2,1,0:T(8,128)(2,1)}, u32[]{:S(2)}, u32[]{:S(2)}) collective-permute-start(bf16[1,384,256]{2,1,0:T(8,128)(2,1)} %get-tuple-element.42.refs_0_), channel_id=1, source_target_pairs={{0,1},{1,0},{2,3},{3,2},{4,5},{5,4},{6,7},{7,6},{8,9},{9,8},{10,11... | collective-permute-start | bytes 589832 | tf_op jit(solution)/shard_map/ppermute | solution.py:600
  31.7 0.6 collective-permute-start.4
  32.3 5.2 %row.3 = (bf16[8,256,256]{2,1,0:T(8,128)(2,1)}, bf16[8,256,256]{2,1,0:T(8,128)(2,1)}, bf16[672,256]{1,0:T(8,128)(2,1)}) custom-call(s32[2]{0:T(128)S(1)} %pad_add_fusion.side_ref, bf16[1,8,512,256]{3,2,1,0:T(8,128)(2,1)S(1)} %copy-done, s32[4,128]{1,0:T(4,128)S(1)} %bitcast.12, ...), custom_call_target="tpu_custom_call", output_to_operand_aliasing={{0}: (6, {}), {1}: (7, {})} | custom-call | flops 1207959552 | bytes 4194304 | tf_op jit(solution)/shard_map/row/pallas_call | solution.py:668
  37.5 1.6 %collective-permute-start.5 = (bf16[672,256]{1,0:T(8,128)(2,1)}, bf16[672,256]{1,0:T(8,128)(2,1)S(1)}, u32[]{:S(2)}, u32[]{:S(2)}) collective-permute-start(bf16[672,256]{1,0:T(8,128)(2,1)} %get-tuple-element.44), channel_id=1, source_target_pairs={{0,1},{1,0},{2,3},{3,2},{4,5},{5,4},{6,7},{7,6},{8,9},{9,8},{10,11... | collective-permute-start | bytes 1032200 | tf_op jit(solution)/shard_map/ppermute | solution.py:600
  39.1 0.0 collective-permute-done.6.refs_5_
  39.1 0.0 collective-permute-done.3.refs_4_.refs_2_
  39.1 1.0 %copy-done.6 = bf16[256,768]{1,0:T(8,128)(2,1)S(1)} copy-done((bf16[256,768]{1,0:T(8,128)(2,1)S(1)}, bf16[256,768]{1,0:T(8,128)(2,1)}, u32[]{:S(2)}) %copy-start.6) | copy-done | bytes 393240
  40.0 0.0 copy-done.7
  40.1 10.2 %attend.2.refs_9_ = bf16[1,8,512,256]{3,2,1,0:T(8,128)(2,1)} custom-call(s32[1]{0:T(128)} %get-tuple-element.31.flag_ref, s32[2]{0:T(128)S(1)} %pad_add_fusion.side_ref, bf16[1,384,256]{2,1,0:T(8,128)(2,1)} %get-tuple-element.42.refs_0_, bf16[7,256,256]{2,1,0:T(8,128)(2,1)} %get-tuple-element.45.refs_1_, bf16[1,384,256]{2,1,0:T(8,128)(2,1)} %get-tuple-element.47.refs_2_, ...), custom_call_target="tpu_custom_call" | custom-call | flops 4294967296 | bytes 5242880 | tf_op jit(solution)/shard_map/attend/pallas_call | solution.py:547
  50.2 0.0 collective-permute-done.4.refs_3_
  50.3 0.0 collective-permute-done.5.refs_4_
  50.3 0.0 copy-done.1
  50.3 0.0 copy-done.8
  50.3 0.0 copy-done.9
  50.3 9.5 %attend.3 = bf16[1,8,512,256]{3,2,1,0:T(8,128)(2,1)} custom-call(s32[1]{0:T(128)} %get-tuple-element.31.flag_ref, s32[2]{0:T(128)S(1)} %pad_add_fusion.side_ref, bf16[8,256,256]{2,1,0:T(8,128)(2,1)S(1)} %copy-done.8, bf16[8,256,256]{2,1,0:T(8,128)(2,1)S(1)} %copy-done.1, ...), custom_call_target="tpu_custom_call", output_to_operand_aliasing={{}: (11, {})} | custom-call | flops 4294967296 | bytes 5242880 | tf_op jit(solution)/shard_map/attend/pallas_call | solution.py:547
  (14 shorter events, 0.0 us)
Async XLA Ops:
  0.0 6.5 %copy-start = (bf16[1,8,512,256]{3,2,1,0:T(8,128)(2,1)S(1)}, bf16[1,8,512,256]{3,2,1,0:T(8,128)(2,1)}, u32[]{:S(2)}) copy-start(bf16[1,8,512,256]{3,2,1,0:T(8,128)(2,1)} %state.5) | copy-start | bytes 6291460
  0.0 6.5 %copy-start.4 = (s32[512]{0:T(512)S(1)}, s32[512]{0:T(512)}, u32[]{:S(2)}) copy-start(s32[512]{0:T(512)} %param.13) | copy-start | bytes 6148
  3.8 11.6 %collective-permute-start.2 = (bf16[1536,256]{1,0:T(8,128)(2,1)}, bf16[1536,256]{1,0:T(8,128)(2,1)}, u32[]{:S(2)}, u32[]{:S(2)}) collective-permute-start(bf16[1536,256]{1,0:T(8,128)(2,1)} %get-tuple-element.33), channel_id=1, source_target_pairs={{0,2},{4,6},{8,10},{12,14},{16,18},{20,22},{24,26},{28,30},{2,0},{... | collective-permute-start | bytes 2359304 | tf_op jit(solution)/shard_map/ppermute | solution.py:596
  3.9 11.5 %copy-start.10 = (s32[4,4]{1,0:T(4,128)S(1)}, s32[4,4]{1,0:T(4,128)}, u32[]{:S(2)}) copy-start(s32[4,4]{1,0:T(4,128)} %param.14) | copy-start | bytes 196
  3.9 21.9 %collective-permute-start.1 = (bf16[1536,256]{1,0:T(8,128)(2,1)}, bf16[1536,256]{1,0:T(8,128)(2,1)S(1)}, u32[]{:S(2)}, u32[]{:S(2)}) collective-permute-start(bf16[1536,256]{1,0:T(8,128)(2,1)} %get-tuple-element.32), channel_id=1, source_target_pairs={{2,4},{6,8},{10,12},{14,16},{18,20},{22,24},{26,28},{4,2},{8,6},{1... | collective-permute-start | bytes 2359304 | tf_op jit(solution)/shard_map/ppermute | solution.py:596
  13.7 25.3 %collective-permute-start.6 = (bf16[1008,256]{1,0:T(8,128)(2,1)}, bf16[1008,256]{1,0:T(8,128)(2,1)S(1)}, u32[]{:S(2)}, u32[]{:S(2)}) collective-permute-start(bf16[1008,256]{1,0:T(8,128)(2,1)} %get-tuple-element.49), channel_id=1, source_target_pairs={{0,1},{1,0},{2,3},{3,2},{4,5},{5,4},{6,7},{7,6},{8,9},{9,8},{10,11... | collective-permute-start | bytes 1548296 | tf_op jit(solution)/shard_map/ppermute | solution.py:600
  15.3 10.5 %copy-start.2 = (bf16[1,512,256]{2,1,0:T(8,128)(2,1)S(1)}, bf16[1,512,256]{2,1,0:T(8,128)(2,1)}, u32[]{:S(2)}) copy-start(bf16[1,512,256]{2,1,0:T(8,128)(2,1)} %atm_ref.1) | copy-start | bytes 786436
  15.3 10.5 %copy-start.3 = (bf16[4,4,128,128]{3,2,1,0:T(8,128)(2,1)S(1)}, bf16[4,4,128,128]{3,2,1,0:T(8,128)(2,1)}, u32[]{:S(2)}) copy-start(bf16[4,4,128,128]{3,2,1,0:T(8,128)(2,1)} %remap.1) | copy-start | bytes 1572868
  15.3 10.5 %copy-start.5 = (s32[4]{0:T(128)S(1)}, s32[4]{0:T(128)}, u32[]{:S(2)}) copy-start(s32[4]{0:T(128)} %live_ref.1) | copy-start | bytes 52
  29.5 9.5 %collective-permute-start.3 = (bf16[1,384,256]{2,1,0:T(8,128)(2,1)}, bf16[1,384,256]{2,1,0:T(8,128)(2,1)}, u32[]{:S(2)}, u32[]{:S(2)}) collective-permute-start(bf16[1,384,256]{2,1,0:T(8,128)(2,1)} %get-tuple-element.42.refs_0_), channel_id=1, source_target_pairs={{0,1},{1,0},{2,3},{3,2},{4,5},{5,4},{6,7},{7,6},{8,9},{9,8},{10,11... | collective-permute-start | bytes 589832 | tf_op jit(solution)/shard_map/ppermute | solution.py:600
  31.7 18.5 %collective-permute-start.4 = (bf16[544,256]{1,0:T(8,128)(2,1)}, bf16[544,256]{1,0:T(8,128)(2,1)}, u32[]{:S(2)}, u32[]{:S(2)}) collective-permute-start(bf16[544,256]{1,0:T(8,128)(2,1)} %get-tuple-element.43), channel_id=1, source_target_pairs={{0,1},{1,0},{2,3},{3,2},{4,5},{5,4},{6,7},{7,6},{8,9},{9,8},{10,11... | collective-permute-start | bytes 835592 | tf_op jit(solution)/shard_map/ppermute | solution.py:600
  37.5 12.8 %collective-permute-start.5 = (bf16[672,256]{1,0:T(8,128)(2,1)}, bf16[672,256]{1,0:T(8,128)(2,1)S(1)}, u32[]{:S(2)}, u32[]{:S(2)}) collective-permute-start(bf16[672,256]{1,0:T(8,128)(2,1)} %get-tuple-element.44), channel_id=1, source_target_pairs={{0,1},{1,0},{2,3},{3,2},{4,5},{5,4},{6,7},{7,6},{8,9},{9,8},{10,11... | collective-permute-start | bytes 1032200 | tf_op jit(solution)/shard_map/ppermute | solution.py:600
  39.0 1.0 %copy-start.6 = (bf16[256,768]{1,0:T(8,128)(2,1)S(1)}, bf16[256,768]{1,0:T(8,128)(2,1)}, u32[]{:S(2)}) copy-start(bf16[256,768]{1,0:T(8,128)(2,1)} %refs_7_.1) | copy-start | bytes 1179652
  39.1 1.0 %copy-start.7 = (bf16[256,256]{1,0:T(8,128)(2,1)S(1)}, bf16[256,256]{1,0:T(8,128)(2,1)}, u32[]{:S(2)}) copy-start(bf16[256,256]{1,0:T(8,128)(2,1)} %refs_8_.3) | copy-start | bytes 393220
  40.1 10.2 %copy-start.1 = (bf16[8,256,256]{2,1,0:T(8,128)(2,1)S(1)}, bf16[8,256,256]{2,1,0:T(8,128)(2,1)}, u32[]{:S(2)}) copy-start(bf16[8,256,256]{2,1,0:T(8,128)(2,1)} %get-tuple-element.41.refs_1_) | copy-start | bytes 3145732
  40.1 10.2 %copy-start.8 = (bf16[8,256,256]{2,1,0:T(8,128)(2,1)S(1)}, bf16[8,256,256]{2,1,0:T(8,128)(2,1)}, u32[]{:S(2)}) copy-start(bf16[8,256,256]{2,1,0:T(8,128)(2,1)} %get-tuple-element.40.refs_0_) | copy-start | bytes 3145732
  40.1 10.2 %copy-start.9 = (bf16[8,256,256]{2,1,0:T(8,128)(2,1)S(1)}, bf16[8,256,256]{2,1,0:T(8,128)(2,1)}, u32[]{:S(2)}) copy-start(bf16[8,256,256]{2,1,0:T(8,128)(2,1)} %get-tuple-element.46.refs_5_) | copy-start | bytes 3145732

commit v10 on v9

--- a/solution.py
+++ b/solution.py
@@ -407,69 +407,79 @@
     depth_ref, qkv_ref, wo_ref = take(3)
     if edges:
         take(1)
-    out_ref, q_ref, k_ref, v_ref, att_ref, token_ref, sem = refs
-    lev, count, width = q_ref.shape
+    out_hbm, x_ref, mixed_ref, q_ref, k_ref, v_ref, att_ref, token_ref, new_ref = refs[:9]
+    in_sem, out_sem, sem = refs[9:]
+    steps, lev, count, width = q_ref.shape
     members = others + 1
     head = width // HEADS
     pair = 2 * head
-    step = pl.program_id(0)
-
-    def keys_values(x, m):
-        rows = slice(m * lev, (m + 1) * lev)
-        kv = jnp.dot(x, qkv_ref[:, width:], preferred_element_type=F32).astype(BF16)
-        k_ref[rows] = kv[:, :width].reshape(lev, count, width)
-        v_ref[rows] = kv[:, width:].reshape(lev, count, width)
-
-    pick = lambda a, b: jnp.where(step == 0, a, b)
+
+    loads = []
+    for kind, (parts, buf) in enumerate(((own_normed, x_ref), (own_mixed, mixed_ref))):
+        for step in range(steps):
+            at = 0
+            for k, part in enumerate(parts):
+                n = part.shape[0]
+                load = pltpu.make_async_copy(
+                    part.at[:, pl.ds(step * count, count)],
+                    buf.at[step, pl.ds(at, n)],
+                    in_sem.at[kind, step, k],
+                )
+                load.start()
+                loads.append((kind, step, load))
+                at += n
+
+    def arrive(kind, step):
+        for k, s, load in loads:
+            if (k, s) == (kind, step):
+                load.wait()
+
     d = depth_ref[...].astype(F32)
     last = d.shape[0] - 1
     if edges:
         rows_d = [jnp.where(side_ref[k] == 0, d[0:1], d[last:]) for k in range(2)]
-        plans = [row_plan(row, lev) for row in rows_d]
-        near, far = offsets(plans[:1], 1, lev), offsets(plans[1:], 0, lev)
-        place = [far[0, 0]] + [pick(near[l, 0], far[l, 0]) for l in range(1, lev)]
     else:
         rows_d = [d[r : r + 1] for r in range(1, last)]
-        plans = [row_plan(row, lev) for row in rows_d]
+    plans = [row_plan(row, lev) for row in rows_d]
+    if edges:
+        near, far = offsets(plans[:1], 1, lev), offsets(plans[1:], 0, lev)
+        place = [{l: at for (l, _), at in p.items()} for p in (near, far)]
+    else:
         both = offsets(plans, 1, lev)
-        place = [None] + [pick(both[l, 0], both[l, 1]) for l in range(1, lev)]
-    wet_row, rank = pick(plans[0][0], plans[1][0]), pick(plans[0][1], plans[1][1])
-    depth_row = pick(*rows_d)
-
-    window = count + 16
-    limits = [p[0].shape[0] - window for p in packed]
-    limit = pick(*limits) if edges else limits[0]
-
-    def restore(l, o):
-        def rows_of(base, size):
-            if not edges:
-                return packed[0][o][pl.ds(base, size), :]
-            near_at, far_at = (pl.multiple_of(jnp.minimum(base, at), 16) for at in limits)
-            return pick(packed[0][o][pl.ds(near_at, size), :], packed[1][o][pl.ds(far_at, size), :])
-
-        return unpack(rows_of, wet_row[l : l + 1], rank[l : l + 1], place[l], limit)
-
-    x = jnp.concatenate([p[...].reshape(-1, width) for p in own_normed], axis=0)
-    q = jnp.dot(x, qkv_ref[:, 0:width], preferred_element_type=F32).astype(BF16)
-    q_ref[...] = (q * (1.0 / math.sqrt(head))).astype(BF16).reshape(lev, count, width)
-    keys_values(x, 0)
+        place = [{l: both[l, step] for l in range(1, lev)} for step in range(steps)]
+
+    def project(x, step, m):
+        rows = slice(m * lev, (m + 1) * lev)
+        kv = jnp.dot(x, qkv_ref[:, width:], preferred_element_type=F32).astype(BF16)
+        k_ref[step, rows] = kv[:, :width].reshape(lev, count, width)
+        v_ref[step, rows] = kv[:, width:].reshape(lev, count, width)
+
     for o in range(others):
-        token_ref[0] = pick(surf[o][0], restore(0, o)) if edges else surf[o][0]
-        for l in range(1, lev):
-            token_ref[l] = restore(l, o)
+        for step in range(steps):
+            source = packed[step if edges else 0][o]
+            window = lambda base, size: source[pl.ds(base, size), :]
+            limit = source.shape[0] - count - 16
+            wet, rank, _ = plans[step]
+            if 0 not in place[step]:
+                at = 0 if edges else step * count
+                token_ref[step, 0] = surf[o][0, at : at + count]
+            for l, at in place[step].items():
+                token_ref[step, l] = unpack(window, wet[l : l + 1], rank[l : l + 1], at, limit)
 
         @pl.when(flag_ref[0] != 0)
         def _():
             first = lev - whole[o].shape[0]
-            copy = pltpu.make_async_copy(
-                whole[o].at[:, pl.ds(pl.multiple_of(step * count, count), count)],
-                token_ref.at[pl.ds(first, lev - first)],
-                sem,
-            )
-            copy.start()
-            copy.wait()
-
-        keys_values(token_ref[...].reshape(-1, width), o + 1)
+            for step in range(steps):
+                copy = pltpu.make_async_copy(
+                    whole[o].at[:, pl.ds(step * count, count)],
+                    token_ref.at[step, pl.ds(first, lev - first)],
+                    sem,
+                )
+                copy.start()
+                copy.wait()
+
+        for step in range(steps):
+            project(token_ref[step].reshape(-1, width), step, o + 1)
 
     nq, nk = lev * GROUP, members * lev * GROUP
     groups = count // GROUP
@@ -478,41 +488,60 @@
     mine = (cell // GROUP == lax.broadcasted_iota(jnp.int32, (groups, count), 0)).astype(F32)
     spread = lax.broadcasted_iota(jnp.int32, (count, lanes_n), 0) % GROUP
     spread = (spread == lax.broadcasted_iota(jnp.int32, (count, lanes_n), 1) % GROUP).astype(F32)
-    key_depth = jnp.dot(
-        (mine * depth_row).astype(BF16), spread.astype(BF16), preferred_element_type=F32
-    )
     key_level = lax.broadcasted_iota(jnp.int32, (groups, lanes_n), 1) // GROUP
-    key_bias = jnp.where(key_depth > key_level.astype(F32), 0.0, NEG)
     qc = lax.broadcasted_iota(jnp.int32, (nq, nk), 0) % GROUP
     kc = lax.broadcasted_iota(jnp.int32, (nq, nk), 1) % GROUP
     same = jnp.where(qc == kc, 0.0, NEG)
     lane = lax.broadcasted_iota(jnp.int32, (1, width), 1)
-    masks = [(lane // head == h).astype(F32).astype(BF16) for h in range(HEADS)]
-    for g in range(groups):
-        cells = slice(g * GROUP, (g + 1) * GROUP)
-        bias = same + jnp.concatenate([key_bias[g : g + 1]] * members, axis=1)
-        bias = jnp.concatenate([bias] * HEADS, axis=0)
-        q = q_ref[:, cells].reshape(nq, width)
-        q = jnp.concatenate([q * mask for mask in masks], axis=0)
-        k = k_ref[:, cells].reshape(nk, width)
-        v = v_ref[:, cells].reshape(nk, width)
-        s = lax.dot_general(q, k, (((1,), (1,)), ((), ())), preferred_element_type=F32) + bias
-        p = jnp.exp(s - jnp.max(s, axis=-1, keepdims=True))
-        norm = 1.0 / jnp.sum(p, axis=-1, keepdims=True)
-        p = p.astype(BF16)
-        for h in range(HEADS // 2):
-            lanes = slice(h * pair, (h + 1) * pair)
-            mine = slice(h * 2 * nq, (h + 1) * 2 * nq)
-            o = jnp.dot(p[mine], v[:, lanes], preferred_element_type=F32) * norm[mine]
-            o = jnp.where(lane[:, :pair] < head, o[:nq], o[nq:])
-            att_ref[:, cells, lanes] = o.astype(BF16).reshape(lev, GROUP, pair)
-    proj = jnp.dot(att_ref[...].reshape(-1, width), wo_ref[...], preferred_element_type=F32)
-    base = jnp.concatenate([p[...].reshape(-1, width) for p in own_mixed], axis=0).astype(F32)
-    deep = column(depth_row)
-    for l in range(lev):
-        rows = slice(l * count, (l + 1) * count)
-        wet = widen((deep > l).astype(F32), width)
-        out_ref[0, l] = (base[rows] + wet * proj[rows]).astype(BF16)
+    scale = 1.0 / math.sqrt(head)
+    masks = [jnp.where(lane // head == h, scale, 0.0).astype(BF16) for h in range(HEADS)]
+    stores = []
+    for step in range(steps):
+        arrive(0, step)
+        x = x_ref[step].reshape(-1, width)
+        q = jnp.dot(x, qkv_ref[:, 0:width], preferred_element_type=F32).astype(BF16)
+        q_ref[step] = q.reshape(lev, count, width)
+        project(x, step, 0)
+        key_depth = jnp.dot(
+            (mine * rows_d[step]).astype(BF16), spread.astype(BF16), preferred_element_type=F32
+        )
+        key_bias = jnp.where(key_depth > key_level.astype(F32), 0.0, NEG)
+        for g in range(groups):
+            cells = slice(g * GROUP, (g + 1) * GROUP)
+            bias = same + jnp.concatenate([key_bias[g : g + 1]] * members, axis=1)
+            bias = jnp.concatenate([bias] * HEADS, axis=0)
+            q = q_ref[step, :, cells].reshape(nq, width)
+            q = jnp.concatenate([q * mask for mask in masks], axis=0)
+            k = k_ref[step, :, cells].reshape(nk, width)
+            v = v_ref[step, :, cells].reshape(nk, width)
+            s = lax.dot_general(q, k, (((1,), (1,)), ((), ())), preferred_element_type=F32) + bias
+            p = jnp.exp(s - jnp.max(s, axis=-1, keepdims=True))
+            norm = 1.0 / jnp.sum(p, axis=-1, keepdims=True)
+            p = p.astype(BF16)
+            for h in range(HEADS // 2):
+                lanes = slice(h * pair, (h + 1) * pair)
+                rows = slice(h * 2 * nq, (h + 1) * 2 * nq)
+                o = jnp.dot(p[rows], v[:, lanes], preferred_element_type=F32) * norm[rows]
+                o = jnp.where(lane[:, :pair] < head, o[:nq], o[nq:])
+                att_ref[step, :, cells, lanes] = o.astype(BF16).reshape(lev, GROUP, pair)
+        proj = jnp.dot(
+            att_ref[step].reshape(-1, width), wo_ref[...], preferred_element_type=F32
+        )
+        arrive(1, step)
+        deep = column(rows_d[step])
+        row = side_ref[step] if edges else step + 1
+        for l in range(lev):
+            rows = slice(l * count, (l + 1) * count)
+            wet = widen((deep > l).astype(F32), width)
+            new_ref[step, l] = (mixed_ref[step, l].astype(F32) + wet * proj[rows]).astype(BF16)
+        at = pl.multiple_of(row * count, count)
+        store = pltpu.make_async_copy(
+            new_ref.at[step], out_hbm.at[0, :, pl.ds(at, count)], out_sem.at[step]
+        )
+        store.start()
+        stores.append(store)
+    for store in stores:
+        store.wait()
 
 
 def attend(
@@ -522,52 +551,49 @@
     others, nparts = len(whole), len(mixed)
     lev = sum(p.shape[0] for p in mixed)
     width = shape[-1]
-    rows, cols = depth.shape
-    row_of = lambda i, s: s[i] if edges else i + 1
-    full2 = lambda a: pl.BlockSpec(a.shape, lambda i, *_: (0, 0))
-    block = lambda n: pl.BlockSpec((n, cols, width), lambda i, *_: (0, i, 0))
-    near = pl.BlockSpec((1, cols, width), lambda i, *_: (0, rows - 2, 0))
-    part = [block(p.shape[0]) for p in mixed]
-    hbm = pl.BlockSpec(memory_space=pl.ANY)
-    in_specs = part * 2
-    in_specs += [near if edges else block(1)] * others
-    in_specs += [full2(p) for p in packed]
-    in_specs += [hbm] * others
-    in_specs += [full2(depth), full2(qkv_weight), full2(out_weight)]
+    cols = depth.shape[1]
+    members = others + 1
+    hbm = pl.BlockSpec(memory_space=pltpu.HBM)
+    vmem = pl.BlockSpec(memory_space=pltpu.VMEM)
+    smem = pl.BlockSpec(memory_space=pltpu.SMEM)
     stay = lambda x: pltpu.with_memory_space_constraint(x, pltpu.HBM)
-    args = [x if edges else stay(x) for x in normed + mixed]
-    args += surf + packed + whole + [depth, qkv_weight, out_weight]
+    if edges:
+        surf = [x[:, shape[2] - 2 * cols :] for x in surf]
+    in_specs = [smem] * 2 + [hbm] * (2 * nparts) + [vmem] * (len(surf) + len(packed))
+    in_specs += [hbm] * others + [vmem] * 3
+    args = [flag, side] + [stay(x) for x in normed + mixed] + surf + packed
+    args += [stay(x) for x in whole] + [depth, qkv_weight, out_weight]
     alias = {}
     if edges:
         in_specs.append(hbm)
-        alias = {len(args) + 2: 0}
-        args.append(out)
+        alias = {len(args): 0}
+        args.append(stay(out))
     tokens = lev * cols * 2
-    members = others + 1
+    rows = pltpu.VMEM((2, lev, cols, width), BF16)
+    keys = pltpu.VMEM((2, members * lev, cols, width), BF16)
     return pl.pallas_call(
         functools.partial(attend_kernel, others, nparts, edges),
-        grid_spec=pltpu.PrefetchScalarGridSpec(
-            num_scalar_prefetch=2,
-            grid=(2,),
-            in_specs=in_specs,
-            out_specs=pl.BlockSpec(
-                (1, lev, cols, width), lambda i, f, s: (0, 0, row_of(i, s), 0)
-            ),
-            scratch_shapes=[
-                pltpu.VMEM((lev, cols, width), BF16),
-                pltpu.VMEM((members * lev, cols, width), BF16),
-                pltpu.VMEM((members * lev, cols, width), BF16),
-                pltpu.VMEM((lev, cols, width), BF16),
-                pltpu.VMEM((lev, cols, width), BF16),
-                pltpu.SemaphoreType.DMA,
-            ],
-        ),
-        out_shape=jax.ShapeDtypeStruct(shape, BF16),
+        in_specs=in_specs,
+        out_specs=hbm,
+        scratch_shapes=[
+            rows,
+            rows,
+            rows,
+            keys,
+            keys,
+            rows,
+            rows,
+            rows,
+            pltpu.SemaphoreType.DMA((2, 2, nparts)),
+            pltpu.SemaphoreType.DMA((2,)),
+            pltpu.SemaphoreType.DMA,
+        ],
+        out_shape=pltpu.HBM(shape, BF16),
         input_output_aliases=alias,
-        compiler_params=params(16 if members <= 2 else 48, 1),
+        compiler_params=params(24 if members <= 2 else 56),
         cost_estimate=cost(tokens * width * width * 8 * (members + 2), tokens * width * 2 * 5),
         name="attend",
-    )(flag, side, *args)
+    )(*args)
 
 
 def body(

time: 60.5 us -> 59.7 us (0.987)
  Pallas kernels: 45.6 us -> 44.7 us
    pallas_call x2, Pallas kernels: 19.6 us -> 18.7 us  [attend(): pl.pallas_call(functools.partial(attend_kernel, others, nparts, edges), i...]
where the time goes in v10:
time: 59.7 us; the launch traced here: 59 us
  Pallas kernels  44.7 us (75%)
  starting transfers between devices  8 us (13%)
  waiting for transfers between devices  4.24 us (7%)
  local copies, waits for them, and re-layouts  1.03 us (2%)
  between operations  0.97 us (2%)
    pallas_call x2, Pallas kernels, attend(): pl.pallas_call(functools.partial(attend_kernel, others, nparts, edges), i...  18.7 us
    pallas_call x2, Pallas kernels, row_conv(): pl.pallas_call(functools.partial(row_kernel, cap, first, which), in_specs...  11.4 us
    pallas_call x1, Pallas kernels, body(): pl.pallas_call(functools.partial(inner_kernel, deep_cap), in_specs=[vmem,...  7.17 us
    ppermute x4, starting transfers between devices, exchange(): lax.ppermute(x, 'mem', [(i, (i + k) % members) for i in range(members)])  5.27 us
    ppermute x2, waiting for transfers between devices, swap(): return lax.ppermute(x, 'tile', pairs + [(b, a) for a, b in pairs])  4.23 us
    pallas_call x1, Pallas kernels, body(): pl.pallas_call(surface_kernel, in_specs=[smem] * 3 + [vmem] + [anywhere]...  3.71 us
    pallas_call x1, Pallas kernels, body(): pl.pallas_call(functools.partial(prep_kernel, (deep_cap, near_cap, far_ca...  3.7 us
    ppermute x2, starting transfers between devices, swap(): return lax.ppermute(x, 'tile', pairs + [(b, a) for a, b in pairs])  2.72 us
  transfers between devices with their start and end apart: 6, of which 1 were waited for; matrix products, arithmetic and copies ran while one was open for 0% of the time, Pallas kernels for 54%

profile of v10, /device:TPU:18, one launch (start us, length us, event | category | flops | bytes accessed | tf_op | source)
XLA Modules:
  0.0 59.0 jit_solution(7234098116851276224)
XLA Ops:
  0.0 0.1 pad_add_fusion.side_ref
  0.1 3.7 %prep.1 = (bf16[1536,256]{1,0:T(8,128)(2,1)}, bf16[1536,256]{1,0:T(8,128)(2,1)}, s32[1]{0:T(128)}) custom-call(s32[2]{0:T(128)S(1)} %pad_add_fusion.side_ref, bf16[1,8,512,256]{3,2,1,0:T(8,128)(2,1)} %state.5, bf16[1,512,256]{2,1,0:T(8,128)(2,1)} %atm_ref.1, s32[4,128]{1,0:T(4,128)} %bitcast.8), custom_call_target="tpu_custom_call" | custom-call | flops 1048576 | bytes 2621440 | tf_op jit(solution)/shard_map/prep/pallas_call | solution.py:647
  3.8 0.1 collective-permute-start.2
  3.9 0.0 copy-start.7
  3.9 2.7 %collective-permute-start.1 = (bf16[1536,256]{1,0:T(8,128)(2,1)}, bf16[1536,256]{1,0:T(8,128)(2,1)S(1)}, u32[]{:S(2)}, u32[]{:S(2)}) collective-permute-start(bf16[1536,256]{1,0:T(8,128)(2,1)} %get-tuple-element.32), channel_id=1, source_target_pairs={{2,4},{6,8},{10,12},{14,16},{18,20},{22,24},{26,28},{4,2},{8,6},{1... | collective-permute-start | bytes 2359304 | tf_op jit(solution)/shard_map/ppermute | solution.py:622
  6.5 0.0 copy-done.3
  6.6 0.0 copy-done
  6.6 7.2 %inner.1 = (bf16[7,256,256]{2,1,0:T(8,128)(2,1)}, bf16[7,256,256]{2,1,0:T(8,128)(2,1)}, bf16[1008,256]{1,0:T(8,128)(2,1)}) custom-call(bf16[1,8,512,256]{3,2,1,0:T(8,128)(2,1)S(1)} %copy-done, s32[4,128]{1,0:T(4,128)S(1)} %bitcast.9, bf16[3,3,256,256]{3,2,1,0:T(8,128)(2,1)} %weight_hbm.5), custom_call_target="tpu_custom_call" | custom-call | flops 2415919104 | bytes 4194304 | tf_op jit(solution)/shard_map/inner/pallas_call | solution.py:668
  13.7 1.6 %collective-permute-start.6 = (bf16[1008,256]{1,0:T(8,128)(2,1)}, bf16[1008,256]{1,0:T(8,128)(2,1)}, u32[]{:S(2)}, u32[]{:S(2)}) collective-permute-start(bf16[1008,256]{1,0:T(8,128)(2,1)} %get-tuple-element.49), channel_id=1, source_target_pairs={{0,1},{1,0},{2,3},{3,2},{4,5},{5,4},{6,7},{7,6},{8,9},{9,8},{10,11... | collective-permute-start | bytes 1548296 | tf_op jit(solution)/shard_map/ppermute | solution.py:626
  15.3 0.0 copy-done.7
  15.4 0.0 copy-start.2
  15.4 0.0 copy-start.4
  15.4 0.0 collective-permute-done.2.halo_hbm.on_hbm
  15.4 6.2 %row.2 = (bf16[8,256,256]{2,1,0:T(8,128)(2,1)}, bf16[8,256,256]{2,1,0:T(8,128)(2,1)}, bf16[544,256]{1,0:T(8,128)(2,1)}, f32[384,256]{1,0:T(8,128)}) custom-call(s32[2]{0:T(128)S(1)} %pad_add_fusion.side_ref, bf16[1,8,512,256]{3,2,1,0:T(8,128)(2,1)S(1)} %copy-done, s32[4,128]{1,0:T(4,128)S(1)} %bitcast.10, bf16[3,3,256,256]{3,2,1,0:T(8,128)(2,1)} %weight_hbm.5, ...), custom_call_target="tpu_custom_call" | custom-call | flops 1207959552 | bytes 4194304 | tf_op jit(solution)/shard_map/row/pallas_call | solution.py:694
  21.6 4.2 %collective-permute-done.1.off_hbm.halo_hbm = bf16[1536,256]{1,0:T(8,128)(2,1)S(1)} collective-permute-done((bf16[1536,256]{1,0:T(8,128)(2,1)}, bf16[1536,256]{1,0:T(8,128)(2,1)S(1)}, u32[]{:S(2)}, u32[]{:S(2)}) %collective-permute-start.1) | collective-permute-done | bytes 786464 | tf_op jit(solution)/shard_map/ppermute | solution.py:622
  25.8 0.0 copy-done.1
  25.8 0.0 copy-done.2
  25.8 0.0 copy-done.4
  25.8 3.7 %surface.1 = (bf16[1,384,256]{2,1,0:T(8,128)(2,1)}, bf16[1,384,256]{2,1,0:T(8,128)(2,1)}, f32[128,256]{1,0:T(8,128)}, bf16[8,256,256]{2,1,0:T(8,128)(2,1)}, bf16[8,256,256]{2,1,0:T(8,128)(2,1)}) custom-call(s32[4,4]{1,0:T(4,128)S(1)} %subtract_clamp_fusion.ids_ref, s32[4]{0:T(128)S(1)} %copy-done.4, ...), custom_call_target="tpu_custom_call", output_to_operand_aliasing={{3}: (9, {}), {4}: (10, {})} | custom-call | flops 301989888 | bytes 2097152 | tf_op jit(solution)/shard_map/surface/pallas_call | solution.py:720
  29.6 1.6 %collective-permute-start.3 = (bf16[1,384,256]{2,1,0:T(8,128)(2,1)}, bf16[1,384,256]{2,1,0:T(8,128)(2,1)S(1)}, u32[]{:S(2)}, u32[]{:S(2)}) collective-permute-start(bf16[1,384,256]{2,1,0:T(8,128)(2,1)} %get-tuple-element.42.refs_0_), channel_id=1, source_target_pairs={{0,1},{1,0},{2,3},{3,2},{4,5},{5,4},{6,7},{7,6},{8,9},{9,8},{10,11... | collective-permute-start | bytes 589832 | tf_op jit(solution)/shard_map/ppermute | solution.py:626
  31.8 0.0 copy-start.8
  31.8 5.2 %row.3 = (bf16[8,256,256]{2,1,0:T(8,128)(2,1)}, bf16[8,256,256]{2,1,0:T(8,128)(2,1)}, bf16[672,256]{1,0:T(8,128)(2,1)}) custom-call(s32[2]{0:T(128)S(1)} %pad_add_fusion.side_ref, bf16[1,8,512,256]{3,2,1,0:T(8,128)(2,1)S(1)} %copy-done, s32[4,128]{1,0:T(4,128)S(1)} %bitcast.12, ...), custom_call_target="tpu_custom_call", output_to_operand_aliasing={{0}: (6, {}), {1}: (7, {})} | custom-call | flops 1207959552 | bytes 4194304 | tf_op jit(solution)/shard_map/row/pallas_call | solution.py:694
  37.0 0.6 collective-permute-start.5
  37.5 1.5 %collective-permute-start.4 = (bf16[544,256]{1,0:T(8,128)(2,1)S(1)}, bf16[544,256]{1,0:T(8,128)(2,1)S(1)}, u32[]{:S(2)}, u32[]{:S(2)}) collective-permute-start(bf16[544,256]{1,0:T(8,128)(2,1)S(1)} %copy-done.8), channel_id=1, source_target_pairs={{0,1},{1,0},{2,3},{3,2},{4,5},{5,4},{6,7},{7,6},{8,9},{9,8},{10,11... | collective-permute-start | bytes 835592 | tf_op jit(solution)/shard_map/ppermute | solution.py:626
  39.1 0.0 collective-permute-done.3.refs_4_
  39.1 0.0 collective-permute-done.6.refs_5_
  39.1 1.0 %copy-done.5 = bf16[256,768]{1,0:T(8,128)(2,1)S(1)} copy-done((bf16[256,768]{1,0:T(8,128)(2,1)S(1)}, bf16[256,768]{1,0:T(8,128)(2,1)}, u32[]{:S(2)}) %copy-start.5) | copy-done | bytes 393240
  40.1 0.0 copy-done.6
  40.1 9.6 %attend.2.refs_9_ = bf16[1,8,512,256]{3,2,1,0:T(8,128)(2,1)} custom-call(s32[1]{0:T(128)} %get-tuple-element.31.flag_ref, s32[2]{0:T(128)S(1)} %pad_add_fusion.side_ref, bf16[1,384,256]{2,1,0:T(8,128)(2,1)} %get-tuple-element.42.refs_0_, bf16[7,256,256]{2,1,0:T(8,128)(2,1)} %get-tuple-element.45.refs_1_, bf16[1,384,256]{2,1,0:T(8,128)(2,1)} %get-tuple-element.47.refs_2_, ...), custom_call_target="tpu_custom_call" | custom-call | flops 4294967296 | bytes 5242880 | tf_op jit(solution)/shard_map/attend/pallas_call | solution.py:574
  49.7 0.0 collective-permute-done.4.refs_3_
  49.7 0.0 collective-permute-done.5.refs_4_
  49.8 9.1 %attend.3 = bf16[1,8,512,256]{3,2,1,0:T(8,128)(2,1)} custom-call(s32[1]{0:T(128)} %get-tuple-element.31.flag_ref, s32[2]{0:T(128)S(1)} %pad_add_fusion.side_ref, bf16[8,256,256]{2,1,0:T(8,128)(2,1)} %get-tuple-element.40.refs_0_, bf16[8,256,256]{2,1,0:T(8,128)(2,1)} %get-tuple-element.41.refs_1_, ...), custom_call_target="tpu_custom_call", output_to_operand_aliasing={{}: (11, {})} | custom-call | flops 4294967296 | bytes 5242880 | tf_op jit(solution)/shard_map/attend/pallas_call | solution.py:574
  (11 shorter events, 0.0 us)
Async XLA Ops:
  0.0 6.5 %copy-start.3 = (s32[512]{0:T(512)S(1)}, s32[512]{0:T(512)}, u32[]{:S(2)}) copy-start(s32[512]{0:T(512)} %param.13) | copy-start | bytes 6148
  0.0 6.6 %copy-start = (bf16[1,8,512,256]{3,2,1,0:T(8,128)(2,1)S(1)}, bf16[1,8,512,256]{3,2,1,0:T(8,128)(2,1)}, u32[]{:S(2)}) copy-start(bf16[1,8,512,256]{3,2,1,0:T(8,128)(2,1)} %state.5) | copy-start | bytes 6291460
  3.8 11.6 %collective-permute-start.2 = (bf16[1536,256]{1,0:T(8,128)(2,1)}, bf16[1536,256]{1,0:T(8,128)(2,1)}, u32[]{:S(2)}, u32[]{:S(2)}) collective-permute-start(bf16[1536,256]{1,0:T(8,128)(2,1)} %get-tuple-element.33), channel_id=1, source_target_pairs={{0,2},{4,6},{8,10},{12,14},{16,18},{20,22},{24,26},{28,30},{2,0},{... | collective-permute-start | bytes 2359304 | tf_op jit(solution)/shard_map/ppermute | solution.py:622
  3.9 11.5 %copy-start.7 = (s32[4,4]{1,0:T(4,128)S(1)}, s32[4,4]{1,0:T(4,128)}, u32[]{:S(2)}) copy-start(s32[4,4]{1,0:T(4,128)} %param.14) | copy-start | bytes 196
  3.9 21.9 %collective-permute-start.1 = (bf16[1536,256]{1,0:T(8,128)(2,1)}, bf16[1536,256]{1,0:T(8,128)(2,1)S(1)}, u32[]{:S(2)}, u32[]{:S(2)}) collective-permute-start(bf16[1536,256]{1,0:T(8,128)(2,1)} %get-tuple-element.32), channel_id=1, source_target_pairs={{2,4},{6,8},{10,12},{14,16},{18,20},{22,24},{26,28},{4,2},{8,6},{1... | collective-permute-start | bytes 2359304 | tf_op jit(solution)/shard_map/ppermute | solution.py:622
  13.7 25.3 %collective-permute-start.6 = (bf16[1008,256]{1,0:T(8,128)(2,1)}, bf16[1008,256]{1,0:T(8,128)(2,1)}, u32[]{:S(2)}, u32[]{:S(2)}) collective-permute-start(bf16[1008,256]{1,0:T(8,128)(2,1)} %get-tuple-element.49), channel_id=1, source_target_pairs={{0,1},{1,0},{2,3},{3,2},{4,5},{5,4},{6,7},{7,6},{8,9},{9,8},{10,11... | collective-permute-start | bytes 1548296 | tf_op jit(solution)/shard_map/ppermute | solution.py:626
  15.3 10.5 %copy-start.1 = (bf16[1,512,256]{2,1,0:T(8,128)(2,1)S(1)}, bf16[1,512,256]{2,1,0:T(8,128)(2,1)}, u32[]{:S(2)}) copy-start(bf16[1,512,256]{2,1,0:T(8,128)(2,1)} %atm_ref.1) | copy-start | bytes 786436
  15.4 10.5 %copy-start.2 = (bf16[4,4,128,128]{3,2,1,0:T(8,128)(2,1)S(1)}, bf16[4,4,128,128]{3,2,1,0:T(8,128)(2,1)}, u32[]{:S(2)}) copy-start(bf16[4,4,128,128]{3,2,1,0:T(8,128)(2,1)} %remap.1) | copy-start | bytes 1572868
  15.4 10.5 %copy-start.4 = (s32[4]{0:T(128)S(1)}, s32[4]{0:T(128)}, u32[]{:S(2)}) copy-start(s32[4]{0:T(128)} %live_ref.1) | copy-start | bytes 52
  29.6 9.5 %collective-permute-start.3 = (bf16[1,384,256]{2,1,0:T(8,128)(2,1)}, bf16[1,384,256]{2,1,0:T(8,128)(2,1)S(1)}, u32[]{:S(2)}, u32[]{:S(2)}) collective-permute-start(bf16[1,384,256]{2,1,0:T(8,128)(2,1)} %get-tuple-element.42.refs_0_), channel_id=1, source_target_pairs={{0,1},{1,0},{2,3},{3,2},{4,5},{5,4},{6,7},{7,6},{8,9},{9,8},{10,11... | collective-permute-start | bytes 589832 | tf_op jit(solution)/shard_map/ppermute | solution.py:626
  31.8 5.8 %copy-start.8 = (bf16[544,256]{1,0:T(8,128)(2,1)S(1)}, bf16[544,256]{1,0:T(8,128)(2,1)}, u32[]{:S(2)}) copy-start(bf16[544,256]{1,0:T(8,128)(2,1)} %get-tuple-element.43) | copy-start | bytes 835588
  37.0 12.8 %collective-permute-start.5 = (bf16[672,256]{1,0:T(8,128)(2,1)}, bf16[672,256]{1,0:T(8,128)(2,1)S(1)}, u32[]{:S(2)}, u32[]{:S(2)}) collective-permute-start(bf16[672,256]{1,0:T(8,128)(2,1)} %get-tuple-element.44), channel_id=1, source_target_pairs={{0,1},{1,0},{2,3},{3,2},{4,5},{5,4},{6,7},{7,6},{8,9},{9,8},{10,11... | collective-permute-start | bytes 1032200 | tf_op jit(solution)/shard_map/ppermute | solution.py:626
  37.5 12.2 %collective-permute-start.4 = (bf16[544,256]{1,0:T(8,128)(2,1)S(1)}, bf16[544,256]{1,0:T(8,128)(2,1)S(1)}, u32[]{:S(2)}, u32[]{:S(2)}) collective-permute-start(bf16[544,256]{1,0:T(8,128)(2,1)S(1)} %copy-done.8), channel_id=1, source_target_pairs={{0,1},{1,0},{2,3},{3,2},{4,5},{5,4},{6,7},{7,6},{8,9},{9,8},{10,11... | collective-permute-start | bytes 835592 | tf_op jit(solution)/shard_map/ppermute | solution.py:626
  39.1 1.0 %copy-start.5 = (bf16[256,768]{1,0:T(8,128)(2,1)S(1)}, bf16[256,768]{1,0:T(8,128)(2,1)}, u32[]{:S(2)}) copy-start(bf16[256,768]{1,0:T(8,128)(2,1)} %refs_7_.1) | copy-start | bytes 1179652
  39.1 1.0 %copy-start.6 = (bf16[256,256]{1,0:T(8,128)(2,1)S(1)}, bf16[256,256]{1,0:T(8,128)(2,1)}, u32[]{:S(2)}) copy-start(bf16[256,256]{1,0:T(8,128)(2,1)} %refs_8_.3) | copy-start | bytes 393220

commit v11 on v10

--- a/solution.py
+++ b/solution.py
@@ -404,11 +404,15 @@
     surf = take(others)
     packed = [take(others) for _ in range(1 + edges)]
     whole = take(others)
-    depth_ref, qkv_ref, wo_ref = take(3)
+    depth_ref, qkv_hbm, wo_hbm = take(3)
     if edges:
         take(1)
-    out_hbm, x_ref, mixed_ref, q_ref, k_ref, v_ref, att_ref, token_ref, new_ref = refs[:9]
-    in_sem, out_sem, sem = refs[9:]
+    out_hbm, qkv_ref, wo_ref, x_ref, mixed_ref, q_ref, k_ref, v_ref, att_ref = refs[:9]
+    token_ref, new_ref, in_sem, out_sem, sem, weight_sem = refs[9:]
+    load_qkv = pltpu.make_async_copy(qkv_hbm, qkv_ref, weight_sem.at[0])
+    load_wo = pltpu.make_async_copy(wo_hbm, wo_ref, weight_sem.at[1])
+    load_qkv.start()
+    load_wo.start()
     steps, lev, count, width = q_ref.shape
     members = others + 1
     head = width // HEADS
@@ -461,7 +465,7 @@
             limit = source.shape[0] - count - 16
             wet, rank, _ = plans[step]
             if 0 not in place[step]:
-                at = 0 if edges else step * count
+                at = surf[o].shape[1] - count if edges else step * count
                 token_ref[step, 0] = surf[o][0, at : at + count]
             for l, at in place[step].items():
                 token_ref[step, l] = unpack(window, wet[l : l + 1], rank[l : l + 1], at, limit)
@@ -478,6 +482,9 @@
                 copy.start()
                 copy.wait()
 
+        if o == 0:
+            load_qkv.wait()
+            load_wo.wait()
         for step in range(steps):
             project(token_ref[step].reshape(-1, width), step, o + 1)
 
@@ -557,12 +564,10 @@
     vmem = pl.BlockSpec(memory_space=pltpu.VMEM)
     smem = pl.BlockSpec(memory_space=pltpu.SMEM)
     stay = lambda x: pltpu.with_memory_space_constraint(x, pltpu.HBM)
-    if edges:
-        surf = [x[:, shape[2] - 2 * cols :] for x in surf]
     in_specs = [smem] * 2 + [hbm] * (2 * nparts) + [vmem] * (len(surf) + len(packed))
-    in_specs += [hbm] * others + [vmem] * 3
+    in_specs += [hbm] * others + [vmem] + [hbm] * 2
     args = [flag, side] + [stay(x) for x in normed + mixed] + surf + packed
-    args += [stay(x) for x in whole] + [depth, qkv_weight, out_weight]
+    args += [stay(x) for x in whole] + [depth, stay(qkv_weight), stay(out_weight)]
     alias = {}
     if edges:
         in_specs.append(hbm)
@@ -576,6 +581,8 @@
         in_specs=in_specs,
         out_specs=hbm,
         scratch_shapes=[
+            pltpu.VMEM(qkv_weight.shape, BF16),
+            pltpu.VMEM(out_weight.shape, BF16),
             rows,
             rows,
             rows,
@@ -587,6 +594,7 @@
             pltpu.SemaphoreType.DMA((2, 2, nparts)),
             pltpu.SemaphoreType.DMA((2,)),
             pltpu.SemaphoreType.DMA,
+            pltpu.SemaphoreType.DMA((2,)),
         ],
         out_shape=pltpu.HBM(shape, BF16),
         input_output_aliases=alias,

time: 59.7 us -> 60.8 us (1.018)
  Pallas kernels: 44.7 us -> 47 us
  local copies, waits for them, and re-layouts: 1.03 us -> 0.03 us
    pallas_call x2, Pallas kernels: 18.7 us -> 21 us  [attend(): pl.pallas_call(functools.partial(attend_kernel, others, nparts, edges), i...]
    unnamed x18 -> x12, local copies, waits for them, and re-layouts: 1.02 us -> 0.03 us
  transfers between devices with their start and end apart: 6 -> 6, of which waited for: 1 -> 1; matrix products, arithmetic and copies ran while one was open for 0% -> 0% of each run, Pallas kernels for 54% -> 55%
where the time goes in v11:
time: 60.8 us; the launch traced here: 60.2 us
  Pallas kernels  47 us (77%)
  starting transfers between devices  8.07 us (13%)
  waiting for transfers between devices  4.21 us (7%)
  between operations  0.86 us (1%)
    pallas_call x2, Pallas kernels, attend(): pl.pallas_call(functools.partial(attend_kernel, others, nparts, edges), i...  21 us
    pallas_call x2, Pallas kernels, row_conv(): pl.pallas_call(functools.partial(row_kernel, cap, first, which), in_specs...  11.4 us
    pallas_call x1, Pallas kernels, body(): pl.pallas_call(functools.partial(inner_kernel, deep_cap), in_specs=[vmem,...  7.17 us
    ppermute x4, starting transfers between devices, exchange(): lax.ppermute(x, 'mem', [(i, (i + k) % members) for i in range(members)])  5.34 us
    ppermute x2, waiting for transfers between devices, swap(): return lax.ppermute(x, 'tile', pairs + [(b, a) for a, b in pairs])  4.2 us
    pallas_call x1, Pallas kernels, body(): pl.pallas_call(functools.partial(prep_kernel, (deep_cap, near_cap, far_ca...  3.7 us
    pallas_call x1, Pallas kernels, body(): pl.pallas_call(surface_kernel, in_specs=[smem] * 3 + [vmem] + [anywhere]...  3.7 us
    ppermute x2, starting transfers between devices, swap(): return lax.ppermute(x, 'tile', pairs + [(b, a) for a, b in pairs])  2.72 us
  transfers between devices with their start and end apart: 6, of which 1 were waited for; matrix products, arithmetic and copies ran while one was open for 0% of the time, Pallas kernels for 55%

profile of v11, /device:TPU:18, one launch (start us, length us, event | category | flops | bytes accessed | tf_op | source)
XLA Modules:
  0.0 60.2 jit_solution(15941430793405381064)
XLA Ops:
  0.0 0.0 copy-start
  0.0 0.0 copy-start.3
  0.0 0.1 pad_add_fusion.side_ref
  0.1 3.7 %prep.1 = (bf16[1536,256]{1,0:T(8,128)(2,1)}, bf16[1536,256]{1,0:T(8,128)(2,1)}, s32[1]{0:T(128)}) custom-call(s32[2]{0:T(128)S(1)} %pad_add_fusion.side_ref, bf16[1,8,512,256]{3,2,1,0:T(8,128)(2,1)} %state.5, bf16[1,512,256]{2,1,0:T(8,128)(2,1)} %atm_ref.1, s32[4,128]{1,0:T(4,128)} %bitcast.8), custom_call_target="tpu_custom_call" | custom-call | flops 1048576 | bytes 2621440 | tf_op jit(solution)/shard_map/prep/pallas_call | solution.py:655
  3.8 0.1 collective-permute-start.2
  3.9 0.0 copy-start.5
  3.9 2.7 %collective-permute-start.1 = (bf16[1536,256]{1,0:T(8,128)(2,1)}, bf16[1536,256]{1,0:T(8,128)(2,1)S(1)}, u32[]{:S(2)}, u32[]{:S(2)}) collective-permute-start(bf16[1536,256]{1,0:T(8,128)(2,1)} %get-tuple-element.32), channel_id=1, source_target_pairs={{2,4},{6,8},{10,12},{14,16},{18,20},{22,24},{26,28},{4,2},{8,6},{1... | collective-permute-start | bytes 2359304 | tf_op jit(solution)/shard_map/ppermute | solution.py:630
  6.5 0.0 copy-done
  6.6 0.0 copy-done.3
  6.6 7.2 %inner.1 = (bf16[7,256,256]{2,1,0:T(8,128)(2,1)}, bf16[7,256,256]{2,1,0:T(8,128)(2,1)}, bf16[1008,256]{1,0:T(8,128)(2,1)}) custom-call(bf16[1,8,512,256]{3,2,1,0:T(8,128)(2,1)S(1)} %copy-done, s32[4,128]{1,0:T(4,128)S(1)} %bitcast.9, bf16[3,3,256,256]{3,2,1,0:T(8,128)(2,1)} %weight_hbm.5), custom_call_target="tpu_custom_call" | custom-call | flops 2415919104 | bytes 4194304 | tf_op jit(solution)/shard_map/inner/pallas_call | solution.py:676
  13.7 1.6 %collective-permute-start.6 = (bf16[1008,256]{1,0:T(8,128)(2,1)}, bf16[1008,256]{1,0:T(8,128)(2,1)S(1)}, u32[]{:S(2)}, u32[]{:S(2)}) collective-permute-start(bf16[1008,256]{1,0:T(8,128)(2,1)} %get-tuple-element.49), channel_id=1, source_target_pairs={{0,1},{1,0},{2,3},{3,2},{4,5},{5,4},{6,7},{7,6},{8,9},{9,8},{10,11... | collective-permute-start | bytes 1548296 | tf_op jit(solution)/shard_map/ppermute | solution.py:634
  15.3 0.0 copy-done.5
  15.3 0.0 copy-start.1
  15.3 0.0 copy-start.2
  15.4 0.0 copy-start.4
  15.4 0.0 collective-permute-done.2.halo_hbm.on_hbm
  15.4 6.2 %row.2 = (bf16[8,256,256]{2,1,0:T(8,128)(2,1)}, bf16[8,256,256]{2,1,0:T(8,128)(2,1)}, bf16[544,256]{1,0:T(8,128)(2,1)}, f32[384,256]{1,0:T(8,128)}) custom-call(s32[2]{0:T(128)S(1)} %pad_add_fusion.side_ref, bf16[1,8,512,256]{3,2,1,0:T(8,128)(2,1)S(1)} %copy-done, s32[4,128]{1,0:T(4,128)S(1)} %bitcast.10, bf16[3,3,256,256]{3,2,1,0:T(8,128)(2,1)} %weight_hbm.5, ...), custom_call_target="tpu_custom_call" | custom-call | flops 1207959552 | bytes 4194304 | tf_op jit(solution)/shard_map/row/pallas_call | solution.py:702
  21.6 4.2 %collective-permute-done.1.off_hbm.halo_hbm = bf16[1536,256]{1,0:T(8,128)(2,1)S(1)} collective-permute-done((bf16[1536,256]{1,0:T(8,128)(2,1)}, bf16[1536,256]{1,0:T(8,128)(2,1)S(1)}, u32[]{:S(2)}, u32[]{:S(2)}) %collective-permute-start.1) | collective-permute-done | bytes 786464 | tf_op jit(solution)/shard_map/ppermute | solution.py:630
  25.8 0.0 copy-done.1
  25.8 0.0 copy-done.2
  25.8 0.0 copy-done.4
  25.8 3.7 %surface.1 = (bf16[1,384,256]{2,1,0:T(8,128)(2,1)}, bf16[1,384,256]{2,1,0:T(8,128)(2,1)}, f32[128,256]{1,0:T(8,128)}, bf16[8,256,256]{2,1,0:T(8,128)(2,1)}, bf16[8,256,256]{2,1,0:T(8,128)(2,1)}) custom-call(s32[4,4]{1,0:T(4,128)S(1)} %subtract_clamp_fusion.ids_ref, s32[4]{0:T(128)S(1)} %copy-done.4, ...), custom_call_target="tpu_custom_call", output_to_operand_aliasing={{3}: (9, {}), {4}: (10, {})} | custom-call | flops 301989888 | bytes 2097152 | tf_op jit(solution)/shard_map/surface/pallas_call | solution.py:728
  29.5 1.6 %collective-permute-start.3 = (bf16[1,384,256]{2,1,0:T(8,128)(2,1)}, bf16[1,384,256]{2,1,0:T(8,128)(2,1)}, u32[]{:S(2)}, u32[]{:S(2)}) collective-permute-start(bf16[1,384,256]{2,1,0:T(8,128)(2,1)} %get-tuple-element.42.refs_0_), channel_id=1, source_target_pairs={{0,1},{1,0},{2,3},{3,2},{4,5},{5,4},{6,7},{7,6},{8,9},{9,8},{10,11... | collective-permute-start | bytes 589832 | tf_op jit(solution)/shard_map/ppermute | solution.py:634
  31.7 0.6 collective-permute-start.4
  32.3 5.1 %row.3 = (bf16[8,256,256]{2,1,0:T(8,128)(2,1)}, bf16[8,256,256]{2,1,0:T(8,128)(2,1)}, bf16[672,256]{1,0:T(8,128)(2,1)}) custom-call(s32[2]{0:T(128)S(1)} %pad_add_fusion.side_ref, bf16[1,8,512,256]{3,2,1,0:T(8,128)(2,1)S(1)} %copy-done, s32[4,128]{1,0:T(4,128)S(1)} %bitcast.12, ...), custom_call_target="tpu_custom_call", output_to_operand_aliasing={{0}: (6, {}), {1}: (7, {})} | custom-call | flops 1207959552 | bytes 4194304 | tf_op jit(solution)/shard_map/row/pallas_call | solution.py:702
  37.4 1.6 %collective-permute-start.5 = (bf16[672,256]{1,0:T(8,128)(2,1)}, bf16[672,256]{1,0:T(8,128)(2,1)S(1)}, u32[]{:S(2)}, u32[]{:S(2)}) collective-permute-start(bf16[672,256]{1,0:T(8,128)(2,1)} %get-tuple-element.44), channel_id=1, source_target_pairs={{0,1},{1,0},{2,3},{3,2},{4,5},{5,4},{6,7},{7,6},{8,9},{9,8},{10,11... | collective-permute-start | bytes 1032200 | tf_op jit(solution)/shard_map/ppermute | solution.py:634
  39.0 0.0 collective-permute-done.6.refs_5_
  39.0 0.0 collective-permute-done.3.refs_4_.refs_2_
  39.0 10.7 %attend.2.refs_9_ = bf16[1,8,512,256]{3,2,1,0:T(8,128)(2,1)} custom-call(s32[1]{0:T(128)} %get-tuple-element.31.flag_ref, s32[2]{0:T(128)S(1)} %pad_add_fusion.side_ref, bf16[1,384,256]{2,1,0:T(8,128)(2,1)} %get-tuple-element.42.refs_0_, bf16[7,256,256]{2,1,0:T(8,128)(2,1)} %get-tuple-element.45.refs_1_, bf16[1,384,256]{2,1,0:T(8,128)(2,1)} %get-tuple-element.47.refs_2_, ...), custom_call_target="tpu_custom_call" | custom-call | flops 4294967296 | bytes 5242880 | tf_op jit(solution)/shard_map/attend/pallas_call | solution.py:579
  49.7 0.0 collective-permute-done.4.refs_3_
  49.7 0.0 collective-permute-done.5.refs_4_
  49.7 10.3 %attend.3 = bf16[1,8,512,256]{3,2,1,0:T(8,128)(2,1)} custom-call(s32[1]{0:T(128)} %get-tuple-element.31.flag_ref, s32[2]{0:T(128)S(1)} %pad_add_fusion.side_ref, bf16[8,256,256]{2,1,0:T(8,128)(2,1)} %get-tuple-element.40.refs_0_, bf16[8,256,256]{2,1,0:T(8,128)(2,1)} %get-tuple-element.41.refs_1_, ...), custom_call_target="tpu_custom_call", output_to_operand_aliasing={{}: (11, {})} | custom-call | flops 4294967296 | bytes 5242880 | tf_op jit(solution)/shard_map/attend/pallas_call | solution.py:579
  (4 shorter events, 0.0 us)
Async XLA Ops:
  0.0 6.5 %copy-start = (bf16[1,8,512,256]{3,2,1,0:T(8,128)(2,1)S(1)}, bf16[1,8,512,256]{3,2,1,0:T(8,128)(2,1)}, u32[]{:S(2)}) copy-start(bf16[1,8,512,256]{3,2,1,0:T(8,128)(2,1)} %state.5) | copy-start | bytes 6291460
  0.0 6.6 %copy-start.3 = (s32[512]{0:T(512)S(1)}, s32[512]{0:T(512)}, u32[]{:S(2)}) copy-start(s32[512]{0:T(512)} %param.13) | copy-start | bytes 6148
  3.8 11.6 %collective-permute-start.2 = (bf16[1536,256]{1,0:T(8,128)(2,1)}, bf16[1536,256]{1,0:T(8,128)(2,1)}, u32[]{:S(2)}, u32[]{:S(2)}) collective-permute-start(bf16[1536,256]{1,0:T(8,128)(2,1)} %get-tuple-element.33), channel_id=1, source_target_pairs={{0,2},{4,6},{8,10},{12,14},{16,18},{20,22},{24,26},{28,30},{2,0},{... | collective-permute-start | bytes 2359304 | tf_op jit(solution)/shard_map/ppermute | solution.py:630
  3.9 11.5 %copy-start.5 = (s32[4,4]{1,0:T(4,128)S(1)}, s32[4,4]{1,0:T(4,128)}, u32[]{:S(2)}) copy-start(s32[4,4]{1,0:T(4,128)} %param.14) | copy-start | bytes 196
  3.9 21.9 %collective-permute-start.1 = (bf16[1536,256]{1,0:T(8,128)(2,1)}, bf16[1536,256]{1,0:T(8,128)(2,1)S(1)}, u32[]{:S(2)}, u32[]{:S(2)}) collective-permute-start(bf16[1536,256]{1,0:T(8,128)(2,1)} %get-tuple-element.32), channel_id=1, source_target_pairs={{2,4},{6,8},{10,12},{14,16},{18,20},{22,24},{26,28},{4,2},{8,6},{1... | collective-permute-start | bytes 2359304 | tf_op jit(solution)/shard_map/ppermute | solution.py:630
  13.7 25.3 %collective-permute-start.6 = (bf16[1008,256]{1,0:T(8,128)(2,1)}, bf16[1008,256]{1,0:T(8,128)(2,1)S(1)}, u32[]{:S(2)}, u32[]{:S(2)}) collective-permute-start(bf16[1008,256]{1,0:T(8,128)(2,1)} %get-tuple-element.49), channel_id=1, source_target_pairs={{0,1},{1,0},{2,3},{3,2},{4,5},{5,4},{6,7},{7,6},{8,9},{9,8},{10,11... | collective-permute-start | bytes 1548296 | tf_op jit(solution)/shard_map/ppermute | solution.py:634
  15.3 10.5 %copy-start.1 = (bf16[1,512,256]{2,1,0:T(8,128)(2,1)S(1)}, bf16[1,512,256]{2,1,0:T(8,128)(2,1)}, u32[]{:S(2)}) copy-start(bf16[1,512,256]{2,1,0:T(8,128)(2,1)} %atm_ref.1) | copy-start | bytes 786436
  15.3 10.5 %copy-start.2 = (bf16[4,4,128,128]{3,2,1,0:T(8,128)(2,1)S(1)}, bf16[4,4,128,128]{3,2,1,0:T(8,128)(2,1)}, u32[]{:S(2)}) copy-start(bf16[4,4,128,128]{3,2,1,0:T(8,128)(2,1)} %remap.1) | copy-start | bytes 1572868
  15.4 10.5 %copy-start.4 = (s32[4]{0:T(128)S(1)}, s32[4]{0:T(128)}, u32[]{:S(2)}) copy-start(s32[4]{0:T(128)} %live_ref.1) | copy-start | bytes 52
  29.5 9.5 %collective-permute-start.3 = (bf16[1,384,256]{2,1,0:T(8,128)(2,1)}, bf16[1,384,256]{2,1,0:T(8,128)(2,1)}, u32[]{:S(2)}, u32[]{:S(2)}) collective-permute-start(bf16[1,384,256]{2,1,0:T(8,128)(2,1)} %get-tuple-element.42.refs_0_), channel_id=1, source_target_pairs={{0,1},{1,0},{2,3},{3,2},{4,5},{5,4},{6,7},{7,6},{8,9},{9,8},{10,11... | collective-permute-start | bytes 589832 | tf_op jit(solution)/shard_map/ppermute | solution.py:634
  31.7 18.0 %collective-permute-start.4 = (bf16[544,256]{1,0:T(8,128)(2,1)}, bf16[544,256]{1,0:T(8,128)(2,1)}, u32[]{:S(2)}, u32[]{:S(2)}) collective-permute-start(bf16[544,256]{1,0:T(8,128)(2,1)} %get-tuple-element.43), channel_id=1, source_target_pairs={{0,1},{1,0},{2,3},{3,2},{4,5},{5,4},{6,7},{7,6},{8,9},{9,8},{10,11... | collective-permute-start | bytes 835592 | tf_op jit(solution)/shard_map/ppermute | solution.py:634
  37.4 12.3 %collective-permute-start.5 = (bf16[672,256]{1,0:T(8,128)(2,1)}, bf16[672,256]{1,0:T(8,128)(2,1)S(1)}, u32[]{:S(2)}, u32[]{:S(2)}) collective-permute-start(bf16[672,256]{1,0:T(8,128)(2,1)} %get-tuple-element.44), channel_id=1, source_target_pairs={{0,1},{1,0},{2,3},{3,2},{4,5},{5,4},{6,7},{7,6},{8,9},{9,8},{10,11... | collective-permute-start | bytes 1032200 | tf_op jit(solution)/shard_map/ppermute | solution.py:634

commit v12 on v10

--- a/solution.py
+++ b/solution.py
@@ -242,6 +242,8 @@
     off_hbm,
     atm_ref,
     remap,
+    qkv_ref,
+    wo_ref,
     base_hbm,
     edge_mixed_in,
     edge_normed_in,
@@ -461,7 +463,7 @@
             limit = source.shape[0] - count - 16
             wet, rank, _ = plans[step]
             if 0 not in place[step]:
-                at = 0 if edges else step * count
+                at = surf[o].shape[1] - count if edges else step * count
                 token_ref[step, 0] = surf[o][0, at : at + count]
             for l, at in place[step].items():
                 token_ref[step, l] = unpack(window, wet[l : l + 1], rank[l : l + 1], at, limit)
@@ -557,8 +559,6 @@
     vmem = pl.BlockSpec(memory_space=pltpu.VMEM)
     smem = pl.BlockSpec(memory_space=pltpu.SMEM)
     stay = lambda x: pltpu.with_memory_space_constraint(x, pltpu.HBM)
-    if edges:
-        surf = [x[:, shape[2] - 2 * cols :] for x in surf]
     in_specs = [smem] * 2 + [hbm] * (2 * nparts) + [vmem] * (len(surf) + len(packed))
     in_specs += [hbm] * others + [vmem] * 3
     args = [flag, side] + [stay(x) for x in normed + mixed] + surf + packed
@@ -719,7 +719,7 @@
     ids = jnp.clip(src_blocks - (tile - R) * atm_blk, 0, 3 * atm_blk - 1)
     surf_mixed, surf_normed, far_forcing, edge_mixed, edge_normed = pl.pallas_call(
         surface_kernel,
-        in_specs=[smem] * 3 + [vmem] + [anywhere] * 2 + [vmem] * 2 + [hbm] * 3,
+        in_specs=[smem] * 3 + [vmem] + [anywhere] * 2 + [vmem] * 4 + [hbm] * 3,
         out_specs=[whole_spec(1, inner + cols, width)] * 2 + [whole_spec(cols, width)] + [hbm] * 2,
         out_shape=[tok(1, inner + cols), tok(1, inner + cols), row_f32]
         + [tok(lev, 2 * cols)] * 2,
@@ -729,7 +729,7 @@
             pltpu.VMEM((rows, cols, width), F32),
             dma((5,)),
         ],
-        input_output_aliases={9: 3, 10: 4},
+        input_output_aliases={11: 3, 12: 4},
         compiler_params=params(12),
         cost_estimate=cost(conv_flops(1, inner), cells * width * 16),
         name="surface",
@@ -742,6 +742,8 @@
         off_halo,
         atm_latent,
         remap_weight,
+        qkv_weight,
+        out_weight,
         stay(base),
         stay(edge_mixed),
         stay(edge_normed),

time: 59.7 us -> 59.2 us (level)
  local copies, waits for them, and re-layouts: 1.03 us -> 0.04 us
    unnamed x18 -> x16, local copies, waits for them, and re-layouts: 1.02 us -> 0.04 us
  transfers between devices with their start and end apart: 6 -> 6, of which waited for: 1 -> 1; matrix products, arithmetic and copies ran while one was open for 0% -> 0% of each run, Pallas kernels for 54% -> 55%
where the time goes in v12:
time: 59.2 us; the launch traced here: 58.5 us
  Pallas kernels  45.2 us (76%)
  starting transfers between devices  8.05 us (14%)
  waiting for transfers between devices  4.22 us (7%)
  between operations  0.9 us (2%)
    pallas_call x2, Pallas kernels, attend(): pl.pallas_call(functools.partial(attend_kernel, others, nparts, edges), i...  19.2 us
    pallas_call x2, Pallas kernels, row_conv(): pl.pallas_call(functools.partial(row_kernel, cap, first, which), in_specs...  11.4 us
    pallas_call x1, Pallas kernels, body(): pl.pallas_call(functools.partial(inner_kernel, deep_cap), in_specs=[vmem,...  7.18 us
    ppermute x4, starting transfers between devices, exchange(): lax.ppermute(x, 'mem', [(i, (i + k) % members) for i in range(members)])  5.33 us
    ppermute x2, waiting for transfers between devices, swap(): return lax.ppermute(x, 'tile', pairs + [(b, a) for a, b in pairs])  4.21 us
    pallas_call x1, Pallas kernels, body(): pl.pallas_call(surface_kernel, in_specs=[smem] * 3 + [vmem] + [anywhere]...  3.72 us
    pallas_call x1, Pallas kernels, body(): pl.pallas_call(functools.partial(prep_kernel, (deep_cap, near_cap, far_ca...  3.7 us
    ppermute x2, starting transfers between devices, swap(): return lax.ppermute(x, 'tile', pairs + [(b, a) for a, b in pairs])  2.72 us
  transfers between devices with their start and end apart: 6, of which 1 were waited for; matrix products, arithmetic and copies ran while one was open for 0% of the time, Pallas kernels for 55%

profile of v12, /device:TPU:18, one launch (start us, length us, event | category | flops | bytes accessed | tf_op | source)
XLA Modules:
  0.0 58.5 jit_solution(10698353158267828691)
XLA Ops:
  0.0 0.1 pad_add_fusion.side_ref
  0.1 3.7 %prep.1 = (bf16[1536,256]{1,0:T(8,128)(2,1)}, bf16[1536,256]{1,0:T(8,128)(2,1)}, s32[1]{0:T(128)}) custom-call(s32[2]{0:T(128)S(1)} %pad_add_fusion.side_ref, bf16[1,8,512,256]{3,2,1,0:T(8,128)(2,1)} %state.5, bf16[1,512,256]{2,1,0:T(8,128)(2,1)} %atm_ref.1, s32[4,128]{1,0:T(4,128)} %bitcast.8), custom_call_target="tpu_custom_call" | custom-call | flops 1048576 | bytes 2621440 | tf_op jit(solution)/shard_map/prep/pallas_call | solution.py:647
  3.8 0.1 collective-permute-start.2
  3.9 0.0 copy-start.7
  3.9 2.7 %collective-permute-start.1 = (bf16[1536,256]{1,0:T(8,128)(2,1)}, bf16[1536,256]{1,0:T(8,128)(2,1)S(1)}, u32[]{:S(2)}, u32[]{:S(2)}) collective-permute-start(bf16[1536,256]{1,0:T(8,128)(2,1)} %get-tuple-element.32), channel_id=1, source_target_pairs={{2,4},{6,8},{10,12},{14,16},{18,20},{22,24},{26,28},{4,2},{8,6},{1... | collective-permute-start | bytes 2359304 | tf_op jit(solution)/shard_map/ppermute | solution.py:622
  6.5 0.0 copy-done
  6.6 0.0 copy-done.5
  6.6 7.2 %inner.1 = (bf16[7,256,256]{2,1,0:T(8,128)(2,1)}, bf16[7,256,256]{2,1,0:T(8,128)(2,1)}, bf16[1008,256]{1,0:T(8,128)(2,1)}) custom-call(bf16[1,8,512,256]{3,2,1,0:T(8,128)(2,1)S(1)} %copy-done, s32[4,128]{1,0:T(4,128)S(1)} %bitcast.9, bf16[3,3,256,256]{3,2,1,0:T(8,128)(2,1)} %weight_hbm.5), custom_call_target="tpu_custom_call" | custom-call | flops 2415919104 | bytes 4194304 | tf_op jit(solution)/shard_map/inner/pallas_call | solution.py:668
  13.8 1.6 %collective-permute-start.6 = (bf16[1008,256]{1,0:T(8,128)(2,1)}, bf16[1008,256]{1,0:T(8,128)(2,1)}, u32[]{:S(2)}, u32[]{:S(2)}) collective-permute-start(bf16[1008,256]{1,0:T(8,128)(2,1)} %get-tuple-element.49), channel_id=1, source_target_pairs={{0,1},{1,0},{2,3},{3,2},{4,5},{5,4},{6,7},{7,6},{8,9},{9,8},{10,11... | collective-permute-start | bytes 1548296 | tf_op jit(solution)/shard_map/ppermute | solution.py:626
  15.3 0.0 copy-done.7
  15.4 0.0 copy-start.2
  15.4 0.0 copy-start.3
  15.4 0.0 copy-start.4
  15.4 0.0 copy-start.6
  15.4 0.0 collective-permute-done.2.halo_hbm.on_hbm
  15.4 6.2 %row.2 = (bf16[8,256,256]{2,1,0:T(8,128)(2,1)}, bf16[8,256,256]{2,1,0:T(8,128)(2,1)}, bf16[544,256]{1,0:T(8,128)(2,1)}, f32[384,256]{1,0:T(8,128)}) custom-call(s32[2]{0:T(128)S(1)} %pad_add_fusion.side_ref, bf16[1,8,512,256]{3,2,1,0:T(8,128)(2,1)S(1)} %copy-done, s32[4,128]{1,0:T(4,128)S(1)} %bitcast.10, bf16[3,3,256,256]{3,2,1,0:T(8,128)(2,1)} %weight_hbm.5, ...), custom_call_target="tpu_custom_call" | custom-call | flops 1207959552 | bytes 4194304 | tf_op jit(solution)/shard_map/row/pallas_call | solution.py:694
  21.6 4.2 %collective-permute-done.1.off_hbm.halo_hbm = bf16[1536,256]{1,0:T(8,128)(2,1)S(1)} collective-permute-done((bf16[1536,256]{1,0:T(8,128)(2,1)}, bf16[1536,256]{1,0:T(8,128)(2,1)S(1)}, u32[]{:S(2)}, u32[]{:S(2)}) %collective-permute-start.1) | collective-permute-done | bytes 786464 | tf_op jit(solution)/shard_map/ppermute | solution.py:622
  25.8 0.0 copy-done.1
  25.8 0.0 copy-done.2
  25.8 0.0 copy-done.3
  25.8 0.0 copy-done.4
  25.9 3.7 %surface.1 = (bf16[1,384,256]{2,1,0:T(8,128)(2,1)}, bf16[1,384,256]{2,1,0:T(8,128)(2,1)}, f32[128,256]{1,0:T(8,128)}, bf16[8,256,256]{2,1,0:T(8,128)(2,1)}, bf16[8,256,256]{2,1,0:T(8,128)(2,1)}) custom-call(s32[4,4]{1,0:T(4,128)S(1)} %subtract_clamp_fusion.ids_ref, s32[4]{0:T(128)S(1)} %copy-done.6, ...), custom_call_target="tpu_custom_call", output_to_operand_aliasing={{3}: (11, {}), {4}: (12, {})} | custom-call | flops 301989888 | bytes 2097152 | tf_op jit(solution)/shard_map/surface/pallas_call | solution.py:720
  29.6 1.6 %collective-permute-start.3 = (bf16[1,384,256]{2,1,0:T(8,128)(2,1)}, bf16[1,384,256]{2,1,0:T(8,128)(2,1)}, u32[]{:S(2)}, u32[]{:S(2)}) collective-permute-start(bf16[1,384,256]{2,1,0:T(8,128)(2,1)} %get-tuple-element.42.refs_0_), channel_id=1, source_target_pairs={{0,1},{1,0},{2,3},{3,2},{4,5},{5,4},{6,7},{7,6},{8,9},{9,8},{10,11... | collective-permute-start | bytes 589832 | tf_op jit(solution)/shard_map/ppermute | solution.py:626
  31.7 0.6 collective-permute-start.4
  32.3 5.2 %row.3 = (bf16[8,256,256]{2,1,0:T(8,128)(2,1)}, bf16[8,256,256]{2,1,0:T(8,128)(2,1)}, bf16[672,256]{1,0:T(8,128)(2,1)}) custom-call(s32[2]{0:T(128)S(1)} %pad_add_fusion.side_ref, bf16[1,8,512,256]{3,2,1,0:T(8,128)(2,1)S(1)} %copy-done, s32[4,128]{1,0:T(4,128)S(1)} %bitcast.12, ...), custom_call_target="tpu_custom_call", output_to_operand_aliasing={{0}: (6, {}), {1}: (7, {})} | custom-call | flops 1207959552 | bytes 4194304 | tf_op jit(solution)/shard_map/row/pallas_call | solution.py:694
  37.5 1.6 %collective-permute-start.5 = (bf16[672,256]{1,0:T(8,128)(2,1)}, bf16[672,256]{1,0:T(8,128)(2,1)S(1)}, u32[]{:S(2)}, u32[]{:S(2)}) collective-permute-start(bf16[672,256]{1,0:T(8,128)(2,1)} %get-tuple-element.44), channel_id=1, source_target_pairs={{0,1},{1,0},{2,3},{3,2},{4,5},{5,4},{6,7},{7,6},{8,9},{9,8},{10,11... | collective-permute-start | bytes 1032200 | tf_op jit(solution)/shard_map/ppermute | solution.py:626
  39.1 0.0 collective-permute-done.6.refs_5_
  39.1 0.0 collective-permute-done.3.refs_4_.refs_2_
  39.1 9.7 %attend.2.refs_9_ = bf16[1,8,512,256]{3,2,1,0:T(8,128)(2,1)} custom-call(s32[1]{0:T(128)} %get-tuple-element.31.flag_ref, s32[2]{0:T(128)S(1)} %pad_add_fusion.side_ref, bf16[1,384,256]{2,1,0:T(8,128)(2,1)} %get-tuple-element.42.refs_0_, bf16[7,256,256]{2,1,0:T(8,128)(2,1)} %get-tuple-element.45.refs_1_, bf16[1,384,256]{2,1,0:T(8,128)(2,1)} %get-tuple-element.47.refs_2_, ...), custom_call_target="tpu_custom_call" | custom-call | flops 4294967296 | bytes 5242880 | tf_op jit(solution)/shard_map/attend/pallas_call | solution.py:574
  48.8 0.0 collective-permute-done.4.refs_3_
  48.8 0.0 collective-permute-done.5.refs_4_
  48.8 9.5 %attend.3 = bf16[1,8,512,256]{3,2,1,0:T(8,128)(2,1)} custom-call(s32[1]{0:T(128)} %get-tuple-element.31.flag_ref, s32[2]{0:T(128)S(1)} %pad_add_fusion.side_ref, bf16[8,256,256]{2,1,0:T(8,128)(2,1)} %get-tuple-element.40.refs_0_, bf16[8,256,256]{2,1,0:T(8,128)(2,1)} %get-tuple-element.41.refs_1_, ...), custom_call_target="tpu_custom_call", output_to_operand_aliasing={{}: (11, {})} | custom-call | flops 4294967296 | bytes 5242880 | tf_op jit(solution)/shard_map/attend/pallas_call | solution.py:574
  (8 shorter events, 0.0 us)
Async XLA Ops:
  0.0 6.5 %copy-start = (bf16[1,8,512,256]{3,2,1,0:T(8,128)(2,1)S(1)}, bf16[1,8,512,256]{3,2,1,0:T(8,128)(2,1)}, u32[]{:S(2)}) copy-start(bf16[1,8,512,256]{3,2,1,0:T(8,128)(2,1)} %state.5) | copy-start | bytes 6291460
  0.0 6.6 %copy-start.5 = (s32[512]{0:T(512)S(1)}, s32[512]{0:T(512)}, u32[]{:S(2)}) copy-start(s32[512]{0:T(512)} %param.13) | copy-start | bytes 6148
  3.8 11.6 %collective-permute-start.2 = (bf16[1536,256]{1,0:T(8,128)(2,1)}, bf16[1536,256]{1,0:T(8,128)(2,1)}, u32[]{:S(2)}, u32[]{:S(2)}) collective-permute-start(bf16[1536,256]{1,0:T(8,128)(2,1)} %get-tuple-element.33), channel_id=1, source_target_pairs={{0,2},{4,6},{8,10},{12,14},{16,18},{20,22},{24,26},{28,30},{2,0},{... | collective-permute-start | bytes 2359304 | tf_op jit(solution)/shard_map/ppermute | solution.py:622
  3.9 11.5 %copy-start.7 = (s32[4,4]{1,0:T(4,128)S(1)}, s32[4,4]{1,0:T(4,128)}, u32[]{:S(2)}) copy-start(s32[4,4]{1,0:T(4,128)} %param.14) | copy-start | bytes 196
  3.9 21.9 %collective-permute-start.1 = (bf16[1536,256]{1,0:T(8,128)(2,1)}, bf16[1536,256]{1,0:T(8,128)(2,1)S(1)}, u32[]{:S(2)}, u32[]{:S(2)}) collective-permute-start(bf16[1536,256]{1,0:T(8,128)(2,1)} %get-tuple-element.32), channel_id=1, source_target_pairs={{2,4},{6,8},{10,12},{14,16},{18,20},{22,24},{26,28},{4,2},{8,6},{1... | collective-permute-start | bytes 2359304 | tf_op jit(solution)/shard_map/ppermute | solution.py:622
  13.8 25.3 %collective-permute-start.6 = (bf16[1008,256]{1,0:T(8,128)(2,1)}, bf16[1008,256]{1,0:T(8,128)(2,1)}, u32[]{:S(2)}, u32[]{:S(2)}) collective-permute-start(bf16[1008,256]{1,0:T(8,128)(2,1)} %get-tuple-element.49), channel_id=1, source_target_pairs={{0,1},{1,0},{2,3},{3,2},{4,5},{5,4},{6,7},{7,6},{8,9},{9,8},{10,11... | collective-permute-start | bytes 1548296 | tf_op jit(solution)/shard_map/ppermute | solution.py:626
  15.3 10.5 %copy-start.1 = (bf16[1,512,256]{2,1,0:T(8,128)(2,1)S(1)}, bf16[1,512,256]{2,1,0:T(8,128)(2,1)}, u32[]{:S(2)}) copy-start(bf16[1,512,256]{2,1,0:T(8,128)(2,1)} %atm_ref.1) | copy-start | bytes 786436
  15.4 10.5 %copy-start.2 = (bf16[4,4,128,128]{3,2,1,0:T(8,128)(2,1)S(1)}, bf16[4,4,128,128]{3,2,1,0:T(8,128)(2,1)}, u32[]{:S(2)}) copy-start(bf16[4,4,128,128]{3,2,1,0:T(8,128)(2,1)} %remap.1) | copy-start | bytes 1572868
  15.4 10.5 %copy-start.3 = (bf16[256,768]{1,0:T(8,128)(2,1)S(1)}, bf16[256,768]{1,0:T(8,128)(2,1)}, u32[]{:S(2)}) copy-start(bf16[256,768]{1,0:T(8,128)(2,1)} %refs_7_.1) | copy-start | bytes 1179652
  15.4 10.5 %copy-start.4 = (bf16[256,256]{1,0:T(8,128)(2,1)S(1)}, bf16[256,256]{1,0:T(8,128)(2,1)}, u32[]{:S(2)}) copy-start(bf16[256,256]{1,0:T(8,128)(2,1)} %refs_8_.3) | copy-start | bytes 393220
  15.4 10.5 %copy-start.6 = (s32[4]{0:T(128)S(1)}, s32[4]{0:T(128)}, u32[]{:S(2)}) copy-start(s32[4]{0:T(128)} %live_ref.1) | copy-start | bytes 52
  29.6 9.5 %collective-permute-start.3 = (bf16[1,384,256]{2,1,0:T(8,128)(2,1)}, bf16[1,384,256]{2,1,0:T(8,128)(2,1)}, u32[]{:S(2)}, u32[]{:S(2)}) collective-permute-start(bf16[1,384,256]{2,1,0:T(8,128)(2,1)} %get-tuple-element.42.refs_0_), channel_id=1, source_target_pairs={{0,1},{1,0},{2,3},{3,2},{4,5},{5,4},{6,7},{7,6},{8,9},{9,8},{10,11... | collective-permute-start | bytes 589832 | tf_op jit(solution)/shard_map/ppermute | solution.py:626
  31.7 17.0 %collective-permute-start.4 = (bf16[544,256]{1,0:T(8,128)(2,1)}, bf16[544,256]{1,0:T(8,128)(2,1)}, u32[]{:S(2)}, u32[]{:S(2)}) collective-permute-start(bf16[544,256]{1,0:T(8,128)(2,1)} %get-tuple-element.43), channel_id=1, source_target_pairs={{0,1},{1,0},{2,3},{3,2},{4,5},{5,4},{6,7},{7,6},{8,9},{9,8},{10,11... | collective-permute-start | bytes 835592 | tf_op jit(solution)/shard_map/ppermute | solution.py:626
  37.5 11.3 %collective-permute-start.5 = (bf16[672,256]{1,0:T(8,128)(2,1)}, bf16[672,256]{1,0:T(8,128)(2,1)S(1)}, u32[]{:S(2)}, u32[]{:S(2)}) collective-permute-start(bf16[672,256]{1,0:T(8,128)(2,1)} %get-tuple-element.44), channel_id=1, source_target_pairs={{0,1},{1,0},{2,3},{3,2},{4,5},{5,4},{6,7},{7,6},{8,9},{9,8},{10,11... | collective-permute-start | bytes 1032200 | tf_op jit(solution)/shard_map/ppermute | solution.py:626

commit v13 on v12

--- a/solution.py
+++ b/solution.py
@@ -285,13 +285,17 @@
     for copy in copies:
         copy.wait()
     for b in range(blocks):
-        acc = jnp.zeros((cols, width), F32)
+        weights, picked = [], []
         for p in range(pairs):
-            on = (p < live_ref[b]).astype(F32)
+            on = jnp.where(p < live_ref[b], 1.0, 0.0)
+            weights.append(remap[b, p] * jnp.full((1, cols), on, F32).astype(BF16))
             start = pl.multiple_of(ids_ref[b, p] * cols, cols)
-            acc = acc + on * jnp.dot(
-                remap[b, p], window[pl.ds(start, cols), :], preferred_element_type=F32
-            )
+            picked.append(window[pl.ds(start, cols), :])
+        acc = jnp.dot(
+            jnp.concatenate(weights, axis=1),
+            jnp.concatenate(picked, axis=0),
+            preferred_element_type=F32,
+        )
         forcing_ref[b] = acc
     for k, wet in enumerate(wets):
         at = slice(k * cols, (k + 1) * cols)
@@ -311,7 +315,7 @@
         store.wait()
 
 
-def row_kernel(cap, first, which, side_ref, state, depth_ref, weight_hbm, halo_hbm, *refs):
+def row_kernel(cap, first, which, side_ref, state, depth_ref, weight_in, halo_hbm, *refs):
     refs = list(refs)
     forcing_hbm = None
     if not first:
@@ -321,8 +325,11 @@
     refs = refs[3:]
     base_ref = refs.pop(0) if first else None
     forcing_ref, weight, tap, mixed, normed, packed, weight_sem, halo_sem, out_sem, packed_sem = refs
-    load = pltpu.make_async_copy(weight_hbm, weight, weight_sem)
-    load.start()
+    if first:
+        load = pltpu.make_async_copy(weight_in, weight, weight_sem)
+        load.start()
+    else:
+        weight = weight_in
     _, lev, cells, width = state.shape
     rows, cols = depth_ref.shape
     row = side_ref[which]
@@ -357,7 +364,8 @@
         )
     stores = []
     half = lev // 2
-    load.wait()
+    if first:
+        load.wait()
     halo.wait()
     if not first:
         forcing.wait()
@@ -693,7 +701,7 @@
         base = pltpu.HBM((inner + cols, width), F32)
         return pl.pallas_call(
             functools.partial(row_kernel, cap, first, which),
-            in_specs=[smem, vmem, vmem, hbm, anywhere] + [hbm] * len(extra),
+            in_specs=[smem, vmem, vmem, hbm if first else vmem, anywhere] + [hbm] * len(extra),
             out_specs=[hbm] * 3 + [whole_spec(inner + cols, width)] * first,
             out_shape=[tok(lev, 2 * cols), tok(lev, 2 * cols), tok(cap)] + [base] * first,
             scratch_shapes=[
@@ -712,7 +720,14 @@
             compiler_params=params(12),
             cost_estimate=cost(conv_flops(lev, cols), lev * cols * width * 16),
             name="row",
-        )(side, ocean_state, depth, stay(conv_weight), halo, *[stay(x) for x in extra])
+        )(
+            side,
+            ocean_state,
+            depth,
+            stay(conv_weight) if first else conv_weight,
+            halo,
+            *[stay(x) for x in extra],
+        )
 
     edge_mixed, edge_normed, near_packed, base = row_conv(0, 1, near_cap, on_halo, [])
 

time: 59.2 us -> 59.2 us (level)
  transfers between devices with their start and end apart: 6 -> 6, of which waited for: 1 -> 1; matrix products, arithmetic and copies ran while one was open for 0% -> 0% of each run, Pallas kernels for 55% -> 54%
where the time goes in v13:
time: 59.2 us; the launch traced here: 58.5 us
  Pallas kernels  45 us (76%)
  starting transfers between devices  8.06 us (14%)
  waiting for transfers between devices  4.27 us (7%)
  between operations  0.97 us (2%)
    pallas_call x2, Pallas kernels, attend(): pl.pallas_call(functools.partial(attend_kernel, others, nparts, edges), i...  19.3 us
    pallas_call x2, Pallas kernels, row_conv(): pl.pallas_call(functools.partial(row_kernel, cap, first, which), in_specs...  11.2 us
    pallas_call x1, Pallas kernels, body(): pl.pallas_call(functools.partial(inner_kernel, deep_cap), in_specs=[vmem,...  7.16 us
    ppermute x4, starting transfers between devices, exchange(): lax.ppermute(x, 'mem', [(i, (i + k) % members) for i in range(members)])  5.33 us
    ppermute x2, waiting for transfers between devices, swap(): return lax.ppermute(x, 'tile', pairs + [(b, a) for a, b in pairs])  4.26 us
    pallas_call x1, Pallas kernels, body(): pl.pallas_call(functools.partial(prep_kernel, (deep_cap, near_cap, far_ca...  3.7 us
    pallas_call x1, Pallas kernels, body(): pl.pallas_call(surface_kernel, in_specs=[smem] * 3 + [vmem] + [anywhere]...  3.61 us
    ppermute x2, starting transfers between devices, swap(): return lax.ppermute(x, 'tile', pairs + [(b, a) for a, b in pairs])  2.72 us
  transfers between devices with their start and end apart: 6, of which 1 were waited for; matrix products, arithmetic and copies ran while one was open for 0% of the time, Pallas kernels for 54%

profile of v13, /device:TPU:18, one launch (start us, length us, event | category | flops | bytes accessed | tf_op | source)
XLA Modules:
  0.0 58.5 jit_solution(6548540334438874338)
XLA Ops:
  0.0 0.1 pad_add_fusion.side_ref
  0.1 3.7 %prep.1 = (bf16[1536,256]{1,0:T(8,128)(2,1)}, bf16[1536,256]{1,0:T(8,128)(2,1)}, s32[1]{0:T(128)}) custom-call(s32[2]{0:T(128)S(1)} %pad_add_fusion.side_ref, bf16[1,8,512,256]{3,2,1,0:T(8,128)(2,1)} %state.5, bf16[1,512,256]{2,1,0:T(8,128)(2,1)} %atm_ref.1, s32[4,128]{1,0:T(4,128)} %bitcast.8), custom_call_target="tpu_custom_call" | custom-call | flops 1048576 | bytes 2621440 | tf_op jit(solution)/shard_map/prep/pallas_call | solution.py:655
  3.8 0.1 collective-permute-start.2
  3.9 0.0 copy-start.8
  3.9 2.7 %collective-permute-start.1 = (bf16[1536,256]{1,0:T(8,128)(2,1)}, bf16[1536,256]{1,0:T(8,128)(2,1)S(1)}, u32[]{:S(2)}, u32[]{:S(2)}) collective-permute-start(bf16[1536,256]{1,0:T(8,128)(2,1)} %get-tuple-element.32), channel_id=1, source_target_pairs={{2,4},{6,8},{10,12},{14,16},{18,20},{22,24},{26,28},{4,2},{8,6},{1... | collective-permute-start | bytes 2359304 | tf_op jit(solution)/shard_map/ppermute | solution.py:630
  6.5 0.0 copy-done
  6.6 0.0 copy-done.6
  6.6 7.2 %inner.1 = (bf16[7,256,256]{2,1,0:T(8,128)(2,1)}, bf16[7,256,256]{2,1,0:T(8,128)(2,1)}, bf16[1008,256]{1,0:T(8,128)(2,1)}) custom-call(bf16[1,8,512,256]{3,2,1,0:T(8,128)(2,1)S(1)} %copy-done, s32[4,128]{1,0:T(4,128)S(1)} %bitcast.9, bf16[3,3,256,256]{3,2,1,0:T(8,128)(2,1)} %weight_hbm.1), custom_call_target="tpu_custom_call" | custom-call | flops 2415919104 | bytes 4194304 | tf_op jit(solution)/shard_map/inner/pallas_call | solution.py:676
  13.7 1.6 %collective-permute-start.6 = (bf16[1008,256]{1,0:T(8,128)(2,1)}, bf16[1008,256]{1,0:T(8,128)(2,1)}, u32[]{:S(2)}, u32[]{:S(2)}) collective-permute-start(bf16[1008,256]{1,0:T(8,128)(2,1)} %get-tuple-element.49), channel_id=1, source_target_pairs={{0,1},{1,0},{2,3},{3,2},{4,5},{5,4},{6,7},{7,6},{8,9},{9,8},{10,11... | collective-permute-start | bytes 1548296 | tf_op jit(solution)/shard_map/ppermute | solution.py:634
  15.3 0.0 copy-done.8
  15.3 0.0 copy-start.3
  15.4 0.0 copy-start.4
  15.4 0.0 copy-start.5
  15.4 0.0 copy-start.7
  15.4 0.0 collective-permute-done.2.halo_hbm.on_hbm
  15.4 6.2 %row.2 = (bf16[8,256,256]{2,1,0:T(8,128)(2,1)}, bf16[8,256,256]{2,1,0:T(8,128)(2,1)}, bf16[544,256]{1,0:T(8,128)(2,1)}, f32[384,256]{1,0:T(8,128)}) custom-call(s32[2]{0:T(128)S(1)} %pad_add_fusion.side_ref, bf16[1,8,512,256]{3,2,1,0:T(8,128)(2,1)S(1)} %copy-done, s32[4,128]{1,0:T(4,128)S(1)} %bitcast.10, bf16[3,3,256,256]{3,2,1,0:T(8,128)(2,1)} %weight_hbm.1, ...), custom_call_target="tpu_custom_call" | custom-call | flops 1207959552 | bytes 4194304 | tf_op jit(solution)/shard_map/row/pallas_call | solution.py:702
  21.6 4.3 %collective-permute-done.1.off_hbm.halo_hbm = bf16[1536,256]{1,0:T(8,128)(2,1)S(1)} collective-permute-done((bf16[1536,256]{1,0:T(8,128)(2,1)}, bf16[1536,256]{1,0:T(8,128)(2,1)S(1)}, u32[]{:S(2)}, u32[]{:S(2)}) %collective-permute-start.1) | collective-permute-done | bytes 786464 | tf_op jit(solution)/shard_map/ppermute | solution.py:630
  25.8 0.0 copy-done.2
  25.8 0.0 copy-done.5
  25.9 0.0 copy-done.7
  25.9 0.0 copy-start.1
  25.9 3.6 %surface.1 = (bf16[1,384,256]{2,1,0:T(8,128)(2,1)}, bf16[1,384,256]{2,1,0:T(8,128)(2,1)}, f32[128,256]{1,0:T(8,128)}, bf16[8,256,256]{2,1,0:T(8,128)(2,1)}, bf16[8,256,256]{2,1,0:T(8,128)(2,1)}) custom-call(s32[4,4]{1,0:T(4,128)S(1)} %subtract_clamp_fusion.ids_ref, s32[4]{0:T(128)S(1)} %copy-done.7, ...), custom_call_target="tpu_custom_call", output_to_operand_aliasing={{3}: (11, {}), {4}: (12, {})} | custom-call | flops 301989888 | bytes 2097152 | tf_op jit(solution)/shard_map/surface/pallas_call | solution.py:735
  29.5 1.6 %collective-permute-start.3 = (bf16[1,384,256]{2,1,0:T(8,128)(2,1)}, bf16[1,384,256]{2,1,0:T(8,128)(2,1)}, u32[]{:S(2)}, u32[]{:S(2)}) collective-permute-start(bf16[1,384,256]{2,1,0:T(8,128)(2,1)} %get-tuple-element.42.refs_0_), channel_id=1, source_target_pairs={{0,1},{1,0},{2,3},{3,2},{4,5},{5,4},{6,7},{7,6},{8,9},{9,8},{10,11... | collective-permute-start | bytes 589832 | tf_op jit(solution)/shard_map/ppermute | solution.py:634
  31.7 0.6 collective-permute-start.4
  32.3 5.0 %row.3 = (bf16[8,256,256]{2,1,0:T(8,128)(2,1)}, bf16[8,256,256]{2,1,0:T(8,128)(2,1)}, bf16[672,256]{1,0:T(8,128)(2,1)}) custom-call(s32[2]{0:T(128)S(1)} %pad_add_fusion.side_ref, bf16[1,8,512,256]{3,2,1,0:T(8,128)(2,1)S(1)} %copy-done, s32[4,128]{1,0:T(4,128)S(1)} %bitcast.12, ...), custom_call_target="tpu_custom_call", output_to_operand_aliasing={{0}: (6, {}), {1}: (7, {})} | custom-call | flops 1207959552 | bytes 4194304 | tf_op jit(solution)/shard_map/row/pallas_call | solution.py:702
  37.3 1.6 %collective-permute-start.5 = (bf16[672,256]{1,0:T(8,128)(2,1)}, bf16[672,256]{1,0:T(8,128)(2,1)S(1)}, u32[]{:S(2)}, u32[]{:S(2)}) collective-permute-start(bf16[672,256]{1,0:T(8,128)(2,1)} %get-tuple-element.44), channel_id=1, source_target_pairs={{0,1},{1,0},{2,3},{3,2},{4,5},{5,4},{6,7},{7,6},{8,9},{9,8},{10,11... | collective-permute-start | bytes 1032200 | tf_op jit(solution)/shard_map/ppermute | solution.py:634
  38.9 0.0 collective-permute-done.6.refs_5_
  38.9 0.0 collective-permute-done.3.refs_4_.refs_2_
  38.9 9.7 %attend.2.refs_9_ = bf16[1,8,512,256]{3,2,1,0:T(8,128)(2,1)} custom-call(s32[1]{0:T(128)} %get-tuple-element.31.flag_ref, s32[2]{0:T(128)S(1)} %pad_add_fusion.side_ref, bf16[1,384,256]{2,1,0:T(8,128)(2,1)} %get-tuple-element.42.refs_0_, bf16[7,256,256]{2,1,0:T(8,128)(2,1)} %get-tuple-element.45.refs_1_, bf16[1,384,256]{2,1,0:T(8,128)(2,1)} %get-tuple-element.47.refs_2_, ...), custom_call_target="tpu_custom_call" | custom-call | flops 4294967296 | bytes 5242880 | tf_op jit(solution)/shard_map/attend/pallas_call | solution.py:582
  48.7 0.0 collective-permute-done.4.refs_3_
  48.7 0.0 collective-permute-done.5.refs_4_
  48.7 9.6 %attend.3 = bf16[1,8,512,256]{3,2,1,0:T(8,128)(2,1)} custom-call(s32[1]{0:T(128)} %get-tuple-element.31.flag_ref, s32[2]{0:T(128)S(1)} %pad_add_fusion.side_ref, bf16[8,256,256]{2,1,0:T(8,128)(2,1)} %get-tuple-element.40.refs_0_, bf16[8,256,256]{2,1,0:T(8,128)(2,1)} %get-tuple-element.41.refs_1_, ...), custom_call_target="tpu_custom_call", output_to_operand_aliasing={{}: (11, {})} | custom-call | flops 4294967296 | bytes 5242880 | tf_op jit(solution)/shard_map/attend/pallas_call | solution.py:582
  (10 shorter events, 0.0 us)
Async XLA Ops:
  0.0 6.5 %copy-start = (bf16[1,8,512,256]{3,2,1,0:T(8,128)(2,1)S(1)}, bf16[1,8,512,256]{3,2,1,0:T(8,128)(2,1)}, u32[]{:S(2)}) copy-start(bf16[1,8,512,256]{3,2,1,0:T(8,128)(2,1)} %state.5) | copy-start | bytes 6291460
  0.0 6.6 %copy-start.6 = (s32[512]{0:T(512)S(1)}, s32[512]{0:T(512)}, u32[]{:S(2)}) copy-start(s32[512]{0:T(512)} %param.13) | copy-start | bytes 6148
  3.8 11.6 %collective-permute-start.2 = (bf16[1536,256]{1,0:T(8,128)(2,1)}, bf16[1536,256]{1,0:T(8,128)(2,1)}, u32[]{:S(2)}, u32[]{:S(2)}) collective-permute-start(bf16[1536,256]{1,0:T(8,128)(2,1)} %get-tuple-element.33), channel_id=1, source_target_pairs={{0,2},{4,6},{8,10},{12,14},{16,18},{20,22},{24,26},{28,30},{2,0},{... | collective-permute-start | bytes 2359304 | tf_op jit(solution)/shard_map/ppermute | solution.py:630
  3.9 11.5 %copy-start.8 = (s32[4,4]{1,0:T(4,128)S(1)}, s32[4,4]{1,0:T(4,128)}, u32[]{:S(2)}) copy-start(s32[4,4]{1,0:T(4,128)} %param.14) | copy-start | bytes 196
  3.9 21.9 %collective-permute-start.1 = (bf16[1536,256]{1,0:T(8,128)(2,1)}, bf16[1536,256]{1,0:T(8,128)(2,1)S(1)}, u32[]{:S(2)}, u32[]{:S(2)}) collective-permute-start(bf16[1536,256]{1,0:T(8,128)(2,1)} %get-tuple-element.32), channel_id=1, source_target_pairs={{2,4},{6,8},{10,12},{14,16},{18,20},{22,24},{26,28},{4,2},{8,6},{1... | collective-permute-start | bytes 2359304 | tf_op jit(solution)/shard_map/ppermute | solution.py:630
  13.7 25.2 %collective-permute-start.6 = (bf16[1008,256]{1,0:T(8,128)(2,1)}, bf16[1008,256]{1,0:T(8,128)(2,1)}, u32[]{:S(2)}, u32[]{:S(2)}) collective-permute-start(bf16[1008,256]{1,0:T(8,128)(2,1)} %get-tuple-element.49), channel_id=1, source_target_pairs={{0,1},{1,0},{2,3},{3,2},{4,5},{5,4},{6,7},{7,6},{8,9},{9,8},{10,11... | collective-permute-start | bytes 1548296 | tf_op jit(solution)/shard_map/ppermute | solution.py:634
  15.3 10.5 %copy-start.2 = (bf16[1,512,256]{2,1,0:T(8,128)(2,1)S(1)}, bf16[1,512,256]{2,1,0:T(8,128)(2,1)}, u32[]{:S(2)}) copy-start(bf16[1,512,256]{2,1,0:T(8,128)(2,1)} %atm_ref.1) | copy-start | bytes 786436
  15.3 10.5 %copy-start.3 = (bf16[4,4,128,128]{3,2,1,0:T(8,128)(2,1)S(1)}, bf16[4,4,128,128]{3,2,1,0:T(8,128)(2,1)}, u32[]{:S(2)}) copy-start(bf16[4,4,128,128]{3,2,1,0:T(8,128)(2,1)} %remap.1) | copy-start | bytes 1572868
  15.4 10.5 %copy-start.4 = (bf16[256,768]{1,0:T(8,128)(2,1)S(1)}, bf16[256,768]{1,0:T(8,128)(2,1)}, u32[]{:S(2)}) copy-start(bf16[256,768]{1,0:T(8,128)(2,1)} %refs_7_.1) | copy-start | bytes 1179652
  15.4 10.5 %copy-start.5 = (bf16[256,256]{1,0:T(8,128)(2,1)S(1)}, bf16[256,256]{1,0:T(8,128)(2,1)}, u32[]{:S(2)}) copy-start(bf16[256,256]{1,0:T(8,128)(2,1)} %refs_8_.3) | copy-start | bytes 393220
  15.4 10.5 %copy-start.7 = (s32[4]{0:T(128)S(1)}, s32[4]{0:T(128)}, u32[]{:S(2)}) copy-start(s32[4]{0:T(128)} %live_ref.1) | copy-start | bytes 52
  25.9 6.4 %copy-start.1 = (bf16[3,3,256,256]{3,2,1,0:T(8,128)(2,1)S(1)}, bf16[3,3,256,256]{3,2,1,0:T(8,128)(2,1)}, u32[]{:S(2)}) copy-start(bf16[3,3,256,256]{3,2,1,0:T(8,128)(2,1)} %weight_hbm.1) | copy-start | bytes 3538948
  29.5 9.4 %collective-permute-start.3 = (bf16[1,384,256]{2,1,0:T(8,128)(2,1)}, bf16[1,384,256]{2,1,0:T(8,128)(2,1)}, u32[]{:S(2)}, u32[]{:S(2)}) collective-permute-start(bf16[1,384,256]{2,1,0:T(8,128)(2,1)} %get-tuple-element.42.refs_0_), channel_id=1, source_target_pairs={{0,1},{1,0},{2,3},{3,2},{4,5},{5,4},{6,7},{7,6},{8,9},{9,8},{10,11... | collective-permute-start | bytes 589832 | tf_op jit(solution)/shard_map/ppermute | solution.py:634
  31.7 17.0 %collective-permute-start.4 = (bf16[544,256]{1,0:T(8,128)(2,1)}, bf16[544,256]{1,0:T(8,128)(2,1)}, u32[]{:S(2)}, u32[]{:S(2)}) collective-permute-start(bf16[544,256]{1,0:T(8,128)(2,1)} %get-tuple-element.43), channel_id=1, source_target_pairs={{0,1},{1,0},{2,3},{3,2},{4,5},{5,4},{6,7},{7,6},{8,9},{9,8},{10,11... | collective-permute-start | bytes 835592 | tf_op jit(solution)/shard_map/ppermute | solution.py:634
  37.3 11.4 %collective-permute-start.5 = (bf16[672,256]{1,0:T(8,128)(2,1)}, bf16[672,256]{1,0:T(8,128)(2,1)S(1)}, u32[]{:S(2)}, u32[]{:S(2)}) collective-permute-start(bf16[672,256]{1,0:T(8,128)(2,1)} %get-tuple-element.44), channel_id=1, source_target_pairs={{0,1},{1,0},{2,3},{3,2},{4,5},{5,4},{6,7},{7,6},{8,9},{9,8},{10,11... | collective-permute-start | bytes 1032200 | tf_op jit(solution)/shard_map/ppermute | solution.py:634

commit v14 on v13

--- a/solution.py
+++ b/solution.py
@@ -418,8 +418,25 @@
     if edges:
         take(1)
     out_hbm, x_ref, mixed_ref, q_ref, k_ref, v_ref, att_ref, token_ref, new_ref = refs[:9]
-    in_sem, out_sem, sem = refs[9:]
+    in_sem, out_sem, sem, got_sem, surf_buf = refs[9:14]
+    pack_bufs = refs[14:]
     steps, lev, count, width = q_ref.shape
+    got = []
+    for o in range(others):
+        copies = []
+        for k, (source, buf) in enumerate(zip(packed, pack_bufs)):
+            copies.append(pltpu.make_async_copy(source[o], buf.at[o], got_sem.at[o, k]))
+        size = surf_buf.shape[1]
+        at = surf[o].shape[1] - size if edges else 0
+        copies.append(
+            pltpu.make_async_copy(
+                surf[o].at[0, pl.ds(at, size)], surf_buf.at[o], got_sem.at[o, len(packed)]
+            )
+        )
+        got.append(copies)
+    for copies in got:
+        for copy in copies:
+            copy.start()
     members = others + 1
     head = width // HEADS
     pair = 2 * head
@@ -465,14 +482,16 @@
         v_ref[step, rows] = kv[:, width:].reshape(lev, count, width)
 
     for o in range(others):
+        for copy in got[o]:
+            copy.wait()
         for step in range(steps):
-            source = packed[step if edges else 0][o]
-            window = lambda base, size: source[pl.ds(base, size), :]
-            limit = source.shape[0] - count - 16
+            buf = pack_bufs[step if edges else 0]
+            window = lambda base, size: buf[o, pl.ds(base, size), :]
+            limit = buf.shape[1] - count - 16
             wet, rank, _ = plans[step]
             if 0 not in place[step]:
-                at = surf[o].shape[1] - count if edges else step * count
-                token_ref[step, 0] = surf[o][0, at : at + count]
+                at = 0 if edges else step * count
+                token_ref[step, 0] = surf_buf[o, at : at + count]
             for l, at in place[step].items():
                 token_ref[step, l] = unpack(window, wet[l : l + 1], rank[l : l + 1], at, limit)
 
@@ -567,7 +586,8 @@
     vmem = pl.BlockSpec(memory_space=pltpu.VMEM)
     smem = pl.BlockSpec(memory_space=pltpu.SMEM)
     stay = lambda x: pltpu.with_memory_space_constraint(x, pltpu.HBM)
-    in_specs = [smem] * 2 + [hbm] * (2 * nparts) + [vmem] * (len(surf) + len(packed))
+    anywhere = pl.BlockSpec(memory_space=pl.ANY)
+    in_specs = [smem] * 2 + [hbm] * (2 * nparts) + [anywhere] * (len(surf) + len(packed))
     in_specs += [hbm] * others + [vmem] * 3
     args = [flag, side] + [stay(x) for x in normed + mixed] + surf + packed
     args += [stay(x) for x in whole] + [depth, qkv_weight, out_weight]
@@ -595,7 +615,10 @@
             pltpu.SemaphoreType.DMA((2, 2, nparts)),
             pltpu.SemaphoreType.DMA((2,)),
             pltpu.SemaphoreType.DMA,
-        ],
+            pltpu.SemaphoreType.DMA((others, 2 + edges)),
+            pltpu.VMEM((others, cols if edges else 2 * cols, width), BF16),
+        ]
+        + [pltpu.VMEM((others, *p.shape), BF16) for p in packed[::others]],
         out_shape=pltpu.HBM(shape, BF16),
         input_output_aliases=alias,
         compiler_params=params(24 if members <= 2 else 56),

time: 59.2 us -> 60.9 us (1.029)
  Pallas kernels: 45 us -> 46.7 us
    pallas_call x2, Pallas kernels: 19.3 us -> 21 us  [attend(): pl.pallas_call(functools.partial(attend_kernel, others, nparts, edges), i...]
where the time goes in v14:
time: 60.9 us; the launch traced here: 60.2 us
  Pallas kernels  46.7 us (77%)
  starting transfers between devices  8.06 us (13%)
  waiting for transfers between devices  4.27 us (7%)
  between operations  0.99 us (2%)
    pallas_call x2, Pallas kernels, attend(): pl.pallas_call(functools.partial(attend_kernel, others, nparts, edges), i...  21 us
    pallas_call x2, Pallas kernels, row_conv(): pl.pallas_call(functools.partial(row_kernel, cap, first, which), in_specs...  11.2 us
    pallas_call x1, Pallas kernels, body(): pl.pallas_call(functools.partial(inner_kernel, deep_cap), in_specs=[vmem,...  7.16 us
    ppermute x4, starting transfers between devices, exchange(): lax.ppermute(x, 'mem', [(i, (i + k) % members) for i in range(members)])  5.33 us
    ppermute x2, waiting for transfers between devices, swap(): return lax.ppermute(x, 'tile', pairs + [(b, a) for a, b in pairs])  4.26 us
    pallas_call x1, Pallas kernels, body(): pl.pallas_call(functools.partial(prep_kernel, (deep_cap, near_cap, far_ca...  3.7 us
    pallas_call x1, Pallas kernels, body(): pl.pallas_call(surface_kernel, in_specs=[smem] * 3 + [vmem] + [anywhere]...  3.61 us
    ppermute x2, starting transfers between devices, swap(): return lax.ppermute(x, 'tile', pairs + [(b, a) for a, b in pairs])  2.72 us
  transfers between devices with their start and end apart: 6, of which 1 were waited for; matrix products, arithmetic and copies ran while one was open for 0% of the time, Pallas kernels for 54%

profile of v14, /device:TPU:18, one launch (start us, length us, event | category | flops | bytes accessed | tf_op | source)
XLA Modules:
  0.0 60.2 jit_solution(11282385571018991171)
XLA Ops:
  0.0 0.1 pad_add_fusion.side_ref
  0.1 3.7 %prep.1 = (bf16[1536,256]{1,0:T(8,128)(2,1)}, bf16[1536,256]{1,0:T(8,128)(2,1)}, s32[1]{0:T(128)}) custom-call(s32[2]{0:T(128)S(1)} %pad_add_fusion.side_ref, bf16[1,8,512,256]{3,2,1,0:T(8,128)(2,1)} %state.5, bf16[1,512,256]{2,1,0:T(8,128)(2,1)} %atm_ref.1, s32[4,128]{1,0:T(4,128)} %bitcast.8), custom_call_target="tpu_custom_call" | custom-call | flops 1048576 | bytes 2621440 | tf_op jit(solution)/shard_map/prep/pallas_call | solution.py:678
  3.8 0.1 collective-permute-start.2
  3.9 0.0 copy-start.8
  3.9 2.7 %collective-permute-start.1 = (bf16[1536,256]{1,0:T(8,128)(2,1)}, bf16[1536,256]{1,0:T(8,128)(2,1)S(1)}, u32[]{:S(2)}, u32[]{:S(2)}) collective-permute-start(bf16[1536,256]{1,0:T(8,128)(2,1)} %get-tuple-element.32), channel_id=1, source_target_pairs={{2,4},{6,8},{10,12},{14,16},{18,20},{22,24},{26,28},{4,2},{8,6},{1... | collective-permute-start | bytes 2359304 | tf_op jit(solution)/shard_map/ppermute | solution.py:653
  6.5 0.0 copy-done
  6.6 0.0 copy-done.6
  6.6 7.2 %inner.1 = (bf16[7,256,256]{2,1,0:T(8,128)(2,1)}, bf16[7,256,256]{2,1,0:T(8,128)(2,1)}, bf16[1008,256]{1,0:T(8,128)(2,1)}) custom-call(bf16[1,8,512,256]{3,2,1,0:T(8,128)(2,1)S(1)} %copy-done, s32[4,128]{1,0:T(4,128)S(1)} %bitcast.9, bf16[3,3,256,256]{3,2,1,0:T(8,128)(2,1)} %weight_hbm.1), custom_call_target="tpu_custom_call" | custom-call | flops 2415919104 | bytes 4194304 | tf_op jit(solution)/shard_map/inner/pallas_call | solution.py:699
  13.7 1.6 %collective-permute-start.6 = (bf16[1008,256]{1,0:T(8,128)(2,1)}, bf16[1008,256]{1,0:T(8,128)(2,1)}, u32[]{:S(2)}, u32[]{:S(2)}) collective-permute-start(bf16[1008,256]{1,0:T(8,128)(2,1)} %get-tuple-element.49), channel_id=1, source_target_pairs={{0,1},{1,0},{2,3},{3,2},{4,5},{5,4},{6,7},{7,6},{8,9},{9,8},{10,11... | collective-permute-start | bytes 1548296 | tf_op jit(solution)/shard_map/ppermute | solution.py:657
  15.3 0.0 copy-done.8
  15.3 0.0 copy-start.3
  15.4 0.0 copy-start.4
  15.4 0.0 copy-start.5
  15.4 0.0 copy-start.7
  15.4 0.0 collective-permute-done.2.halo_hbm.on_hbm
  15.4 6.2 %row.2 = (bf16[8,256,256]{2,1,0:T(8,128)(2,1)}, bf16[8,256,256]{2,1,0:T(8,128)(2,1)}, bf16[544,256]{1,0:T(8,128)(2,1)}, f32[384,256]{1,0:T(8,128)}) custom-call(s32[2]{0:T(128)S(1)} %pad_add_fusion.side_ref, bf16[1,8,512,256]{3,2,1,0:T(8,128)(2,1)S(1)} %copy-done, s32[4,128]{1,0:T(4,128)S(1)} %bitcast.10, bf16[3,3,256,256]{3,2,1,0:T(8,128)(2,1)} %weight_hbm.1, ...), custom_call_target="tpu_custom_call" | custom-call | flops 1207959552 | bytes 4194304 | tf_op jit(solution)/shard_map/row/pallas_call | solution.py:725
  21.6 4.3 %collective-permute-done.1.off_hbm.halo_hbm = bf16[1536,256]{1,0:T(8,128)(2,1)S(1)} collective-permute-done((bf16[1536,256]{1,0:T(8,128)(2,1)}, bf16[1536,256]{1,0:T(8,128)(2,1)S(1)}, u32[]{:S(2)}, u32[]{:S(2)}) %collective-permute-start.1) | collective-permute-done | bytes 786464 | tf_op jit(solution)/shard_map/ppermute | solution.py:653
  25.8 0.0 copy-done.2
  25.8 0.0 copy-done.3
  25.8 0.0 copy-done.4
  25.9 0.0 copy-start.1
  25.9 3.6 %surface.1 = (bf16[1,384,256]{2,1,0:T(8,128)(2,1)}, bf16[1,384,256]{2,1,0:T(8,128)(2,1)}, f32[128,256]{1,0:T(8,128)}, bf16[8,256,256]{2,1,0:T(8,128)(2,1)}, bf16[8,256,256]{2,1,0:T(8,128)(2,1)}) custom-call(s32[4,4]{1,0:T(4,128)S(1)} %subtract_clamp_fusion.ids_ref, s32[4]{0:T(128)S(1)} %copy-done.7, ...), custom_call_target="tpu_custom_call", output_to_operand_aliasing={{3}: (11, {}), {4}: (12, {})} | custom-call | flops 301989888 | bytes 2097152 | tf_op jit(solution)/shard_map/surface/pallas_call | solution.py:758
  29.5 1.6 %collective-permute-start.3 = (bf16[1,384,256]{2,1,0:T(8,128)(2,1)}, bf16[1,384,256]{2,1,0:T(8,128)(2,1)}, u32[]{:S(2)}, u32[]{:S(2)}) collective-permute-start(bf16[1,384,256]{2,1,0:T(8,128)(2,1)} %get-tuple-element.42.refs_0_), channel_id=1, source_target_pairs={{0,1},{1,0},{2,3},{3,2},{4,5},{5,4},{6,7},{7,6},{8,9},{9,8},{10,11... | collective-permute-start | bytes 589832 | tf_op jit(solution)/shard_map/ppermute | solution.py:657
  31.7 0.6 collective-permute-start.4
  32.3 5.0 %row.3 = (bf16[8,256,256]{2,1,0:T(8,128)(2,1)}, bf16[8,256,256]{2,1,0:T(8,128)(2,1)}, bf16[672,256]{1,0:T(8,128)(2,1)}) custom-call(s32[2]{0:T(128)S(1)} %pad_add_fusion.side_ref, bf16[1,8,512,256]{3,2,1,0:T(8,128)(2,1)S(1)} %copy-done, s32[4,128]{1,0:T(4,128)S(1)} %bitcast.12, ...), custom_call_target="tpu_custom_call", output_to_operand_aliasing={{0}: (6, {}), {1}: (7, {})} | custom-call | flops 1207959552 | bytes 4194304 | tf_op jit(solution)/shard_map/row/pallas_call | solution.py:725
  37.3 1.6 %collective-permute-start.5 = (bf16[672,256]{1,0:T(8,128)(2,1)}, bf16[672,256]{1,0:T(8,128)(2,1)S(1)}, u32[]{:S(2)}, u32[]{:S(2)}) collective-permute-start(bf16[672,256]{1,0:T(8,128)(2,1)} %get-tuple-element.44), channel_id=1, source_target_pairs={{0,1},{1,0},{2,3},{3,2},{4,5},{5,4},{6,7},{7,6},{8,9},{9,8},{10,11... | collective-permute-start | bytes 1032200 | tf_op jit(solution)/shard_map/ppermute | solution.py:657
  38.9 0.0 collective-permute-done.6.refs_5_
  38.9 0.0 collective-permute-done.3.refs_4_.refs_2_
  38.9 10.5 %attend.2.refs_9_ = bf16[1,8,512,256]{3,2,1,0:T(8,128)(2,1)} custom-call(s32[1]{0:T(128)} %get-tuple-element.31.flag_ref, s32[2]{0:T(128)S(1)} %pad_add_fusion.side_ref, bf16[1,384,256]{2,1,0:T(8,128)(2,1)} %get-tuple-element.42.refs_0_, bf16[7,256,256]{2,1,0:T(8,128)(2,1)} %get-tuple-element.45.refs_1_, bf16[1,384,256]{2,1,0:T(8,128)(2,1)} %get-tuple-element.47.refs_2_, ...), custom_call_target="tpu_custom_call" | custom-call | flops 4294967296 | bytes 5242880 | tf_op jit(solution)/shard_map/attend/pallas_call | solution.py:602
  49.4 0.0 collective-permute-done.4.refs_3_
  49.4 0.0 collective-permute-done.5.refs_4_
  49.4 10.6 %attend.3 = bf16[1,8,512,256]{3,2,1,0:T(8,128)(2,1)} custom-call(s32[1]{0:T(128)} %get-tuple-element.31.flag_ref, s32[2]{0:T(128)S(1)} %pad_add_fusion.side_ref, bf16[8,256,256]{2,1,0:T(8,128)(2,1)} %get-tuple-element.40.refs_0_, bf16[8,256,256]{2,1,0:T(8,128)(2,1)} %get-tuple-element.41.refs_1_, ...), custom_call_target="tpu_custom_call", output_to_operand_aliasing={{}: (11, {})} | custom-call | flops 4294967296 | bytes 5242880 | tf_op jit(solution)/shard_map/attend/pallas_call | solution.py:602
  (10 shorter events, 0.0 us)
Async XLA Ops:
  0.0 6.5 %copy-start = (bf16[1,8,512,256]{3,2,1,0:T(8,128)(2,1)S(1)}, bf16[1,8,512,256]{3,2,1,0:T(8,128)(2,1)}, u32[]{:S(2)}) copy-start(bf16[1,8,512,256]{3,2,1,0:T(8,128)(2,1)} %state.5) | copy-start | bytes 6291460
  0.0 6.6 %copy-start.6 = (s32[512]{0:T(512)S(1)}, s32[512]{0:T(512)}, u32[]{:S(2)}) copy-start(s32[512]{0:T(512)} %param.13) | copy-start | bytes 6148
  3.8 11.6 %collective-permute-start.2 = (bf16[1536,256]{1,0:T(8,128)(2,1)}, bf16[1536,256]{1,0:T(8,128)(2,1)}, u32[]{:S(2)}, u32[]{:S(2)}) collective-permute-start(bf16[1536,256]{1,0:T(8,128)(2,1)} %get-tuple-element.33), channel_id=1, source_target_pairs={{0,2},{4,6},{8,10},{12,14},{16,18},{20,22},{24,26},{28,30},{2,0},{... | collective-permute-start | bytes 2359304 | tf_op jit(solution)/shard_map/ppermute | solution.py:653
  3.9 11.5 %copy-start.8 = (s32[4,4]{1,0:T(4,128)S(1)}, s32[4,4]{1,0:T(4,128)}, u32[]{:S(2)}) copy-start(s32[4,4]{1,0:T(4,128)} %param.14) | copy-start | bytes 196
  3.9 21.9 %collective-permute-start.1 = (bf16[1536,256]{1,0:T(8,128)(2,1)}, bf16[1536,256]{1,0:T(8,128)(2,1)S(1)}, u32[]{:S(2)}, u32[]{:S(2)}) collective-permute-start(bf16[1536,256]{1,0:T(8,128)(2,1)} %get-tuple-element.32), channel_id=1, source_target_pairs={{2,4},{6,8},{10,12},{14,16},{18,20},{22,24},{26,28},{4,2},{8,6},{1... | collective-permute-start | bytes 2359304 | tf_op jit(solution)/shard_map/ppermute | solution.py:653
  13.7 25.2 %collective-permute-start.6 = (bf16[1008,256]{1,0:T(8,128)(2,1)}, bf16[1008,256]{1,0:T(8,128)(2,1)}, u32[]{:S(2)}, u32[]{:S(2)}) collective-permute-start(bf16[1008,256]{1,0:T(8,128)(2,1)} %get-tuple-element.49), channel_id=1, source_target_pairs={{0,1},{1,0},{2,3},{3,2},{4,5},{5,4},{6,7},{7,6},{8,9},{9,8},{10,11... | collective-permute-start | bytes 1548296 | tf_op jit(solution)/shard_map/ppermute | solution.py:657
  15.3 10.5 %copy-start.2 = (bf16[1,512,256]{2,1,0:T(8,128)(2,1)S(1)}, bf16[1,512,256]{2,1,0:T(8,128)(2,1)}, u32[]{:S(2)}) copy-start(bf16[1,512,256]{2,1,0:T(8,128)(2,1)} %atm_ref.1) | copy-start | bytes 786436
  15.3 10.5 %copy-start.3 = (bf16[4,4,128,128]{3,2,1,0:T(8,128)(2,1)S(1)}, bf16[4,4,128,128]{3,2,1,0:T(8,128)(2,1)}, u32[]{:S(2)}) copy-start(bf16[4,4,128,128]{3,2,1,0:T(8,128)(2,1)} %remap.1) | copy-start | bytes 1572868
  15.4 10.5 %copy-start.4 = (bf16[256,768]{1,0:T(8,128)(2,1)S(1)}, bf16[256,768]{1,0:T(8,128)(2,1)}, u32[]{:S(2)}) copy-start(bf16[256,768]{1,0:T(8,128)(2,1)} %refs_7_.1) | copy-start | bytes 1179652
  15.4 10.5 %copy-start.5 = (bf16[256,256]{1,0:T(8,128)(2,1)S(1)}, bf16[256,256]{1,0:T(8,128)(2,1)}, u32[]{:S(2)}) copy-start(bf16[256,256]{1,0:T(8,128)(2,1)} %refs_8_.3) | copy-start | bytes 393220
  15.4 10.5 %copy-start.7 = (s32[4]{0:T(128)S(1)}, s32[4]{0:T(128)}, u32[]{:S(2)}) copy-start(s32[4]{0:T(128)} %live_ref.1) | copy-start | bytes 52
  25.9 6.4 %copy-start.1 = (bf16[3,3,256,256]{3,2,1,0:T(8,128)(2,1)S(1)}, bf16[3,3,256,256]{3,2,1,0:T(8,128)(2,1)}, u32[]{:S(2)}) copy-start(bf16[3,3,256,256]{3,2,1,0:T(8,128)(2,1)} %weight_hbm.1) | copy-start | bytes 3538948
  29.5 9.4 %collective-permute-start.3 = (bf16[1,384,256]{2,1,0:T(8,128)(2,1)}, bf16[1,384,256]{2,1,0:T(8,128)(2,1)}, u32[]{:S(2)}, u32[]{:S(2)}) collective-permute-start(bf16[1,384,256]{2,1,0:T(8,128)(2,1)} %get-tuple-element.42.refs_0_), channel_id=1, source_target_pairs={{0,1},{1,0},{2,3},{3,2},{4,5},{5,4},{6,7},{7,6},{8,9},{9,8},{10,11... | collective-permute-start | bytes 589832 | tf_op jit(solution)/shard_map/ppermute | solution.py:657
  31.7 17.7 %collective-permute-start.4 = (bf16[544,256]{1,0:T(8,128)(2,1)}, bf16[544,256]{1,0:T(8,128)(2,1)}, u32[]{:S(2)}, u32[]{:S(2)}) collective-permute-start(bf16[544,256]{1,0:T(8,128)(2,1)} %get-tuple-element.43), channel_id=1, source_target_pairs={{0,1},{1,0},{2,3},{3,2},{4,5},{5,4},{6,7},{7,6},{8,9},{9,8},{10,11... | collective-permute-start | bytes 835592 | tf_op jit(solution)/shard_map/ppermute | solution.py:657
  37.3 12.1 %collective-permute-start.5 = (bf16[672,256]{1,0:T(8,128)(2,1)}, bf16[672,256]{1,0:T(8,128)(2,1)S(1)}, u32[]{:S(2)}, u32[]{:S(2)}) collective-permute-start(bf16[672,256]{1,0:T(8,128)(2,1)} %get-tuple-element.44), channel_id=1, source_target_pairs={{0,1},{1,0},{2,3},{3,2},{4,5},{5,4},{6,7},{7,6},{8,9},{9,8},{10,11... | collective-permute-start | bytes 1032200 | tf_op jit(solution)/shard_map/ppermute | solution.py:657

commit v15 on v12

--- a/solution.py
+++ b/solution.py
@@ -144,6 +144,15 @@
     d = depth_ref[...].astype(F32)
     pick = lambda k: jnp.where(side_ref[k] == 0, d[0:1], d[rows - 1 :])
     deep = [column(pick(k)) for k in range(2)]
+    counts = [
+        jnp.sum(jnp.maximum(d[1 : rows - 1] - 1.0, 0.0)),
+        jnp.sum(jnp.maximum(pick(0) - 1.0, 0.0)),
+        jnp.sum(pick(1)),
+    ]
+    over = jnp.int32(0)
+    for count, cap in zip(counts, caps):
+        over = over | (count > cap).astype(jnp.int32)
+    flag_ref[0] = over
     for k, l, load in loads:
         wet = widen((deep[k] > l).astype(F32).astype(BF16), width)
         load.wait()
@@ -160,15 +169,6 @@
         )
         store.start()
         stores.append(store)
-    counts = [
-        jnp.sum(jnp.maximum(d[1 : rows - 1] - 1.0, 0.0)),
-        jnp.sum(jnp.maximum(pick(0) - 1.0, 0.0)),
-        jnp.sum(pick(1)),
-    ]
-    over = jnp.int32(0)
-    for count, cap in zip(counts, caps):
-        over = over | (count > cap).astype(jnp.int32)
-    flag_ref[0] = over
     for store in stores:
         store.wait()
 

time: 59.2 us -> 59.2 us (level)
  no operation moved by 1% of the time
where the time goes in v15:
time: 59.2 us; the launch traced here: 58.5 us
  Pallas kernels  45.2 us (76%)
  starting transfers between devices  8.04 us (14%)
  waiting for transfers between devices  4.24 us (7%)
  between operations  0.9 us (2%)
    pallas_call x2, Pallas kernels, attend(): pl.pallas_call(functools.partial(attend_kernel, others, nparts, edges), i...  19.2 us
    pallas_call x2, Pallas kernels, row_conv(): pl.pallas_call(functools.partial(row_kernel, cap, first, which), in_specs...  11.4 us
    pallas_call x1, Pallas kernels, body(): pl.pallas_call(functools.partial(inner_kernel, deep_cap), in_specs=[vmem,...  7.18 us
    ppermute x4, starting transfers between devices, exchange(): lax.ppermute(x, 'mem', [(i, (i + k) % members) for i in range(members)])  5.32 us
    ppermute x2, waiting for transfers between devices, swap(): return lax.ppermute(x, 'tile', pairs + [(b, a) for a, b in pairs])  4.23 us
    pallas_call x1, Pallas kernels, body(): pl.pallas_call(functools.partial(prep_kernel, (deep_cap, near_cap, far_ca...  3.74 us
    pallas_call x1, Pallas kernels, body(): pl.pallas_call(surface_kernel, in_specs=[smem] * 3 + [vmem] + [anywhere]...  3.72 us
    ppermute x2, starting transfers between devices, swap(): return lax.ppermute(x, 'tile', pairs + [(b, a) for a, b in pairs])  2.72 us
  transfers between devices with their start and end apart: 6, of which 1 were waited for; matrix products, arithmetic and copies ran while one was open for 0% of the time, Pallas kernels for 55%

profile of v15, /device:TPU:18, one launch (start us, length us, event | category | flops | bytes accessed | tf_op | source)
XLA Modules:
  0.0 58.5 jit_solution(11319949904114593664)
XLA Ops:
  0.0 0.1 pad_add_fusion.side_ref
  0.1 3.7 %prep.1 = (bf16[1536,256]{1,0:T(8,128)(2,1)}, bf16[1536,256]{1,0:T(8,128)(2,1)}, s32[1]{0:T(128)}) custom-call(s32[2]{0:T(128)S(1)} %pad_add_fusion.side_ref, bf16[1,8,512,256]{3,2,1,0:T(8,128)(2,1)} %state.5, bf16[1,512,256]{2,1,0:T(8,128)(2,1)} %atm_ref.1, s32[4,128]{1,0:T(4,128)} %bitcast.8), custom_call_target="tpu_custom_call" | custom-call | flops 1048576 | bytes 2621440 | tf_op jit(solution)/shard_map/prep/pallas_call | solution.py:647
  3.8 0.1 collective-permute-start.2
  3.9 0.0 copy-start.7
  3.9 2.7 %collective-permute-start.1 = (bf16[1536,256]{1,0:T(8,128)(2,1)}, bf16[1536,256]{1,0:T(8,128)(2,1)S(1)}, u32[]{:S(2)}, u32[]{:S(2)}) collective-permute-start(bf16[1536,256]{1,0:T(8,128)(2,1)} %get-tuple-element.32), channel_id=1, source_target_pairs={{2,4},{6,8},{10,12},{14,16},{18,20},{22,24},{26,28},{4,2},{8,6},{1... | collective-permute-start | bytes 2359304 | tf_op jit(solution)/shard_map/ppermute | solution.py:622
  6.6 0.0 copy-done
  6.6 0.0 copy-done.5
  6.6 7.2 %inner.1 = (bf16[7,256,256]{2,1,0:T(8,128)(2,1)}, bf16[7,256,256]{2,1,0:T(8,128)(2,1)}, bf16[1008,256]{1,0:T(8,128)(2,1)}) custom-call(bf16[1,8,512,256]{3,2,1,0:T(8,128)(2,1)S(1)} %copy-done, s32[4,128]{1,0:T(4,128)S(1)} %bitcast.9, bf16[3,3,256,256]{3,2,1,0:T(8,128)(2,1)} %weight_hbm.5), custom_call_target="tpu_custom_call" | custom-call | flops 2415919104 | bytes 4194304 | tf_op jit(solution)/shard_map/inner/pallas_call | solution.py:668
  13.8 1.6 %collective-permute-start.6 = (bf16[1008,256]{1,0:T(8,128)(2,1)}, bf16[1008,256]{1,0:T(8,128)(2,1)}, u32[]{:S(2)}, u32[]{:S(2)}) collective-permute-start(bf16[1008,256]{1,0:T(8,128)(2,1)} %get-tuple-element.49), channel_id=1, source_target_pairs={{0,1},{1,0},{2,3},{3,2},{4,5},{5,4},{6,7},{7,6},{8,9},{9,8},{10,11... | collective-permute-start | bytes 1548296 | tf_op jit(solution)/shard_map/ppermute | solution.py:626
  15.4 0.0 copy-done.7
  15.4 0.0 copy-start.2
  15.4 0.0 copy-start.3
  15.4 0.0 copy-start.4
  15.4 0.0 copy-start.6
  15.4 0.0 collective-permute-done.2.halo_hbm.on_hbm
  15.4 6.2 %row.2 = (bf16[8,256,256]{2,1,0:T(8,128)(2,1)}, bf16[8,256,256]{2,1,0:T(8,128)(2,1)}, bf16[544,256]{1,0:T(8,128)(2,1)}, f32[384,256]{1,0:T(8,128)}) custom-call(s32[2]{0:T(128)S(1)} %pad_add_fusion.side_ref, bf16[1,8,512,256]{3,2,1,0:T(8,128)(2,1)S(1)} %copy-done, s32[4,128]{1,0:T(4,128)S(1)} %bitcast.10, bf16[3,3,256,256]{3,2,1,0:T(8,128)(2,1)} %weight_hbm.5, ...), custom_call_target="tpu_custom_call" | custom-call | flops 1207959552 | bytes 4194304 | tf_op jit(solution)/shard_map/row/pallas_call | solution.py:694
  21.6 4.2 %collective-permute-done.1.off_hbm.halo_hbm = bf16[1536,256]{1,0:T(8,128)(2,1)S(1)} collective-permute-done((bf16[1536,256]{1,0:T(8,128)(2,1)}, bf16[1536,256]{1,0:T(8,128)(2,1)S(1)}, u32[]{:S(2)}, u32[]{:S(2)}) %collective-permute-start.1) | collective-permute-done | bytes 786464 | tf_op jit(solution)/shard_map/ppermute | solution.py:622
  25.9 0.0 copy-done.1
  25.9 0.0 copy-done.2
  25.9 0.0 copy-done.3
  25.9 0.0 copy-done.4
  25.9 3.7 %surface.1 = (bf16[1,384,256]{2,1,0:T(8,128)(2,1)}, bf16[1,384,256]{2,1,0:T(8,128)(2,1)}, f32[128,256]{1,0:T(8,128)}, bf16[8,256,256]{2,1,0:T(8,128)(2,1)}, bf16[8,256,256]{2,1,0:T(8,128)(2,1)}) custom-call(s32[4,4]{1,0:T(4,128)S(1)} %subtract_clamp_fusion.ids_ref, s32[4]{0:T(128)S(1)} %copy-done.6, ...), custom_call_target="tpu_custom_call", output_to_operand_aliasing={{3}: (11, {}), {4}: (12, {})} | custom-call | flops 301989888 | bytes 2097152 | tf_op jit(solution)/shard_map/surface/pallas_call | solution.py:720
  29.6 1.6 %collective-permute-start.3 = (bf16[1,384,256]{2,1,0:T(8,128)(2,1)}, bf16[1,384,256]{2,1,0:T(8,128)(2,1)}, u32[]{:S(2)}, u32[]{:S(2)}) collective-permute-start(bf16[1,384,256]{2,1,0:T(8,128)(2,1)} %get-tuple-element.42.refs_0_), channel_id=1, source_target_pairs={{0,1},{1,0},{2,3},{3,2},{4,5},{5,4},{6,7},{7,6},{8,9},{9,8},{10,11... | collective-permute-start | bytes 589832 | tf_op jit(solution)/shard_map/ppermute | solution.py:626
  31.8 0.6 collective-permute-start.4
  32.3 5.2 %row.3 = (bf16[8,256,256]{2,1,0:T(8,128)(2,1)}, bf16[8,256,256]{2,1,0:T(8,128)(2,1)}, bf16[672,256]{1,0:T(8,128)(2,1)}) custom-call(s32[2]{0:T(128)S(1)} %pad_add_fusion.side_ref, bf16[1,8,512,256]{3,2,1,0:T(8,128)(2,1)S(1)} %copy-done, s32[4,128]{1,0:T(4,128)S(1)} %bitcast.12, ...), custom_call_target="tpu_custom_call", output_to_operand_aliasing={{0}: (6, {}), {1}: (7, {})} | custom-call | flops 1207959552 | bytes 4194304 | tf_op jit(solution)/shard_map/row/pallas_call | solution.py:694
  37.5 1.6 %collective-permute-start.5 = (bf16[672,256]{1,0:T(8,128)(2,1)}, bf16[672,256]{1,0:T(8,128)(2,1)S(1)}, u32[]{:S(2)}, u32[]{:S(2)}) collective-permute-start(bf16[672,256]{1,0:T(8,128)(2,1)} %get-tuple-element.44), channel_id=1, source_target_pairs={{0,1},{1,0},{2,3},{3,2},{4,5},{5,4},{6,7},{7,6},{8,9},{9,8},{10,11... | collective-permute-start | bytes 1032200 | tf_op jit(solution)/shard_map/ppermute | solution.py:626
  39.1 0.0 collective-permute-done.6.refs_5_
  39.1 0.0 collective-permute-done.3.refs_4_.refs_2_
  39.1 9.7 %attend.2.refs_9_ = bf16[1,8,512,256]{3,2,1,0:T(8,128)(2,1)} custom-call(s32[1]{0:T(128)} %get-tuple-element.31.flag_ref, s32[2]{0:T(128)S(1)} %pad_add_fusion.side_ref, bf16[1,384,256]{2,1,0:T(8,128)(2,1)} %get-tuple-element.42.refs_0_, bf16[7,256,256]{2,1,0:T(8,128)(2,1)} %get-tuple-element.45.refs_1_, bf16[1,384,256]{2,1,0:T(8,128)(2,1)} %get-tuple-element.47.refs_2_, ...), custom_call_target="tpu_custom_call" | custom-call | flops 4294967296 | bytes 5242880 | tf_op jit(solution)/shard_map/attend/pallas_call | solution.py:574
  48.8 0.0 collective-permute-done.4.refs_3_
  48.8 0.0 collective-permute-done.5.refs_4_
  48.8 9.5 %attend.3 = bf16[1,8,512,256]{3,2,1,0:T(8,128)(2,1)} custom-call(s32[1]{0:T(128)} %get-tuple-element.31.flag_ref, s32[2]{0:T(128)S(1)} %pad_add_fusion.side_ref, bf16[8,256,256]{2,1,0:T(8,128)(2,1)} %get-tuple-element.40.refs_0_, bf16[8,256,256]{2,1,0:T(8,128)(2,1)} %get-tuple-element.41.refs_1_, ...), custom_call_target="tpu_custom_call", output_to_operand_aliasing={{}: (11, {})} | custom-call | flops 4294967296 | bytes 5242880 | tf_op jit(solution)/shard_map/attend/pallas_call | solution.py:574
  (8 shorter events, 0.0 us)
Async XLA Ops:
  0.0 6.6 %copy-start = (bf16[1,8,512,256]{3,2,1,0:T(8,128)(2,1)S(1)}, bf16[1,8,512,256]{3,2,1,0:T(8,128)(2,1)}, u32[]{:S(2)}) copy-start(bf16[1,8,512,256]{3,2,1,0:T(8,128)(2,1)} %state.5) | copy-start | bytes 6291460
  0.0 6.6 %copy-start.5 = (s32[512]{0:T(512)S(1)}, s32[512]{0:T(512)}, u32[]{:S(2)}) copy-start(s32[512]{0:T(512)} %param.13) | copy-start | bytes 6148
  3.8 11.6 %collective-permute-start.2 = (bf16[1536,256]{1,0:T(8,128)(2,1)}, bf16[1536,256]{1,0:T(8,128)(2,1)}, u32[]{:S(2)}, u32[]{:S(2)}) collective-permute-start(bf16[1536,256]{1,0:T(8,128)(2,1)} %get-tuple-element.33), channel_id=1, source_target_pairs={{0,2},{4,6},{8,10},{12,14},{16,18},{20,22},{24,26},{28,30},{2,0},{... | collective-permute-start | bytes 2359304 | tf_op jit(solution)/shard_map/ppermute | solution.py:622
  3.9 11.5 %copy-start.7 = (s32[4,4]{1,0:T(4,128)S(1)}, s32[4,4]{1,0:T(4,128)}, u32[]{:S(2)}) copy-start(s32[4,4]{1,0:T(4,128)} %param.14) | copy-start | bytes 196
  3.9 21.9 %collective-permute-start.1 = (bf16[1536,256]{1,0:T(8,128)(2,1)}, bf16[1536,256]{1,0:T(8,128)(2,1)S(1)}, u32[]{:S(2)}, u32[]{:S(2)}) collective-permute-start(bf16[1536,256]{1,0:T(8,128)(2,1)} %get-tuple-element.32), channel_id=1, source_target_pairs={{2,4},{6,8},{10,12},{14,16},{18,20},{22,24},{26,28},{4,2},{8,6},{1... | collective-permute-start | bytes 2359304 | tf_op jit(solution)/shard_map/ppermute | solution.py:622
  13.8 25.3 %collective-permute-start.6 = (bf16[1008,256]{1,0:T(8,128)(2,1)}, bf16[1008,256]{1,0:T(8,128)(2,1)}, u32[]{:S(2)}, u32[]{:S(2)}) collective-permute-start(bf16[1008,256]{1,0:T(8,128)(2,1)} %get-tuple-element.49), channel_id=1, source_target_pairs={{0,1},{1,0},{2,3},{3,2},{4,5},{5,4},{6,7},{7,6},{8,9},{9,8},{10,11... | collective-permute-start | bytes 1548296 | tf_op jit(solution)/shard_map/ppermute | solution.py:626
  15.4 10.5 %copy-start.1 = (bf16[1,512,256]{2,1,0:T(8,128)(2,1)S(1)}, bf16[1,512,256]{2,1,0:T(8,128)(2,1)}, u32[]{:S(2)}) copy-start(bf16[1,512,256]{2,1,0:T(8,128)(2,1)} %atm_ref.1) | copy-start | bytes 786436
  15.4 10.5 %copy-start.2 = (bf16[4,4,128,128]{3,2,1,0:T(8,128)(2,1)S(1)}, bf16[4,4,128,128]{3,2,1,0:T(8,128)(2,1)}, u32[]{:S(2)}) copy-start(bf16[4,4,128,128]{3,2,1,0:T(8,128)(2,1)} %remap.1) | copy-start | bytes 1572868
  15.4 10.5 %copy-start.3 = (bf16[256,768]{1,0:T(8,128)(2,1)S(1)}, bf16[256,768]{1,0:T(8,128)(2,1)}, u32[]{:S(2)}) copy-start(bf16[256,768]{1,0:T(8,128)(2,1)} %refs_7_.1) | copy-start | bytes 1179652
  15.4 10.5 %copy-start.4 = (bf16[256,256]{1,0:T(8,128)(2,1)S(1)}, bf16[256,256]{1,0:T(8,128)(2,1)}, u32[]{:S(2)}) copy-start(bf16[256,256]{1,0:T(8,128)(2,1)} %refs_8_.3) | copy-start | bytes 393220
  15.4 10.5 %copy-start.6 = (s32[4]{0:T(128)S(1)}, s32[4]{0:T(128)}, u32[]{:S(2)}) copy-start(s32[4]{0:T(128)} %live_ref.1) | copy-start | bytes 52
  29.6 9.5 %collective-permute-start.3 = (bf16[1,384,256]{2,1,0:T(8,128)(2,1)}, bf16[1,384,256]{2,1,0:T(8,128)(2,1)}, u32[]{:S(2)}, u32[]{:S(2)}) collective-permute-start(bf16[1,384,256]{2,1,0:T(8,128)(2,1)} %get-tuple-element.42.refs_0_), channel_id=1, source_target_pairs={{0,1},{1,0},{2,3},{3,2},{4,5},{5,4},{6,7},{7,6},{8,9},{9,8},{10,11... | collective-permute-start | bytes 589832 | tf_op jit(solution)/shard_map/ppermute | solution.py:626
  31.8 17.0 %collective-permute-start.4 = (bf16[544,256]{1,0:T(8,128)(2,1)}, bf16[544,256]{1,0:T(8,128)(2,1)}, u32[]{:S(2)}, u32[]{:S(2)}) collective-permute-start(bf16[544,256]{1,0:T(8,128)(2,1)} %get-tuple-element.43), channel_id=1, source_target_pairs={{0,1},{1,0},{2,3},{3,2},{4,5},{5,4},{6,7},{7,6},{8,9},{9,8},{10,11... | collective-permute-start | bytes 835592 | tf_op jit(solution)/shard_map/ppermute | solution.py:626
  37.5 11.3 %collective-permute-start.5 = (bf16[672,256]{1,0:T(8,128)(2,1)}, bf16[672,256]{1,0:T(8,128)(2,1)S(1)}, u32[]{:S(2)}, u32[]{:S(2)}) collective-permute-start(bf16[672,256]{1,0:T(8,128)(2,1)} %get-tuple-element.44), channel_id=1, source_target_pairs={{0,1},{1,0},{2,3},{3,2},{4,5},{5,4},{6,7},{7,6},{8,9},{9,8},{10,11... | collective-permute-start | bytes 1032200 | tf_op jit(solution)/shard_map/ppermute | solution.py:626

commit v16 on v15

--- a/solution.py
+++ b/solution.py
@@ -132,9 +132,12 @@
     loads, stores = [], []
     for k in (1, 0):
         at = pl.multiple_of(side_ref[k] * cols, cols)
-        for l in range(lev):
+        half = lev // 2
+        for l in range(0, lev, half):
             load = pltpu.make_async_copy(
-                state_hbm.at[0, l, pl.ds(at, cols)], rows_in.at[k, l], in_sem.at[k, l]
+                state_hbm.at[0, pl.ds(l, half), pl.ds(at, cols)],
+                rows_in.at[k, pl.ds(l, half)],
+                in_sem.at[k, l],
             )
             load.start()
             loads.append((k, l, load))
@@ -154,14 +157,15 @@
         over = over | (count > cap).astype(jnp.int32)
     flag_ref[0] = over
     for k, l, load in loads:
-        wet = widen((deep[k] > l).astype(F32).astype(BF16), width)
         load.wait()
-        rows_in[k, l] = rows_in[k, l] * wet
-        store = pltpu.make_async_copy(
-            rows_in.at[k, l], sides[k].at[pl.ds(l * cols, cols)], out_sem.at[k, l]
-        )
-        store.start()
-        stores.append(store)
+        for level in range(l, l + half):
+            wet = widen((deep[k] > level).astype(F32).astype(BF16), width)
+            rows_in[k, level] = rows_in[k, level] * wet
+            store = pltpu.make_async_copy(
+                rows_in.at[k, level], sides[k].at[pl.ds(level * cols, cols)], out_sem.at[k, level]
+            )
+            store.start()
+            stores.append(store)
     load_atm.wait()
     for k in (1, 0):
         store = pltpu.make_async_copy(

time: 59.2 us -> 59.2 us (level)
  no operation moved by 1% of the time
where the time goes in v16:
time: 59.2 us; the launch traced here: 58.5 us
  Pallas kernels  45.2 us (76%)
  starting transfers between devices  8.05 us (14%)
  waiting for transfers between devices  4.23 us (7%)
  between operations  0.9 us (2%)
    pallas_call x2, Pallas kernels, attend(): pl.pallas_call(functools.partial(attend_kernel, others, nparts, edges), i...  19.2 us
    pallas_call x2, Pallas kernels, row_conv(): pl.pallas_call(functools.partial(row_kernel, cap, first, which), in_specs...  11.4 us
    pallas_call x1, Pallas kernels, body(): pl.pallas_call(functools.partial(inner_kernel, deep_cap), in_specs=[vmem,...  7.18 us
    ppermute x4, starting transfers between devices, exchange(): lax.ppermute(x, 'mem', [(i, (i + k) % members) for i in range(members)])  5.33 us
    ppermute x2, waiting for transfers between devices, swap(): return lax.ppermute(x, 'tile', pairs + [(b, a) for a, b in pairs])  4.21 us
    pallas_call x1, Pallas kernels, body(): pl.pallas_call(surface_kernel, in_specs=[smem] * 3 + [vmem] + [anywhere]...  3.72 us
    pallas_call x1, Pallas kernels, body(): pl.pallas_call(functools.partial(prep_kernel, (deep_cap, near_cap, far_ca...  3.68 us
    ppermute x2, starting transfers between devices, swap(): return lax.ppermute(x, 'tile', pairs + [(b, a) for a, b in pairs])  2.72 us
  transfers between devices with their start and end apart: 6, of which 1 were waited for; matrix products, arithmetic and copies ran while one was open for 0% of the time, Pallas kernels for 55%

profile of v16, /device:TPU:18, one launch (start us, length us, event | category | flops | bytes accessed | tf_op | source)
XLA Modules:
  0.0 58.5 jit_solution(11841444527713213396)
XLA Ops:
  0.0 0.1 pad_add_fusion.side_ref
  0.1 3.7 %prep.1 = (bf16[1536,256]{1,0:T(8,128)(2,1)}, bf16[1536,256]{1,0:T(8,128)(2,1)}, s32[1]{0:T(128)}) custom-call(s32[2]{0:T(128)S(1)} %pad_add_fusion.side_ref, bf16[1,8,512,256]{3,2,1,0:T(8,128)(2,1)} %state.5, bf16[1,512,256]{2,1,0:T(8,128)(2,1)} %atm_ref.1, s32[4,128]{1,0:T(4,128)} %bitcast.8), custom_call_target="tpu_custom_call" | custom-call | flops 1048576 | bytes 2621440 | tf_op jit(solution)/shard_map/prep/pallas_call | solution.py:651
  3.8 0.1 collective-permute-start.2
  3.8 0.0 copy-start.7
  3.9 2.7 %collective-permute-start.1 = (bf16[1536,256]{1,0:T(8,128)(2,1)}, bf16[1536,256]{1,0:T(8,128)(2,1)S(1)}, u32[]{:S(2)}, u32[]{:S(2)}) collective-permute-start(bf16[1536,256]{1,0:T(8,128)(2,1)} %get-tuple-element.32), channel_id=1, source_target_pairs={{2,4},{6,8},{10,12},{14,16},{18,20},{22,24},{26,28},{4,2},{8,6},{1... | collective-permute-start | bytes 2359304 | tf_op jit(solution)/shard_map/ppermute | solution.py:626
  6.5 0.0 copy-done
  6.5 0.0 copy-done.5
  6.5 7.2 %inner.1 = (bf16[7,256,256]{2,1,0:T(8,128)(2,1)}, bf16[7,256,256]{2,1,0:T(8,128)(2,1)}, bf16[1008,256]{1,0:T(8,128)(2,1)}) custom-call(bf16[1,8,512,256]{3,2,1,0:T(8,128)(2,1)S(1)} %copy-done, s32[4,128]{1,0:T(4,128)S(1)} %bitcast.9, bf16[3,3,256,256]{3,2,1,0:T(8,128)(2,1)} %weight_hbm.5), custom_call_target="tpu_custom_call" | custom-call | flops 2415919104 | bytes 4194304 | tf_op jit(solution)/shard_map/inner/pallas_call | solution.py:672
  13.7 1.6 %collective-permute-start.6 = (bf16[1008,256]{1,0:T(8,128)(2,1)}, bf16[1008,256]{1,0:T(8,128)(2,1)}, u32[]{:S(2)}, u32[]{:S(2)}) collective-permute-start(bf16[1008,256]{1,0:T(8,128)(2,1)} %get-tuple-element.49), channel_id=1, source_target_pairs={{0,1},{1,0},{2,3},{3,2},{4,5},{5,4},{6,7},{7,6},{8,9},{9,8},{10,11... | collective-permute-start | bytes 1548296 | tf_op jit(solution)/shard_map/ppermute | solution.py:630
  15.3 0.0 copy-done.7
  15.3 0.0 copy-start.2
  15.3 0.0 copy-start.3
  15.4 0.0 copy-start.4
  15.4 0.0 copy-start.6
  15.4 0.0 collective-permute-done.2.halo_hbm.on_hbm
  15.4 6.2 %row.2 = (bf16[8,256,256]{2,1,0:T(8,128)(2,1)}, bf16[8,256,256]{2,1,0:T(8,128)(2,1)}, bf16[544,256]{1,0:T(8,128)(2,1)}, f32[384,256]{1,0:T(8,128)}) custom-call(s32[2]{0:T(128)S(1)} %pad_add_fusion.side_ref, bf16[1,8,512,256]{3,2,1,0:T(8,128)(2,1)S(1)} %copy-done, s32[4,128]{1,0:T(4,128)S(1)} %bitcast.10, bf16[3,3,256,256]{3,2,1,0:T(8,128)(2,1)} %weight_hbm.5, ...), custom_call_target="tpu_custom_call" | custom-call | flops 1207959552 | bytes 4194304 | tf_op jit(solution)/shard_map/row/pallas_call | solution.py:698
  21.6 4.2 %collective-permute-done.1.off_hbm.halo_hbm = bf16[1536,256]{1,0:T(8,128)(2,1)S(1)} collective-permute-done((bf16[1536,256]{1,0:T(8,128)(2,1)}, bf16[1536,256]{1,0:T(8,128)(2,1)S(1)}, u32[]{:S(2)}, u32[]{:S(2)}) %collective-permute-start.1) | collective-permute-done | bytes 786464 | tf_op jit(solution)/shard_map/ppermute | solution.py:626
  25.8 0.0 copy-done.1
  25.8 0.0 copy-done.2
  25.8 0.0 copy-done.3
  25.8 0.0 copy-done.4
  25.8 3.7 %surface.1 = (bf16[1,384,256]{2,1,0:T(8,128)(2,1)}, bf16[1,384,256]{2,1,0:T(8,128)(2,1)}, f32[128,256]{1,0:T(8,128)}, bf16[8,256,256]{2,1,0:T(8,128)(2,1)}, bf16[8,256,256]{2,1,0:T(8,128)(2,1)}) custom-call(s32[4,4]{1,0:T(4,128)S(1)} %subtract_clamp_fusion.ids_ref, s32[4]{0:T(128)S(1)} %copy-done.6, ...), custom_call_target="tpu_custom_call", output_to_operand_aliasing={{3}: (11, {}), {4}: (12, {})} | custom-call | flops 301989888 | bytes 2097152 | tf_op jit(solution)/shard_map/surface/pallas_call | solution.py:724
  29.6 1.6 %collective-permute-start.3 = (bf16[1,384,256]{2,1,0:T(8,128)(2,1)}, bf16[1,384,256]{2,1,0:T(8,128)(2,1)}, u32[]{:S(2)}, u32[]{:S(2)}) collective-permute-start(bf16[1,384,256]{2,1,0:T(8,128)(2,1)} %get-tuple-element.42.refs_0_), channel_id=1, source_target_pairs={{0,1},{1,0},{2,3},{3,2},{4,5},{5,4},{6,7},{7,6},{8,9},{9,8},{10,11... | collective-permute-start | bytes 589832 | tf_op jit(solution)/shard_map/ppermute | solution.py:630
  31.7 0.6 collective-permute-start.4
  32.3 5.2 %row.3 = (bf16[8,256,256]{2,1,0:T(8,128)(2,1)}, bf16[8,256,256]{2,1,0:T(8,128)(2,1)}, bf16[672,256]{1,0:T(8,128)(2,1)}) custom-call(s32[2]{0:T(128)S(1)} %pad_add_fusion.side_ref, bf16[1,8,512,256]{3,2,1,0:T(8,128)(2,1)S(1)} %copy-done, s32[4,128]{1,0:T(4,128)S(1)} %bitcast.12, ...), custom_call_target="tpu_custom_call", output_to_operand_aliasing={{0}: (6, {}), {1}: (7, {})} | custom-call | flops 1207959552 | bytes 4194304 | tf_op jit(solution)/shard_map/row/pallas_call | solution.py:698
  37.5 1.6 %collective-permute-start.5 = (bf16[672,256]{1,0:T(8,128)(2,1)}, bf16[672,256]{1,0:T(8,128)(2,1)S(1)}, u32[]{:S(2)}, u32[]{:S(2)}) collective-permute-start(bf16[672,256]{1,0:T(8,128)(2,1)} %get-tuple-element.44), channel_id=1, source_target_pairs={{0,1},{1,0},{2,3},{3,2},{4,5},{5,4},{6,7},{7,6},{8,9},{9,8},{10,11... | collective-permute-start | bytes 1032200 | tf_op jit(solution)/shard_map/ppermute | solution.py:630
  39.0 0.0 collective-permute-done.6.refs_5_
  39.0 0.0 collective-permute-done.3.refs_4_.refs_2_
  39.0 9.7 %attend.2.refs_9_ = bf16[1,8,512,256]{3,2,1,0:T(8,128)(2,1)} custom-call(s32[1]{0:T(128)} %get-tuple-element.31.flag_ref, s32[2]{0:T(128)S(1)} %pad_add_fusion.side_ref, bf16[1,384,256]{2,1,0:T(8,128)(2,1)} %get-tuple-element.42.refs_0_, bf16[7,256,256]{2,1,0:T(8,128)(2,1)} %get-tuple-element.45.refs_1_, bf16[1,384,256]{2,1,0:T(8,128)(2,1)} %get-tuple-element.47.refs_2_, ...), custom_call_target="tpu_custom_call" | custom-call | flops 4294967296 | bytes 5242880 | tf_op jit(solution)/shard_map/attend/pallas_call | solution.py:578
  48.7 0.0 collective-permute-done.4.refs_3_
  48.7 0.0 collective-permute-done.5.refs_4_
  48.8 9.5 %attend.3 = bf16[1,8,512,256]{3,2,1,0:T(8,128)(2,1)} custom-call(s32[1]{0:T(128)} %get-tuple-element.31.flag_ref, s32[2]{0:T(128)S(1)} %pad_add_fusion.side_ref, bf16[8,256,256]{2,1,0:T(8,128)(2,1)} %get-tuple-element.40.refs_0_, bf16[8,256,256]{2,1,0:T(8,128)(2,1)} %get-tuple-element.41.refs_1_, ...), custom_call_target="tpu_custom_call", output_to_operand_aliasing={{}: (11, {})} | custom-call | flops 4294967296 | bytes 5242880 | tf_op jit(solution)/shard_map/attend/pallas_call | solution.py:578
  (8 shorter events, 0.0 us)
Async XLA Ops:
  0.0 6.5 %copy-start = (bf16[1,8,512,256]{3,2,1,0:T(8,128)(2,1)S(1)}, bf16[1,8,512,256]{3,2,1,0:T(8,128)(2,1)}, u32[]{:S(2)}) copy-start(bf16[1,8,512,256]{3,2,1,0:T(8,128)(2,1)} %state.5) | copy-start | bytes 6291460
  0.0 6.5 %copy-start.5 = (s32[512]{0:T(512)S(1)}, s32[512]{0:T(512)}, u32[]{:S(2)}) copy-start(s32[512]{0:T(512)} %param.13) | copy-start | bytes 6148
  3.8 11.6 %collective-permute-start.2 = (bf16[1536,256]{1,0:T(8,128)(2,1)}, bf16[1536,256]{1,0:T(8,128)(2,1)}, u32[]{:S(2)}, u32[]{:S(2)}) collective-permute-start(bf16[1536,256]{1,0:T(8,128)(2,1)} %get-tuple-element.33), channel_id=1, source_target_pairs={{0,2},{4,6},{8,10},{12,14},{16,18},{20,22},{24,26},{28,30},{2,0},{... | collective-permute-start | bytes 2359304 | tf_op jit(solution)/shard_map/ppermute | solution.py:626
  3.8 11.5 %copy-start.7 = (s32[4,4]{1,0:T(4,128)S(1)}, s32[4,4]{1,0:T(4,128)}, u32[]{:S(2)}) copy-start(s32[4,4]{1,0:T(4,128)} %param.14) | copy-start | bytes 196
  3.9 21.9 %collective-permute-start.1 = (bf16[1536,256]{1,0:T(8,128)(2,1)}, bf16[1536,256]{1,0:T(8,128)(2,1)S(1)}, u32[]{:S(2)}, u32[]{:S(2)}) collective-permute-start(bf16[1536,256]{1,0:T(8,128)(2,1)} %get-tuple-element.32), channel_id=1, source_target_pairs={{2,4},{6,8},{10,12},{14,16},{18,20},{22,24},{26,28},{4,2},{8,6},{1... | collective-permute-start | bytes 2359304 | tf_op jit(solution)/shard_map/ppermute | solution.py:626
  13.7 25.3 %collective-permute-start.6 = (bf16[1008,256]{1,0:T(8,128)(2,1)}, bf16[1008,256]{1,0:T(8,128)(2,1)}, u32[]{:S(2)}, u32[]{:S(2)}) collective-permute-start(bf16[1008,256]{1,0:T(8,128)(2,1)} %get-tuple-element.49), channel_id=1, source_target_pairs={{0,1},{1,0},{2,3},{3,2},{4,5},{5,4},{6,7},{7,6},{8,9},{9,8},{10,11... | collective-permute-start | bytes 1548296 | tf_op jit(solution)/shard_map/ppermute | solution.py:630
  15.3 10.5 %copy-start.1 = (bf16[1,512,256]{2,1,0:T(8,128)(2,1)S(1)}, bf16[1,512,256]{2,1,0:T(8,128)(2,1)}, u32[]{:S(2)}) copy-start(bf16[1,512,256]{2,1,0:T(8,128)(2,1)} %atm_ref.1) | copy-start | bytes 786436
  15.3 10.5 %copy-start.2 = (bf16[4,4,128,128]{3,2,1,0:T(8,128)(2,1)S(1)}, bf16[4,4,128,128]{3,2,1,0:T(8,128)(2,1)}, u32[]{:S(2)}) copy-start(bf16[4,4,128,128]{3,2,1,0:T(8,128)(2,1)} %remap.1) | copy-start | bytes 1572868
  15.3 10.5 %copy-start.3 = (bf16[256,768]{1,0:T(8,128)(2,1)S(1)}, bf16[256,768]{1,0:T(8,128)(2,1)}, u32[]{:S(2)}) copy-start(bf16[256,768]{1,0:T(8,128)(2,1)} %refs_7_.1) | copy-start | bytes 1179652
  15.4 10.5 %copy-start.4 = (bf16[256,256]{1,0:T(8,128)(2,1)S(1)}, bf16[256,256]{1,0:T(8,128)(2,1)}, u32[]{:S(2)}) copy-start(bf16[256,256]{1,0:T(8,128)(2,1)} %refs_8_.3) | copy-start | bytes 393220
  15.4 10.5 %copy-start.6 = (s32[4]{0:T(128)S(1)}, s32[4]{0:T(128)}, u32[]{:S(2)}) copy-start(s32[4]{0:T(128)} %live_ref.1) | copy-start | bytes 52
  29.6 9.5 %collective-permute-start.3 = (bf16[1,384,256]{2,1,0:T(8,128)(2,1)}, bf16[1,384,256]{2,1,0:T(8,128)(2,1)}, u32[]{:S(2)}, u32[]{:S(2)}) collective-permute-start(bf16[1,384,256]{2,1,0:T(8,128)(2,1)} %get-tuple-element.42.refs_0_), channel_id=1, source_target_pairs={{0,1},{1,0},{2,3},{3,2},{4,5},{5,4},{6,7},{7,6},{8,9},{9,8},{10,11... | collective-permute-start | bytes 589832 | tf_op jit(solution)/shard_map/ppermute | solution.py:630
  31.7 17.0 %collective-permute-start.4 = (bf16[544,256]{1,0:T(8,128)(2,1)}, bf16[544,256]{1,0:T(8,128)(2,1)}, u32[]{:S(2)}, u32[]{:S(2)}) collective-permute-start(bf16[544,256]{1,0:T(8,128)(2,1)} %get-tuple-element.43), channel_id=1, source_target_pairs={{0,1},{1,0},{2,3},{3,2},{4,5},{5,4},{6,7},{7,6},{8,9},{9,8},{10,11... | collective-permute-start | bytes 835592 | tf_op jit(solution)/shard_map/ppermute | solution.py:630
  37.5 11.3 %collective-permute-start.5 = (bf16[672,256]{1,0:T(8,128)(2,1)}, bf16[672,256]{1,0:T(8,128)(2,1)S(1)}, u32[]{:S(2)}, u32[]{:S(2)}) collective-permute-start(bf16[672,256]{1,0:T(8,128)(2,1)} %get-tuple-element.44), channel_id=1, source_target_pairs={{0,1},{1,0},{2,3},{3,2},{4,5},{5,4},{6,7},{7,6},{8,9},{9,8},{10,11... | collective-permute-start | bytes 1032200 | tf_op jit(solution)/shard_map/ppermute | solution.py:630
